TPU v7x, 256 devices: a whole 4x4x8 slice. The times are simulated.
256 devices in a mesh: dp: 8 (over y, core), tm: 4 (over x), height: 8 (over z).
Axes of the slice: x: 4, y: 4, z: 8, core: 2. Of those that a mesh axis runs over, the one named last changes fastest.
Arguments:
- video_latents: bfloat16 [8, 8, 64, 128, 256], P('dp', 'tm', 'height'), may hold values from -48 to 48
- cotangent: bfloat16 [8, 8, 64, 128, 256], P('dp', 'tm', 'height'), may hold values from -48 to 48
- spatial_kernel: bfloat16 [3, 3, 256, 256], replicated, may hold values from -0.125 to 0.125
- temporal_kernel: bfloat16 [3, 256, 256], replicated, may hold values from -0.21875 to 0.21875
Outputs:
- block_output: bfloat16 [8, 8, 64, 128, 256], P('dp', 'tm', 'height')
- input_grad: bfloat16 [8, 8, 64, 128, 256], P('dp', 'tm', 'height')
- clipped_spatial: float32 [3, 3, 256, 256], replicated
- clipped_temporal: float32 [3, 256, 256], replicated
All inputs are finite; a program needn't handle non-finite values.
Results may differ from a plain program's by a relative error of at most 0.0018.
The roundings to bfloat16 on the way count: a program that leaves them out, or rounds other values in their place, can miss the bound.
Values may be sent and summed in bfloat16 or wider, within the bound.
No kernel may reach another device: no remote copies, remote signals or barrier semaphores. Data moves between devices by JAX's collectives and lax.ppermute only.
A program may use at most 128 MiB of HBM per device.

v0:
```python
import math

import jax
import jax.numpy as jnp
from jax import lax
from jax.sharding import Mesh
from jax.sharding import PartitionSpec as P

GROUPS = 32
DP = ("dp_0", "dp_1")


EPSILON = 1e-05
CLIP_DIVISOR = 20.0


def from_everyone(x, axis):
    copies = jnp.broadcast_to(x, (lax.axis_size(axis), *x.shape))
    return lax.all_to_all(copies, axis, split_axis=0, concat_axis=0, tiled=True)


def of_everyone(x, axis):
    return from_everyone(x, axis).sum(axis=0)


def together(arrays, axis):
    ends = [0]
    for a in arrays:
        ends.append(ends[-1] + a.size)
    subtotal = of_everyone(jnp.concatenate([a.ravel() for a in arrays]), axis)
    return tuple((subtotal[b:e].reshape(a.shape) for a, b, e in zip(arrays, ends, ends[1:])))


def extended_2(x, sides, width):
    for axis, dim in sides:
        peers, length = (lax.axis_size(axis), x.shape[dim])
        up = [(i, (i + 1) % peers) for i in range(peers - 1)]
        down = [(j, i) for i, j in up]
        last = lax.slice_in_dim(x, length - width, length, axis=dim)
        initial = lax.slice_in_dim(x, 0, width, axis=dim)
        before = lax.ppermute(last, axis, up)
        after = lax.ppermute(initial, axis, down)
        x = jnp.concatenate([before, x, after], axis=dim)
    return x


def shifted_2(block, axis, distance):
    devices = range(lax.axis_size(axis))
    route = [(i - distance, i) for i in devices if i - distance in devices]
    return lax.ppermute(block, axis, route)


def split_up(x, dim, peers):
    before, after = (x.shape[:dim], x.shape[dim + 1 :])
    return jnp.moveaxis(x.reshape(*before, peers, -1, *after), dim, 0)


def sum_at_owner(x, axis, dim):
    peers = lax.axis_size(axis)
    pieces = lax.all_to_all(split_up(x, dim, peers), axis, 0, 0, tiled=True)
    return jnp.sum(pieces, axis=0)


def sum_by_axis(x, axes, dim):
    far, near = axes
    own = sum_at_owner(split_up(x, dim, lax.axis_size(far)), near, dim + 1)
    return jnp.sum(lax.all_to_all(own, far, 0, 0, tiled=True), axis=0)


def rows_for(lines, peers):
    spare = -len(lines) % peers
    return jnp.pad(lines, [(0, spare)] + [(0, 0)] * (lines.ndim - 1))


def joined_along(pieces, dim):
    pieces = jnp.moveaxis(pieces, 0, dim)
    shape = pieces.shape
    return pieces.reshape(*shape[:dim], shape[dim] * shape[dim + 1], *shape[dim + 2 :])


def gathered_by_axis(x, axes, dim):
    far, near = axes
    pieces = from_everyone(from_everyone(x, far), near)
    return joined_along(pieces.swapaxes(0, 1).reshape(-1, *x.shape), dim)


def sum_by_parts(x, axes):
    own = sum_by_axis(rows_for(x, lax.axis_size(axes[0]) * lax.axis_size(axes[1])), axes, 0)
    whole = gathered_by_axis(own, axes, 0)
    return whole[: len(x)].reshape(x.shape)


def packed_total(arrays, axis):
    ravelled, at, done = (jnp.concatenate([a.reshape(-1) for a in arrays]), 0, [])
    subtotal = sum_by_parts(ravelled, axis)
    for a in arrays:
        done.append(subtotal[at : at + a.size].reshape(a.shape))
        at += a.size
    return tuple(done)


def silu_slope(values):
    sigmoid = jax.nn.sigmoid(values)
    return sigmoid * (1.0 + values * (1.0 - sigmoid))


def clip_pair(spatial_total, temporal_total, clip_level):
    squares = jnp.sum(spatial_total * spatial_total) + jnp.sum(temporal_total * temporal_total)
    scale = clip_level / jnp.maximum(jnp.sqrt(squares), clip_level)
    return (spatial_total * scale, temporal_total * scale)


def body(video_latents, cotangent, spatial_kernel, temporal_kernel):
    batch, frames, height_rows, columns, channels = video_latents.shape
    group_width = channels // GROUPS
    members = height_rows * lax.axis_size("height") * columns * group_width
    clip_level = (
        channels
        * height_rows
        * lax.axis_size("height")
        * columns
        * math.sqrt(batch * lax.axis_size(DP) * frames * lax.axis_size("tm"))
        / CLIP_DIVISOR
    )
    latents = video_latents.astype(jnp.float32)
    grouped = latents.reshape(batch, frames, height_rows, columns, GROUPS, group_width)
    first_sum = jnp.sum(grouped, axis=(2, 3, 5), keepdims=True)
    second_sum = jnp.sum(grouped * grouped, axis=(2, 3, 5), keepdims=True)
    first_sum, second_sum = together((first_sum, second_sum), "height")
    mean_value = first_sum / members
    inverse_std = lax.rsqrt(second_sum / members - mean_value * mean_value + EPSILON)
    normed_grouped = (grouped - mean_value) * inverse_std
    normed = normed_grouped.reshape(latents.shape)
    activated = jax.nn.silu(normed).astype(jnp.bfloat16)
    row_padded = extended_2(activated, (("height", 2),), 1)
    padded = jnp.pad(row_padded, ((0, 0), (0, 0), (0, 0), (1, 1), (0, 0)))
    spatial_pre = jnp.zeros(latents.shape, jnp.float32)
    for tap_row in range(3):
        for tap_col in range(3):
            window = padded[:, :, tap_row : tap_row + height_rows, tap_col : tap_col + columns]
            spatial_pre = spatial_pre + jnp.einsum(
                "bfhwc,cd->bfhwd",
                window,
                spatial_kernel[tap_row, tap_col],
                preferred_element_type=jnp.float32,
            )
    hidden = jax.nn.silu(spatial_pre).astype(jnp.bfloat16)
    earlier = shifted_2(hidden, "tm", 1)
    extended = jnp.concatenate((earlier, hidden), axis=1)
    temporal_sum = jnp.zeros(latents.shape, jnp.float32)
    for tap in range(3):
        temporal_sum = temporal_sum + jnp.einsum(
            "bfhwc,cd->bfhwd",
            extended[:, tap : tap + frames],
            temporal_kernel[tap],
            preferred_element_type=jnp.float32,
        )
    block_output = (latents + temporal_sum).astype(jnp.bfloat16)
    later = shifted_2(cotangent, "tm", -1)
    cot_extended = jnp.concatenate((cotangent, later), axis=1)
    hidden_grad = jnp.zeros(latents.shape, jnp.float32)
    for tap in range(3):
        hidden_grad = hidden_grad + jnp.einsum(
            "bfhwd,cd->bfhwc",
            cot_extended[:, 2 - tap : 2 - tap + frames],
            temporal_kernel[tap],
            preferred_element_type=jnp.float32,
        )
    temporal_grad = jnp.stack(
        [
            jnp.einsum(
                "bfhwc,bfhwd->cd",
                extended[:, tap : tap + frames],
                cotangent,
                preferred_element_type=jnp.float32,
            )
            for tap in range(3)
        ]
    )
    pre_grad = (hidden_grad * silu_slope(spatial_pre)).astype(jnp.bfloat16)
    grad_rows = extended_2(pre_grad, (("height", 2),), 1)
    grad_padded = jnp.pad(grad_rows, ((0, 0), (0, 0), (0, 0), (1, 1), (0, 0)))
    act_grad = jnp.zeros(latents.shape, jnp.float32)
    spatial_list = []
    for tap_row in range(3):
        for tap_col in range(3):
            shifted = grad_padded[
                :, :, 2 - tap_row : 2 - tap_row + height_rows, 2 - tap_col : 2 - tap_col + columns
            ]
            act_grad = act_grad + jnp.einsum(
                "bfhwd,cd->bfhwc",
                shifted,
                spatial_kernel[tap_row, tap_col],
                preferred_element_type=jnp.float32,
            )
            window = padded[:, :, tap_row : tap_row + height_rows, tap_col : tap_col + columns]
            spatial_list.append(
                jnp.einsum("bfhwc,bfhwd->cd", window, pre_grad, preferred_element_type=jnp.float32)
            )
    spatial_grad = jnp.stack(spatial_list).reshape(3, 3, channels, channels)
    norm_grad = (act_grad * silu_slope(normed)).reshape(grouped.shape)
    grad_first = jnp.sum(norm_grad, axis=(2, 3, 5), keepdims=True)
    grad_second = jnp.sum(norm_grad * normed_grouped, axis=(2, 3, 5), keepdims=True)
    grad_first, grad_second = together((grad_first, grad_second), "height")
    input_term = inverse_std * (
        norm_grad - grad_first / members - normed_grouped * (grad_second / members)
    )
    input_grad = (cotangent.astype(jnp.float32) + input_term.reshape(latents.shape)).astype(
        jnp.bfloat16
    )
    spatial_total, temporal_total = packed_total(
        (spatial_grad, temporal_grad), (("dp_0", "dp_1"), ("tm", "height"))
    )
    clipped_spatial, clipped_temporal = clip_pair(spatial_total, temporal_total, clip_level)
    return (block_output, input_grad, clipped_spatial, clipped_temporal)


def solution(mesh):
    torus = Mesh(
        mesh.devices.reshape(4, 2, mesh.shape["tm"], mesh.shape["height"]),
        ("dp_0", "dp_1", "tm", "height"),
    )
    in_specs = (P(DP, "tm", "height", None, None), P(DP, "tm", "height", None, None), P(), P())
    out_specs = (P(DP, "tm", "height", None, None), P(DP, "tm", "height", None, None), P(), P())
    return jax.shard_map(body, mesh=torus, in_specs=in_specs, out_specs=out_specs, check_vma=False)
```

profile of v0, /device:TPU:1, one launch (start us, length us, event | category | flops | bytes accessed | tf_op | source)
XLA Modules:
  0.0 305.5 jit_solution(17290625596675470217)
XLA Ops:
  0.6 1.6 convert_reduce_fusion
  3.5 9.0 %all-to-all-start = ((f32[8,1,128]{2,1,0:T(1,128)}), f32[8,1,128]{2,1,0:T(1,128)S(1)}, u32[]{:S(2)}, u32[]{:S(2)}) async-start(f32[8,1,128]{2,1,0:T(1,128)} %broadcast_in_dim.12), calls=%async_computation | async-start | bytes 8192 | tf_op jit(solution)/shard_map/all_to_all | solution.py:19
  12.5 1.4 collective-permute-start.3
  13.9 2.7 fusion.60
  16.6 2.3 all-to-all-done
  20.2 2.2 collective-permute-start
  22.4 1.3 collective-permute-start.1
  24.3 4.2 %collective-permute-done.1 = bf16[1,2,1,128,256]{4,3,2,1,0:T(8,128)(2,1)S(1)} collective-permute-done((bf16[1,2,1,128,256]{4,3,2,1,0:T(8,128)(2,1)S(1)}, bf16[1,2,1,128,256]{4,3,2,1,0:T(8,128)(2,1)S(1)}, u32[]{:S(2)}, u32[]{:S(2)}) %collective-permute-start.1) | collective-permute-done | bytes 131104 | tf_op jit(solution)/shard_map/ppermute | solution.py:42
  32.3 2.1 multiply_convert_fusion.1
  34.4 3.5 %collective-permute-start.2 = (bf16[1,2,8,128,256]{4,3,2,1,0:T(8,128)(2,1)S(1)}, bf16[1,2,8,128,256]{4,3,2,1,0:T(8,128)(2,1)S(1)}, u32[]{:S(2)}, u32[]{:S(2)}) collective-permute-start(bf16[1,2,8,128,256]{4,3,2,1,0:T(8,128)(2,1)S(1)} %bitcast.352), channel_id=1, source_target_pairs={{0,8},{8,16},{16,24},{1,9},{9,17},{17,25},{2,10},{10,18},{18,26},{... | collective-permute-start | bytes 3145736 | tf_op jit(solution)/shard_map/ppermute | solution.py:50
  38.6 1.6 fusion.51
  40.2 2.3 multiply_convert_fusion
  47.2 1.2 copy.144
  48.4 8.7 %collective-permute-done.2 = bf16[1,2,8,128,256]{4,3,2,1,0:T(8,128)(2,1)S(1)} collective-permute-done((bf16[1,2,8,128,256]{4,3,2,1,0:T(8,128)(2,1)S(1)}, bf16[1,2,8,128,256]{4,3,2,1,0:T(8,128)(2,1)S(1)}, u32[]{:S(2)}, u32[]{:S(2)}) %collective-permute-start.2) | collective-permute-done | bytes 1048608 | tf_op jit(solution)/shard_map/ppermute | solution.py:50
  58.5 1.9 pad_maximum_fusion
  60.4 4.5 %reshape_reshape.8 = f32[8,32,3072]{2,1,0:T(8,128)} reshape(f32[786432]{0:T(1024)} %pad_maximum_fusion) | data formatting | bytes 6291456 | tf_op jit(solution)/shard_map/reshape;reshape | solution.py:55
  65.0 5.4 %copy.105 = f32[32,8,3072]{2,1,0:T(8,128)} copy(f32[32,8,3072]{2,0,1:T(8,128)} %bitcast.359) | data formatting | bytes 6291456 | tf_op jit(solution)/shard_map/transpose | solution.py:55
  70.3 11.1 %all-to-all-start.2 = ((f32[32,8,3072]{2,1,0:T(8,128)}), f32[32,8,3072]{2,1,0:T(8,128)}, u32[]{:S(2)}, u32[]{:S(2)}) async-start(f32[32,8,3072]{2,1,0:T(8,128)} %copy.105), calls=%async_computation.2 | async-start | bytes 6291456 | tf_op jit(solution)/shard_map/all_to_all | solution.py:60
  81.5 1.3 collective-permute-start.5
  82.8 4.2 %collective-permute-start.4 = (bf16[1,2,1,128,256]{4,3,2,1,0:T(8,128)(2,1)S(1)}, bf16[1,2,1,128,256]{4,3,2,1,0:T(8,128)(2,1)S(1)}, u32[]{:S(2)}, u32[]{:S(2)}) collective-permute-start(bf16[1,2,1,128,256]{4,3,2,1,0:T(8,128)(2,1)S(1)} %get-tuple-element.6), channel_id=1, source_target_pairs={{0,1},{1,2},{2,3},{3,4},{4,5},{5,6},{6,7},{8,9},{9,10},{10,11},{11... | collective-permute-start | bytes 393224 | tf_op jit(solution)/shard_map/ppermute | solution.py:41
  87.0 2.7 fusion.90
  89.7 61.4 %collective-permute-done.5 = bf16[1,2,1,128,256]{4,3,2,1,0:T(8,128)(2,1)S(1)} collective-permute-done((bf16[1,2,1,128,256]{4,3,2,1,0:T(8,128)(2,1)S(1)}, bf16[1,2,1,128,256]{4,3,2,1,0:T(8,128)(2,1)S(1)}, u32[]{:S(2)}, u32[]{:S(2)}) %collective-permute-start.5) | collective-permute-done | bytes 131104 | tf_op jit(solution)/shard_map/ppermute | solution.py:42
  151.8 1.9 fusion.46
  153.7 1.8 fusion.37
  155.4 1.8 fusion.41
  157.2 1.8 fusion.42
  159.0 1.9 fusion.43
  160.8 1.8 fusion.44
  162.6 1.8 fusion.49
  164.5 2.7 reduce_sum.132
  167.1 1.6 all_to_all.29
  168.7 8.0 %all-to-all-start.3 = ((f32[8,1,3072]{2,1,0:T(1,128)}), f32[8,1,3072]{2,1,0:T(1,128)}, u32[]{:S(2)}, u32[]{:S(2)}) async-start(f32[8,1,3072]{2,1,0:T(1,128)} %all_to_all.29), calls=%async_computation.3 | async-start | bytes 196608 | tf_op jit(solution)/shard_map/all_to_all | solution.py:67
  176.8 9.3 %fusion.11 = (f32[2,256]{1,0:T(2,128)S(1)}, f32[2,8,128,256]{3,2,1,0:T(8,128)}) fusion(bf16[1,2,8,128,256]{4,3,2,1,0:T(8,128)(2,1)} %param.4, f32[2,256]{1,0:T(2,128)S(1)} %mul.136, f32[2,256]{1,0:T(2,128)S(1)} %sub.68, f32[2,8,128,256]{3,2,1,0:T(8,128)} %fusion.37, bf16[3,3,256,256]{3,2,1,0:T(8,128)(2,1)} %param.6, ...), kind=kOutput, calls=%fused_computation.22 | convolution fusion | flops 281017856 | bytes 21243904 | tf_op jit(solution)/shard_map/bfhwd,cd->bfhwc/dot_general | solution.py:190
  186.1 1.8 reduce_sum.125
  190.1 4.8 %all-to-all-start.4 = ((f32[8,1,3072]{2,1,0:T(1,128)}), f32[8,1,3072]{2,1,0:T(1,128)S(1)}, u32[]{:S(2)}, u32[]{:S(2)}) async-start(f32[8,1,3072]{2,1,0:T(1,128)} %broadcast_in_dim.14), calls=%async_computation.4 | async-start | bytes 196608 | tf_op jit(solution)/shard_map/all_to_all | solution.py:19
  194.9 4.9 %all-to-all-done.4 = f32[8,1,3072]{2,1,0:T(1,128)S(1)} async-done(((f32[8,1,3072]{2,1,0:T(1,128)}), f32[8,1,3072]{2,1,0:T(1,128)S(1)}, u32[]{:S(2)}, u32[]{:S(2)}) %all-to-all-start.4) | async-done | bytes 98336 | tf_op jit(solution)/shard_map/all_to_all | solution.py:19
  200.4 5.4 %all-to-all-start.1 = ((f32[8,1,128]{2,1,0:T(1,128)}), f32[8,1,128]{2,1,0:T(1,128)S(1)}, u32[]{:S(2)}, u32[]{:S(2)}) async-start(f32[8,1,128]{2,1,0:T(1,128)} %broadcast_in_dim.13), calls=%async_computation.1 | async-start | bytes 8192 | tf_op jit(solution)/shard_map/all_to_all | solution.py:19
  205.9 6.5 %all-to-all-done.1 = f32[8,1,128]{2,1,0:T(1,128)S(1)} async-done(((f32[8,1,128]{2,1,0:T(1,128)}), f32[8,1,128]{2,1,0:T(1,128)S(1)}, u32[]{:S(2)}, u32[]{:S(2)}) %all-to-all-start.1) | async-done | bytes 4128 | tf_op jit(solution)/shard_map/all_to_all | solution.py:19
  212.3 2.1 broadcast_in_dim.15
  214.4 5.1 %all-to-all-start.5 = ((f32[32,8,3072]{2,1,0:T(8,128)}), f32[32,8,3072]{2,1,0:T(8,128)}, u32[]{:S(2)}, u32[]{:S(2)}) async-start(f32[32,8,3072]{2,1,0:T(8,128)} %broadcast_in_dim.15), calls=%async_computation.5 | async-start | bytes 6291456 | tf_op jit(solution)/shard_map/all_to_all | solution.py:19
  219.5 1.7 fusion.102
  226.4 3.3 %fusion.15 = bf16[1,2,8,128,256]{4,3,2,1,0:T(8,128)(2,1)} fusion(bf16[1,2,8,128,256]{4,3,2,1,0:T(8,128)(2,1)S(1)} %copy-done.2, f32[2,8,128,256]{3,2,1,0:T(8,128)} %get-tuple-element.17, bf16[1,2,8,128,256]{4,3,2,1,0:T(8,128)(2,1)S(1)} %copy-done, f32[2,256]{1,0:T(2,128)S(1)} %mul.152, f32[2,256]{1,0:T(2,128)S(1)} %sub.77, f32[2,256]{1,0:T(2,128)S(1)} %mul.136, ...), kind=kLoop, calls=%fused_computation.26 | loop fusion | flops 5242880 | bytes 5251072 | tf_op jit(solution)/shard_map/convert_element_type | solution.py:208
  231.3 1.5 fusion.16
  232.8 57.4 %all-to-all-done.5 = f32[32,8,3072]{2,1,0:T(8,128)} async-done(((f32[32,8,3072]{2,1,0:T(8,128)}), f32[32,8,3072]{2,1,0:T(8,128)}, u32[]{:S(2)}, u32[]{:S(2)}) %all-to-all-start.5) | async-done | bytes 3145760 | tf_op jit(solution)/shard_map/all_to_all | solution.py:19
  290.2 3.7 %copy.148 = f32[32,8,3072]{2,0,1:T(8,128)S(1)} copy(f32[32,8,3072]{2,1,0:T(8,128)} %all-to-all-done.5) | data formatting | bytes 6291456 | tf_op jit(solution)/shard_map/all_to_all | solution.py:19
  298.2 1.6 slice_multiply_fusion
  299.8 2.2 mul.163
  302.1 3.5 %mul.160 = f32[3,3,256,256]{3,2,1,0:T(8,128)} reshape(f32[6,32,3072]{2,1,0:T(8,128)} %slice_multiply_fusion) | data formatting | bytes 4718592 | tf_op jit(solution)/shard_map/mul | solution.py:110
  (94 shorter events, 26.7 us)
Async XLA Ops:
  0.6 13.3 %copy-start = (bf16[1,2,8,128,256]{4,3,2,1,0:T(8,128)(2,1)S(1)}, bf16[1,2,8,128,256]{4,3,2,1,0:T(8,128)(2,1)}, u32[]{:S(2)}) copy-start(bf16[1,2,8,128,256]{4,3,2,1,0:T(8,128)(2,1)} %param.5) | copy-start | bytes 3145732
  3.5 15.5 %all-to-all-start = ((f32[8,1,128]{2,1,0:T(1,128)}), f32[8,1,128]{2,1,0:T(1,128)S(1)}, u32[]{:S(2)}, u32[]{:S(2)}) async-start(f32[8,1,128]{2,1,0:T(1,128)} %broadcast_in_dim.12), calls=%async_computation | async-start | bytes 8192 | tf_op jit(solution)/shard_map/all_to_all | solution.py:19
  12.5 7.1 %copy-start.1 = (bf16[1,2,8,128,256]{4,3,2,1,0:T(8,128)(2,1)S(1)}, bf16[1,2,8,128,256]{4,3,2,1,0:T(8,128)(2,1)}, u32[]{:S(2)}) copy-start(bf16[1,2,8,128,256]{4,3,2,1,0:T(8,128)(2,1)} %param.4) | copy-start | bytes 3145732
  12.5 26.1 %collective-permute-start.3 = (bf16[1,2,8,128,256]{4,3,2,1,0:T(8,128)(2,1)}, bf16[1,2,8,128,256]{4,3,2,1,0:T(8,128)(2,1)}, u32[]{:S(2)}, u32[]{:S(2)}) collective-permute-start(bf16[1,2,8,128,256]{4,3,2,1,0:T(8,128)(2,1)} %param.5), channel_id=1, source_target_pairs={{8,0},{16,8},{24,16},{9,1},{17,9},{25,17},{10,2},{18,10},{26,18},{... | collective-permute-start | bytes 3145736 | tf_op jit(solution)/shard_map/ppermute | solution.py:50
  16.6 7.1 %copy-start.7 = (bf16[3,3,256,256]{3,2,1,0:T(8,128)(2,1)S(1)}, bf16[3,3,256,256]{3,2,1,0:T(8,128)(2,1)}, u32[]{:S(2)}) copy-start(bf16[3,3,256,256]{3,2,1,0:T(8,128)(2,1)} %param.6) | copy-start | bytes 3538948
  20.2 4.1 %collective-permute-start = (bf16[1,2,1,128,256]{4,3,2,1,0:T(8,128)(2,1)S(1)}, bf16[1,2,1,128,256]{4,3,2,1,0:T(8,128)(2,1)S(1)}, u32[]{:S(2)}, u32[]{:S(2)}) collective-permute-start(bf16[1,2,1,128,256]{4,3,2,1,0:T(8,128)(2,1)S(1)} %get-tuple-element.8), channel_id=1, source_target_pairs={{0,1},{1,2},{2,3},{3,4},{4,5},{5,6},{6,7},{8,9},{9,10},{10,11},{11... | collective-permute-start | bytes 393224 | tf_op jit(solution)/shard_map/ppermute | solution.py:41
  22.4 6.1 %collective-permute-start.1 = (bf16[1,2,1,128,256]{4,3,2,1,0:T(8,128)(2,1)S(1)}, bf16[1,2,1,128,256]{4,3,2,1,0:T(8,128)(2,1)S(1)}, u32[]{:S(2)}, u32[]{:S(2)}) collective-permute-start(bf16[1,2,1,128,256]{4,3,2,1,0:T(8,128)(2,1)S(1)} %get-tuple-element.9), channel_id=1, source_target_pairs={{1,0},{2,1},{3,2},{4,3},{5,4},{6,5},{7,6},{9,8},{10,9},{11,10},{12... | collective-permute-start | bytes 393224 | tf_op jit(solution)/shard_map/ppermute | solution.py:42
  34.4 4.2 %copy-start.9 = (bf16[3,256,256]{2,1,0:T(8,128)(2,1)S(1)}, bf16[3,256,256]{2,1,0:T(8,128)(2,1)}, u32[]{:S(2)}) copy-start(bf16[3,256,256]{2,1,0:T(8,128)(2,1)} %param.7) | copy-start | bytes 1179652
  34.4 22.6 %collective-permute-start.2 = (bf16[1,2,8,128,256]{4,3,2,1,0:T(8,128)(2,1)S(1)}, bf16[1,2,8,128,256]{4,3,2,1,0:T(8,128)(2,1)S(1)}, u32[]{:S(2)}, u32[]{:S(2)}) collective-permute-start(bf16[1,2,8,128,256]{4,3,2,1,0:T(8,128)(2,1)S(1)} %bitcast.352), channel_id=1, source_target_pairs={{0,8},{8,16},{16,24},{1,9},{9,17},{17,25},{2,10},{10,18},{18,26},{... | collective-permute-start | bytes 3145736 | tf_op jit(solution)/shard_map/ppermute | solution.py:50
  38.4 1.8 copy-start.6
  57.1 1.0 copy-start.3
  70.3 94.1 %all-to-all-start.2 = ((f32[32,8,3072]{2,1,0:T(8,128)}), f32[32,8,3072]{2,1,0:T(8,128)}, u32[]{:S(2)}, u32[]{:S(2)}) async-start(f32[32,8,3072]{2,1,0:T(8,128)} %copy.105), calls=%async_computation.2 | async-start | bytes 6291456 | tf_op jit(solution)/shard_map/all_to_all | solution.py:60
  81.5 69.6 %collective-permute-start.5 = (bf16[1,2,1,128,256]{4,3,2,1,0:T(8,128)(2,1)S(1)}, bf16[1,2,1,128,256]{4,3,2,1,0:T(8,128)(2,1)S(1)}, u32[]{:S(2)}, u32[]{:S(2)}) collective-permute-start(bf16[1,2,1,128,256]{4,3,2,1,0:T(8,128)(2,1)S(1)} %get-tuple-element.7), channel_id=1, source_target_pairs={{1,0},{2,1},{3,2},{4,3},{5,4},{6,5},{7,6},{9,8},{10,9},{11,10},{12... | collective-permute-start | bytes 393224 | tf_op jit(solution)/shard_map/ppermute | solution.py:42
  82.8 68.3 %collective-permute-start.4 = (bf16[1,2,1,128,256]{4,3,2,1,0:T(8,128)(2,1)S(1)}, bf16[1,2,1,128,256]{4,3,2,1,0:T(8,128)(2,1)S(1)}, u32[]{:S(2)}, u32[]{:S(2)}) collective-permute-start(bf16[1,2,1,128,256]{4,3,2,1,0:T(8,128)(2,1)S(1)} %get-tuple-element.6), channel_id=1, source_target_pairs={{0,1},{1,2},{2,3},{3,4},{4,5},{5,6},{6,7},{8,9},{9,10},{10,11},{11... | collective-permute-start | bytes 393224 | tf_op jit(solution)/shard_map/ppermute | solution.py:41
  89.7 62.1 %copy-start.8 = (bf16[3,3,256,256]{3,2,1,0:T(8,128)(2,1)S(1)}, bf16[3,3,256,256]{3,2,1,0:T(8,128)(2,1)}, u32[]{:S(2)}) copy-start(bf16[3,3,256,256]{3,2,1,0:T(8,128)(2,1)} %param.6) | copy-start | bytes 3538948
  151.1 2.6 copy-start.10
  168.7 19.7 %all-to-all-start.3 = ((f32[8,1,3072]{2,1,0:T(1,128)}), f32[8,1,3072]{2,1,0:T(1,128)}, u32[]{:S(2)}, u32[]{:S(2)}) async-start(f32[8,1,3072]{2,1,0:T(1,128)} %all_to_all.29), calls=%async_computation.3 | async-start | bytes 196608 | tf_op jit(solution)/shard_map/all_to_all | solution.py:67
  190.1 9.8 %all-to-all-start.4 = ((f32[8,1,3072]{2,1,0:T(1,128)}), f32[8,1,3072]{2,1,0:T(1,128)S(1)}, u32[]{:S(2)}, u32[]{:S(2)}) async-start(f32[8,1,3072]{2,1,0:T(1,128)} %broadcast_in_dim.14), calls=%async_computation.4 | async-start | bytes 196608 | tf_op jit(solution)/shard_map/all_to_all | solution.py:19
  200.4 11.9 %all-to-all-start.1 = ((f32[8,1,128]{2,1,0:T(1,128)}), f32[8,1,128]{2,1,0:T(1,128)S(1)}, u32[]{:S(2)}, u32[]{:S(2)}) async-start(f32[8,1,128]{2,1,0:T(1,128)} %broadcast_in_dim.13), calls=%async_computation.1 | async-start | bytes 8192 | tf_op jit(solution)/shard_map/all_to_all | solution.py:19
  214.4 75.8 %all-to-all-start.5 = ((f32[32,8,3072]{2,1,0:T(8,128)}), f32[32,8,3072]{2,1,0:T(8,128)}, u32[]{:S(2)}, u32[]{:S(2)}) async-start(f32[32,8,3072]{2,1,0:T(8,128)} %broadcast_in_dim.15), calls=%async_computation.5 | async-start | bytes 6291456 | tf_op jit(solution)/shard_map/all_to_all | solution.py:19
  219.5 6.9 %copy-start.2 = (bf16[1,2,8,128,256]{4,3,2,1,0:T(8,128)(2,1)S(1)}, bf16[1,2,8,128,256]{4,3,2,1,0:T(8,128)(2,1)}, u32[]{:S(2)}) copy-start(bf16[1,2,8,128,256]{4,3,2,1,0:T(8,128)(2,1)} %param.4) | copy-start | bytes 3145732
  226.4 3.3 %copy-start.4 = (bf16[1,2,8,128,256]{4,3,2,1,0:T(8,128)(2,1)S(1)}, bf16[1,2,8,128,256]{4,3,2,1,0:T(8,128)(2,1)}, u32[]{:S(2)}) copy-start(bf16[1,2,8,128,256]{4,3,2,1,0:T(8,128)(2,1)} %copy-done.3) | copy-start | bytes 3145732
  229.7 1.6 copy-start.5
where the time goes:
time: 309 us; the launch traced here: 306 us
  waiting for transfers between devices  146 us (47%)
  starting transfers between devices  57.3 us (19%)
  matrix products  46.6 us (15%)
  local copies, waits for them, and re-layouts  33.5 us (11%)
  other arithmetic  20 us (6%)
    all_to_all x4, waiting for transfers between devices, from_everyone(): return lax.all_to_all(copies, axis, split_axis=0, concat_axis=0, tiled=True)  71.1 us
    ppermute x2, waiting for transfers between devices, extended_2(): after = lax.ppermute(initial, axis, down)  65.5 us
    dot_general x9, matrix products, body(): jnp.einsum('bfhwd,cd->bfhwc', shifted, spatial_kernel[tap_row, tap_col],...  24.7 us
    all_to_all x4, starting transfers between devices, from_everyone(): return lax.all_to_all(copies, axis, split_axis=0, concat_axis=0, tiled=True)  24.3 us
    all_to_all x1, starting transfers between devices, sum_at_owner(): pieces = lax.all_to_all(split_up(x, dim, peers), axis, 0, 0, tiled=True)  11.1 us
    ppermute x2, waiting for transfers between devices, shifted_2(): return lax.ppermute(block, axis, route)  8.83 us
    all_to_all x1, starting transfers between devices, sum_by_axis(): return jnp.sum(lax.all_to_all(own, far, 0, 0, tiled=True), axis=0)  8.02 us
    dot_general x3, matrix products, body(): jnp.einsum('bfhwd,cd->bfhwc', cot_extended[:, 2 - tap:2 - tap + frames],...  6.63 us
  transfers between devices with their start and end apart: 12, of which 9 were waited for; matrix products, arithmetic and copies ran while one was open for 20% of the time, Pallas kernels for 0%

commit v1 on v0

v1 whole, which is shorter than its diff:
```python
import math

import jax
import jax.numpy as jnp
from jax import lax
from jax.experimental import pallas as pl
from jax.experimental.pallas import tpu as pltpu
from jax.sharding import Mesh
from jax.sharding import PartitionSpec as P

GROUPS = 32
EPSILON = 1e-05
CLIP_DIVISOR = 20.0
F32 = jnp.float32
BF16 = jnp.bfloat16
DP = ("yh", "yl", "core")
TM = ("xh", "xl")
HEIGHT = ("zh", "zl")
REST = ("yh", "xh", "zh")
ORDERS = (("xl", "yl", "zl"), ("yl", "zl", "xl"), ("zl", "xl", "yl"))
VMEM = pl.BlockSpec(memory_space=pltpu.VMEM)
SMEM = pl.BlockSpec(memory_space=pltpu.SMEM)
NT = (((1,), (1,)), ((), ()))
TN = (((0,), (0,)), ((), ()))


def call(kernel, outs, args, flops, scratch=(), smem=0, limit=40):
    nbytes = sum(a.size * a.dtype.itemsize for a in (*args, *outs))
    specs = [SMEM] * smem + [VMEM] * (len(args) - smem)
    return pl.pallas_call(
        kernel,
        out_shape=tuple(outs),
        in_specs=specs,
        out_specs=tuple(VMEM for _ in outs),
        scratch_shapes=list(scratch),
        compiler_params=pltpu.CompilerParams(vmem_limit_bytes=limit << 20),
        cost_estimate=pl.CostEstimate(flops=flops, bytes_accessed=nbytes, transcendentals=0),
    )(*args)


def out(shape, dtype):
    return jax.ShapeDtypeStruct(shape, dtype)


def dot(a, b, dims=None):
    if dims is None:
        return jnp.dot(a, b, preferred_element_type=F32)
    return lax.dot_general(a, b, dims, preferred_element_type=F32)


def sigmoid(v):
    return 1.0 / (1.0 + jnp.exp(-v))


def store_stats(o_ref, sums):
    rows = []
    for first, second in sums:
        for v in (first, second):
            t = jnp.sum(v, axis=0, keepdims=True)
            rows += [t[:, :128], t[:, 128:]]
    packed = jnp.concatenate(rows, axis=0)
    for peer in range(o_ref.shape[0]):
        o_ref[peer] = packed


def group_totals(st_ref):
    tot = st_ref[0]
    for peer in range(1, st_ref.shape[0]):
        tot = tot + st_ref[peer]
    lane = lax.broadcasted_iota(jnp.int32, tot.shape, 1)
    for d in (1, 2, 4):
        low = (lane & d) == 0
        tot = tot + jnp.where(low, pltpu.roll(tot, 128 - d, 1), pltpu.roll(tot, d, 1))
    res = []
    for f in range(tot.shape[0] // 4):
        r = [tot[4 * f + k : 4 * f + k + 1] for k in range(4)]
        res.append((jnp.concatenate(r[:2], axis=1), jnp.concatenate(r[2:], axis=1)))
    return res


def moments(st_ref, members):
    res = []
    for first, second in group_totals(st_ref):
        mean = first / members
        res.append((mean, lax.rsqrt(second / members - mean * mean + EPSILON)))
    return res


def fold(v):
    return jnp.sum(v.reshape(v.shape[0] // 8, 8, v.shape[1]), axis=0)


def stats_kernel(x_ref, o_ref):
    sums = []
    for f in range(2):

        def step(r, carry):
            v = x_ref[f, pl.ds(pl.multiple_of(r * 128, 128), 128), :].astype(F32)
            return carry[0] + fold(v), carry[1] + fold(v * v)

        zero = jnp.zeros((8, 256), F32)
        sums.append(lax.fori_loop(0, 8, step, (zero, zero)))
    store_stats(o_ref, sums)


def shifted(v):
    row = lax.broadcasted_iota(jnp.int32, v.shape, 0)
    before = jnp.where(row == 0, 0.0, pltpu.roll(v, 1, 0))
    after = jnp.where(row == v.shape[0] - 1, 0.0, pltpu.roll(v, v.shape[0] - 1, 0))
    return before, after


def forward_kernel(members, info, x_ref, up_ref, dn_ref, st_ref, w_ref, act_ref, hid_ref, slope_ref):
    keep_up, keep_dn = info[4].astype(F32), info[5].astype(F32)
    stats = moments(st_ref, members)
    for f in range(2):
        mean, inv = stats[f]

        def put(v, row, keep=None):
            n = (v.astype(F32) - mean) * inv
            a = n * sigmoid(n)
            if keep is not None:
                a = a * keep
            before, after = shifted(a)
            at = pl.ds(row, 128)
            act_ref[f, at, 0:256] = before.astype(BF16)
            act_ref[f, at, 256:512] = a.astype(BF16)
            act_ref[f, at, 512:768] = after.astype(BF16)

        put(up_ref[f], 0, keep_up)
        put(dn_ref[f], 9 * 128, keep_dn)

        def line(r, _):
            at = pl.multiple_of(r * 128, 128)
            put(x_ref[f, pl.ds(at, 128), :], pl.multiple_of(at + 128, 128))
            return 0

        lax.fori_loop(0, 8, line, 0)

        def conv(r, _):
            at = pl.multiple_of(r * 256, 256)
            v = None
            for i in range(3):
                lhs = act_ref[f, pl.ds(pl.multiple_of(at + i * 128, 128), 256), :]
                part = dot(lhs, w_ref[i])
                v = part if v is None else v + part
            s = sigmoid(v)
            hid_ref[f, pl.ds(at, 256), :] = (v * s).astype(BF16)
            slope_ref[f, pl.ds(at, 256), :] = s * (1.0 + v * (1.0 - s))
            return 0

        lax.fori_loop(0, 4, conv, 0)


def pregrad_kernel(cot_ref, later_ref, slope_ref, w_ref, pg_ref, top_ref, bot_ref):
    for f in range(2):

        def part(r, _):
            at = pl.ds(pl.multiple_of(r * 256, 256), 256)
            v = None
            for k in range(3):
                g = f + 2 - k
                lhs = cot_ref[g, at, :] if g < 2 else later_ref[g - 2, at, :]
                p = dot(lhs, w_ref[k], NT)
                v = p if v is None else v + p
            pg_ref[f, at, :] = (v * slope_ref[f, at, :]).astype(BF16)
            return 0

        lax.fori_loop(0, 4, part, 0)
        top_ref[f] = pg_ref[f, 0:128, :]
        bot_ref[f] = pg_ref[f, 896:1024, :]


def grads_kernel(info, act_ref, pg_ref, hid_ref, cot_ref, later_ref, g_ref):
    def put(tap, v):
        for q in range(4):
            b = 4 * tap + q
            pair, third, bits = b // 24, (b % 24) // 8, b % 8
            at = (pair ^ info[0]) * 24 + third * 8 + (bits ^ info[1 + third])
            rh, lh = q % 2, q // 2
            g_ref[at] = v[rh * 128 : rh * 128 + 128, lh * 128 : lh * 128 + 128]

    for i in range(3):
        for j in range(3):
            v = None
            for f in range(2):
                lhs = act_ref[f, i * 128 : i * 128 + 1024, j * 256 : j * 256 + 256]
                p = dot(lhs, pg_ref[f], TN)
                v = p if v is None else v + p
            put(3 * i + j, v)
    for k in range(3):
        v = None
        for f in range(2):
            g = f + 2 - k
            rhs = cot_ref[g] if g < 2 else later_ref[g - 2]
            p = dot(hid_ref[f], rhs, TN)
            v = p if v is None else v + p
        put(9 + k, v)


def backward_kernel(members, pg_ref, up_ref, dn_ref, w_ref, x_ref, st_ref, ng_ref, o_ref, a_ref, b_ref, c_ref):
    stats = moments(st_ref, members)
    sums = []
    for f in range(2):
        mean, inv = stats[f]

        def put(v, row):
            v = v.astype(F32)
            before, after = shifted(v)
            at = pl.ds(row, 128)
            a_ref[f, at, :] = after.astype(BF16)
            b_ref[f, at, :] = v.astype(BF16)
            c_ref[f, at, :] = before.astype(BF16)

        put(up_ref[f], 0)
        put(dn_ref[f], 9 * 128)

        def line(r, _):
            at = pl.multiple_of(r * 128, 128)
            put(pg_ref[f, pl.ds(at, 128), :], pl.multiple_of(at + 128, 128))
            return 0

        lax.fori_loop(0, 8, line, 0)

        def conv(r, carry):
            at = pl.multiple_of(r * 256, 256)
            v = None
            for i in range(3):
                rows = pl.ds(pl.multiple_of(at + (2 - i) * 128, 128), 256)
                for j, ref in enumerate((a_ref, b_ref, c_ref)):
                    p = dot(ref[f, rows, :], w_ref[i, j], NT)
                    v = p if v is None else v + p
            n = (x_ref[f, pl.ds(at, 256), :].astype(F32) - mean) * inv
            s = sigmoid(n)
            ng = v * (s * (1.0 + n * (1.0 - s)))
            ng_ref[f, pl.ds(at, 256), :] = ng
            return carry[0] + fold(ng), carry[1] + fold(ng * n)

        zero = jnp.zeros((8, 256), F32)
        sums.append(lax.fori_loop(0, 4, conv, (zero, zero)))
    store_stats(o_ref, sums)


def input_grad_kernel(members, x_ref, cot_ref, ng_ref, st_ref, gst_ref, o_ref):
    stats = moments(st_ref, members)
    gstats = group_totals(gst_ref)
    for f in range(2):
        mean, inv = stats[f]
        first, second = gstats[f][0] / members, gstats[f][1] / members

        def part(r, _):
            at = pl.ds(pl.multiple_of(r * 128, 128), 128)
            n = (x_ref[f, at, :].astype(F32) - mean) * inv
            term = inv * (ng_ref[f, at, :] - first - n * second)
            o_ref[f, at, :] = (cot_ref[f, at, :].astype(F32) + term).astype(BF16)
            return 0

        lax.fori_loop(0, 8, part, 0)


def block_kernel(x_ref, hid_ref, prev_ref, w_ref, o_ref):
    for f in range(2):

        def part(r, _):
            at = pl.ds(pl.multiple_of(r * 256, 256), 256)
            v = None
            for k in range(3):
                g = f - 2 + k
                lhs = hid_ref[g, at, :] if g >= 0 else prev_ref[g + 2, at, :]
                p = dot(lhs, w_ref[k])
                v = p if v is None else v + p
            o_ref[f, at, :] = (x_ref[f, at, :].astype(F32) + v).astype(BF16)
            return 0

        lax.fori_loop(0, 4, part, 0)


def clip_kernel(clip_level, info, own_ref, other_ref, s_ref, t_ref):
    core = info[0]

    def block(tap, q):
        b = 4 * tap + q
        pair, third, bits = b // 24, (b % 24) // 8, b % 8
        at = third * 8 + (bits ^ info[1 + third])
        mine = (pair ^ core) == 0
        return jnp.where(mine, own_ref[at], other_ref[at])

    acc = jnp.zeros((8, 128), F32)
    for tap in range(12):
        ref, k = (s_ref, tap) if tap < 9 else (t_ref, tap - 9)
        for q in range(4):
            v = block(tap, q)
            rh, lh = q % 2, q // 2
            ref[k, rh * 128 : rh * 128 + 128, lh * 128 : lh * 128 + 128] = v
            acc = acc + fold(v * v)
    total = jnp.sum(jnp.sum(acc, axis=0, keepdims=True), axis=1, keepdims=True)
    scale = clip_level / jnp.maximum(jnp.sqrt(total), clip_level)

    def finish(k, _):
        s_ref[k] = s_ref[k] * scale
        return 0

    lax.fori_loop(0, 9, finish, 0)
    for k in range(3):
        t_ref[k] = t_ref[k] * scale


def swapped(x, axis):
    return lax.ppermute(x, axis, [(0, 1), (1, 0)])


def moved(x, axes, distance):
    n = lax.axis_size(axes)
    route = [(i, i + distance) for i in range(n) if 0 <= i + distance < n]
    return lax.ppermute(x, axes, route)


def reduced(g):
    g = g[:24] + swapped(g[24:], "core")
    parts = [g[8 * t : 8 * t + 8] for t in range(3)]
    for step, half in enumerate((4, 2, 1)):
        got = [swapped(p[half:], ORDERS[t][step]) for t, p in enumerate(parts)]
        parts = [p[:half] + r for p, r in zip(parts, got)]
    pieces = jnp.concatenate([p.reshape(16, 8, 128) for p in parts], axis=1)
    return jnp.sum(lax.all_to_all(pieces, REST, 0, 0, tiled=True), axis=0)


def gathered(own):
    copies = jnp.broadcast_to(own, (16, *own.shape))
    pieces = lax.all_to_all(copies, REST, 0, 0, tiled=True)
    parts = [pieces[:, 8 * t : 8 * t + 8].reshape(1, 128, 128) for t in range(3)]
    for step in (2, 1, 0):
        got = [swapped(p, ORDERS[t][step]) for t, p in enumerate(parts)]
        parts = [jnp.concatenate([p, r], axis=0) for p, r in zip(parts, got)]
    mine = jnp.concatenate(parts, axis=0)
    return mine, swapped(mine, "core")


def body(video_latents, cotangent, spatial_kernel, temporal_kernel):
    batch, frames, rows, columns, channels = video_latents.shape
    peers = lax.axis_size(HEIGHT)
    members = float(rows * peers * columns * (channels // GROUPS))
    clip_level = (
        channels * rows * peers * columns
        * math.sqrt(batch * lax.axis_size(DP) * frames * lax.axis_size(TM))
        / CLIP_DIVISOR
    )
    z = lax.axis_index(HEIGHT)
    bit = {a: lax.axis_index(a) for a in ("xl", "yl", "zl")}
    codes = [4 * bit[a] + 2 * bit[b] + bit[c] for a, b, c in ORDERS]
    info = jnp.stack(
        [lax.axis_index("core"), *codes, (z > 0).astype(jnp.int32), (z < peers - 1).astype(jnp.int32)]
    ).astype(jnp.int32)
    pixels = rows * columns
    flat = (2, pixels, 256)
    x = video_latents.reshape(flat)
    cot = cotangent.reshape(flat)
    w9 = spatial_kernel
    w3 = spatial_kernel.reshape(3, 768, 256)
    gflop = 2 * 2048 * 256 * 256

    later = moved(cot, TM, -1)
    up = moved(x[:, pixels - columns :], HEIGHT, 1)
    dn = moved(x[:, :columns], HEIGHT, -1)
    small = out((8, 8, 128), F32)
    (st,) = call(stats_kernel, [small], [x], 1 << 21)
    st = lax.all_to_all(st, HEIGHT, 0, 0, tiled=True)
    act, hid, slope = call(
        lambda *refs: forward_kernel(members, *refs),
        [out((2, 1280, 768), BF16), out(flat, BF16), out(flat, F32)],
        [info, x, up, dn, st, w3],
        9 * gflop,
        smem=1,
    )
    edge = out((2, columns, 256), BF16)
    pg, top, bot = call(
        pregrad_kernel, [out(flat, BF16), edge, edge], [cot, later, slope, temporal_kernel], 3 * gflop
    )
    gup = moved(bot, HEIGHT, 1)
    gdn = moved(top, HEIGHT, -1)
    (g,) = call(
        grads_kernel, [out((48, 128, 128), F32)], [info, act, pg, hid, cot, later], 12 * gflop, smem=1
    )
    own = reduced(g)
    mine, other = gathered(own)
    clipped_spatial, clipped_temporal = call(
        lambda *refs: clip_kernel(clip_level, *refs),
        [out((9, 256, 256), F32), out((3, 256, 256), F32)],
        [info, mine, other],
        1 << 21,
        smem=1,
    )
    ng, gst = call(
        lambda *refs: backward_kernel(members, *refs),
        [out(flat, F32), small],
        [pg, gup, gdn, w9, x, st],
        9 * gflop,
        scratch=[pltpu.VMEM((2, 1280, 256), BF16)] * 3,
    )
    gst = lax.all_to_all(gst, HEIGHT, 0, 0, tiled=True)
    (input_grad,) = call(
        lambda *refs: input_grad_kernel(members, *refs), [out(flat, BF16)], [x, cot, ng, st, gst], 1 << 21
    )
    prev = moved(hid, TM, 1)
    (block_output,) = call(block_kernel, [out(flat, BF16)], [x, hid, prev, temporal_kernel], 3 * gflop)
    return (
        block_output.reshape(video_latents.shape),
        input_grad.reshape(video_latents.shape),
        clipped_spatial.reshape(spatial_kernel.shape),
        clipped_temporal,
    )


def solution(mesh):
    torus = Mesh(mesh.devices.reshape(2, 2, 2, 2, 2, 4, 2), (*DP, *TM, *HEIGHT))
    field = P(DP, TM, HEIGHT, None, None)
    return jax.shard_map(
        body, mesh=torus, in_specs=(field, field, P(), P()), out_specs=(field, field, P(), P()), check_vma=False
    )
```

time: 309 us -> 189 us (0.61)
  waiting for transfers between devices: 146 us -> 41.7 us
  matrix products: 46.6 us -> 0 us
  blocking collectives: 0 us -> 35.3 us
  Pallas kernels: 0 us -> 30.2 us
  other arithmetic: 20 us -> 0.53 us
  local copies, waits for them, and re-layouts: 33.5 us -> 23 us
    all_to_all x6 -> x2, waiting for transfers between devices: 71.1 us -> 7.64 us  [the longest x1 6.83 us: body(): st = lax.all_to_all(st, HEIGHT, 0, 0, tiled=True)]
    dot_general x36 -> x0, matrix products: 46.6 us -> none  [the longest x9 24.7 us: body(): jnp.einsum('bfhwd,cd->bfhwc', shifted, spatial_kernel[tap_row, tap_col],...]
    ppermute x6 -> x26, waiting for transfers between devices: 74.6 us -> 34 us  [the longest x20 27.2 us: swapped(): return lax.ppermute(x, axis, [(0, 1), (1, 0)])]
    all_to_all x0 -> x2, blocking collectives: none -> 35.3 us  [the longest x1 19.6 us: reduced(): return jnp.sum(lax.all_to_all(pieces, REST, 0, 0, tiled=True), axis=0)]
    all_to_all x6 -> x2, starting transfers between devices: 43.4 us -> 12 us  [the longest x1 8 us: body(): st = lax.all_to_all(st, HEIGHT, 0, 0, tiled=True)]
    pallas_call x0 -> x8, Pallas kernels: none -> 30.2 us  [call(): pl.pallas_call(kernel, out_shape=tuple(outs), in_specs=specs, out_specs=t...]
    ppermute x6 -> x26, starting transfers between devices: 13.9 us -> 43.6 us  [the longest x20 28.1 us: swapped(): return lax.ppermute(x, axis, [(0, 1), (1, 0)])]
    unnamed x25 -> x59, local copies, waits for them, and re-layouts: 2.84 us -> 21 us
  transfers between devices with their start and end apart: 12 -> 28, of which waited for: 9 -> 18; matrix products, arithmetic and copies ran while one was open for 20% -> 5% of each run, Pallas kernels for 0% -> 10%
where the time goes in v1:
time: 189 us; the launch traced here: 187 us
  starting transfers between devices  55.5 us (29%)
  waiting for transfers between devices  41.7 us (22%)
  blocking collectives  35.3 us (19%)
  Pallas kernels  30.2 us (16%)
  local copies, waits for them, and re-layouts  23 us (12%)
    pallas_call x8, Pallas kernels, call(): pl.pallas_call(kernel, out_shape=tuple(outs), in_specs=specs, out_specs=t...  30.2 us
    ppermute x20, starting transfers between devices, swapped(): return lax.ppermute(x, axis, [(0, 1), (1, 0)])  28.1 us
    ppermute x20, waiting for transfers between devices, swapped(): return lax.ppermute(x, axis, [(0, 1), (1, 0)])  27.2 us
    unnamed x59, local copies, waits for them, and re-layouts  21 us
    all_to_all x1, blocking collectives, reduced(): return jnp.sum(lax.all_to_all(pieces, REST, 0, 0, tiled=True), axis=0)  19.6 us
    all_to_all x1, blocking collectives, gathered(): pieces = lax.all_to_all(copies, REST, 0, 0, tiled=True)  15.7 us
    ppermute x6, starting transfers between devices, moved(): return lax.ppermute(x, axes, route)  15.4 us
    all_to_all x1, starting transfers between devices, body(): st = lax.all_to_all(st, HEIGHT, 0, 0, tiled=True)  8 us
  transfers between devices with their start and end apart: 28, of which 18 were waited for; matrix products, arithmetic and copies ran while one was open for 5% of the time, Pallas kernels for 10%

profile of v1, /device:TPU:1, one launch (start us, length us, event | category | flops | bytes accessed | tf_op | source)
XLA Modules:
  0.0 187.3 jit_solution(3765588496814417239)
XLA Ops:
  0.6 1.3 collective-permute-start.3
  1.9 1.0 fusion.3
  2.9 1.3 collective-permute-start.1
  4.2 5.0 %collective-permute-start = (bf16[2,128,256]{2,1,0:T(8,128)(2,1)S(1)}, bf16[2,128,256]{2,1,0:T(8,128)(2,1)S(1)}, u32[]{:S(2)}, u32[]{:S(2)}) collective-permute-start(bf16[2,128,256]{2,1,0:T(8,128)(2,1)S(1)} %get-tuple-element.30), channel_id=1, source_target_pairs={{0,1},{1,2},{2,3},{3,4},{4,5},{5,6},{6,7},{8,9},{9,10},{10,11},{11... | collective-permute-start | bytes 393224 | tf_op jit(solution)/shard_map/ppermute | solution.py:315
  9.2 1.2 copy-done
  10.5 1.0 shard_map.75
  11.4 8.0 %all-to-all-start = ((f32[8,8,128]{2,1,0:T(8,128)}), f32[8,8,128]{2,1,0:T(8,128)S(1)}, u32[]{:S(2)}, u32[]{:S(2)}) async-start(f32[8,8,128]{2,1,0:T(8,128)} %shard_map.75), calls=%async_computation | async-start | bytes 65536 | tf_op jit(solution)/shard_map/all_to_all | solution.py:367
  19.5 6.8 %all-to-all-done.refs_4_.refs_5_.refs_3_ = f32[8,8,128]{2,1,0:T(8,128)S(1)} async-done(((f32[8,8,128]{2,1,0:T(8,128)}), f32[8,8,128]{2,1,0:T(8,128)S(1)}, u32[]{:S(2)}, u32[]{:S(2)}) %all-to-all-start) | async-done | bytes 32800 | tf_op jit(solution)/shard_map/all_to_all | solution.py:367
  28.2 1.2 copy-done.1
  30.2 1.3 copy-done.12
  33.3 6.3 %shard_map.76 = (bf16[2,1280,768]{2,1,0:T(8,128)(2,1)S(1)}, bf16[2,1024,256]{2,1,0:T(8,128)(2,1)S(1)}, f32[2,1024,256]{2,1,0:T(8,128)S(1)}) custom-call(s32[6]{0:T(128)S(1)} %stack.35.refs_0_.info, bf16[2,1024,256]{2,1,0:T(8,128)(2,1)S(1)} %bitcast.32, bf16[2,128,256]{2,1,0:T(8,128)(2,1)S(1)} %copy-done.23, bf16[2,128,256]{2,1,0:T(8,128)(2,1)S(1)} %copy-done.21, ...), custom_call_target="tpu_custom_call" | custom-call | flops 2415919104 | bytes 9601048 | tf_op jit(solution)/shard_map/pallas_call | solution.py:30
  39.6 2.4 %shard_map.78 = (bf16[2,1024,256]{2,1,0:T(8,128)(2,1)S(1)}, bf16[2,128,256]{2,1,0:T(8,128)(2,1)S(1)}, bf16[2,128,256]{2,1,0:T(8,128)(2,1)S(1)}) custom-call(bf16[2,1024,256]{2,1,0:T(8,128)(2,1)S(1)} %bitcast.37, bf16[2,1024,256]{2,1,0:T(8,128)(2,1)S(1)} %collective-permute-done.3.later_ref, f32[2,1024,256]{2,1,0:T(8,128)S(1)} %get-tuple-element.15.slope_ref, ...), custom_call_target="tpu_custom_call" | custom-call | flops 805306368 | bytes 5898240 | tf_op jit(solution)/shard_map/pallas_call | solution.py:30
  43.4 4.0 %shard_map.81 = f32[48,128,128]{2,1,0:T(8,128)S(1)} custom-call(s32[6]{0:T(128)S(1)} %stack.35.refs_0_.info, bf16[2,1280,768]{2,1,0:T(8,128)(2,1)S(1)} %get-tuple-element.21.act_ref, bf16[2,1024,256]{2,1,0:T(8,128)(2,1)S(1)} %get-tuple-element.16.refs_0_.pg_ref, bf16[2,1024,256]{2,1,0:T(8,128)(2,1)S(1)} %get-tuple-element.14.hid_ref, ...), custom_call_target="tpu_custom_call" | custom-call | flops 3221225472 | bytes 11272216 | tf_op jit(solution)/shard_map/pallas_call | solution.py:30
  47.6 2.7 %collective-permute-start.6 = (f32[24,128,128]{2,1,0:T(8,128)S(1)}, f32[24,128,128]{2,1,0:T(8,128)S(1)}, u32[]{:S(2)}, u32[]{:S(2)}) collective-permute-start(f32[24,128,128]{2,1,0:T(8,128)S(1)} %slice.112), channel_id=1, source_target_pairs={{0,32},{32,0},{1,33},{33,1},{2,34},{34,2},{3,35},{35,3},{4,36},{36... | collective-permute-start | bytes 4718600 | tf_op jit(solution)/shard_map/ppermute | solution.py:309
  50.3 3.0 %collective-permute-done.6 = f32[24,128,128]{2,1,0:T(8,128)S(1)} collective-permute-done((f32[24,128,128]{2,1,0:T(8,128)S(1)}, f32[24,128,128]{2,1,0:T(8,128)S(1)}, u32[]{:S(2)}, u32[]{:S(2)}) %collective-permute-start.6) | collective-permute-done | bytes 1572896 | tf_op jit(solution)/shard_map/ppermute | solution.py:309
  53.6 2.4 %collective-permute-start.7 = (f32[4,128,128]{2,1,0:T(8,128)S(1)}, f32[4,128,128]{2,1,0:T(8,128)S(1)}, u32[]{:S(2)}, u32[]{:S(2)}) collective-permute-start(f32[4,128,128]{2,1,0:T(8,128)S(1)} %slice.114), channel_id=1, source_target_pairs={{0,8},{8,0},{1,9},{9,1},{2,10},{10,2},{3,11},{11,3},{4,12},{12,4},... | collective-permute-start | bytes 786440 | tf_op jit(solution)/shard_map/ppermute | solution.py:309
  56.1 6.3 %collective-permute-done.7 = f32[4,128,128]{2,1,0:T(8,128)S(1)} collective-permute-done((f32[4,128,128]{2,1,0:T(8,128)S(1)}, f32[4,128,128]{2,1,0:T(8,128)S(1)}, u32[]{:S(2)}, u32[]{:S(2)}) %collective-permute-start.7) | collective-permute-done | bytes 262176 | tf_op jit(solution)/shard_map/ppermute | solution.py:309
  62.5 1.4 collective-permute-start.8
  64.3 2.1 %collective-permute-done.8 = f32[2,128,128]{2,1,0:T(8,128)S(1)} collective-permute-done((f32[2,128,128]{2,1,0:T(8,128)S(1)}, f32[2,128,128]{2,1,0:T(8,128)S(1)}, u32[]{:S(2)}, u32[]{:S(2)}) %collective-permute-start.8) | collective-permute-done | bytes 131104 | tf_op jit(solution)/shard_map/ppermute | solution.py:309
  66.8 3.7 %collective-permute-done.13 = f32[4,128,128]{2,1,0:T(8,128)S(1)} collective-permute-done((f32[4,128,128]{2,1,0:T(8,128)S(1)}, f32[4,128,128]{2,1,0:T(8,128)S(1)}, u32[]{:S(2)}, u32[]{:S(2)}) %collective-permute-start.13) | collective-permute-done | bytes 262176 | tf_op jit(solution)/shard_map/ppermute | solution.py:309
  70.5 2.0 %collective-permute-done.10 = f32[4,128,128]{2,1,0:T(8,128)S(1)} collective-permute-done((f32[4,128,128]{2,1,0:T(8,128)S(1)}, f32[4,128,128]{2,1,0:T(8,128)S(1)}, u32[]{:S(2)}, u32[]{:S(2)}) %collective-permute-start.10) | collective-permute-done | bytes 262176 | tf_op jit(solution)/shard_map/ppermute | solution.py:309
  72.5 1.1 collective-permute-start.14
  74.1 2.4 %collective-permute-done.14 = f32[2,128,128]{2,1,0:T(8,128)S(1)} collective-permute-done((f32[2,128,128]{2,1,0:T(8,128)S(1)}, f32[2,128,128]{2,1,0:T(8,128)S(1)}, u32[]{:S(2)}, u32[]{:S(2)}) %collective-permute-start.14) | collective-permute-done | bytes 131104 | tf_op jit(solution)/shard_map/ppermute | solution.py:309
  76.5 1.2 collective-permute-start.15
  78.7 1.3 collective-permute-done.15
  80.0 1.2 collective-permute-done.12
  81.2 19.6 %all_to_all.20 = f32[16,24,128]{2,1,0:T(8,128)S(1)} all-to-all(f32[16,24,128]{2,1,0:T(8,128)S(1)} %pad_maximum_fusion.3), channel_id=1, replica_groups=mesh['yh'=2,'yl'=2,'core'=2,'xh'=2,'xl'=2,'zh'=4,'zl'=2] {'yh','xh','zh'}, dimensions={0} | all-to-all | bytes 393216 | tf_op jit(solution)/shard_map/all_to_all | solution.py:325
  100.9 15.7 %all_to_all.21 = f32[16,24,128]{2,1,0:T(8,128)S(1)} all-to-all(f32[16,24,128]{2,1,0:T(8,128)S(1)} %broadcast_in_dim.3), channel_id=1, replica_groups=mesh['yh'=2,'yl'=2,'core'=2,'xh'=2,'xl'=2,'zh'=4,'zl'=2] {'yh','xh','zh'}, dimensions={0} | all-to-all | bytes 393216 | tf_op jit(solution)/shard_map/all_to_all | solution.py:330
  118.1 2.0 %collective-permute-done.22 = f32[1,128,128]{2,1,0:T(8,128)S(1)} collective-permute-done((f32[1,128,128]{2,1,0:T(8,128)S(1)}, f32[1,128,128]{2,1,0:T(8,128)S(1)}, u32[]{:S(2)}, u32[]{:S(2)}) %collective-permute-start.22) | collective-permute-done | bytes 65568 | tf_op jit(solution)/shard_map/ppermute | solution.py:309
  120.3 1.4 collective-permute-start.17
  122.9 1.3 collective-permute-done.17
  124.2 1.5 collective-permute-start.18
  126.6 1.3 collective-permute-start.21
  128.5 1.7 collective-permute-done.18
  136.2 10.8 %collective-permute-start.25 = (f32[24,128,128]{2,1,0:T(8,128)}, f32[24,128,128]{2,1,0:T(8,128)}, u32[]{:S(2)}, u32[]{:S(2)}) collective-permute-start(f32[24,128,128]{2,1,0:T(8,128)} %constant_dynamic-update-slice_fusion.refs_1_), channel_id=1, source_target_pairs={{0,32},{32,0},{1,33},{33,1},{2,34},{34,2},{3,35},{35,3},{4,36},{36... | collective-permute-start | bytes 4718600 | tf_op jit(solution)/shard_map/ppermute | solution.py:309
  147.0 4.3 %collective-permute-start.2 = (bf16[2,1024,256]{2,1,0:T(8,128)(2,1)S(1)}, bf16[2,1024,256]{2,1,0:T(8,128)(2,1)}, u32[]{:S(2)}, u32[]{:S(2)}) collective-permute-start(bf16[2,1024,256]{2,1,0:T(8,128)(2,1)S(1)} %get-tuple-element.14.hid_ref), channel_id=1, source_target_pairs={{0,8},{8,16},{16,24},{1,9},{9,17},{17,25},{2,10},{10,18},{18,26},{... | collective-permute-start | bytes 3145736 | tf_op jit(solution)/shard_map/ppermute | solution.py:315
  151.3 2.3 %collective-permute-start.4 = (bf16[2,128,256]{2,1,0:T(8,128)(2,1)S(1)}, bf16[2,128,256]{2,1,0:T(8,128)(2,1)S(1)}, u32[]{:S(2)}, u32[]{:S(2)}) collective-permute-start(bf16[2,128,256]{2,1,0:T(8,128)(2,1)S(1)} %copy-done.19), channel_id=1, source_target_pairs={{0,1},{1,2},{2,3},{3,4},{4,5},{5,6},{6,7},{8,9},{9,10},{10,11},{11... | collective-permute-start | bytes 393224 | tf_op jit(solution)/shard_map/ppermute | solution.py:315
  153.6 1.3 collective-permute-start.5
  154.9 1.2 collective-permute-done.4.refs_1_
  156.2 3.8 %collective-permute-done.5.refs_2_ = bf16[2,128,256]{2,1,0:T(8,128)(2,1)S(1)} collective-permute-done((bf16[2,128,256]{2,1,0:T(8,128)(2,1)S(1)}, bf16[2,128,256]{2,1,0:T(8,128)(2,1)S(1)}, u32[]{:S(2)}, u32[]{:S(2)}) %collective-permute-start.5) | collective-permute-done | bytes 131104 | tf_op jit(solution)/shard_map/ppermute | solution.py:315
  160.0 5.2 %shard_map.79 = (f32[2,1024,256]{2,1,0:T(8,128)S(1)}, f32[8,8,128]{2,1,0:T(8,128)S(1)}) custom-call(bf16[2,1024,256]{2,1,0:T(8,128)(2,1)S(1)} %copy-done.15, bf16[2,128,256]{2,1,0:T(8,128)(2,1)S(1)} %collective-permute-done.4.refs_1_, bf16[2,128,256]{2,1,0:T(8,128)(2,1)S(1)} %collective-permute-done.5.refs_2_, bf16[3,3,256,256]{3,2,1,0:T(8,128)(2,1)S(1)} %copy-done.13, ...), custom_call_target="tpu_custom_call" | custom-call | flops 2415919104 | bytes 5701632 | tf_op jit(solution)/shard_map/pallas_call | solution.py:30
  165.3 1.3 copy-done.4
  167.2 4.0 %all-to-all-start.1 = ((f32[8,8,128]{2,1,0:T(8,128)}), f32[8,8,128]{2,1,0:T(8,128)}, u32[]{:S(2)}, u32[]{:S(2)}) async-start(f32[8,8,128]{2,1,0:T(8,128)} %copy-done.11), calls=%async_computation.1 | async-start | bytes 65536 | tf_op jit(solution)/shard_map/all_to_all | solution.py:400
  171.2 1.7 collective-permute-done.2.prev_ref
  172.9 4.4 %shard_map.77 = bf16[2,1024,256]{2,1,0:T(8,128)(2,1)} custom-call(bf16[2,1024,256]{2,1,0:T(8,128)(2,1)S(1)} %bitcast.34, bf16[2,1024,256]{2,1,0:T(8,128)(2,1)S(1)} %get-tuple-element.14.hid_ref, bf16[2,1024,256]{2,1,0:T(8,128)(2,1)} %collective-permute-done.2.prev_ref, bf16[3,256,256]{2,1,0:T(8,128)(2,1)S(1)} %copy-done.6), custom_call_target="tpu_custom_call" | custom-call | flops 805306368 | bytes 4587520 | tf_op jit(solution)/shard_map/pallas_call | solution.py:30
  178.0 1.6 copy-done.5
  180.4 2.7 %shard_map.80 = bf16[2,1024,256]{2,1,0:T(8,128)(2,1)} custom-call(bf16[2,1024,256]{2,1,0:T(8,128)(2,1)S(1)} %bitcast.35, bf16[2,1024,256]{2,1,0:T(8,128)(2,1)S(1)} %bitcast.39, f32[2,1024,256]{2,1,0:T(8,128)S(1)} %copy-done.5, f32[8,8,128]{2,1,0:T(8,128)S(1)} %copy-done.10, f32[8,8,128]{2,1,0:T(8,128)} %all-to-all-done.1.refs_4_), custom_call_target="tpu_custom_call" | custom-call | flops 2097152 | bytes 5308416 | tf_op jit(solution)/shard_map/pallas_call | solution.py:30
  183.1 4.2 %shard_map.82 = (f32[9,256,256]{2,1,0:T(8,128)}, f32[3,256,256]{2,1,0:T(8,128)}) custom-call(s32[6]{0:T(128)S(1)} %stack.35.refs_0_.info, f32[24,128,128]{2,1,0:T(8,128)} %constant_dynamic-update-slice_fusion.refs_1_, f32[24,128,128]{2,1,0:T(8,128)} %collective-permute-done.25.refs_2_), custom_call_target="tpu_custom_call" | custom-call | flops 2097152 | bytes 6291480 | tf_op jit(solution)/shard_map/pallas_call | solution.py:30
  (107 shorter events, 21.4 us)
Async XLA Ops:
  0.6 39.0 %collective-permute-start.3 = (bf16[2,1024,256]{2,1,0:T(8,128)(2,1)}, bf16[2,1024,256]{2,1,0:T(8,128)(2,1)S(1)}, u32[]{:S(2)}, u32[]{:S(2)}) collective-permute-start(bf16[2,1024,256]{2,1,0:T(8,128)(2,1)} %bitcast.36), channel_id=1, source_target_pairs={{8,0},{16,8},{24,16},{9,1},{17,9},{25,17},{10,2},{18,10},{26,18},{... | collective-permute-start | bytes 3145736 | tf_op jit(solution)/shard_map/ppermute | solution.py:315
  2.9 24.0 %collective-permute-start.1 = (bf16[2,128,256]{2,1,0:T(8,128)(2,1)S(1)}, bf16[2,128,256]{2,1,0:T(8,128)(2,1)S(1)}, u32[]{:S(2)}, u32[]{:S(2)}) collective-permute-start(bf16[2,128,256]{2,1,0:T(8,128)(2,1)S(1)} %get-tuple-element.29), channel_id=1, source_target_pairs={{1,0},{2,1},{3,2},{4,3},{5,4},{6,5},{7,6},{9,8},{10,9},{11,10},{12... | collective-permute-start | bytes 393224 | tf_op jit(solution)/shard_map/ppermute | solution.py:315
  4.2 23.4 %collective-permute-start = (bf16[2,128,256]{2,1,0:T(8,128)(2,1)S(1)}, bf16[2,128,256]{2,1,0:T(8,128)(2,1)S(1)}, u32[]{:S(2)}, u32[]{:S(2)}) collective-permute-start(bf16[2,128,256]{2,1,0:T(8,128)(2,1)S(1)} %get-tuple-element.30), channel_id=1, source_target_pairs={{0,1},{1,2},{2,3},{3,4},{4,5},{5,6},{6,7},{8,9},{9,10},{10,11},{11... | collective-permute-start | bytes 393224 | tf_op jit(solution)/shard_map/ppermute | solution.py:315
  9.2 1.2 copy-start
  11.4 14.9 %all-to-all-start = ((f32[8,8,128]{2,1,0:T(8,128)}), f32[8,8,128]{2,1,0:T(8,128)S(1)}, u32[]{:S(2)}, u32[]{:S(2)}) async-start(f32[8,8,128]{2,1,0:T(8,128)} %shard_map.75), calls=%async_computation | async-start | bytes 65536 | tf_op jit(solution)/shard_map/all_to_all | solution.py:367
  26.9 0.7 copy-start.20
  28.2 1.2 copy-start.1
  29.5 0.8 copy-start.8
  30.2 1.3 copy-start.12
  31.5 0.9 copy-start.21
  32.4 0.9 copy-start.23
  33.3 6.3 %copy-start.3 = (bf16[1,2,8,128,256]{4,3,2,1,0:T(8,128)(2,1)S(1)}, bf16[1,2,8,128,256]{4,3,2,1,0:T(8,128)(2,1)}, u32[]{:S(2)}) copy-start(bf16[1,2,8,128,256]{4,3,2,1,0:T(8,128)(2,1)} %param.5) | copy-start | bytes 3145732
  33.3 6.3 %copy-start.6 = (bf16[3,256,256]{2,1,0:T(8,128)(2,1)S(1)}, bf16[3,256,256]{2,1,0:T(8,128)(2,1)}, u32[]{:S(2)}) copy-start(bf16[3,256,256]{2,1,0:T(8,128)(2,1)} %w_ref.3) | copy-start | bytes 1179652
  42.1 0.7 copy-start.16
  43.4 4.0 %copy-start.14 = (bf16[2,1024,256]{2,1,0:T(8,128)(2,1)}, bf16[2,1024,256]{2,1,0:T(8,128)(2,1)S(1)}, u32[]{:S(2)}) copy-start(bf16[2,1024,256]{2,1,0:T(8,128)(2,1)S(1)} %get-tuple-element.16.refs_0_.pg_ref) | copy-start | bytes 3145732
  47.6 5.8 %collective-permute-start.6 = (f32[24,128,128]{2,1,0:T(8,128)S(1)}, f32[24,128,128]{2,1,0:T(8,128)S(1)}, u32[]{:S(2)}, u32[]{:S(2)}) collective-permute-start(f32[24,128,128]{2,1,0:T(8,128)S(1)} %slice.112), channel_id=1, source_target_pairs={{0,32},{32,0},{1,33},{33,1},{2,34},{34,2},{3,35},{35,3},{4,36},{36... | collective-permute-start | bytes 4718600 | tf_op jit(solution)/shard_map/ppermute | solution.py:309
  53.6 8.8 %collective-permute-start.7 = (f32[4,128,128]{2,1,0:T(8,128)S(1)}, f32[4,128,128]{2,1,0:T(8,128)S(1)}, u32[]{:S(2)}, u32[]{:S(2)}) collective-permute-start(f32[4,128,128]{2,1,0:T(8,128)S(1)} %slice.114), channel_id=1, source_target_pairs={{0,8},{8,0},{1,9},{9,1},{2,10},{10,2},{3,11},{11,3},{4,12},{12,4},... | collective-permute-start | bytes 786440 | tf_op jit(solution)/shard_map/ppermute | solution.py:309
  62.5 3.9 %collective-permute-start.8 = (f32[2,128,128]{2,1,0:T(8,128)S(1)}, f32[2,128,128]{2,1,0:T(8,128)S(1)}, u32[]{:S(2)}, u32[]{:S(2)}) collective-permute-start(f32[2,128,128]{2,1,0:T(8,128)S(1)} %slice.116), channel_id=1, source_target_pairs={{0,64},{64,0},{1,65},{65,1},{2,66},{66,2},{3,67},{67,3},{4,68},{68... | collective-permute-start | bytes 393224 | tf_op jit(solution)/shard_map/ppermute | solution.py:309
  63.9 6.6 %collective-permute-start.13 = (f32[4,128,128]{2,1,0:T(8,128)S(1)}, f32[4,128,128]{2,1,0:T(8,128)S(1)}, u32[]{:S(2)}, u32[]{:S(2)}) collective-permute-start(f32[4,128,128]{2,1,0:T(8,128)S(1)} %get-tuple-element.25), channel_id=1, source_target_pairs={{0,1},{1,0},{2,3},{3,2},{4,5},{5,4},{6,7},{7,6},{8,9},{9,8},{10,11... | collective-permute-start | bytes 786440 | tf_op jit(solution)/shard_map/ppermute | solution.py:309
  64.1 8.3 %collective-permute-start.10 = (f32[4,128,128]{2,1,0:T(8,128)S(1)}, f32[4,128,128]{2,1,0:T(8,128)S(1)}, u32[]{:S(2)}, u32[]{:S(2)}) collective-permute-start(f32[4,128,128]{2,1,0:T(8,128)S(1)} %get-tuple-element.26), channel_id=1, source_target_pairs={{0,64},{64,0},{1,65},{65,1},{2,66},{66,2},{3,67},{67,3},{4,68},{68... | collective-permute-start | bytes 786440 | tf_op jit(solution)/shard_map/ppermute | solution.py:309
  66.4 7.3 %collective-permute-start.9 = (f32[1,128,128]{2,1,0:T(8,128)S(1)}, f32[1,128,128]{2,1,0:T(8,128)S(1)}, u32[]{:S(2)}, u32[]{:S(2)}) collective-permute-start(f32[1,128,128]{2,1,0:T(8,128)S(1)} %slice.118), channel_id=1, source_target_pairs={{0,1},{1,0},{2,3},{3,2},{4,5},{5,4},{6,7},{7,6},{8,9},{9,8},{10,11... | collective-permute-start | bytes 196616 | tf_op jit(solution)/shard_map/ppermute | solution.py:309
  72.5 3.9 %collective-permute-start.14 = (f32[2,128,128]{2,1,0:T(8,128)S(1)}, f32[2,128,128]{2,1,0:T(8,128)S(1)}, u32[]{:S(2)}, u32[]{:S(2)}) collective-permute-start(f32[2,128,128]{2,1,0:T(8,128)S(1)} %slice.128), channel_id=1, source_target_pairs={{0,8},{8,0},{1,9},{9,1},{2,10},{10,2},{3,11},{11,3},{4,12},{12,4},... | collective-permute-start | bytes 393224 | tf_op jit(solution)/shard_map/ppermute | solution.py:309
  73.7 4.2 %collective-permute-start.11 = (f32[2,128,128]{2,1,0:T(8,128)S(1)}, f32[2,128,128]{2,1,0:T(8,128)S(1)}, u32[]{:S(2)}, u32[]{:S(2)}) collective-permute-start(f32[2,128,128]{2,1,0:T(8,128)S(1)} %slice.122), channel_id=1, source_target_pairs={{0,1},{1,0},{2,3},{3,2},{4,5},{5,4},{6,7},{7,6},{8,9},{9,8},{10,11... | collective-permute-start | bytes 393224 | tf_op jit(solution)/shard_map/ppermute | solution.py:309
  76.5 3.5 %collective-permute-start.15 = (f32[1,128,128]{2,1,0:T(8,128)S(1)}, f32[1,128,128]{2,1,0:T(8,128)S(1)}, u32[]{:S(2)}, u32[]{:S(2)}) collective-permute-start(f32[1,128,128]{2,1,0:T(8,128)S(1)} %slice.130), channel_id=1, source_target_pairs={{0,64},{64,0},{1,65},{65,1},{2,66},{66,2},{3,67},{67,3},{4,68},{68... | collective-permute-start | bytes 196616 | tf_op jit(solution)/shard_map/ppermute | solution.py:309
  77.9 3.2 %collective-permute-start.12 = (f32[1,128,128]{2,1,0:T(8,128)S(1)}, f32[1,128,128]{2,1,0:T(8,128)S(1)}, u32[]{:S(2)}, u32[]{:S(2)}) collective-permute-start(f32[1,128,128]{2,1,0:T(8,128)S(1)} %slice.124), channel_id=1, source_target_pairs={{0,8},{8,0},{1,9},{9,1},{2,10},{10,2},{3,11},{11,3},{4,12},{12,4},... | collective-permute-start | bytes 196616 | tf_op jit(solution)/shard_map/ppermute | solution.py:309
  116.6 3.5 %collective-permute-start.22 = (f32[1,128,128]{2,1,0:T(8,128)S(1)}, f32[1,128,128]{2,1,0:T(8,128)S(1)}, u32[]{:S(2)}, u32[]{:S(2)}) collective-permute-start(f32[1,128,128]{2,1,0:T(8,128)S(1)} %get-tuple-element.31), channel_id=1, source_target_pairs={{0,64},{64,0},{1,65},{65,1},{2,66},{66,2},{3,67},{67,3},{4,68},{68... | collective-permute-start | bytes 196616 | tf_op jit(solution)/shard_map/ppermute | solution.py:309
  116.7 5.0 %collective-permute-start.19 = (f32[1,128,128]{2,1,0:T(8,128)S(1)}, f32[1,128,128]{2,1,0:T(8,128)S(1)}, u32[]{:S(2)}, u32[]{:S(2)}) collective-permute-start(f32[1,128,128]{2,1,0:T(8,128)S(1)} %get-tuple-element.32), channel_id=1, source_target_pairs={{0,8},{8,0},{1,9},{9,1},{2,10},{10,2},{3,11},{11,3},{4,12},{12,4},... | collective-permute-start | bytes 196616 | tf_op jit(solution)/shard_map/ppermute | solution.py:309
  116.8 3.5 %collective-permute-start.16 = (f32[1,128,128]{2,1,0:T(8,128)S(1)}, f32[1,128,128]{2,1,0:T(8,128)S(1)}, u32[]{:S(2)}, u32[]{:S(2)}) collective-permute-start(f32[1,128,128]{2,1,0:T(8,128)S(1)} %get-tuple-element.33), channel_id=1, source_target_pairs={{0,1},{1,0},{2,3},{3,2},{4,5},{5,4},{6,7},{7,6},{8,9},{9,8},{10,11... | collective-permute-start | bytes 196616 | tf_op jit(solution)/shard_map/ppermute | solution.py:309
  120.1 5.6 %collective-permute-start.23 = (f32[2,128,128]{2,1,0:T(8,128)S(1)}, f32[2,128,128]{2,1,0:T(8,128)S(1)}, u32[]{:S(2)}, u32[]{:S(2)}) collective-permute-start(f32[2,128,128]{2,1,0:T(8,128)S(1)} %pad_maximum_fusion.6), channel_id=1, source_target_pairs={{0,8},{8,0},{1,9},{9,1},{2,10},{10,2},{3,11},{11,3},{4,12},{12,4},... | collective-permute-start | bytes 393224 | tf_op jit(solution)/shard_map/ppermute | solution.py:309
  120.3 3.9 %collective-permute-start.17 = (f32[2,128,128]{2,1,0:T(8,128)S(1)}, f32[2,128,128]{2,1,0:T(8,128)S(1)}, u32[]{:S(2)}, u32[]{:S(2)}) collective-permute-start(f32[2,128,128]{2,1,0:T(8,128)S(1)} %pad_maximum_fusion.4), channel_id=1, source_target_pairs={{0,64},{64,0},{1,65},{65,1},{2,66},{66,2},{3,67},{67,3},{4,68},{68... | collective-permute-start | bytes 393224 | tf_op jit(solution)/shard_map/ppermute | solution.py:309
  121.7 4.8 %collective-permute-start.20 = (f32[2,128,128]{2,1,0:T(8,128)S(1)}, f32[2,128,128]{2,1,0:T(8,128)S(1)}, u32[]{:S(2)}, u32[]{:S(2)}) collective-permute-start(f32[2,128,128]{2,1,0:T(8,128)S(1)} %pad_maximum_fusion.5), channel_id=1, source_target_pairs={{0,1},{1,0},{2,3},{3,2},{4,5},{5,4},{6,7},{7,6},{8,9},{9,8},{10,11... | collective-permute-start | bytes 393224 | tf_op jit(solution)/shard_map/ppermute | solution.py:309
  124.2 6.0 %collective-permute-start.18 = (f32[4,128,128]{2,1,0:T(8,128)S(1)}, f32[4,128,128]{2,1,0:T(8,128)S(1)}, u32[]{:S(2)}, u32[]{:S(2)}) collective-permute-start(f32[4,128,128]{2,1,0:T(8,128)S(1)} %pad_maximum_fusion), channel_id=1, source_target_pairs={{0,8},{8,0},{1,9},{9,1},{2,10},{10,2},{3,11},{11,3},{4,12},{12,4},... | collective-permute-start | bytes 786440 | tf_op jit(solution)/shard_map/ppermute | solution.py:309
  125.7 25.6 %copy-start.19 = (bf16[2,128,256]{2,1,0:T(8,128)(2,1)S(1)}, bf16[2,128,256]{2,1,0:T(8,128)(2,1)}, u32[]{:S(2)}) copy-start(bf16[2,128,256]{2,1,0:T(8,128)(2,1)} %copy-done.18) | copy-start | bytes 393220
  125.7 27.9 %copy-start.17 = (bf16[2,128,256]{2,1,0:T(8,128)(2,1)S(1)}, bf16[2,128,256]{2,1,0:T(8,128)(2,1)}, u32[]{:S(2)}) copy-start(bf16[2,128,256]{2,1,0:T(8,128)(2,1)} %copy-done.16) | copy-start | bytes 393220
  125.7 9.8 %collective-permute-start.24 = (f32[4,128,128]{2,1,0:T(8,128)S(1)}, f32[4,128,128]{2,1,0:T(8,128)S(1)}, u32[]{:S(2)}, u32[]{:S(2)}) collective-permute-start(f32[4,128,128]{2,1,0:T(8,128)S(1)} %pad_maximum_fusion.2), channel_id=1, source_target_pairs={{0,1},{1,0},{2,3},{3,2},{4,5},{5,4},{6,7},{7,6},{8,9},{9,8},{10,11... | collective-permute-start | bytes 786440 | tf_op jit(solution)/shard_map/ppermute | solution.py:309
  126.5 33.5 %copy-start.15 = (bf16[2,1024,256]{2,1,0:T(8,128)(2,1)S(1)}, bf16[2,1024,256]{2,1,0:T(8,128)(2,1)}, u32[]{:S(2)}) copy-start(bf16[2,1024,256]{2,1,0:T(8,128)(2,1)} %copy-done.14) | copy-start | bytes 3145732
  126.5 33.5 %copy-start.2 = (bf16[1,2,8,128,256]{4,3,2,1,0:T(8,128)(2,1)S(1)}, bf16[1,2,8,128,256]{4,3,2,1,0:T(8,128)(2,1)}, u32[]{:S(2)}) copy-start(bf16[1,2,8,128,256]{4,3,2,1,0:T(8,128)(2,1)} %param.4) | copy-start | bytes 3145732
  126.5 33.5 %copy-start.9 = (f32[8,8,128]{2,1,0:T(8,128)S(1)}, f32[8,8,128]{2,1,0:T(8,128)}, u32[]{:S(2)}) copy-start(f32[8,8,128]{2,1,0:T(8,128)} %copy-done.7) | copy-start | bytes 98308
  126.5 33.5 %copy-start.13 = (bf16[3,3,256,256]{3,2,1,0:T(8,128)(2,1)S(1)}, bf16[3,3,256,256]{3,2,1,0:T(8,128)(2,1)}, u32[]{:S(2)}) copy-start(bf16[3,3,256,256]{3,2,1,0:T(8,128)(2,1)} %refs_3_.1) | copy-start | bytes 3538948
  126.6 6.3 %collective-permute-start.21 = (f32[4,128,128]{2,1,0:T(8,128)S(1)}, f32[4,128,128]{2,1,0:T(8,128)S(1)}, u32[]{:S(2)}, u32[]{:S(2)}) collective-permute-start(f32[4,128,128]{2,1,0:T(8,128)S(1)} %pad_maximum_fusion.1), channel_id=1, source_target_pairs={{0,64},{64,0},{1,65},{65,1},{2,66},{66,2},{3,67},{67,3},{4,68},{68... | collective-permute-start | bytes 786440 | tf_op jit(solution)/shard_map/ppermute | solution.py:309
  136.2 46.9 %collective-permute-start.25 = (f32[24,128,128]{2,1,0:T(8,128)}, f32[24,128,128]{2,1,0:T(8,128)}, u32[]{:S(2)}, u32[]{:S(2)}) collective-permute-start(f32[24,128,128]{2,1,0:T(8,128)} %constant_dynamic-update-slice_fusion.refs_1_), channel_id=1, source_target_pairs={{0,32},{32,0},{1,33},{33,1},{2,34},{34,2},{3,35},{35,3},{4,36},{36... | collective-permute-start | bytes 4718600 | tf_op jit(solution)/shard_map/ppermute | solution.py:309
  147.0 25.8 %collective-permute-start.2 = (bf16[2,1024,256]{2,1,0:T(8,128)(2,1)S(1)}, bf16[2,1024,256]{2,1,0:T(8,128)(2,1)}, u32[]{:S(2)}, u32[]{:S(2)}) collective-permute-start(bf16[2,1024,256]{2,1,0:T(8,128)(2,1)S(1)} %get-tuple-element.14.hid_ref), channel_id=1, source_target_pairs={{0,8},{8,16},{16,24},{1,9},{9,17},{17,25},{2,10},{10,18},{18,26},{... | collective-permute-start | bytes 3145736 | tf_op jit(solution)/shard_map/ppermute | solution.py:315
  151.3 4.8 %collective-permute-start.4 = (bf16[2,128,256]{2,1,0:T(8,128)(2,1)S(1)}, bf16[2,128,256]{2,1,0:T(8,128)(2,1)S(1)}, u32[]{:S(2)}, u32[]{:S(2)}) collective-permute-start(bf16[2,128,256]{2,1,0:T(8,128)(2,1)S(1)} %copy-done.19), channel_id=1, source_target_pairs={{0,1},{1,2},{2,3},{3,4},{4,5},{5,6},{6,7},{8,9},{9,10},{10,11},{11... | collective-permute-start | bytes 393224 | tf_op jit(solution)/shard_map/ppermute | solution.py:315
  153.6 6.4 %collective-permute-start.5 = (bf16[2,128,256]{2,1,0:T(8,128)(2,1)S(1)}, bf16[2,128,256]{2,1,0:T(8,128)(2,1)S(1)}, u32[]{:S(2)}, u32[]{:S(2)}) collective-permute-start(bf16[2,128,256]{2,1,0:T(8,128)(2,1)S(1)} %copy-done.17), channel_id=1, source_target_pairs={{1,0},{2,1},{3,2},{4,3},{5,4},{6,5},{7,6},{9,8},{10,9},{11,10},{12... | collective-permute-start | bytes 393224 | tf_op jit(solution)/shard_map/ppermute | solution.py:315
  165.3 1.3 copy-start.4
  167.2 10.8 %all-to-all-start.1 = ((f32[8,8,128]{2,1,0:T(8,128)}), f32[8,8,128]{2,1,0:T(8,128)}, u32[]{:S(2)}, u32[]{:S(2)}) async-start(f32[8,8,128]{2,1,0:T(8,128)} %copy-done.11), calls=%async_computation.1 | async-start | bytes 65536 | tf_op jit(solution)/shard_map/all_to_all | solution.py:400
  178.0 1.6 copy-start.5
  179.6 0.8 copy-start.10
  (4 other events, 2.5 us)

commit v2 on v1

--- a/solution.py
+++ b/solution.py
@@ -9,6 +9,7 @@
 from jax.sharding import PartitionSpec as P
 
 GROUPS = 32
+tied = lax.optimization_barrier
 EPSILON = 1e-05
 CLIP_DIVISOR = 20.0
 F32 = jnp.float32
@@ -16,7 +17,7 @@
 DP = ("yh", "yl", "core")
 TM = ("xh", "xl")
 HEIGHT = ("zh", "zl")
-REST = ("yh", "xh", "zh")
+ROUNDS = (("yh", "xh"), ("zh",))
 ORDERS = (("xl", "yl", "zl"), ("yl", "zl", "xl"), ("zl", "xl", "yl"))
 VMEM = pl.BlockSpec(memory_space=pltpu.VMEM)
 SMEM = pl.BlockSpec(memory_space=pltpu.SMEM)
@@ -24,7 +25,7 @@
 TN = (((0,), (0,)), ((), ()))
 
 
-def call(kernel, outs, args, flops, scratch=(), smem=0, limit=40):
+def call(kernel, outs, args, flops, scratch=(), smem=0, limit=16):
     nbytes = sum(a.size * a.dtype.itemsize for a in (*args, *outs))
     specs = [SMEM] * smem + [VMEM] * (len(args) - smem)
     return pl.pallas_call(
@@ -90,9 +91,11 @@
     return jnp.sum(v.reshape(v.shape[0] // 8, 8, v.shape[1]), axis=0)
 
 
-def stats_kernel(x_ref, o_ref):
+def stats_kernel(x_ref, o_ref, top_ref, bot_ref):
     sums = []
     for f in range(2):
+        top_ref[f] = x_ref[f, 0:128, :]
+        bot_ref[f] = x_ref[f, 896:1024, :]
 
         def step(r, carry):
             v = x_ref[f, pl.ds(pl.multiple_of(r * 128, 128), 128), :].astype(F32)
@@ -171,14 +174,24 @@
         bot_ref[f] = pg_ref[f, 896:1024, :]
 
 
+def row_places(info):
+    return [
+        pl.multiple_of((((s // 4) ^ info[6]) * 4 + ((s % 4) ^ info[7])) * 8, 8) for s in range(16)
+    ]
+
+
 def grads_kernel(info, act_ref, pg_ref, hid_ref, cot_ref, later_ref, g_ref):
+    places = row_places(info)
+
     def put(tap, v):
         for q in range(4):
             b = 4 * tap + q
             pair, third, bits = b // 24, (b % 24) // 8, b % 8
             at = (pair ^ info[0]) * 24 + third * 8 + (bits ^ info[1 + third])
             rh, lh = q % 2, q // 2
-            g_ref[at] = v[rh * 128 : rh * 128 + 128, lh * 128 : lh * 128 + 128]
+            for s in range(16):
+                row = rh * 128 + s * 8
+                g_ref[at, pl.ds(places[s], 8), :] = v[row : row + 8, lh * 128 : lh * 128 + 128]
 
     for i in range(3):
         for j in range(3):
@@ -275,24 +288,30 @@
         lax.fori_loop(0, 4, part, 0)
 
 
-def clip_kernel(clip_level, info, own_ref, other_ref, s_ref, t_ref):
-    core = info[0]
-
-    def block(tap, q):
-        b = 4 * tap + q
-        pair, third, bits = b // 24, (b % 24) // 8, b % 8
-        at = third * 8 + (bits ^ info[1 + third])
-        mine = (pair ^ core) == 0
-        return jnp.where(mine, own_ref[at], other_ref[at])
-
+def clip_kernel(clip_level, info, *refs):
+    s_ref, t_ref = refs[12:]
+    places = row_places(info)
     acc = jnp.zeros((8, 128), F32)
     for tap in range(12):
         ref, k = (s_ref, tap) if tap < 9 else (t_ref, tap - 9)
         for q in range(4):
-            v = block(tap, q)
+            b = 4 * tap + q
+            pair, third, bits = b // 24, (b % 24) // 8, b % 8
+            at = bits ^ info[1 + third]
+            low, slot = at < 4, at & 3
+            mine = (pair ^ info[0]) == 0
             rh, lh = q % 2, q // 2
-            ref[k, rh * 128 : rh * 128 + 128, lh * 128 : lh * 128 + 128] = v
-            acc = acc + fold(v * v)
+            for s in range(16):
+                rows = pl.ds(places[s], 8)
+                own_low, own_high, low_ref, high_ref = refs[4 * third : 4 * third + 4]
+                v = jnp.where(
+                    mine,
+                    jnp.where(low, own_low[slot, rows, :], own_high[slot, rows, :]),
+                    jnp.where(low, low_ref[slot, rows, :], high_ref[slot, rows, :]),
+                )
+                row = rh * 128 + s * 8
+                ref[k, row : row + 8, lh * 128 : lh * 128 + 128] = v
+                acc = acc + v * v
     total = jnp.sum(jnp.sum(acc, axis=0, keepdims=True), axis=1, keepdims=True)
     scale = clip_level / jnp.maximum(jnp.sqrt(total), clip_level)
 
@@ -303,6 +322,10 @@
     lax.fori_loop(0, 9, finish, 0)
     for k in range(3):
         t_ref[k] = t_ref[k] * scale
+
+
+def in_hbm(x):
+    return pltpu.with_memory_space_constraint(x, pltpu.HBM)
 
 
 def swapped(x, axis):
@@ -315,25 +338,35 @@
     return lax.ppermute(x, axes, route)
 
 
-def reduced(g):
-    g = g[:24] + swapped(g[24:], "core")
-    parts = [g[8 * t : 8 * t + 8] for t in range(3)]
-    for step, half in enumerate((4, 2, 1)):
-        got = [swapped(p[half:], ORDERS[t][step]) for t, p in enumerate(parts)]
-        parts = [p[:half] + r for p, r in zip(parts, got)]
-    pieces = jnp.concatenate([p.reshape(16, 8, 128) for p in parts], axis=1)
-    return jnp.sum(lax.all_to_all(pieces, REST, 0, 0, tiled=True), axis=0)
-
-
-def gathered(own):
-    copies = jnp.broadcast_to(own, (16, *own.shape))
-    pieces = lax.all_to_all(copies, REST, 0, 0, tiled=True)
-    parts = [pieces[:, 8 * t : 8 * t + 8].reshape(1, 128, 128) for t in range(3)]
-    for step in (2, 1, 0):
-        got = [swapped(p, ORDERS[t][step]) for t, p in enumerate(parts)]
-        parts = [jnp.concatenate([p, r], axis=0) for p, r in zip(parts, got)]
-    mine = jnp.concatenate(parts, axis=0)
-    return mine, swapped(mine, "core")
+def others(pieces, axes):
+    n = lax.axis_size(axes)
+    return [
+        lax.ppermute(pieces(d), axes, [(i, i ^ d) for i in range(n)]) for d in range(1, n)
+    ]
+
+
+def halved(parts, step):
+    half = parts[0].shape[0] // 2
+    keep, send = tied(([p[:half] for p in parts], [p[half:] for p in parts]))
+    got = tied([swapped(p, ORDERS[t][step]) for t, p in enumerate(send)])
+    return [p + r for p, r in zip(keep, got)]
+
+
+def doubled(parts, step):
+    return tied([swapped(p, ORDERS[t][step]) for t, p in enumerate(parts)])
+
+
+def quartered(m, axes):
+    m = m.reshape(3, 4, m.shape[1] // 4, 128)
+    total = m[:, 0]
+    for r in others(lambda d: m[:, d], axes):
+        total = total + r
+    return total
+
+
+def spread(m, axes):
+    pieces = [m, *others(lambda d: m, axes)]
+    return jnp.stack(pieces, axis=1).reshape(3, 4 * m.shape[1], 128)
 
 
 def body(video_latents, cotangent, spatial_kernel, temporal_kernel):
@@ -349,7 +382,13 @@
     bit = {a: lax.axis_index(a) for a in ("xl", "yl", "zl")}
     codes = [4 * bit[a] + 2 * bit[b] + bit[c] for a, b, c in ORDERS]
     info = jnp.stack(
-        [lax.axis_index("core"), *codes, (z > 0).astype(jnp.int32), (z < peers - 1).astype(jnp.int32)]
+        [
+            lax.axis_index("core"),
+            *codes,
+            (z > 0).astype(jnp.int32),
+            (z < peers - 1).astype(jnp.int32),
+            *[lax.axis_index(axes) for axes in ROUNDS],
+        ]
     ).astype(jnp.int32)
     pixels = rows * columns
     flat = (2, pixels, 256)
@@ -360,11 +399,12 @@
     gflop = 2 * 2048 * 256 * 256
 
     later = moved(cot, TM, -1)
-    up = moved(x[:, pixels - columns :], HEIGHT, 1)
-    dn = moved(x[:, :columns], HEIGHT, -1)
     small = out((8, 8, 128), F32)
-    (st,) = call(stats_kernel, [small], [x], 1 << 21)
-    st = lax.all_to_all(st, HEIGHT, 0, 0, tiled=True)
+    edge = out((2, columns, 256), BF16)
+    st, x_top, x_bot = call(stats_kernel, [small, edge, edge], [x], 1 << 21)
+    st = in_hbm(lax.all_to_all(st, HEIGHT, 0, 0, tiled=True))
+    up = in_hbm(moved(x_bot, HEIGHT, 1))
+    dn = in_hbm(moved(x_top, HEIGHT, -1))
     act, hid, slope = call(
         lambda *refs: forward_kernel(members, *refs),
         [out((2, 1280, 768), BF16), out(flat, BF16), out(flat, F32)],
@@ -372,7 +412,6 @@
         9 * gflop,
         smem=1,
     )
-    edge = out((2, columns, 256), BF16)
     pg, top, bot = call(
         pregrad_kernel, [out(flat, BF16), edge, edge], [cot, later, slope, temporal_kernel], 3 * gflop
     )
@@ -381,15 +420,9 @@
     (g,) = call(
         grads_kernel, [out((48, 128, 128), F32)], [info, act, pg, hid, cot, later], 12 * gflop, smem=1
     )
-    own = reduced(g)
-    mine, other = gathered(own)
-    clipped_spatial, clipped_temporal = call(
-        lambda *refs: clip_kernel(clip_level, *refs),
-        [out((9, 256, 256), F32), out((3, 256, 256), F32)],
-        [info, mine, other],
-        1 << 21,
-        smem=1,
-    )
+    g, gup, gdn = tied((g, gup, gdn))
+    g = g[:24] + swapped(g[24:], "core")
+    parts = halved([g[8 * t : 8 * t + 8] for t in range(3)], 0)
     ng, gst = call(
         lambda *refs: backward_kernel(members, *refs),
         [out(flat, F32), small],
@@ -397,12 +430,36 @@
         9 * gflop,
         scratch=[pltpu.VMEM((2, 1280, 256), BF16)] * 3,
     )
-    gst = lax.all_to_all(gst, HEIGHT, 0, 0, tiled=True)
+    parts, ng, gst = tied((parts, ng, gst))
+    gst = in_hbm(lax.all_to_all(gst, HEIGHT, 0, 0, tiled=True))
+    parts = halved(parts, 1)
+    parts = halved(parts, 2)
+    parts, hid_sent, gst = tied((parts, hid, gst))
+    prev = moved(hid_sent, TM, 1)
+    own = quartered(jnp.concatenate(parts, axis=0), ROUNDS[0])
+    own = quartered(own, ROUNDS[1])
     (input_grad,) = call(
         lambda *refs: input_grad_kernel(members, *refs), [out(flat, BF16)], [x, cot, ng, st, gst], 1 << 21
     )
-    prev = moved(hid, TM, 1)
+    full = spread(own, ROUNDS[1])
+    full, input_grad = tied((full, input_grad))
+    full = spread(full, ROUNDS[0])
+    parts = [full[t : t + 1] for t in range(3)]
+    parts = [jnp.concatenate([p, r]) for p, r in zip(parts, doubled(parts, 2))]
     (block_output,) = call(block_kernel, [out(flat, BF16)], [x, hid, prev, temporal_kernel], 3 * gflop)
+    parts, block_output = tied((parts, block_output))
+    parts = [jnp.concatenate([p, r]) for p, r in zip(parts, doubled(parts, 1))]
+    high = doubled(parts, 0)
+    pieces = []
+    for p, h in zip(parts, high):
+        pieces += [p, h, swapped(p, "core"), swapped(h, "core")]
+    clipped_spatial, clipped_temporal = call(
+        lambda *refs: clip_kernel(clip_level, *refs),
+        [out((9, 256, 256), F32), out((3, 256, 256), F32)],
+        [info, *pieces],
+        1 << 21,
+        smem=1,
+    )
     return (
         block_output.reshape(video_latents.shape),
         input_grad.reshape(video_latents.shape),

time: 189 us -> 168 us (0.89)
  blocking collectives: 35.3 us -> 0 us
  starting transfers between devices: 55.5 us -> 87.2 us
  local copies, waits for them, and re-layouts: 23 us -> 10.2 us
  waiting for transfers between devices: 41.7 us -> 32.3 us
  other arithmetic: 0.53 us -> 5.9 us
    all_to_all x2 -> x0, blocking collectives: 35.3 us -> none  [the longest x1 19.6 us: reduced(): return jnp.sum(lax.all_to_all(pieces, REST, 0, 0, tiled=True), axis=0)]
    ppermute x0 -> x12, starting transfers between devices: none -> 23 us  [others(): lax.ppermute(pieces(d), axes, [(i, i ^ d) for i in range(n)])]
    ppermute x20 -> x25, waiting for transfers between devices: 27.2 us -> 13.4 us  [swapped(): return lax.ppermute(x, axis, [(0, 1), (1, 0)])]
    unnamed x59 -> x29, local copies, waits for them, and re-layouts: 21 us -> 7.75 us
    ppermute x0 -> x12, waiting for transfers between devices: none -> 9.46 us  [others(): lax.ppermute(pieces(d), axes, [(i, i ^ d) for i in range(n)])]
    ppermute x20 -> x25, starting transfers between devices: 28.1 us -> 37.2 us  [swapped(): return lax.ppermute(x, axis, [(0, 1), (1, 0)])]
    ppermute x6, waiting for transfers between devices: 6.78 us -> 0.28 us  [moved(): return lax.ppermute(x, axes, route)]
    add x6 -> x11, other arithmetic: 0.39 us -> 4.9 us  [the longest x9 4.68 us: halved(): return [p + r for p, r in zip(keep, got)]]
  transfers between devices with their start and end apart: 28 -> 45, of which waited for: 18 -> 19; matrix products, arithmetic and copies ran while one was open for 5% -> 3% of each run, Pallas kernels for 10% -> 12%
where the time goes in v2:
time: 168 us; the launch traced here: 167 us
  starting transfers between devices  87.2 us (52%)
  waiting for transfers between devices  32.3 us (19%)
  Pallas kernels  30.4 us (18%)
  local copies, waits for them, and re-layouts  10.2 us (6%)
  other arithmetic  5.9 us (4%)
    ppermute x25, starting transfers between devices, swapped(): return lax.ppermute(x, axis, [(0, 1), (1, 0)])  37.2 us
    pallas_call x8, Pallas kernels, call(): pl.pallas_call(kernel, out_shape=tuple(outs), in_specs=specs, out_specs=t...  30.4 us
    ppermute x12, starting transfers between devices, others(): lax.ppermute(pieces(d), axes, [(i, i ^ d) for i in range(n)])  23 us
    ppermute x25, waiting for transfers between devices, swapped(): return lax.ppermute(x, axis, [(0, 1), (1, 0)])  13.4 us
    ppermute x6, starting transfers between devices, moved(): return lax.ppermute(x, axes, route)  13.2 us
    all_to_all x1, starting transfers between devices, body(): st = in_hbm(lax.all_to_all(st, HEIGHT, 0, 0, tiled=True))  9.85 us
    ppermute x12, waiting for transfers between devices, others(): lax.ppermute(pieces(d), axes, [(i, i ^ d) for i in range(n)])  9.46 us
    unnamed x29, local copies, waits for them, and re-layouts  7.75 us
  transfers between devices with their start and end apart: 45, of which 19 were waited for; matrix products, arithmetic and copies ran while one was open for 3% of the time, Pallas kernels for 12%

profile of v2, /device:TPU:1, one launch (start us, length us, event | category | flops | bytes accessed | tf_op | source)
XLA Modules:
  0.0 167.0 jit_solution(11265352857731612767)
XLA Ops:
  0.6 1.3 collective-permute-start.2
  1.9 1.2 copy-done
  4.1 4.4 %collective-permute-start = (bf16[2,128,256]{2,1,0:T(8,128)(2,1)S(1)}, bf16[2,128,256]{2,1,0:T(8,128)(2,1)S(1)}, u32[]{:S(2)}, u32[]{:S(2)}) collective-permute-start(bf16[2,128,256]{2,1,0:T(8,128)(2,1)S(1)} %get-tuple-element.72), channel_id=1, source_target_pairs={{0,1},{1,2},{2,3},{3,4},{4,5},{5,6},{6,7},{8,9},{9,10},{10,11},{11... | collective-permute-start | bytes 393224 | tf_op jit(solution)/shard_map/ppermute | solution.py:338
  8.5 1.3 collective-permute-start.1
  9.8 9.8 %all-to-all-start = ((f32[8,8,128]{2,1,0:T(8,128)}), f32[8,8,128]{2,1,0:T(8,128)S(1)}, u32[]{:S(2)}, u32[]{:S(2)}) async-start(f32[8,8,128]{2,1,0:T(8,128)} %get-tuple-element.74), calls=%async_computation | async-start | bytes 65536 | tf_op jit(solution)/shard_map/all_to_all | solution.py:405
  19.7 6.8 %all-to-all-done.refs_4_.refs_5_.refs_3_ = f32[8,8,128]{2,1,0:T(8,128)S(1)} async-done(((f32[8,8,128]{2,1,0:T(8,128)}), f32[8,8,128]{2,1,0:T(8,128)S(1)}, u32[]{:S(2)}, u32[]{:S(2)}) %all-to-all-start) | async-done | bytes 32800 | tf_op jit(solution)/shard_map/all_to_all | solution.py:405
  27.9 1.2 copy-done.1
  29.1 1.3 copy-done.8
  30.4 6.9 %shard_map.76 = (bf16[2,1280,768]{2,1,0:T(8,128)(2,1)S(1)}, bf16[2,1024,256]{2,1,0:T(8,128)(2,1)S(1)}, f32[2,1024,256]{2,1,0:T(8,128)S(1)}) custom-call(s32[8]{0:T(128)S(1)} %stack.73.refs_0_.info, bf16[2,1024,256]{2,1,0:T(8,128)(2,1)S(1)} %bitcast.87, bf16[2,128,256]{2,1,0:T(8,128)(2,1)} %copy-done.11, bf16[2,128,256]{2,1,0:T(8,128)(2,1)} %copy-done.12, ...), custom_call_target="tpu_custom_call" | custom-call | flops 2415919104 | bytes 9601056 | tf_op jit(solution)/shard_map/pallas_call | solution.py:31
  37.3 2.4 %shard_map.77 = (bf16[2,1024,256]{2,1,0:T(8,128)(2,1)S(1)}, bf16[2,128,256]{2,1,0:T(8,128)(2,1)S(1)}, bf16[2,128,256]{2,1,0:T(8,128)(2,1)S(1)}) custom-call(bf16[2,1024,256]{2,1,0:T(8,128)(2,1)S(1)} %bitcast.92, bf16[2,1024,256]{2,1,0:T(8,128)(2,1)S(1)} %collective-permute-done.2.later_ref, f32[2,1024,256]{2,1,0:T(8,128)S(1)} %get-tuple-element.76.slope_ref, ...), custom_call_target="tpu_custom_call" | custom-call | flops 805306368 | bytes 5898240 | tf_op jit(solution)/shard_map/pallas_call | solution.py:31
  39.7 2.2 %collective-permute-start.3 = (bf16[2,128,256]{2,1,0:T(8,128)(2,1)S(1)}, bf16[2,128,256]{2,1,0:T(8,128)(2,1)S(1)}, u32[]{:S(2)}, u32[]{:S(2)}) collective-permute-start(bf16[2,128,256]{2,1,0:T(8,128)(2,1)S(1)} %get-tuple-element.79), channel_id=1, source_target_pairs={{0,1},{1,2},{2,3},{3,4},{4,5},{5,6},{6,7},{8,9},{9,10},{10,11},{11... | collective-permute-start | bytes 393224 | tf_op jit(solution)/shard_map/ppermute | solution.py:338
  41.9 1.3 collective-permute-start.4
  43.2 4.1 %shard_map.78 = f32[48,128,128]{2,1,0:T(8,128)S(1)} custom-call(s32[8]{0:T(128)S(1)} %stack.73.refs_0_.info, bf16[2,1280,768]{2,1,0:T(8,128)(2,1)S(1)} %get-tuple-element.75.act_ref, bf16[2,1024,256]{2,1,0:T(8,128)(2,1)S(1)} %get-tuple-element.77.pg_ref.refs_0_, bf16[2,1024,256]{2,1,0:T(8,128)(2,1)S(1)} %get-tuple-element.126.hid_ref, ...), custom_call_target="tpu_custom_call" | custom-call | flops 3221225472 | bytes 11272224 | tf_op jit(solution)/shard_map/pallas_call | solution.py:31
  47.8 4.2 %collective-permute-start.5 = (f32[24,128,128]{2,1,0:T(8,128)S(1)}, f32[24,128,128]{2,1,0:T(8,128)S(1)}, u32[]{:S(2)}, u32[]{:S(2)}) collective-permute-start(f32[24,128,128]{2,1,0:T(8,128)S(1)} %slice.112), channel_id=1, source_target_pairs={{0,32},{32,0},{1,33},{33,1},{2,34},{34,2},{3,35},{35,3},{4,36},{36... | collective-permute-start | bytes 4718600 | tf_op jit(solution)/shard_map/ppermute | solution.py:332
  51.9 3.0 %collective-permute-done.5 = f32[24,128,128]{2,1,0:T(8,128)S(1)} collective-permute-done((f32[24,128,128]{2,1,0:T(8,128)S(1)}, f32[24,128,128]{2,1,0:T(8,128)S(1)}, u32[]{:S(2)}, u32[]{:S(2)}) %collective-permute-start.5) | collective-permute-done | bytes 1572896 | tf_op jit(solution)/shard_map/ppermute | solution.py:332
  55.3 2.4 %collective-permute-start.6 = (f32[4,128,128]{2,1,0:T(8,128)S(1)}, f32[4,128,128]{2,1,0:T(8,128)S(1)}, u32[]{:S(2)}, u32[]{:S(2)}) collective-permute-start(f32[4,128,128]{2,1,0:T(8,128)S(1)} %get-tuple-element.83), channel_id=1, source_target_pairs={{0,8},{8,0},{1,9},{9,1},{2,10},{10,2},{3,11},{11,3},{4,12},{12,4},... | collective-permute-start | bytes 786440 | tf_op jit(solution)/shard_map/ppermute | solution.py:332
  57.8 1.3 collective-permute-start.7
  60.1 6.0 %shard_map.79 = (f32[2,1024,256]{2,1,0:T(8,128)S(1)}, f32[8,8,128]{2,1,0:T(8,128)S(1)}) custom-call(bf16[2,1024,256]{2,1,0:T(8,128)(2,1)S(1)} %get-tuple-element.77.pg_ref.refs_0_, bf16[2,128,256]{2,1,0:T(8,128)(2,1)S(1)} %collective-permute-done.3.refs_1_, bf16[2,128,256]{2,1,0:T(8,128)(2,1)S(1)} %collective-permute-done.4.refs_2_, ...), custom_call_target="tpu_custom_call" | custom-call | flops 2415919104 | bytes 5701632 | tf_op jit(solution)/shard_map/pallas_call | solution.py:31
  68.7 2.5 %collective-permute-done.9 = f32[2,128,128]{2,1,0:T(8,128)S(1)} collective-permute-done((f32[2,128,128]{2,1,0:T(8,128)S(1)}, f32[2,128,128]{2,1,0:T(8,128)S(1)}, u32[]{:S(2)}, u32[]{:S(2)}) %collective-permute-start.9) | collective-permute-done | bytes 131104 | tf_op jit(solution)/shard_map/ppermute | solution.py:332
  75.4 1.2 collective-permute-start.14
  76.5 3.9 %all-to-all-start.1 = ((f32[8,8,128]{2,1,0:T(8,128)}), f32[8,8,128]{2,1,0:T(8,128)}, u32[]{:S(2)}, u32[]{:S(2)}) async-start(f32[8,8,128]{2,1,0:T(8,128)} %copy-done.7), calls=%async_computation.1 | async-start | bytes 65536 | tf_op jit(solution)/shard_map/all_to_all | solution.py:434
  80.5 1.5 add.89
  82.0 1.5 add.87
  83.5 1.5 add.88
  85.0 2.3 %all-to-all-done.1.refs_4_ = f32[8,8,128]{2,1,0:T(8,128)} async-done(((f32[8,8,128]{2,1,0:T(8,128)}), f32[8,8,128]{2,1,0:T(8,128)}, u32[]{:S(2)}, u32[]{:S(2)}) %all-to-all-start.1) | async-done | bytes 32800 | tf_op jit(solution)/shard_map/all_to_all | solution.py:434
  88.3 3.0 %collective-permute-start.15 = (f32[3,32,128]{2,1,0:T(8,128)S(1)}, f32[3,32,128]{2,1,0:T(8,128)S(1)}, u32[]{:S(2)}, u32[]{:S(2)}) collective-permute-start(f32[3,32,128]{2,1,0:T(8,128)S(1)} %get-tuple-element.155), channel_id=1, source_target_pairs={{0,16},{16,0},{128,144},{144,128},{1,17},{17,1},{129,145},{145,129... | collective-permute-start | bytes 147464 | tf_op jit(solution)/shard_map/ppermute | solution.py:344
  91.3 2.4 %collective-permute-start.17 = (f32[3,32,128]{2,1,0:T(8,128)S(1)}, f32[3,32,128]{2,1,0:T(8,128)S(1)}, u32[]{:S(2)}, u32[]{:S(2)}) collective-permute-start(f32[3,32,128]{2,1,0:T(8,128)S(1)} %get-tuple-element.156), channel_id=1, source_target_pairs={{0,144},{16,128},{128,16},{144,0},{1,145},{17,129},{129,17},{145,1... | collective-permute-start | bytes 147464 | tf_op jit(solution)/shard_map/ppermute | solution.py:344
  94.1 4.1 %collective-permute-done.17 = f32[3,32,128]{2,1,0:T(8,128)S(1)} collective-permute-done((f32[3,32,128]{2,1,0:T(8,128)S(1)}, f32[3,32,128]{2,1,0:T(8,128)S(1)}, u32[]{:S(2)}, u32[]{:S(2)}) %collective-permute-start.17) | collective-permute-done | bytes 49184 | tf_op jit(solution)/shard_map/ppermute | solution.py:344
  98.9 3.1 %collective-permute-start.19 = (f32[3,8,128]{2,1,0:T(8,128)S(1)}, f32[3,8,128]{2,1,0:T(8,128)S(1)}, u32[]{:S(2)}, u32[]{:S(2)}) collective-permute-start(f32[3,8,128]{2,1,0:T(8,128)S(1)} %get-tuple-element.165), channel_id=1, source_target_pairs={{0,4},{2,6},{4,0},{6,2},{1,5},{3,7},{5,1},{7,3},{8,12},{10,14},{12... | collective-permute-start | bytes 36872 | tf_op jit(solution)/shard_map/ppermute | solution.py:344
  102.0 2.4 %collective-permute-start.20 = (f32[3,8,128]{2,1,0:T(8,128)S(1)}, f32[3,8,128]{2,1,0:T(8,128)S(1)}, u32[]{:S(2)}, u32[]{:S(2)}) collective-permute-start(f32[3,8,128]{2,1,0:T(8,128)S(1)} %get-tuple-element.166), channel_id=1, source_target_pairs={{0,6},{2,4},{4,2},{6,0},{1,7},{3,5},{5,3},{7,1},{8,14},{10,12},{12... | collective-permute-start | bytes 36872 | tf_op jit(solution)/shard_map/ppermute | solution.py:344
  104.4 2.8 %collective-permute-start.30 = (bf16[2,1024,256]{2,1,0:T(8,128)(2,1)S(1)}, bf16[2,1024,256]{2,1,0:T(8,128)(2,1)S(1)}, u32[]{:S(2)}, u32[]{:S(2)}) collective-permute-start(bf16[2,1024,256]{2,1,0:T(8,128)(2,1)S(1)} %get-tuple-element.126.hid_ref), channel_id=1, source_target_pairs={{0,8},{8,16},{16,24},{1,9},{9,17},{17,25},{2,10},{10,18},{18,26},{... | collective-permute-start | bytes 3145736 | tf_op jit(solution)/shard_map/ppermute | solution.py:338
  107.3 1.9 %collective-permute-start.23 = (f32[3,8,128]{2,1,0:T(8,128)S(1)}, f32[3,8,128]{2,1,0:T(8,128)S(1)}, u32[]{:S(2)}, u32[]{:S(2)}) collective-permute-start(f32[3,8,128]{2,1,0:T(8,128)S(1)} %fusion.6), channel_id=1, source_target_pairs={{0,6},{2,4},{4,2},{6,0},{1,7},{3,5},{5,3},{7,1},{8,14},{10,12},{12... | collective-permute-start | bytes 36872 | tf_op jit(solution)/shard_map/ppermute | solution.py:344
  109.2 2.9 %collective-permute-start.22 = (f32[3,8,128]{2,1,0:T(8,128)S(1)}, f32[3,8,128]{2,1,0:T(8,128)S(1)}, u32[]{:S(2)}, u32[]{:S(2)}) collective-permute-start(f32[3,8,128]{2,1,0:T(8,128)S(1)} %fusion.6), channel_id=1, source_target_pairs={{0,4},{2,6},{4,0},{6,2},{1,5},{3,7},{5,1},{7,3},{8,12},{10,14},{12... | collective-permute-start | bytes 36872 | tf_op jit(solution)/shard_map/ppermute | solution.py:344
  113.0 1.6 copy-done.5
  114.6 2.7 %shard_map.80 = bf16[2,1024,256]{2,1,0:T(8,128)(2,1)} custom-call(bf16[2,1024,256]{2,1,0:T(8,128)(2,1)S(1)} %bitcast.89, bf16[2,1024,256]{2,1,0:T(8,128)(2,1)S(1)} %bitcast.94, f32[2,1024,256]{2,1,0:T(8,128)S(1)} %copy-done.5, f32[8,8,128]{2,1,0:T(8,128)} %copy-done.10, f32[8,8,128]{2,1,0:T(8,128)} %all-to-all-done.1.refs_4_), custom_call_target="tpu_custom_call" | custom-call | flops 2097152 | bytes 5308416 | tf_op jit(solution)/shard_map/pallas_call | solution.py:31
  117.4 3.4 %collective-permute-start.26 = (f32[3,32,128]{2,1,0:T(8,128)S(1)}, f32[3,32,128]{2,1,0:T(8,128)S(1)}, u32[]{:S(2)}, u32[]{:S(2)}) collective-permute-start(f32[3,32,128]{2,1,0:T(8,128)S(1)} %maximum_bitcast_fusion), channel_id=1, source_target_pairs={{0,144},{16,128},{128,16},{144,0},{1,145},{17,129},{129,17},{145,1... | collective-permute-start | bytes 147464 | tf_op jit(solution)/shard_map/ppermute | solution.py:344
  120.8 2.2 %collective-permute-start.25 = (f32[3,32,128]{2,1,0:T(8,128)S(1)}, f32[3,32,128]{2,1,0:T(8,128)S(1)}, u32[]{:S(2)}, u32[]{:S(2)}) collective-permute-start(f32[3,32,128]{2,1,0:T(8,128)S(1)} %maximum_bitcast_fusion), channel_id=1, source_target_pairs={{0,128},{16,144},{128,0},{144,16},{1,129},{17,145},{129,1},{145,17... | collective-permute-start | bytes 147464 | tf_op jit(solution)/shard_map/ppermute | solution.py:344
  123.1 4.4 %collective-permute-done.26 = f32[3,32,128]{2,1,0:T(8,128)S(1)} collective-permute-done((f32[3,32,128]{2,1,0:T(8,128)S(1)}, f32[3,32,128]{2,1,0:T(8,128)S(1)}, u32[]{:S(2)}, u32[]{:S(2)}) %collective-permute-start.26) | collective-permute-done | bytes 49184 | tf_op jit(solution)/shard_map/ppermute | solution.py:344
  128.9 2.5 %collective-permute-done.28 = f32[1,128,128]{2,1,0:T(8,128)S(1)} collective-permute-done((f32[1,128,128]{2,1,0:T(8,128)S(1)}, f32[1,128,128]{2,1,0:T(8,128)S(1)}, u32[]{:S(2)}, u32[]{:S(2)}) %collective-permute-start.28) | collective-permute-done | bytes 65568 | tf_op jit(solution)/shard_map/ppermute | solution.py:332
  131.7 3.2 %shard_map.81 = bf16[2,1024,256]{2,1,0:T(8,128)(2,1)} custom-call(bf16[2,1024,256]{2,1,0:T(8,128)(2,1)S(1)} %bitcast.90, bf16[2,1024,256]{2,1,0:T(8,128)(2,1)S(1)} %get-tuple-element.126.hid_ref, bf16[2,1024,256]{2,1,0:T(8,128)(2,1)S(1)} %collective-permute-done.30.prev_ref, bf16[3,256,256]{2,1,0:T(8,128)(2,1)S(1)} %copy-done.6), custom_call_target="tpu_custom_call" | custom-call | flops 805306368 | bytes 4587520 | tf_op jit(solution)/shard_map/pallas_call | solution.py:31
  134.9 1.1 collective-permute-start.31
  136.4 1.7 %collective-permute-start.33 = (f32[2,128,128]{2,1,0:T(8,128)S(1)}, f32[2,128,128]{2,1,0:T(8,128)S(1)}, u32[]{:S(2)}, u32[]{:S(2)}) collective-permute-start(f32[2,128,128]{2,1,0:T(8,128)S(1)} %pad_maximum_fusion.4), channel_id=1, source_target_pairs={{0,8},{8,0},{1,9},{9,1},{2,10},{10,2},{3,11},{11,3},{4,12},{12,4},... | collective-permute-start | bytes 393224 | tf_op jit(solution)/shard_map/ppermute | solution.py:332
  138.7 1.2 collective-permute-done.32
  140.8 1.6 collective-permute-start.36
  143.7 12.8 %collective-permute-start.41 = (f32[4,128,128]{2,1,0:T(8,128)S(1)}, f32[4,128,128]{2,1,0:T(8,128)S(1)}, u32[]{:S(2)}, u32[]{:S(2)}) collective-permute-start(f32[4,128,128]{2,1,0:T(8,128)S(1)} %constant_dynamic-update-slice_fusion.4.refs_9_), channel_id=1, source_target_pairs={{0,32},{32,0},{1,33},{33,1},{2,34},{34,2},{3,35},{35,3},{4,36},{36... | collective-permute-start | bytes 786440 | tf_op jit(solution)/shard_map/ppermute | solution.py:332
  156.6 2.8 %collective-permute-start.37 = (f32[4,128,128]{2,1,0:T(8,128)S(1)}, f32[4,128,128]{2,1,0:T(8,128)S(1)}, u32[]{:S(2)}, u32[]{:S(2)}) collective-permute-start(f32[4,128,128]{2,1,0:T(8,128)S(1)} %constant_dynamic-update-slice_fusion.refs_1_), channel_id=1, source_target_pairs={{0,32},{32,0},{1,33},{33,1},{2,34},{34,2},{3,35},{35,3},{4,36},{36... | collective-permute-start | bytes 786440 | tf_op jit(solution)/shard_map/ppermute | solution.py:332
  159.4 1.6 collective-permute-start.38
  162.9 4.1 %shard_map.82 = (f32[9,256,256]{2,1,0:T(8,128)}, f32[3,256,256]{2,1,0:T(8,128)}) custom-call(s32[8]{0:T(128)S(1)} %stack.73.refs_0_.info, f32[4,128,128]{2,1,0:T(8,128)S(1)} %constant_dynamic-update-slice_fusion.refs_1_, f32[4,128,128]{2,1,0:T(8,128)S(1)} %collective-permute-done.34.refs_2_, f32[4,128,128]{2,1,0:T(8,128)S(1)} %collective-permute-done.37.refs_3_, ...), custom_call_target="tpu_custom_call" | custom-call | flops 2097152 | bytes 6291488 | tf_op jit(solution)/shard_map/pallas_call | solution.py:31
  (111 shorter events, 20.7 us)
Async XLA Ops:
  0.6 36.6 %collective-permute-start.2 = (bf16[2,1024,256]{2,1,0:T(8,128)(2,1)}, bf16[2,1024,256]{2,1,0:T(8,128)(2,1)S(1)}, u32[]{:S(2)}, u32[]{:S(2)}) collective-permute-start(bf16[2,1024,256]{2,1,0:T(8,128)(2,1)} %bitcast.91), channel_id=1, source_target_pairs={{8,0},{16,8},{24,16},{9,1},{17,9},{25,17},{10,2},{18,10},{26,18},{... | collective-permute-start | bytes 3145736 | tf_op jit(solution)/shard_map/ppermute | solution.py:338
  4.1 22.4 %collective-permute-start = (bf16[2,128,256]{2,1,0:T(8,128)(2,1)S(1)}, bf16[2,128,256]{2,1,0:T(8,128)(2,1)S(1)}, u32[]{:S(2)}, u32[]{:S(2)}) collective-permute-start(bf16[2,128,256]{2,1,0:T(8,128)(2,1)S(1)} %get-tuple-element.72), channel_id=1, source_target_pairs={{0,1},{1,2},{2,3},{3,4},{4,5},{5,6},{6,7},{8,9},{9,10},{10,11},{11... | collective-permute-start | bytes 393224 | tf_op jit(solution)/shard_map/ppermute | solution.py:338
  8.5 18.1 %collective-permute-start.1 = (bf16[2,128,256]{2,1,0:T(8,128)(2,1)S(1)}, bf16[2,128,256]{2,1,0:T(8,128)(2,1)S(1)}, u32[]{:S(2)}, u32[]{:S(2)}) collective-permute-start(bf16[2,128,256]{2,1,0:T(8,128)(2,1)S(1)} %get-tuple-element.73), channel_id=1, source_target_pairs={{1,0},{2,1},{3,2},{4,3},{5,4},{6,5},{7,6},{9,8},{10,9},{11,10},{12... | collective-permute-start | bytes 393224 | tf_op jit(solution)/shard_map/ppermute | solution.py:338
  9.8 16.8 %all-to-all-start = ((f32[8,8,128]{2,1,0:T(8,128)}), f32[8,8,128]{2,1,0:T(8,128)S(1)}, u32[]{:S(2)}, u32[]{:S(2)}) async-start(f32[8,8,128]{2,1,0:T(8,128)} %get-tuple-element.74), calls=%async_computation | async-start | bytes 65536 | tf_op jit(solution)/shard_map/all_to_all | solution.py:405
  30.4 6.9 %copy-start.3 = (bf16[1,2,8,128,256]{4,3,2,1,0:T(8,128)(2,1)S(1)}, bf16[1,2,8,128,256]{4,3,2,1,0:T(8,128)(2,1)}, u32[]{:S(2)}) copy-start(bf16[1,2,8,128,256]{4,3,2,1,0:T(8,128)(2,1)} %param.5) | copy-start | bytes 3145732
  30.4 6.9 %copy-start.6 = (bf16[3,256,256]{2,1,0:T(8,128)(2,1)S(1)}, bf16[3,256,256]{2,1,0:T(8,128)(2,1)}, u32[]{:S(2)}) copy-start(bf16[3,256,256]{2,1,0:T(8,128)(2,1)} %w_ref.3) | copy-start | bytes 1179652
  39.7 7.6 %collective-permute-start.3 = (bf16[2,128,256]{2,1,0:T(8,128)(2,1)S(1)}, bf16[2,128,256]{2,1,0:T(8,128)(2,1)S(1)}, u32[]{:S(2)}, u32[]{:S(2)}) collective-permute-start(bf16[2,128,256]{2,1,0:T(8,128)(2,1)S(1)} %get-tuple-element.79), channel_id=1, source_target_pairs={{0,1},{1,2},{2,3},{3,4},{4,5},{5,6},{6,7},{8,9},{9,10},{10,11},{11... | collective-permute-start | bytes 393224 | tf_op jit(solution)/shard_map/ppermute | solution.py:338
  41.9 5.7 %collective-permute-start.4 = (bf16[2,128,256]{2,1,0:T(8,128)(2,1)S(1)}, bf16[2,128,256]{2,1,0:T(8,128)(2,1)S(1)}, u32[]{:S(2)}, u32[]{:S(2)}) collective-permute-start(bf16[2,128,256]{2,1,0:T(8,128)(2,1)S(1)} %get-tuple-element.80), channel_id=1, source_target_pairs={{1,0},{2,1},{3,2},{4,3},{5,4},{6,5},{7,6},{9,8},{10,9},{11,10},{12... | collective-permute-start | bytes 393224 | tf_op jit(solution)/shard_map/ppermute | solution.py:338
  47.8 7.2 %collective-permute-start.5 = (f32[24,128,128]{2,1,0:T(8,128)S(1)}, f32[24,128,128]{2,1,0:T(8,128)S(1)}, u32[]{:S(2)}, u32[]{:S(2)}) collective-permute-start(f32[24,128,128]{2,1,0:T(8,128)S(1)} %slice.112), channel_id=1, source_target_pairs={{0,32},{32,0},{1,33},{33,1},{2,34},{34,2},{3,35},{35,3},{4,36},{36... | collective-permute-start | bytes 4718600 | tf_op jit(solution)/shard_map/ppermute | solution.py:332
  55.2 4.8 %copy-start.2 = (bf16[1,2,8,128,256]{4,3,2,1,0:T(8,128)(2,1)S(1)}, bf16[1,2,8,128,256]{4,3,2,1,0:T(8,128)(2,1)}, u32[]{:S(2)}) copy-start(bf16[1,2,8,128,256]{4,3,2,1,0:T(8,128)(2,1)} %param.4) | copy-start | bytes 3145732
  55.3 10.7 %collective-permute-start.6 = (f32[4,128,128]{2,1,0:T(8,128)S(1)}, f32[4,128,128]{2,1,0:T(8,128)S(1)}, u32[]{:S(2)}, u32[]{:S(2)}) collective-permute-start(f32[4,128,128]{2,1,0:T(8,128)S(1)} %get-tuple-element.83), channel_id=1, source_target_pairs={{0,8},{8,0},{1,9},{9,1},{2,10},{10,2},{3,11},{11,3},{4,12},{12,4},... | collective-permute-start | bytes 786440 | tf_op jit(solution)/shard_map/ppermute | solution.py:332
  57.8 8.3 %collective-permute-start.7 = (f32[4,128,128]{2,1,0:T(8,128)S(1)}, f32[4,128,128]{2,1,0:T(8,128)S(1)}, u32[]{:S(2)}, u32[]{:S(2)}) collective-permute-start(f32[4,128,128]{2,1,0:T(8,128)S(1)} %get-tuple-element.84), channel_id=1, source_target_pairs={{0,64},{64,0},{1,65},{65,1},{2,66},{66,2},{3,67},{67,3},{4,68},{68... | collective-permute-start | bytes 786440 | tf_op jit(solution)/shard_map/ppermute | solution.py:332
  59.1 7.0 %collective-permute-start.8 = (f32[4,128,128]{2,1,0:T(8,128)S(1)}, f32[4,128,128]{2,1,0:T(8,128)S(1)}, u32[]{:S(2)}, u32[]{:S(2)}) collective-permute-start(f32[4,128,128]{2,1,0:T(8,128)S(1)} %get-tuple-element.85), channel_id=1, source_target_pairs={{0,1},{1,0},{2,3},{3,2},{4,5},{5,4},{6,7},{7,6},{8,9},{9,8},{10,11... | collective-permute-start | bytes 786440 | tf_op jit(solution)/shard_map/ppermute | solution.py:332
  67.4 3.8 %collective-permute-start.9 = (f32[2,128,128]{2,1,0:T(8,128)S(1)}, f32[2,128,128]{2,1,0:T(8,128)S(1)}, u32[]{:S(2)}, u32[]{:S(2)}) collective-permute-start(f32[2,128,128]{2,1,0:T(8,128)S(1)} %get-tuple-element.99), channel_id=1, source_target_pairs={{0,64},{64,0},{1,65},{65,1},{2,66},{66,2},{3,67},{67,3},{4,68},{68... | collective-permute-start | bytes 393224 | tf_op jit(solution)/shard_map/ppermute | solution.py:332
  67.5 3.8 %collective-permute-start.10 = (f32[2,128,128]{2,1,0:T(8,128)S(1)}, f32[2,128,128]{2,1,0:T(8,128)S(1)}, u32[]{:S(2)}, u32[]{:S(2)}) collective-permute-start(f32[2,128,128]{2,1,0:T(8,128)S(1)} %get-tuple-element.100), channel_id=1, source_target_pairs={{0,1},{1,0},{2,3},{3,2},{4,5},{5,4},{6,7},{7,6},{8,9},{9,8},{10,11... | collective-permute-start | bytes 393224 | tf_op jit(solution)/shard_map/ppermute | solution.py:332
  68.0 4.1 %collective-permute-start.11 = (f32[2,128,128]{2,1,0:T(8,128)S(1)}, f32[2,128,128]{2,1,0:T(8,128)S(1)}, u32[]{:S(2)}, u32[]{:S(2)}) collective-permute-start(f32[2,128,128]{2,1,0:T(8,128)S(1)} %get-tuple-element.101), channel_id=1, source_target_pairs={{0,8},{8,0},{1,9},{9,1},{2,10},{10,2},{3,11},{11,3},{4,12},{12,4},... | collective-permute-start | bytes 393224 | tf_op jit(solution)/shard_map/ppermute | solution.py:332
  74.2 6.3 %collective-permute-start.12 = (f32[1,128,128]{2,1,0:T(8,128)}, f32[1,128,128]{2,1,0:T(8,128)}, u32[]{:S(2)}, u32[]{:S(2)}) collective-permute-start(f32[1,128,128]{2,1,0:T(8,128)} %get-tuple-element.108), channel_id=1, source_target_pairs={{0,1},{1,0},{2,3},{3,2},{4,5},{5,4},{6,7},{7,6},{8,9},{9,8},{10,11... | collective-permute-start | bytes 196616 | tf_op jit(solution)/shard_map/ppermute | solution.py:332
  75.1 5.4 %collective-permute-start.13 = (f32[1,128,128]{2,1,0:T(8,128)}, f32[1,128,128]{2,1,0:T(8,128)}, u32[]{:S(2)}, u32[]{:S(2)}) collective-permute-start(f32[1,128,128]{2,1,0:T(8,128)} %get-tuple-element.109), channel_id=1, source_target_pairs={{0,8},{8,0},{1,9},{9,1},{2,10},{10,2},{3,11},{11,3},{4,12},{12,4},... | collective-permute-start | bytes 196616 | tf_op jit(solution)/shard_map/ppermute | solution.py:332
  75.4 5.1 %collective-permute-start.14 = (f32[1,128,128]{2,1,0:T(8,128)}, f32[1,128,128]{2,1,0:T(8,128)}, u32[]{:S(2)}, u32[]{:S(2)}) collective-permute-start(f32[1,128,128]{2,1,0:T(8,128)} %get-tuple-element.110), channel_id=1, source_target_pairs={{0,64},{64,0},{1,65},{65,1},{2,66},{66,2},{3,67},{67,3},{4,68},{68... | collective-permute-start | bytes 196616 | tf_op jit(solution)/shard_map/ppermute | solution.py:332
  76.5 10.8 %all-to-all-start.1 = ((f32[8,8,128]{2,1,0:T(8,128)}), f32[8,8,128]{2,1,0:T(8,128)}, u32[]{:S(2)}, u32[]{:S(2)}) async-start(f32[8,8,128]{2,1,0:T(8,128)} %copy-done.7), calls=%async_computation.1 | async-start | bytes 65536 | tf_op jit(solution)/shard_map/all_to_all | solution.py:434
  88.3 5.8 %collective-permute-start.15 = (f32[3,32,128]{2,1,0:T(8,128)S(1)}, f32[3,32,128]{2,1,0:T(8,128)S(1)}, u32[]{:S(2)}, u32[]{:S(2)}) collective-permute-start(f32[3,32,128]{2,1,0:T(8,128)S(1)} %get-tuple-element.155), channel_id=1, source_target_pairs={{0,16},{16,0},{128,144},{144,128},{1,17},{17,1},{129,145},{145,129... | collective-permute-start | bytes 147464 | tf_op jit(solution)/shard_map/ppermute | solution.py:344
  91.3 6.9 %collective-permute-start.17 = (f32[3,32,128]{2,1,0:T(8,128)S(1)}, f32[3,32,128]{2,1,0:T(8,128)S(1)}, u32[]{:S(2)}, u32[]{:S(2)}) collective-permute-start(f32[3,32,128]{2,1,0:T(8,128)S(1)} %get-tuple-element.156), channel_id=1, source_target_pairs={{0,144},{16,128},{128,16},{144,0},{1,145},{17,129},{129,17},{145,1... | collective-permute-start | bytes 147464 | tf_op jit(solution)/shard_map/ppermute | solution.py:344
  93.7 4.9 %collective-permute-start.16 = (f32[3,32,128]{2,1,0:T(8,128)S(1)}, f32[3,32,128]{2,1,0:T(8,128)S(1)}, u32[]{:S(2)}, u32[]{:S(2)}) collective-permute-start(f32[3,32,128]{2,1,0:T(8,128)S(1)} %get-tuple-element.157), channel_id=1, source_target_pairs={{0,128},{16,144},{128,0},{144,16},{1,129},{17,145},{129,1},{145,17... | collective-permute-start | bytes 147464 | tf_op jit(solution)/shard_map/ppermute | solution.py:344
  98.7 8.6 %collective-permute-start.18 = (f32[3,8,128]{2,1,0:T(8,128)S(1)}, f32[3,8,128]{2,1,0:T(8,128)S(1)}, u32[]{:S(2)}, u32[]{:S(2)}) collective-permute-start(f32[3,8,128]{2,1,0:T(8,128)S(1)} %get-tuple-element.164), channel_id=1, source_target_pairs={{0,2},{2,0},{4,6},{6,4},{1,3},{3,1},{5,7},{7,5},{8,10},{10,8},{12,... | collective-permute-start | bytes 36872 | tf_op jit(solution)/shard_map/ppermute | solution.py:344
  98.9 8.3 %collective-permute-start.19 = (f32[3,8,128]{2,1,0:T(8,128)S(1)}, f32[3,8,128]{2,1,0:T(8,128)S(1)}, u32[]{:S(2)}, u32[]{:S(2)}) collective-permute-start(f32[3,8,128]{2,1,0:T(8,128)S(1)} %get-tuple-element.165), channel_id=1, source_target_pairs={{0,4},{2,6},{4,0},{6,2},{1,5},{3,7},{5,1},{7,3},{8,12},{10,14},{12... | collective-permute-start | bytes 36872 | tf_op jit(solution)/shard_map/ppermute | solution.py:344
  102.0 5.2 %collective-permute-start.20 = (f32[3,8,128]{2,1,0:T(8,128)S(1)}, f32[3,8,128]{2,1,0:T(8,128)S(1)}, u32[]{:S(2)}, u32[]{:S(2)}) collective-permute-start(f32[3,8,128]{2,1,0:T(8,128)S(1)} %get-tuple-element.166), channel_id=1, source_target_pairs={{0,6},{2,4},{4,2},{6,0},{1,7},{3,5},{5,3},{7,1},{8,14},{10,12},{12... | collective-permute-start | bytes 36872 | tf_op jit(solution)/shard_map/ppermute | solution.py:344
  104.4 27.3 %collective-permute-start.30 = (bf16[2,1024,256]{2,1,0:T(8,128)(2,1)S(1)}, bf16[2,1024,256]{2,1,0:T(8,128)(2,1)S(1)}, u32[]{:S(2)}, u32[]{:S(2)}) collective-permute-start(bf16[2,1024,256]{2,1,0:T(8,128)(2,1)S(1)} %get-tuple-element.126.hid_ref), channel_id=1, source_target_pairs={{0,8},{8,16},{16,24},{1,9},{9,17},{17,25},{2,10},{10,18},{18,26},{... | collective-permute-start | bytes 3145736 | tf_op jit(solution)/shard_map/ppermute | solution.py:338
  107.3 10.1 %collective-permute-start.23 = (f32[3,8,128]{2,1,0:T(8,128)S(1)}, f32[3,8,128]{2,1,0:T(8,128)S(1)}, u32[]{:S(2)}, u32[]{:S(2)}) collective-permute-start(f32[3,8,128]{2,1,0:T(8,128)S(1)} %fusion.6), channel_id=1, source_target_pairs={{0,6},{2,4},{4,2},{6,0},{1,7},{3,5},{5,3},{7,1},{8,14},{10,12},{12... | collective-permute-start | bytes 36872 | tf_op jit(solution)/shard_map/ppermute | solution.py:344
  109.2 8.1 %collective-permute-start.22 = (f32[3,8,128]{2,1,0:T(8,128)S(1)}, f32[3,8,128]{2,1,0:T(8,128)S(1)}, u32[]{:S(2)}, u32[]{:S(2)}) collective-permute-start(f32[3,8,128]{2,1,0:T(8,128)S(1)} %fusion.6), channel_id=1, source_target_pairs={{0,4},{2,6},{4,0},{6,2},{1,5},{3,7},{5,1},{7,3},{8,12},{10,14},{12... | collective-permute-start | bytes 36872 | tf_op jit(solution)/shard_map/ppermute | solution.py:344
  112.2 5.2 %collective-permute-start.21 = (f32[3,8,128]{2,1,0:T(8,128)S(1)}, f32[3,8,128]{2,1,0:T(8,128)S(1)}, u32[]{:S(2)}, u32[]{:S(2)}) collective-permute-start(f32[3,8,128]{2,1,0:T(8,128)S(1)} %fusion.6), channel_id=1, source_target_pairs={{0,2},{2,0},{4,6},{6,4},{1,3},{3,1},{5,7},{7,5},{8,10},{10,8},{12,... | collective-permute-start | bytes 36872 | tf_op jit(solution)/shard_map/ppermute | solution.py:344
  117.4 10.2 %collective-permute-start.26 = (f32[3,32,128]{2,1,0:T(8,128)S(1)}, f32[3,32,128]{2,1,0:T(8,128)S(1)}, u32[]{:S(2)}, u32[]{:S(2)}) collective-permute-start(f32[3,32,128]{2,1,0:T(8,128)S(1)} %maximum_bitcast_fusion), channel_id=1, source_target_pairs={{0,144},{16,128},{128,16},{144,0},{1,145},{17,129},{129,17},{145,1... | collective-permute-start | bytes 147464 | tf_op jit(solution)/shard_map/ppermute | solution.py:344
  120.8 6.8 %collective-permute-start.25 = (f32[3,32,128]{2,1,0:T(8,128)S(1)}, f32[3,32,128]{2,1,0:T(8,128)S(1)}, u32[]{:S(2)}, u32[]{:S(2)}) collective-permute-start(f32[3,32,128]{2,1,0:T(8,128)S(1)} %maximum_bitcast_fusion), channel_id=1, source_target_pairs={{0,128},{16,144},{128,0},{144,16},{1,129},{17,145},{129,1},{145,17... | collective-permute-start | bytes 147464 | tf_op jit(solution)/shard_map/ppermute | solution.py:344
  123.0 5.0 %collective-permute-start.24 = (f32[3,32,128]{2,1,0:T(8,128)S(1)}, f32[3,32,128]{2,1,0:T(8,128)S(1)}, u32[]{:S(2)}, u32[]{:S(2)}) collective-permute-start(f32[3,32,128]{2,1,0:T(8,128)S(1)} %maximum_bitcast_fusion), channel_id=1, source_target_pairs={{0,16},{16,0},{128,144},{144,128},{1,17},{17,1},{129,145},{145,129... | collective-permute-start | bytes 147464 | tf_op jit(solution)/shard_map/ppermute | solution.py:344
  128.0 3.4 %collective-permute-start.28 = (f32[1,128,128]{2,1,0:T(8,128)S(1)}, f32[1,128,128]{2,1,0:T(8,128)S(1)}, u32[]{:S(2)}, u32[]{:S(2)}) collective-permute-start(f32[1,128,128]{2,1,0:T(8,128)S(1)} %bitcast.102), channel_id=1, source_target_pairs={{0,8},{8,0},{1,9},{9,1},{2,10},{10,2},{3,11},{11,3},{4,12},{12,4},... | collective-permute-start | bytes 196616 | tf_op jit(solution)/shard_map/ppermute | solution.py:332
  128.1 3.3 %collective-permute-start.29 = (f32[1,128,128]{2,1,0:T(8,128)S(1)}, f32[1,128,128]{2,1,0:T(8,128)S(1)}, u32[]{:S(2)}, u32[]{:S(2)}) collective-permute-start(f32[1,128,128]{2,1,0:T(8,128)S(1)} %bitcast.100), channel_id=1, source_target_pairs={{0,64},{64,0},{1,65},{65,1},{2,66},{66,2},{3,67},{67,3},{4,68},{68... | collective-permute-start | bytes 196616 | tf_op jit(solution)/shard_map/ppermute | solution.py:332
  128.6 3.1 %collective-permute-start.27 = (f32[1,128,128]{2,1,0:T(8,128)S(1)}, f32[1,128,128]{2,1,0:T(8,128)S(1)}, u32[]{:S(2)}, u32[]{:S(2)}) collective-permute-start(f32[1,128,128]{2,1,0:T(8,128)S(1)} %bitcast.104), channel_id=1, source_target_pairs={{0,1},{1,0},{2,3},{3,2},{4,5},{5,4},{6,7},{7,6},{8,9},{9,8},{10,11... | collective-permute-start | bytes 196616 | tf_op jit(solution)/shard_map/ppermute | solution.py:332
  134.9 3.8 %collective-permute-start.31 = (f32[2,128,128]{2,1,0:T(8,128)S(1)}, f32[2,128,128]{2,1,0:T(8,128)S(1)}, u32[]{:S(2)}, u32[]{:S(2)}) collective-permute-start(f32[2,128,128]{2,1,0:T(8,128)S(1)} %pad_maximum_fusion.2), channel_id=1, source_target_pairs={{0,64},{64,0},{1,65},{65,1},{2,66},{66,2},{3,67},{67,3},{4,68},{68... | collective-permute-start | bytes 393224 | tf_op jit(solution)/shard_map/ppermute | solution.py:332
  136.0 3.9 %collective-permute-start.32 = (f32[2,128,128]{2,1,0:T(8,128)S(1)}, f32[2,128,128]{2,1,0:T(8,128)S(1)}, u32[]{:S(2)}, u32[]{:S(2)}) collective-permute-start(f32[2,128,128]{2,1,0:T(8,128)S(1)} %pad_maximum_fusion.3), channel_id=1, source_target_pairs={{0,1},{1,0},{2,3},{3,2},{4,5},{5,4},{6,7},{7,6},{8,9},{9,8},{10,11... | collective-permute-start | bytes 393224 | tf_op jit(solution)/shard_map/ppermute | solution.py:332
  136.4 4.4 %collective-permute-start.33 = (f32[2,128,128]{2,1,0:T(8,128)S(1)}, f32[2,128,128]{2,1,0:T(8,128)S(1)}, u32[]{:S(2)}, u32[]{:S(2)}) collective-permute-start(f32[2,128,128]{2,1,0:T(8,128)S(1)} %pad_maximum_fusion.4), channel_id=1, source_target_pairs={{0,8},{8,0},{1,9},{9,1},{2,10},{10,2},{3,11},{11,3},{4,12},{12,4},... | collective-permute-start | bytes 393224 | tf_op jit(solution)/shard_map/ppermute | solution.py:332
  140.8 15.7 %collective-permute-start.36 = (f32[4,128,128]{2,1,0:T(8,128)S(1)}, f32[4,128,128]{2,1,0:T(8,128)S(1)}, u32[]{:S(2)}, u32[]{:S(2)}) collective-permute-start(f32[4,128,128]{2,1,0:T(8,128)S(1)} %constant_dynamic-update-slice_fusion.4.refs_9_), channel_id=1, source_target_pairs={{0,1},{1,0},{2,3},{3,2},{4,5},{5,4},{6,7},{7,6},{8,9},{9,8},{10,11... | collective-permute-start | bytes 786440 | tf_op jit(solution)/shard_map/ppermute | solution.py:332
  142.4 17.0 %collective-permute-start.35 = (f32[4,128,128]{2,1,0:T(8,128)S(1)}, f32[4,128,128]{2,1,0:T(8,128)S(1)}, u32[]{:S(2)}, u32[]{:S(2)}) collective-permute-start(f32[4,128,128]{2,1,0:T(8,128)S(1)} %constant_dynamic-update-slice_fusion.2.refs_5_), channel_id=1, source_target_pairs={{0,64},{64,0},{1,65},{65,1},{2,66},{66,2},{3,67},{67,3},{4,68},{68... | collective-permute-start | bytes 786440 | tf_op jit(solution)/shard_map/ppermute | solution.py:332
  142.8 16.6 %collective-permute-start.34 = (f32[4,128,128]{2,1,0:T(8,128)S(1)}, f32[4,128,128]{2,1,0:T(8,128)S(1)}, u32[]{:S(2)}, u32[]{:S(2)}) collective-permute-start(f32[4,128,128]{2,1,0:T(8,128)S(1)} %constant_dynamic-update-slice_fusion.refs_1_), channel_id=1, source_target_pairs={{0,8},{8,0},{1,9},{9,1},{2,10},{10,2},{3,11},{11,3},{4,12},{12,4},... | collective-permute-start | bytes 786440 | tf_op jit(solution)/shard_map/ppermute | solution.py:332
  143.7 17.3 %collective-permute-start.41 = (f32[4,128,128]{2,1,0:T(8,128)S(1)}, f32[4,128,128]{2,1,0:T(8,128)S(1)}, u32[]{:S(2)}, u32[]{:S(2)}) collective-permute-start(f32[4,128,128]{2,1,0:T(8,128)S(1)} %constant_dynamic-update-slice_fusion.4.refs_9_), channel_id=1, source_target_pairs={{0,32},{32,0},{1,33},{33,1},{2,34},{34,2},{3,35},{35,3},{4,36},{36... | collective-permute-start | bytes 786440 | tf_op jit(solution)/shard_map/ppermute | solution.py:332
  156.5 5.0 %collective-permute-start.39 = (f32[4,128,128]{2,1,0:T(8,128)S(1)}, f32[4,128,128]{2,1,0:T(8,128)S(1)}, u32[]{:S(2)}, u32[]{:S(2)}) collective-permute-start(f32[4,128,128]{2,1,0:T(8,128)S(1)} %constant_dynamic-update-slice_fusion.2.refs_5_), channel_id=1, source_target_pairs={{0,32},{32,0},{1,33},{33,1},{2,34},{34,2},{3,35},{35,3},{4,36},{36... | collective-permute-start | bytes 786440 | tf_op jit(solution)/shard_map/ppermute | solution.py:332
  156.6 5.0 %collective-permute-start.37 = (f32[4,128,128]{2,1,0:T(8,128)S(1)}, f32[4,128,128]{2,1,0:T(8,128)S(1)}, u32[]{:S(2)}, u32[]{:S(2)}) collective-permute-start(f32[4,128,128]{2,1,0:T(8,128)S(1)} %constant_dynamic-update-slice_fusion.refs_1_), channel_id=1, source_target_pairs={{0,32},{32,0},{1,33},{33,1},{2,34},{34,2},{3,35},{35,3},{4,36},{36... | collective-permute-start | bytes 786440 | tf_op jit(solution)/shard_map/ppermute | solution.py:332
  159.4 2.7 %collective-permute-start.38 = (f32[4,128,128]{2,1,0:T(8,128)S(1)}, f32[4,128,128]{2,1,0:T(8,128)S(1)}, u32[]{:S(2)}, u32[]{:S(2)}) collective-permute-start(f32[4,128,128]{2,1,0:T(8,128)S(1)} %collective-permute-done.34.refs_2_), channel_id=1, source_target_pairs={{0,32},{32,0},{1,33},{33,1},{2,34},{34,2},{3,35},{35,3},{4,36},{36... | collective-permute-start | bytes 786440 | tf_op jit(solution)/shard_map/ppermute | solution.py:332
  161.0 1.5 collective-permute-start.40
  161.0 1.9 %collective-permute-start.42 = (f32[4,128,128]{2,1,0:T(8,128)S(1)}, f32[4,128,128]{2,1,0:T(8,128)S(1)}, u32[]{:S(2)}, u32[]{:S(2)}) collective-permute-start(f32[4,128,128]{2,1,0:T(8,128)S(1)} %collective-permute-done.36.refs_10_), channel_id=1, source_target_pairs={{0,32},{32,0},{1,33},{33,1},{2,34},{34,2},{3,35},{35,3},{4,36},{36... | collective-permute-start | bytes 786440 | tf_op jit(solution)/shard_map/ppermute | solution.py:332
  (10 other events, 14.7 us)

commit v3 on v1

--- a/solution.py
+++ b/solution.py
@@ -9,24 +9,26 @@
 from jax.sharding import PartitionSpec as P
 
 GROUPS = 32
+tied = lax.optimization_barrier
 EPSILON = 1e-05
 CLIP_DIVISOR = 20.0
 F32 = jnp.float32
 BF16 = jnp.bfloat16
-DP = ("yh", "yl", "core")
-TM = ("xh", "xl")
-HEIGHT = ("zh", "zl")
-REST = ("yh", "xh", "zh")
-ORDERS = (("xl", "yl", "zl"), ("yl", "zl", "xl"), ("zl", "xl", "yl"))
+DP = ("y", "core")
+TM = "tm"
+HEIGHT = "height"
+CHIPS = ("y", "tm", "height")
+UNIT = 2.0**40
 VMEM = pl.BlockSpec(memory_space=pltpu.VMEM)
 SMEM = pl.BlockSpec(memory_space=pltpu.SMEM)
+ANY = pl.BlockSpec(memory_space=pl.ANY)
 NT = (((1,), (1,)), ((), ()))
 TN = (((0,), (0,)), ((), ()))
 
 
-def call(kernel, outs, args, flops, scratch=(), smem=0, limit=40):
+def call(kernel, outs, args, flops, scratch=(), smem=0, limit=16, loose=()):
     nbytes = sum(a.size * a.dtype.itemsize for a in (*args, *outs))
-    specs = [SMEM] * smem + [VMEM] * (len(args) - smem)
+    specs = [SMEM] * smem + [ANY if i in loose else VMEM for i in range(smem, len(args))]
     return pl.pallas_call(
         kernel,
         out_shape=tuple(outs),
@@ -86,13 +88,23 @@
     return res
 
 
+def fetched(*pairs, sems):
+    copies = [pltpu.make_async_copy(a, b, sems.at[i]) for i, (a, b) in enumerate(pairs)]
+    for c in copies:
+        c.start()
+    for c in copies:
+        c.wait()
+
+
 def fold(v):
     return jnp.sum(v.reshape(v.shape[0] // 8, 8, v.shape[1]), axis=0)
 
 
-def stats_kernel(x_ref, o_ref):
+def stats_kernel(x_ref, o_ref, top_ref, bot_ref):
     sums = []
     for f in range(2):
+        top_ref[f] = x_ref[f, 0:128, :]
+        bot_ref[f] = x_ref[f, 896:1024, :]
 
         def step(r, carry):
             v = x_ref[f, pl.ds(pl.multiple_of(r * 128, 128), 128), :].astype(F32)
@@ -110,8 +122,12 @@
     return before, after
 
 
-def forward_kernel(members, info, x_ref, up_ref, dn_ref, st_ref, w_ref, act_ref, hid_ref, slope_ref):
-    keep_up, keep_dn = info[4].astype(F32), info[5].astype(F32)
+def forward_kernel(
+    members, info, x_ref, up_hbm, dn_hbm, st_hbm, w_ref, act_ref, hid_ref, slope_ref, up_ref, dn_ref, st_ref, sems
+):
+    fetched((st_hbm, st_ref), (up_hbm, up_ref), (dn_hbm, dn_ref), sems=sems)
+    keep_up = (info[1] > 0).astype(F32)
+    keep_dn = (info[2] > 0).astype(F32)
     stats = moments(st_ref, members)
     for f in range(2):
         mean, inv = stats[f]
@@ -171,14 +187,20 @@
         bot_ref[f] = pg_ref[f, 896:1024, :]
 
 
-def grads_kernel(info, act_ref, pg_ref, hid_ref, cot_ref, later_ref, g_ref):
+def grads_kernel(info, act_ref, pg_ref, hid_ref, cot_ref, later_ref, keep_ref, send_ref):
     def put(tap, v):
-        for q in range(4):
-            b = 4 * tap + q
-            pair, third, bits = b // 24, (b % 24) // 8, b % 8
-            at = (pair ^ info[0]) * 24 + third * 8 + (bits ^ info[1 + third])
-            rh, lh = q % 2, q // 2
-            g_ref[at] = v[rh * 128 : rh * 128 + 128, lh * 128 : lh * 128 + 128]
+        mine = info[0] == tap // 6
+        for lh in range(2):
+            at = ((tap % 6) * 2 + lh) * 256
+            half = v[:, lh * 128 : lh * 128 + 128]
+
+            @pl.when(mine)
+            def _():
+                keep_ref[at : at + 256, :] = half
+
+            @pl.when(jnp.logical_not(mine))
+            def _():
+                send_ref[at : at + 256, :] = half
 
     for i in range(3):
         for j in range(3):
@@ -275,23 +297,53 @@
         lax.fori_loop(0, 4, part, 0)
 
 
+def coded(v):
+    t = v * UNIT
+    return (t * jnp.sqrt(jnp.abs(t))).astype(BF16)
+
+
+def decoded(u):
+    u = u.astype(F32)
+    size = jnp.abs(u)
+    root = jnp.exp(jnp.log(jnp.maximum(size, 1e-37)) * (2.0 / 3.0)) * (1.0 / UNIT)
+    return jnp.where(size < 1e-37, 0.0, jnp.where(u < 0, -root, root))
+
+
+def encode_kernel(a_ref, b_ref, o_ref):
+    def part(r, _):
+        at = pl.ds(pl.multiple_of(r * 256, 256), 256)
+        o_ref[at, :] = coded(a_ref[at, :] + b_ref[at, :])
+        return 0
+
+    lax.fori_loop(0, a_ref.shape[0] // 256, part, 0)
+
+
+def own_kernel(u_ref, o_ref):
+    rows = u_ref.shape[0] // 64
+
+    def part(r, acc):
+        return acc + decoded(u_ref[pl.ds(pl.multiple_of(r * rows, rows), rows), :])
+
+    acc = lax.fori_loop(0, 64, part, jnp.zeros((rows, 128), F32))
+    total = acc[: rows // 2] + acc[rows // 2 :]
+    copy = coded(jnp.concatenate([total, total], axis=0))
+
+    def put(r, _):
+        o_ref[pl.ds(pl.multiple_of(r * rows, rows), rows), :] = copy
+        return 0
+
+    lax.fori_loop(0, 64, put, 0)
+
+
 def clip_kernel(clip_level, info, own_ref, other_ref, s_ref, t_ref):
-    core = info[0]
-
-    def block(tap, q):
-        b = 4 * tap + q
-        pair, third, bits = b // 24, (b % 24) // 8, b % 8
-        at = third * 8 + (bits ^ info[1 + third])
-        mine = (pair ^ core) == 0
-        return jnp.where(mine, own_ref[at], other_ref[at])
-
     acc = jnp.zeros((8, 128), F32)
     for tap in range(12):
         ref, k = (s_ref, tap) if tap < 9 else (t_ref, tap - 9)
-        for q in range(4):
-            v = block(tap, q)
-            rh, lh = q % 2, q // 2
-            ref[k, rh * 128 : rh * 128 + 128, lh * 128 : lh * 128 + 128] = v
+        mine = info[0] == tap // 6
+        for lh in range(2):
+            at = ((tap % 6) * 2 + lh) * 256
+            v = decoded(jnp.where(mine, own_ref[at : at + 256, :], other_ref[at : at + 256, :]))
+            ref[k, :, lh * 128 : lh * 128 + 128] = v
             acc = acc + fold(v * v)
     total = jnp.sum(jnp.sum(acc, axis=0, keepdims=True), axis=1, keepdims=True)
     scale = clip_level / jnp.maximum(jnp.sqrt(total), clip_level)
@@ -313,27 +365,6 @@
     n = lax.axis_size(axes)
     route = [(i, i + distance) for i in range(n) if 0 <= i + distance < n]
     return lax.ppermute(x, axes, route)
-
-
-def reduced(g):
-    g = g[:24] + swapped(g[24:], "core")
-    parts = [g[8 * t : 8 * t + 8] for t in range(3)]
-    for step, half in enumerate((4, 2, 1)):
-        got = [swapped(p[half:], ORDERS[t][step]) for t, p in enumerate(parts)]
-        parts = [p[:half] + r for p, r in zip(parts, got)]
-    pieces = jnp.concatenate([p.reshape(16, 8, 128) for p in parts], axis=1)
-    return jnp.sum(lax.all_to_all(pieces, REST, 0, 0, tiled=True), axis=0)
-
-
-def gathered(own):
-    copies = jnp.broadcast_to(own, (16, *own.shape))
-    pieces = lax.all_to_all(copies, REST, 0, 0, tiled=True)
-    parts = [pieces[:, 8 * t : 8 * t + 8].reshape(1, 128, 128) for t in range(3)]
-    for step in (2, 1, 0):
-        got = [swapped(p, ORDERS[t][step]) for t, p in enumerate(parts)]
-        parts = [jnp.concatenate([p, r], axis=0) for p, r in zip(parts, got)]
-    mine = jnp.concatenate(parts, axis=0)
-    return mine, swapped(mine, "core")
 
 
 def body(video_latents, cotangent, spatial_kernel, temporal_kernel):
@@ -346,11 +377,7 @@
         / CLIP_DIVISOR
     )
     z = lax.axis_index(HEIGHT)
-    bit = {a: lax.axis_index(a) for a in ("xl", "yl", "zl")}
-    codes = [4 * bit[a] + 2 * bit[b] + bit[c] for a, b, c in ORDERS]
-    info = jnp.stack(
-        [lax.axis_index("core"), *codes, (z > 0).astype(jnp.int32), (z < peers - 1).astype(jnp.int32)]
-    ).astype(jnp.int32)
+    info = jnp.stack([lax.axis_index("core"), z, peers - 1 - z]).astype(jnp.int32)
     pixels = rows * columns
     flat = (2, pixels, 256)
     x = video_latents.reshape(flat)
@@ -360,49 +387,69 @@
     gflop = 2 * 2048 * 256 * 256
 
     later = moved(cot, TM, -1)
-    up = moved(x[:, pixels - columns :], HEIGHT, 1)
-    dn = moved(x[:, :columns], HEIGHT, -1)
     small = out((8, 8, 128), F32)
-    (st,) = call(stats_kernel, [small], [x], 1 << 21)
+    edge = out((2, columns, 256), BF16)
+    st, x_top, x_bot = call(stats_kernel, [small, edge, edge], [x], 1 << 21)
     st = lax.all_to_all(st, HEIGHT, 0, 0, tiled=True)
+    up = moved(x_bot, HEIGHT, 1)
+    dn = moved(x_top, HEIGHT, -1)
     act, hid, slope = call(
         lambda *refs: forward_kernel(members, *refs),
         [out((2, 1280, 768), BF16), out(flat, BF16), out(flat, F32)],
         [info, x, up, dn, st, w3],
         9 * gflop,
         smem=1,
-    )
-    edge = out((2, columns, 256), BF16)
+        loose=(2, 3, 4),
+        scratch=[
+            pltpu.VMEM(edge.shape, BF16),
+            pltpu.VMEM(edge.shape, BF16),
+            pltpu.VMEM(small.shape, F32),
+            pltpu.SemaphoreType.DMA((3,)),
+        ],
+    )
     pg, top, bot = call(
         pregrad_kernel, [out(flat, BF16), edge, edge], [cot, later, slope, temporal_kernel], 3 * gflop
     )
     gup = moved(bot, HEIGHT, 1)
     gdn = moved(top, HEIGHT, -1)
-    (g,) = call(
-        grads_kernel, [out((48, 128, 128), F32)], [info, act, pg, hid, cot, later], 12 * gflop, smem=1
-    )
-    own = reduced(g)
-    mine, other = gathered(own)
+    slab = (3072, 128)
+    keep, send = call(
+        grads_kernel,
+        [out(slab, F32), out(slab, F32)],
+        [info, act, pg, hid, cot, later],
+        12 * gflop,
+        smem=1,
+    )
+    send, gup, gdn = tied((send, gup, gdn))
+    (code,) = call(encode_kernel, [out(slab, BF16)], [keep, swapped(send, "core")], 1 << 21)
+    code, gup, gdn, hid_sent = tied((code, gup, gdn, hid))
+    code = lax.all_to_all(code.reshape(128, 24, 128), CHIPS, 0, 0, tiled=True)
+    ng, gst = call(
+        lambda *refs: backward_kernel(members, *refs),
+        [out(flat, F32), out((1, 8, 128), F32)],
+        [pg, gup, gdn, w9, x, st],
+        9 * gflop,
+        scratch=[pltpu.VMEM((2, 1280, 256), BF16)] * 3,
+    )
+    for d in (1, 2, 4):
+        gst = gst + lax.ppermute(gst, HEIGHT, [(i, i ^ d) for i in range(peers)])
+    prev = moved(hid_sent, TM, 1)
+    code, ng, gst, prev = tied((code, ng, gst, prev))
+    (copies,) = call(own_kernel, [out(slab, BF16)], [code.reshape(slab)], 1 << 21)
+    mine = lax.all_to_all(copies.reshape(128, 24, 128), CHIPS, 0, 0, tiled=True)
+    (input_grad,) = call(
+        lambda *refs: input_grad_kernel(members, *refs), [out(flat, BF16)], [x, cot, ng, st, gst], 1 << 21
+    )
+    (block_output,) = call(block_kernel, [out(flat, BF16)], [x, hid, prev, temporal_kernel], 3 * gflop)
+    mine, input_grad, block_output = tied((mine, input_grad, block_output))
+    mine = mine.reshape(slab)
     clipped_spatial, clipped_temporal = call(
         lambda *refs: clip_kernel(clip_level, *refs),
         [out((9, 256, 256), F32), out((3, 256, 256), F32)],
-        [info, mine, other],
+        [info, mine, swapped(mine, "core")],
         1 << 21,
         smem=1,
     )
-    ng, gst = call(
-        lambda *refs: backward_kernel(members, *refs),
-        [out(flat, F32), small],
-        [pg, gup, gdn, w9, x, st],
-        9 * gflop,
-        scratch=[pltpu.VMEM((2, 1280, 256), BF16)] * 3,
-    )
-    gst = lax.all_to_all(gst, HEIGHT, 0, 0, tiled=True)
-    (input_grad,) = call(
-        lambda *refs: input_grad_kernel(members, *refs), [out(flat, BF16)], [x, cot, ng, st, gst], 1 << 21
-    )
-    prev = moved(hid, TM, 1)
-    (block_output,) = call(block_kernel, [out(flat, BF16)], [x, hid, prev, temporal_kernel], 3 * gflop)
     return (
         block_output.reshape(video_latents.shape),
         input_grad.reshape(video_latents.shape),
@@ -412,7 +459,8 @@
 
 
 def solution(mesh):
-    torus = Mesh(mesh.devices.reshape(2, 2, 2, 2, 2, 4, 2), (*DP, *TM, *HEIGHT))
+    sizes = (mesh.shape["dp"] // 2, 2, mesh.shape[TM], mesh.shape[HEIGHT])
+    torus = Mesh(mesh.devices.reshape(sizes), (*DP, TM, HEIGHT))
     field = P(DP, TM, HEIGHT, None, None)
     return jax.shard_map(
         body, mesh=torus, in_specs=(field, field, P(), P()), out_specs=(field, field, P(), P()), check_vma=False

time: 189 us -> 156 us (0.83)
  blocking collectives: 35.3 us -> 0 us
  local copies, waits for them, and re-layouts: 23 us -> 12.8 us
  starting transfers between devices: 55.5 us -> 63.4 us
  Pallas kernels: 30.2 us -> 37.2 us
    all_to_all x2 -> x0, blocking collectives: 35.3 us -> none  [the longest x1 19.6 us: reduced(): return jnp.sum(lax.all_to_all(pieces, REST, 0, 0, tiled=True), axis=0)]
    all_to_all x1 -> x2, starting transfers between devices: 3.96 us -> 26.8 us  [the longest x1 13.5 us: body(): mine = lax.all_to_all(copies.reshape(128, 24, 128), CHIPS, 0, 0, tiled=True)]
    ppermute x20 -> x2, waiting for transfers between devices: 27.2 us -> 4.95 us  [swapped(): return lax.ppermute(x, axis, [(0, 1), (1, 0)])]
    ppermute x20 -> x2, starting transfers between devices: 28.1 us -> 6.11 us  [swapped(): return lax.ppermute(x, axis, [(0, 1), (1, 0)])]
    all_to_all x1 -> x2, waiting for transfers between devices: 0.81 us -> 17.5 us  [the longest x1 17.5 us: body(): mine = lax.all_to_all(copies.reshape(128, 24, 128), CHIPS, 0, 0, tiled=True)]
    unnamed x59 -> x38, local copies, waits for them, and re-layouts: 21 us -> 12.8 us
    ppermute x0 -> x3, starting transfers between devices: none -> 7.69 us  [body(): gst = gst + lax.ppermute(gst, HEIGHT, [(i, i ^ d) for i in range(peers)])]
    pallas_call x8 -> x10, Pallas kernels: 30.2 us -> 37.2 us  [call(): pl.pallas_call(kernel, out_shape=tuple(outs), in_specs=specs, out_specs=t...]
  transfers between devices with their start and end apart: 28 -> 14, of which waited for: 18 -> 8; matrix products, arithmetic and copies ran while one was open for 5% -> 0% of each run, Pallas kernels for 10% -> 18%
where the time goes in v3:
time: 156 us; the launch traced here: 155 us
  starting transfers between devices  63.4 us (41%)
  waiting for transfers between devices  40.6 us (26%)
  Pallas kernels  37.2 us (24%)
  local copies, waits for them, and re-layouts  12.8 us (8%)
    pallas_call x10, Pallas kernels, call(): pl.pallas_call(kernel, out_shape=tuple(outs), in_specs=specs, out_specs=t...  37.2 us
    all_to_all x1, waiting for transfers between devices, body(): mine = lax.all_to_all(copies.reshape(128, 24, 128), CHIPS, 0, 0, tiled=True)  17.5 us
    all_to_all x1, starting transfers between devices, body(): mine = lax.all_to_all(copies.reshape(128, 24, 128), CHIPS, 0, 0, tiled=True)  13.5 us
    all_to_all x1, starting transfers between devices, body(): code = lax.all_to_all(code.reshape(128, 24, 128), CHIPS, 0, 0, tiled=True)  13.3 us
    ppermute x6, starting transfers between devices, moved(): return lax.ppermute(x, axes, route)  12.9 us
    unnamed x38, local copies, waits for them, and re-layouts  12.8 us
    all_to_all x1, starting transfers between devices, body(): st = lax.all_to_all(st, HEIGHT, 0, 0, tiled=True)  9.85 us
    ppermute x3, starting transfers between devices, body(): gst = gst + lax.ppermute(gst, HEIGHT, [(i, i ^ d) for i in range(peers)])  7.69 us
  transfers between devices with their start and end apart: 14, of which 8 were waited for; matrix products, arithmetic and copies ran while one was open for 0% of the time, Pallas kernels for 18%

profile of v3, /device:TPU:1, one launch (start us, length us, event | category | flops | bytes accessed | tf_op | source)
XLA Modules:
  0.0 155.0 jit_solution(18159484872204451867)
XLA Ops:
  0.6 1.3 collective-permute-start.2
  1.9 0.0 copy-start
  1.9 1.2 copy-done
  3.2 1.0 shard_map.75
  4.1 4.4 %collective-permute-start = (bf16[2,128,256]{2,1,0:T(8,128)(2,1)S(1)}, bf16[2,128,256]{2,1,0:T(8,128)(2,1)S(1)}, u32[]{:S(2)}, u32[]{:S(2)}) collective-permute-start(bf16[2,128,256]{2,1,0:T(8,128)(2,1)S(1)} %get-tuple-element.33), channel_id=1, source_target_pairs={{0,1},{1,2},{2,3},{3,4},{4,5},{5,6},{6,7},{8,9},{9,10},{10,11},{11... | collective-permute-start | bytes 393224 | tf_op jit(solution)/shard_map/ppermute | solution.py:367
  8.5 1.3 collective-permute-start.1
  9.8 9.8 %all-to-all-start = ((f32[8,8,128]{2,1,0:T(8,128)}), f32[8,8,128]{2,1,0:T(8,128)S(1)}, u32[]{:S(2)}, u32[]{:S(2)}) async-start(f32[8,8,128]{2,1,0:T(8,128)} %get-tuple-element.35), calls=%async_computation | async-start | bytes 65536 | tf_op jit(solution)/shard_map/all_to_all | solution.py:393
  19.6 0.1 pad_add_fusion.refs_0_.info
  19.7 6.8 %all-to-all-done.refs_4_.refs_5_.refs_3_ = f32[8,8,128]{2,1,0:T(8,128)S(1)} async-done(((f32[8,8,128]{2,1,0:T(8,128)}), f32[8,8,128]{2,1,0:T(8,128)S(1)}, u32[]{:S(2)}, u32[]{:S(2)}) %all-to-all-start) | async-done | bytes 32800 | tf_op jit(solution)/shard_map/all_to_all | solution.py:393
  26.6 1.2 copy-done.1
  27.8 1.3 copy-done.13
  29.1 6.7 %shard_map.76 = (bf16[2,1280,768]{2,1,0:T(8,128)(2,1)S(1)}, bf16[2,1024,256]{2,1,0:T(8,128)(2,1)S(1)}, f32[2,1024,256]{2,1,0:T(8,128)S(1)}) custom-call(s32[3]{0:T(128)S(1)} %pad_add_fusion.refs_0_.info, bf16[2,1024,256]{2,1,0:T(8,128)(2,1)S(1)} %bitcast.14, bf16[2,128,256]{2,1,0:T(8,128)(2,1)S(1)} %collective-permute-done.refs_2_, ...), custom_call_target="tpu_custom_call" | custom-call | flops 2415919104 | bytes 9601036 | tf_op jit(solution)/shard_map/pallas_call | solution.py:32
  35.9 2.4 %shard_map.77 = (bf16[2,1024,256]{2,1,0:T(8,128)(2,1)S(1)}, bf16[2,128,256]{2,1,0:T(8,128)(2,1)S(1)}, bf16[2,128,256]{2,1,0:T(8,128)(2,1)S(1)}) custom-call(bf16[2,1024,256]{2,1,0:T(8,128)(2,1)S(1)} %bitcast.19, bf16[2,1024,256]{2,1,0:T(8,128)(2,1)S(1)} %collective-permute-done.2.later_ref, f32[2,1024,256]{2,1,0:T(8,128)S(1)} %get-tuple-element.37.slope_ref, ...), custom_call_target="tpu_custom_call" | custom-call | flops 805306368 | bytes 5898240 | tf_op jit(solution)/shard_map/pallas_call | solution.py:32
  38.3 0.0 copy-start.15
  38.3 2.2 %collective-permute-start.3 = (bf16[2,128,256]{2,1,0:T(8,128)(2,1)S(1)}, bf16[2,128,256]{2,1,0:T(8,128)(2,1)S(1)}, u32[]{:S(2)}, u32[]{:S(2)}) collective-permute-start(bf16[2,128,256]{2,1,0:T(8,128)(2,1)S(1)} %get-tuple-element.42), channel_id=1, source_target_pairs={{0,1},{1,2},{2,3},{3,4},{4,5},{5,6},{6,7},{8,9},{9,10},{10,11},{11... | collective-permute-start | bytes 393224 | tf_op jit(solution)/shard_map/ppermute | solution.py:367
  40.5 1.3 collective-permute-start.4
  41.8 9.2 %shard_map.78 = (f32[3072,128]{1,0:T(8,128)S(1)}, f32[3072,128]{1,0:T(8,128)S(1)}) custom-call(s32[3]{0:T(128)S(1)} %pad_add_fusion.refs_0_.info, bf16[2,1280,768]{2,1,0:T(8,128)(2,1)S(1)} %get-tuple-element.36.act_ref, bf16[2,1024,256]{2,1,0:T(8,128)(2,1)S(1)} %get-tuple-element.38.pg_ref.refs_0_, bf16[2,1024,256]{2,1,0:T(8,128)(2,1)S(1)} %get-tuple-element.52.hid_ref, ...), custom_call_target="tpu_custom_call" | custom-call | flops 3221225472 | bytes 11272204 | tf_op jit(solution)/shard_map/pallas_call | solution.py:32
  51.1 3.0 %collective-permute-start.5 = (f32[3072,128]{1,0:T(8,128)S(1)}, f32[3072,128]{1,0:T(8,128)S(1)}, u32[]{:S(2)}, u32[]{:S(2)}) collective-permute-start(f32[3072,128]{1,0:T(8,128)S(1)} %get-tuple-element.44), channel_id=1, source_target_pairs={{0,32},{32,0},{1,33},{33,1},{2,34},{34,2},{3,35},{35,3},{4,36},{36... | collective-permute-start | bytes 4718600 | tf_op jit(solution)/shard_map/ppermute | solution.py:361
  54.1 3.0 %collective-permute-done.5.b_ref = f32[3072,128]{1,0:T(8,128)S(1)} collective-permute-done((f32[3072,128]{1,0:T(8,128)S(1)}, f32[3072,128]{1,0:T(8,128)S(1)}, u32[]{:S(2)}, u32[]{:S(2)}) %collective-permute-start.5) | collective-permute-done | bytes 1572896 | tf_op jit(solution)/shard_map/ppermute | solution.py:361
  57.2 0.7 shard_map.79
  57.9 0.9 copy-done.5
  58.7 13.3 %all-to-all-start.1 = ((bf16[128,24,128]{2,1,0:T(8,128)(2,1)}), bf16[128,24,128]{2,1,0:T(8,128)(2,1)S(1)}, u32[]{:S(2)}, u32[]{:S(2)}) async-start(bf16[128,24,128]{2,1,0:T(8,128)(2,1)} %bitcast.26), calls=%async_computation.1 | async-start | bytes 1572864 | tf_op jit(solution)/shard_map/all_to_all | solution.py:426
  72.1 2.5 %collective-permute-start.9 = (bf16[2,1024,256]{2,1,0:T(8,128)(2,1)}, bf16[2,1024,256]{2,1,0:T(8,128)(2,1)S(1)}, u32[]{:S(2)}, u32[]{:S(2)}) collective-permute-start(bf16[2,1024,256]{2,1,0:T(8,128)(2,1)} %copy-done.9), channel_id=1, source_target_pairs={{0,8},{8,16},{16,24},{1,9},{9,17},{17,25},{2,10},{10,18},{18,26},{... | collective-permute-start | bytes 3145736 | tf_op jit(solution)/shard_map/ppermute | solution.py:367
  74.7 1.3 copy-done.14
  75.9 1.2 copy-done.16
  77.2 0.9 copy-done.18
  78.1 5.2 %shard_map.80 = (f32[2,1024,256]{2,1,0:T(8,128)S(1)}, f32[1,8,128]{2,1,0:T(8,128)S(1)}) custom-call(bf16[2,1024,256]{2,1,0:T(8,128)(2,1)S(1)} %copy-done.16, bf16[2,128,256]{2,1,0:T(8,128)(2,1)S(1)} %collective-permute-done.3.refs_1_, bf16[2,128,256]{2,1,0:T(8,128)(2,1)S(1)} %copy-done.18, bf16[3,3,256,256]{3,2,1,0:T(8,128)(2,1)S(1)} %copy-done.14, ...), custom_call_target="tpu_custom_call" | custom-call | flops 2415919104 | bytes 5672960 | tf_op jit(solution)/shard_map/pallas_call | solution.py:32
  83.3 1.3 copy-done.6
  84.6 1.2 collective-permute-start.6
  85.8 2.6 %collective-permute-done.6 = f32[1,8,128]{2,1,0:T(8,128)S(1)} collective-permute-done((f32[1,8,128]{2,1,0:T(8,128)S(1)}, f32[1,8,128]{2,1,0:T(8,128)S(1)}, u32[]{:S(2)}, u32[]{:S(2)}) %collective-permute-start.6) | collective-permute-done | bytes 4128 | tf_op jit(solution)/shard_map/ppermute | solution.py:435
  88.4 1.4 collective-permute-start.7
  89.8 2.3 %collective-permute-done.7 = f32[1,8,128]{2,1,0:T(8,128)S(1)} collective-permute-done((f32[1,8,128]{2,1,0:T(8,128)S(1)}, f32[1,8,128]{2,1,0:T(8,128)S(1)}, u32[]{:S(2)}, u32[]{:S(2)}) %collective-permute-start.7) | collective-permute-done | bytes 4128 | tf_op jit(solution)/shard_map/ppermute | solution.py:435
  92.1 5.1 %collective-permute-start.8 = (f32[1,8,128]{2,1,0:T(8,128)S(1)}, f32[1,8,128]{2,1,0:T(8,128)S(1)}, u32[]{:S(2)}, u32[]{:S(2)}) collective-permute-start(f32[1,8,128]{2,1,0:T(8,128)S(1)} %add.10), channel_id=1, source_target_pairs={{0,4},{1,5},{2,6},{3,7},{4,0},{5,1},{6,2},{7,3},{8,12},{9,13},{10,... | collective-permute-start | bytes 12296 | tf_op jit(solution)/shard_map/ppermute | solution.py:435
  97.2 1.6 %collective-permute-done.8 = f32[1,8,128]{2,1,0:T(8,128)S(1)} collective-permute-done((f32[1,8,128]{2,1,0:T(8,128)S(1)}, f32[1,8,128]{2,1,0:T(8,128)S(1)}, u32[]{:S(2)}, u32[]{:S(2)}) %collective-permute-start.8) | collective-permute-done | bytes 4128 | tf_op jit(solution)/shard_map/ppermute | solution.py:435
  98.7 4.9 %collective-permute-done.9.prev_ref = bf16[2,1024,256]{2,1,0:T(8,128)(2,1)S(1)} collective-permute-done((bf16[2,1024,256]{2,1,0:T(8,128)(2,1)}, bf16[2,1024,256]{2,1,0:T(8,128)(2,1)S(1)}, u32[]{:S(2)}, u32[]{:S(2)}) %collective-permute-start.9) | collective-permute-done | bytes 1048608 | tf_op jit(solution)/shard_map/ppermute | solution.py:367
  103.6 1.0 copy-done.11
  104.6 2.0 %shard_map.81 = bf16[3072,128]{1,0:T(8,128)(2,1)S(1)} custom-call(bf16[3072,128]{1,0:T(8,128)(2,1)S(1)} %bitcast.22), custom_call_target="tpu_custom_call" | custom-call | flops 2097152 | bytes 1572864 | tf_op jit(solution)/shard_map/pallas_call | solution.py:32
  106.6 0.0 copy-start.4
  106.6 0.9 copy-done.4
  107.5 13.5 %all-to-all-start.2 = ((bf16[128,24,128]{2,1,0:T(8,128)(2,1)}), bf16[128,24,128]{2,1,0:T(8,128)(2,1)S(1)}, u32[]{:S(2)}, u32[]{:S(2)}) async-start(bf16[128,24,128]{2,1,0:T(8,128)(2,1)} %bitcast.25), calls=%async_computation.2 | async-start | bytes 1572864 | tf_op jit(solution)/shard_map/all_to_all | solution.py:439
  121.0 0.0 copy-start.7
  121.0 1.6 %copy-done.7 = f32[2,1024,256]{2,1,0:T(8,128)S(1)} copy-done((f32[2,1024,256]{2,1,0:T(8,128)S(1)}, f32[2,1024,256]{2,1,0:T(8,128)}, u32[]{:S(2)}) %copy-start.7) | copy-done | bytes 2097176
  122.6 1.9 %shard_map.82 = bf16[2,1024,256]{2,1,0:T(8,128)(2,1)} custom-call(bf16[2,1024,256]{2,1,0:T(8,128)(2,1)S(1)} %bitcast.16, bf16[2,1024,256]{2,1,0:T(8,128)(2,1)S(1)} %bitcast.21, f32[2,1024,256]{2,1,0:T(8,128)S(1)} %copy-done.7, f32[8,8,128]{2,1,0:T(8,128)S(1)} %all-to-all-done.refs_4_.refs_5_.refs_3_, f32[1,8,128]{2,1,0:T(8,128)S(1)} %add.11.refs_4_), custom_call_target="tpu_custom_call" | custom-call | flops 2097152 | bytes 5279744 | tf_op jit(solution)/shard_map/pallas_call | solution.py:32
  124.5 3.2 %shard_map.83 = bf16[2,1024,256]{2,1,0:T(8,128)(2,1)} custom-call(bf16[2,1024,256]{2,1,0:T(8,128)(2,1)S(1)} %bitcast.17, bf16[2,1024,256]{2,1,0:T(8,128)(2,1)S(1)} %copy-done.10, bf16[2,1024,256]{2,1,0:T(8,128)(2,1)S(1)} %copy-done.12, bf16[3,256,256]{2,1,0:T(8,128)(2,1)S(1)} %copy-done.8), custom_call_target="tpu_custom_call" | custom-call | flops 805306368 | bytes 4587520 | tf_op jit(solution)/shard_map/pallas_call | solution.py:32
  127.7 17.5 %all-to-all-done.2 = bf16[128,24,128]{2,1,0:T(8,128)(2,1)S(1)} async-done(((bf16[128,24,128]{2,1,0:T(8,128)(2,1)}), bf16[128,24,128]{2,1,0:T(8,128)(2,1)S(1)}, u32[]{:S(2)}, u32[]{:S(2)}) %all-to-all-start.2) | async-done | bytes 786464 | tf_op jit(solution)/shard_map/all_to_all | solution.py:439
  145.2 3.1 %collective-permute-start.10 = (bf16[3072,128]{1,0:T(8,128)(2,1)S(1)}, bf16[3072,128]{1,0:T(8,128)(2,1)S(1)}, u32[]{:S(2)}, u32[]{:S(2)}) collective-permute-start(bf16[3072,128]{1,0:T(8,128)(2,1)S(1)} %bitcast.23), channel_id=1, source_target_pairs={{0,32},{32,0},{1,33},{33,1},{2,34},{34,2},{3,35},{35,3},{4,36},{36... | collective-permute-start | bytes 2359304 | tf_op jit(solution)/shard_map/ppermute | solution.py:361
  148.2 1.9 %collective-permute-done.10.refs_2_ = bf16[3072,128]{1,0:T(8,128)(2,1)S(1)} collective-permute-done((bf16[3072,128]{1,0:T(8,128)(2,1)S(1)}, bf16[3072,128]{1,0:T(8,128)(2,1)S(1)}, u32[]{:S(2)}, u32[]{:S(2)}) %collective-permute-start.10) | collective-permute-done | bytes 786464 | tf_op jit(solution)/shard_map/ppermute | solution.py:361
  150.2 4.8 %shard_map.84 = (f32[9,256,256]{2,1,0:T(8,128)}, f32[3,256,256]{2,1,0:T(8,128)}) custom-call(s32[3]{0:T(128)S(1)} %pad_add_fusion.refs_0_.info, bf16[3072,128]{1,0:T(8,128)(2,1)S(1)} %bitcast.24, bf16[3072,128]{1,0:T(8,128)(2,1)S(1)} %collective-permute-done.10.refs_2_), custom_call_target="tpu_custom_call" | custom-call | flops 2097152 | bytes 4718604 | tf_op jit(solution)/shard_map/pallas_call | solution.py:32
  (32 shorter events, 0.1 us)
Async XLA Ops:
  0.6 35.2 %collective-permute-start.2 = (bf16[2,1024,256]{2,1,0:T(8,128)(2,1)}, bf16[2,1024,256]{2,1,0:T(8,128)(2,1)S(1)}, u32[]{:S(2)}, u32[]{:S(2)}) collective-permute-start(bf16[2,1024,256]{2,1,0:T(8,128)(2,1)} %bitcast.18), channel_id=1, source_target_pairs={{8,0},{16,8},{24,16},{9,1},{17,9},{25,17},{10,2},{18,10},{26,18},{... | collective-permute-start | bytes 3145736 | tf_op jit(solution)/shard_map/ppermute | solution.py:367
  1.9 1.2 copy-start
  4.1 22.4 %collective-permute-start = (bf16[2,128,256]{2,1,0:T(8,128)(2,1)S(1)}, bf16[2,128,256]{2,1,0:T(8,128)(2,1)S(1)}, u32[]{:S(2)}, u32[]{:S(2)}) collective-permute-start(bf16[2,128,256]{2,1,0:T(8,128)(2,1)S(1)} %get-tuple-element.33), channel_id=1, source_target_pairs={{0,1},{1,2},{2,3},{3,4},{4,5},{5,6},{6,7},{8,9},{9,10},{10,11},{11... | collective-permute-start | bytes 393224 | tf_op jit(solution)/shard_map/ppermute | solution.py:367
  8.5 18.1 %collective-permute-start.1 = (bf16[2,128,256]{2,1,0:T(8,128)(2,1)S(1)}, bf16[2,128,256]{2,1,0:T(8,128)(2,1)S(1)}, u32[]{:S(2)}, u32[]{:S(2)}) collective-permute-start(bf16[2,128,256]{2,1,0:T(8,128)(2,1)S(1)} %get-tuple-element.34), channel_id=1, source_target_pairs={{1,0},{2,1},{3,2},{4,3},{5,4},{6,5},{7,6},{9,8},{10,9},{11,10},{12... | collective-permute-start | bytes 393224 | tf_op jit(solution)/shard_map/ppermute | solution.py:367
  9.8 16.8 %all-to-all-start = ((f32[8,8,128]{2,1,0:T(8,128)}), f32[8,8,128]{2,1,0:T(8,128)S(1)}, u32[]{:S(2)}, u32[]{:S(2)}) async-start(f32[8,8,128]{2,1,0:T(8,128)} %get-tuple-element.35), calls=%async_computation | async-start | bytes 65536 | tf_op jit(solution)/shard_map/all_to_all | solution.py:393
  26.6 1.2 copy-start.1
  27.8 1.3 copy-start.13
  29.1 6.8 %copy-start.3 = (bf16[1,2,8,128,256]{4,3,2,1,0:T(8,128)(2,1)S(1)}, bf16[1,2,8,128,256]{4,3,2,1,0:T(8,128)(2,1)}, u32[]{:S(2)}) copy-start(bf16[1,2,8,128,256]{4,3,2,1,0:T(8,128)(2,1)} %param.5) | copy-start | bytes 3145732
  29.1 6.8 %copy-start.8 = (bf16[3,256,256]{2,1,0:T(8,128)(2,1)S(1)}, bf16[3,256,256]{2,1,0:T(8,128)(2,1)}, u32[]{:S(2)}) copy-start(bf16[3,256,256]{2,1,0:T(8,128)(2,1)} %w_ref.3) | copy-start | bytes 1179652
  35.8 6.0 %copy-start.9 = (bf16[2,1024,256]{2,1,0:T(8,128)(2,1)}, bf16[2,1024,256]{2,1,0:T(8,128)(2,1)S(1)}, u32[]{:S(2)}) copy-start(bf16[2,1024,256]{2,1,0:T(8,128)(2,1)S(1)} %get-tuple-element.52.hid_ref) | copy-start | bytes 3145732
  38.3 12.7 %copy-start.15 = (bf16[2,1024,256]{2,1,0:T(8,128)(2,1)}, bf16[2,1024,256]{2,1,0:T(8,128)(2,1)S(1)}, u32[]{:S(2)}) copy-start(bf16[2,1024,256]{2,1,0:T(8,128)(2,1)S(1)} %get-tuple-element.38.pg_ref.refs_0_) | copy-start | bytes 3145732
  38.3 12.7 %collective-permute-start.3 = (bf16[2,128,256]{2,1,0:T(8,128)(2,1)S(1)}, bf16[2,128,256]{2,1,0:T(8,128)(2,1)S(1)}, u32[]{:S(2)}, u32[]{:S(2)}) collective-permute-start(bf16[2,128,256]{2,1,0:T(8,128)(2,1)S(1)} %get-tuple-element.42), channel_id=1, source_target_pairs={{0,1},{1,2},{2,3},{3,4},{4,5},{5,6},{6,7},{8,9},{9,10},{10,11},{11... | collective-permute-start | bytes 393224 | tf_op jit(solution)/shard_map/ppermute | solution.py:367
  40.5 10.6 %collective-permute-start.4 = (bf16[2,128,256]{2,1,0:T(8,128)(2,1)S(1)}, bf16[2,128,256]{2,1,0:T(8,128)(2,1)S(1)}, u32[]{:S(2)}, u32[]{:S(2)}) collective-permute-start(bf16[2,128,256]{2,1,0:T(8,128)(2,1)S(1)} %get-tuple-element.43), channel_id=1, source_target_pairs={{1,0},{2,1},{3,2},{4,3},{5,4},{6,5},{7,6},{9,8},{10,9},{11,10},{12... | collective-permute-start | bytes 393224 | tf_op jit(solution)/shard_map/ppermute | solution.py:367
  51.1 7.7 %copy-start.17 = (bf16[2,128,256]{2,1,0:T(8,128)(2,1)}, bf16[2,128,256]{2,1,0:T(8,128)(2,1)S(1)}, u32[]{:S(2)}) copy-start(bf16[2,128,256]{2,1,0:T(8,128)(2,1)S(1)} %collective-permute-done.4.refs_2_) | copy-start | bytes 393220
  51.1 6.1 %collective-permute-start.5 = (f32[3072,128]{1,0:T(8,128)S(1)}, f32[3072,128]{1,0:T(8,128)S(1)}, u32[]{:S(2)}, u32[]{:S(2)}) collective-permute-start(f32[3072,128]{1,0:T(8,128)S(1)} %get-tuple-element.44), channel_id=1, source_target_pairs={{0,32},{32,0},{1,33},{33,1},{2,34},{34,2},{3,35},{35,3},{4,36},{36... | collective-permute-start | bytes 4718600 | tf_op jit(solution)/shard_map/ppermute | solution.py:361
  57.2 17.5 %copy-start.2 = (bf16[1,2,8,128,256]{4,3,2,1,0:T(8,128)(2,1)S(1)}, bf16[1,2,8,128,256]{4,3,2,1,0:T(8,128)(2,1)}, u32[]{:S(2)}) copy-start(bf16[1,2,8,128,256]{4,3,2,1,0:T(8,128)(2,1)} %param.4) | copy-start | bytes 3145732
  57.8 0.9 copy-start.5
  58.7 45.9 %all-to-all-start.1 = ((bf16[128,24,128]{2,1,0:T(8,128)(2,1)}), bf16[128,24,128]{2,1,0:T(8,128)(2,1)S(1)}, u32[]{:S(2)}, u32[]{:S(2)}) async-start(bf16[128,24,128]{2,1,0:T(8,128)(2,1)} %bitcast.26), calls=%async_computation.1 | async-start | bytes 1572864 | tf_op jit(solution)/shard_map/all_to_all | solution.py:426
  72.1 31.6 %collective-permute-start.9 = (bf16[2,1024,256]{2,1,0:T(8,128)(2,1)}, bf16[2,1024,256]{2,1,0:T(8,128)(2,1)S(1)}, u32[]{:S(2)}, u32[]{:S(2)}) collective-permute-start(bf16[2,1024,256]{2,1,0:T(8,128)(2,1)} %copy-done.9), channel_id=1, source_target_pairs={{0,8},{8,16},{16,24},{1,9},{9,17},{17,25},{2,10},{10,18},{18,26},{... | collective-permute-start | bytes 3145736 | tf_op jit(solution)/shard_map/ppermute | solution.py:367
  74.7 1.3 copy-start.14
  75.9 1.2 copy-start.16
  77.1 0.9 copy-start.18
  83.3 1.3 copy-start.6
  84.6 3.8 %collective-permute-start.6 = (f32[1,8,128]{2,1,0:T(8,128)S(1)}, f32[1,8,128]{2,1,0:T(8,128)S(1)}, u32[]{:S(2)}, u32[]{:S(2)}) collective-permute-start(f32[1,8,128]{2,1,0:T(8,128)S(1)} %get-tuple-element.51), channel_id=1, source_target_pairs={{0,1},{1,0},{2,3},{3,2},{4,5},{5,4},{6,7},{7,6},{8,9},{9,8},{10,11... | collective-permute-start | bytes 12296 | tf_op jit(solution)/shard_map/ppermute | solution.py:435
  88.4 3.7 %collective-permute-start.7 = (f32[1,8,128]{2,1,0:T(8,128)S(1)}, f32[1,8,128]{2,1,0:T(8,128)S(1)}, u32[]{:S(2)}, u32[]{:S(2)}) collective-permute-start(f32[1,8,128]{2,1,0:T(8,128)S(1)} %add.9), channel_id=1, source_target_pairs={{0,2},{1,3},{2,0},{3,1},{4,6},{5,7},{6,4},{7,5},{8,10},{9,11},{10,... | collective-permute-start | bytes 12296 | tf_op jit(solution)/shard_map/ppermute | solution.py:435
  92.1 6.7 %collective-permute-start.8 = (f32[1,8,128]{2,1,0:T(8,128)S(1)}, f32[1,8,128]{2,1,0:T(8,128)S(1)}, u32[]{:S(2)}, u32[]{:S(2)}) collective-permute-start(f32[1,8,128]{2,1,0:T(8,128)S(1)} %add.10), channel_id=1, source_target_pairs={{0,4},{1,5},{2,6},{3,7},{4,0},{5,1},{6,2},{7,3},{8,12},{9,13},{10,... | collective-permute-start | bytes 12296 | tf_op jit(solution)/shard_map/ppermute | solution.py:435
  103.6 1.0 copy-start.11
  106.6 0.9 copy-start.4
  107.5 37.7 %all-to-all-start.2 = ((bf16[128,24,128]{2,1,0:T(8,128)(2,1)}), bf16[128,24,128]{2,1,0:T(8,128)(2,1)S(1)}, u32[]{:S(2)}, u32[]{:S(2)}) async-start(bf16[128,24,128]{2,1,0:T(8,128)(2,1)} %bitcast.25), calls=%async_computation.2 | async-start | bytes 1572864 | tf_op jit(solution)/shard_map/all_to_all | solution.py:439
  121.0 1.6 %copy-start.7 = (f32[2,1024,256]{2,1,0:T(8,128)S(1)}, f32[2,1024,256]{2,1,0:T(8,128)}, u32[]{:S(2)}) copy-start(f32[2,1024,256]{2,1,0:T(8,128)} %copy-done.6) | copy-start | bytes 6291460
  122.6 1.9 %copy-start.10 = (bf16[2,1024,256]{2,1,0:T(8,128)(2,1)S(1)}, bf16[2,1024,256]{2,1,0:T(8,128)(2,1)}, u32[]{:S(2)}) copy-start(bf16[2,1024,256]{2,1,0:T(8,128)(2,1)} %copy-done.9) | copy-start | bytes 3145732
  122.6 1.9 %copy-start.12 = (bf16[2,1024,256]{2,1,0:T(8,128)(2,1)S(1)}, bf16[2,1024,256]{2,1,0:T(8,128)(2,1)}, u32[]{:S(2)}) copy-start(bf16[2,1024,256]{2,1,0:T(8,128)(2,1)} %copy-done.11) | copy-start | bytes 3145732
  145.2 5.0 %collective-permute-start.10 = (bf16[3072,128]{1,0:T(8,128)(2,1)S(1)}, bf16[3072,128]{1,0:T(8,128)(2,1)S(1)}, u32[]{:S(2)}, u32[]{:S(2)}) collective-permute-start(bf16[3072,128]{1,0:T(8,128)(2,1)S(1)} %bitcast.23), channel_id=1, source_target_pairs={{0,32},{32,0},{1,33},{33,1},{2,34},{34,2},{3,35},{35,3},{4,36},{36... | collective-permute-start | bytes 2359304 | tf_op jit(solution)/shard_map/ppermute | solution.py:361

commit v4 on v3

--- a/solution.py
+++ b/solution.py
@@ -17,7 +17,6 @@
 DP = ("y", "core")
 TM = "tm"
 HEIGHT = "height"
-CHIPS = ("y", "tm", "height")
 UNIT = 2.0**40
 VMEM = pl.BlockSpec(memory_space=pltpu.VMEM)
 SMEM = pl.BlockSpec(memory_space=pltpu.SMEM)
@@ -187,20 +186,19 @@
         bot_ref[f] = pg_ref[f, 896:1024, :]
 
 
-def grads_kernel(info, act_ref, pg_ref, hid_ref, cot_ref, later_ref, keep_ref, send_ref):
+def slab_rows(info, unit, part):
+    piece = (unit % 3) * 4 + part
+    x, y = (unit // 3 - info[3]) & 3, (piece // 3 - info[4]) & 3
+    return pl.multiple_of(x * 768 + y * 192 + (piece % 3) * 64, 64)
+
+
+def grads_kernel(info, act_ref, pg_ref, hid_ref, cot_ref, later_ref, g_ref):
     def put(tap, v):
-        mine = info[0] == tap // 6
+        base = ((tap // 6) ^ info[0]) * 3072
         for lh in range(2):
-            at = ((tap % 6) * 2 + lh) * 256
-            half = v[:, lh * 128 : lh * 128 + 128]
-
-            @pl.when(mine)
-            def _():
-                keep_ref[at : at + 256, :] = half
-
-            @pl.when(jnp.logical_not(mine))
-            def _():
-                send_ref[at : at + 256, :] = half
+            for part in range(4):
+                at = pl.multiple_of(base + slab_rows(info, (tap % 6) * 2 + lh, part), 64)
+                g_ref[pl.ds(at, 64), :] = v[part * 64 : part * 64 + 64, lh * 128 : lh * 128 + 128]
 
     for i in range(3):
         for j in range(3):
@@ -309,30 +307,50 @@
     return jnp.where(size < 1e-37, 0.0, jnp.where(u < 0, -root, root))
 
 
-def encode_kernel(a_ref, b_ref, o_ref):
-    def part(r, _):
-        at = pl.ds(pl.multiple_of(r * 256, 256), 256)
-        o_ref[at, :] = coded(a_ref[at, :] + b_ref[at, :])
-        return 0
-
-    lax.fori_loop(0, a_ref.shape[0] // 256, part, 0)
-
-
-def own_kernel(u_ref, o_ref):
-    rows = u_ref.shape[0] // 64
-
-    def part(r, acc):
-        return acc + decoded(u_ref[pl.ds(pl.multiple_of(r * rows, rows), rows), :])
-
-    acc = lax.fori_loop(0, 64, part, jnp.zeros((rows, 128), F32))
-    total = acc[: rows // 2] + acc[rows // 2 :]
-    copy = coded(jnp.concatenate([total, total], axis=0))
-
-    def put(r, _):
-        o_ref[pl.ds(pl.multiple_of(r * rows, rows), rows), :] = copy
-        return 0
-
-    lax.fori_loop(0, 64, put, 0)
+def pair_kernel(g_ref, got_ref, own_ref, *sent):
+    for k in range(4):
+
+        def part(r, _):
+            at = pl.multiple_of(r * 128, 128)
+            rows = pl.ds(pl.multiple_of(at + k * 768, 128), 128)
+            v = g_ref[rows, :] + got_ref[rows, :]
+            if k == 0:
+                own_ref[pl.ds(at, 128), :] = v
+            else:
+                sent[k - 1][pl.ds(at, 128), :] = coded(v)
+            return 0
+
+        lax.fori_loop(0, 6, part, 0)
+
+
+def x_kernel(own_ref, a_ref, b_ref, c_ref, mine_ref, *sent):
+    for k in range(4):
+
+        def part(r, _):
+            at = pl.multiple_of(r * 64, 64)
+            rows = pl.ds(pl.multiple_of(at + k * 192, 64), 64)
+            v = own_ref[rows, :] + decoded(a_ref[rows, :]) + decoded(b_ref[rows, :]) + decoded(c_ref[rows, :])
+            (mine_ref, *sent)[k][pl.ds(at, 64), :] = v
+            return 0
+
+        lax.fori_loop(0, 3, part, 0)
+
+
+def y_kernel(own_ref, a_ref, b_ref, c_ref, gst_ref, o_ref):
+    for peer in range(8):
+        rows = slice(peer * 24, peer * 24 + 24)
+        o_ref[peer, 0:24, :] = own_ref[rows, :] + a_ref[rows, :] + b_ref[rows, :] + c_ref[rows, :]
+        o_ref[peer, 24:32, :] = gst_ref[0]
+
+
+def z_kernel(u_ref, o_ref, gst_ref):
+    total = u_ref[0]
+    for peer in range(1, 8):
+        total = total + u_ref[peer]
+    gst_ref[0] = total[24:32]
+    mine = coded(total[:24])
+    for peer in range(8):
+        o_ref[peer] = mine
 
 
 def clip_kernel(clip_level, info, own_ref, other_ref, s_ref, t_ref):
@@ -341,10 +359,11 @@
         ref, k = (s_ref, tap) if tap < 9 else (t_ref, tap - 9)
         mine = info[0] == tap // 6
         for lh in range(2):
-            at = ((tap % 6) * 2 + lh) * 256
-            v = decoded(jnp.where(mine, own_ref[at : at + 256, :], other_ref[at : at + 256, :]))
-            ref[k, :, lh * 128 : lh * 128 + 128] = v
-            acc = acc + fold(v * v)
+            for part in range(4):
+                at = pl.ds(slab_rows(info, (tap % 6) * 2 + lh, part), 64)
+                v = decoded(jnp.where(mine, own_ref[at, :], other_ref[at, :]))
+                ref[k, part * 64 : part * 64 + 64, lh * 128 : lh * 128 + 128] = v
+                acc = acc + fold(v * v)
     total = jnp.sum(jnp.sum(acc, axis=0, keepdims=True), axis=1, keepdims=True)
     scale = clip_level / jnp.maximum(jnp.sqrt(total), clip_level)
 
@@ -355,6 +374,10 @@
     lax.fori_loop(0, 9, finish, 0)
     for k in range(3):
         t_ref[k] = t_ref[k] * scale
+
+
+def in_hbm(x):
+    return pltpu.with_memory_space_constraint(x, pltpu.HBM)
 
 
 def swapped(x, axis):
@@ -365,6 +388,18 @@
     n = lax.axis_size(axes)
     route = [(i, i + distance) for i in range(n) if 0 <= i + distance < n]
     return lax.ppermute(x, axes, route)
+
+
+def shifts(sent, axis):
+    n = lax.axis_size(axis)
+    return [
+        lax.ppermute(m, axis, [(i, (i + d) % n) for i in range(n)]) for d, m in enumerate(sent, 1)
+    ]
+
+
+def gathered(mine, axis):
+    got = tied(shifts([mine] * 3, axis))
+    return jnp.concatenate([mine, got[2], got[1], got[0]], axis=0)
 
 
 def body(video_latents, cotangent, spatial_kernel, temporal_kernel):
@@ -377,7 +412,9 @@
         / CLIP_DIVISOR
     )
     z = lax.axis_index(HEIGHT)
-    info = jnp.stack([lax.axis_index("core"), z, peers - 1 - z]).astype(jnp.int32)
+    info = jnp.stack(
+        [lax.axis_index("core"), z, peers - 1 - z, lax.axis_index(TM), lax.axis_index("y")]
+    ).astype(jnp.int32)
     pixels = rows * columns
     flat = (2, pixels, 256)
     x = video_latents.reshape(flat)
@@ -396,7 +433,7 @@
     act, hid, slope = call(
         lambda *refs: forward_kernel(members, *refs),
         [out((2, 1280, 768), BF16), out(flat, BF16), out(flat, F32)],
-        [info, x, up, dn, st, w3],
+        [info, in_hbm(x), in_hbm(up), in_hbm(dn), in_hbm(st), in_hbm(w3)],
         9 * gflop,
         smem=1,
         loose=(2, 3, 4),
@@ -410,20 +447,19 @@
     pg, top, bot = call(
         pregrad_kernel, [out(flat, BF16), edge, edge], [cot, later, slope, temporal_kernel], 3 * gflop
     )
+    (g,) = call(
+        grads_kernel, [out((6144, 128), F32)], [info, act, pg, hid, cot, later], 12 * gflop, smem=1
+    )
+    send, top, bot = tied((g[3072:], top, bot))
+    got = swapped(send, "core")
     gup = moved(bot, HEIGHT, 1)
     gdn = moved(top, HEIGHT, -1)
-    slab = (3072, 128)
-    keep, send = call(
-        grads_kernel,
-        [out(slab, F32), out(slab, F32)],
-        [info, act, pg, hid, cot, later],
-        12 * gflop,
-        smem=1,
-    )
-    send, gup, gdn = tied((send, gup, gdn))
-    (code,) = call(encode_kernel, [out(slab, BF16)], [keep, swapped(send, "core")], 1 << 21)
-    code, gup, gdn, hid_sent = tied((code, gup, gdn, hid))
-    code = lax.all_to_all(code.reshape(128, 24, 128), CHIPS, 0, 0, tiled=True)
+    quarter = out((768, 128), BF16)
+    own, *sent = call(
+        pair_kernel, [out((768, 128), F32), quarter, quarter, quarter], [g, got], 1 << 21
+    )
+    own, sent, gup, gdn = tied((own, sent, gup, gdn))
+    got = shifts(sent, TM)
     ng, gst = call(
         lambda *refs: backward_kernel(members, *refs),
         [out(flat, F32), out((1, 8, 128), F32)],
@@ -431,18 +467,24 @@
         9 * gflop,
         scratch=[pltpu.VMEM((2, 1280, 256), BF16)] * 3,
     )
-    for d in (1, 2, 4):
-        gst = gst + lax.ppermute(gst, HEIGHT, [(i, i ^ d) for i in range(peers)])
+    got, ng, gst = tied((got, ng, gst))
+    part = out((192, 128), F32)
+    own, *sent = call(x_kernel, [part] * 4, [own, *got], 1 << 21)
+    own, sent, hid_sent = tied((own, sent, hid))
+    got = tied(shifts(sent, "y"))
     prev = moved(hid_sent, TM, 1)
-    code, ng, gst, prev = tied((code, ng, gst, prev))
-    (copies,) = call(own_kernel, [out(slab, BF16)], [code.reshape(slab)], 1 << 21)
-    mine = lax.all_to_all(copies.reshape(128, 24, 128), CHIPS, 0, 0, tiled=True)
+    (pieces,) = call(y_kernel, [out((8, 32, 128), F32)], [own, *got, gst], 1 << 20)
+    pieces = lax.all_to_all(pieces, HEIGHT, 0, 0, tiled=True)
+    copies, gst = call(z_kernel, [out((8, 24, 128), BF16), out((1, 8, 128), F32)], [pieces], 1 << 20)
+    mine = lax.all_to_all(copies, HEIGHT, 0, 0, tiled=True).reshape(192, 128)
     (input_grad,) = call(
         lambda *refs: input_grad_kernel(members, *refs), [out(flat, BF16)], [x, cot, ng, st, gst], 1 << 21
     )
+    mine, input_grad = tied((mine, input_grad))
+    mine, prev = tied((gathered(mine, "y"), prev))
     (block_output,) = call(block_kernel, [out(flat, BF16)], [x, hid, prev, temporal_kernel], 3 * gflop)
-    mine, input_grad, block_output = tied((mine, input_grad, block_output))
-    mine = mine.reshape(slab)
+    mine = gathered(mine, TM)
+    mine, block_output = tied((mine, block_output))
     clipped_spatial, clipped_temporal = call(
         lambda *refs: clip_kernel(clip_level, *refs),
         [out((9, 256, 256), F32), out((3, 256, 256), F32)],

time: 156 us -> 134 us (0.86)
  waiting for transfers between devices: 40.6 us -> 26.6 us
  blocking collectives: 0 us -> 10.6 us
  starting transfers between devices: 63.4 us -> 54.6 us
  local copies, waits for them, and re-layouts: 12.8 us -> 7.01 us
  Pallas kernels: 37.2 us -> 33.1 us
    all_to_all x2 -> x1, starting transfers between devices: 26.8 us -> 3.95 us  [body(): mine = lax.all_to_all(copies, HEIGHT, 0, 0, tiled=True).reshape(192, 128)]
    all_to_all x2 -> x1, waiting for transfers between devices: 17.5 us -> 2.76 us  [body(): mine = lax.all_to_all(copies, HEIGHT, 0, 0, tiled=True).reshape(192, 128)]
    all_to_all x0 -> x1, blocking collectives: none -> 10.6 us  [body(): pieces = lax.all_to_all(pieces, HEIGHT, 0, 0, tiled=True)]
    ppermute x3 -> x12, starting transfers between devices: 7.69 us -> 15.7 us  [shifts(): lax.ppermute(m, axis, [(i, (i + d) % n) for i in range(n)])]
    unnamed x38 -> x26, local copies, waits for them, and re-layouts: 12.8 us -> 6.83 us
    ppermute x3 -> x12, waiting for transfers between devices: 6.44 us -> 10.6 us  [shifts(): lax.ppermute(m, axis, [(i, (i + d) % n) for i in range(n)])]
    pallas_call x10 -> x12, Pallas kernels: 37.2 us -> 33.1 us  [call(): pl.pallas_call(kernel, out_shape=tuple(outs), in_specs=specs, out_specs=t...]
    ppermute x2, starting transfers between devices: 6.11 us -> 9.76 us  [swapped(): return lax.ppermute(x, axis, [(0, 1), (1, 0)])]
  transfers between devices with their start and end apart: 14 -> 22, of which waited for: 8 -> 13; matrix products, arithmetic and copies ran while one was open for 0% -> 1% of each run, Pallas kernels for 18% -> 16%
where the time goes in v4:
time: 134 us
  starting transfers between devices  54.6 us (41%)
  Pallas kernels  33.1 us (25%)
  waiting for transfers between devices  26.6 us (20%)
  blocking collectives  10.6 us (8%)
  local copies, waits for them, and re-layouts  7.01 us (5%)
    pallas_call x12, Pallas kernels, call(): pl.pallas_call(kernel, out_shape=tuple(outs), in_specs=specs, out_specs=t...  33.1 us
    ppermute x12, starting transfers between devices, shifts(): lax.ppermute(m, axis, [(i, (i + d) % n) for i in range(n)])  15.7 us
    ppermute x6, starting transfers between devices, moved(): return lax.ppermute(x, axes, route)  15.3 us
    ppermute x12, waiting for transfers between devices, shifts(): lax.ppermute(m, axis, [(i, (i + d) % n) for i in range(n)])  10.6 us
    all_to_all x1, blocking collectives, body(): pieces = lax.all_to_all(pieces, HEIGHT, 0, 0, tiled=True)  10.6 us
    all_to_all x1, starting transfers between devices, body(): st = lax.all_to_all(st, HEIGHT, 0, 0, tiled=True)  9.85 us
    ppermute x2, starting transfers between devices, swapped(): return lax.ppermute(x, axis, [(0, 1), (1, 0)])  9.76 us
    all_to_all x1, waiting for transfers between devices, body(): st = lax.all_to_all(st, HEIGHT, 0, 0, tiled=True)  6.83 us
  transfers between devices with their start and end apart: 22, of which 13 were waited for; matrix products, arithmetic and copies ran while one was open for 1% of the time, Pallas kernels for 16%

profile of v4, /device:TPU:1, one launch (start us, length us, event | category | flops | bytes accessed | tf_op | source)
XLA Modules:
  0.0 133.6 jit_solution(1949235651090072013)
XLA Ops:
  0.6 1.3 collective-permute-start.2
  1.9 1.2 copy-done
  3.2 1.0 shard_map.75
  4.1 4.4 %collective-permute-start = (bf16[2,128,256]{2,1,0:T(8,128)(2,1)S(1)}, bf16[2,128,256]{2,1,0:T(8,128)(2,1)S(1)}, u32[]{:S(2)}, u32[]{:S(2)}) collective-permute-start(bf16[2,128,256]{2,1,0:T(8,128)(2,1)S(1)} %get-tuple-element.61), channel_id=1, source_target_pairs={{0,1},{1,2},{2,3},{3,4},{4,5},{5,6},{6,7},{8,9},{9,10},{10,11},{11... | collective-permute-start | bytes 393224 | tf_op jit(solution)/shard_map/ppermute | solution.py:390
  8.5 1.3 collective-permute-start.1
  9.8 9.8 %all-to-all-start = ((f32[8,8,128]{2,1,0:T(8,128)}), f32[8,8,128]{2,1,0:T(8,128)S(1)}, u32[]{:S(2)}, u32[]{:S(2)}) async-start(f32[8,8,128]{2,1,0:T(8,128)} %get-tuple-element.63), calls=%async_computation | async-start | bytes 65536 | tf_op jit(solution)/shard_map/all_to_all | solution.py:430
  19.7 6.8 %all-to-all-done.refs_4_.refs_5_.refs_3_ = f32[8,8,128]{2,1,0:T(8,128)S(1)} async-done(((f32[8,8,128]{2,1,0:T(8,128)}), f32[8,8,128]{2,1,0:T(8,128)S(1)}, u32[]{:S(2)}, u32[]{:S(2)}) %all-to-all-start) | async-done | bytes 32800 | tf_op jit(solution)/shard_map/all_to_all | solution.py:430
  26.6 0.6 copy-done.6
  27.2 0.7 copy-done.12
  27.9 8.5 %shard_map.76 = (bf16[2,1280,768]{2,1,0:T(8,128)(2,1)S(1)}, bf16[2,1024,256]{2,1,0:T(8,128)(2,1)S(1)}, f32[2,1024,256]{2,1,0:T(8,128)S(1)}) custom-call(s32[5]{0:T(128)S(1)} %stack.23.refs_0_.info, bf16[2,1024,256]{2,1,0:T(8,128)(2,1)} %bitcast.12, bf16[2,128,256]{2,1,0:T(8,128)(2,1)} %copy-done.11, bf16[2,128,256]{2,1,0:T(8,128)(2,1)} %copy-done.12, ...), custom_call_target="tpu_custom_call" | custom-call | flops 2415919104 | bytes 9601044 | tf_op jit(solution)/shard_map/pallas_call | solution.py:31
  36.4 2.4 %shard_map.77 = (bf16[2,1024,256]{2,1,0:T(8,128)(2,1)S(1)}, bf16[2,128,256]{2,1,0:T(8,128)(2,1)S(1)}, bf16[2,128,256]{2,1,0:T(8,128)(2,1)S(1)}) custom-call(bf16[2,1024,256]{2,1,0:T(8,128)(2,1)S(1)} %bitcast.18, bf16[2,1024,256]{2,1,0:T(8,128)(2,1)S(1)} %collective-permute-done.2.later_ref, f32[2,1024,256]{2,1,0:T(8,128)S(1)} %get-tuple-element.65.slope_ref, ...), custom_call_target="tpu_custom_call" | custom-call | flops 805306368 | bytes 5898240 | tf_op jit(solution)/shard_map/pallas_call | solution.py:31
  38.8 4.0 %shard_map.78.g_ref = f32[6144,128]{1,0:T(8,128)S(1)} custom-call(s32[5]{0:T(128)S(1)} %stack.23.refs_0_.info, bf16[2,1280,768]{2,1,0:T(8,128)(2,1)S(1)} %get-tuple-element.64.act_ref, bf16[2,1024,256]{2,1,0:T(8,128)(2,1)S(1)} %get-tuple-element.66.pg_ref.refs_0_, bf16[2,1024,256]{2,1,0:T(8,128)(2,1)S(1)} %get-tuple-element.107.hid_ref, ...), custom_call_target="tpu_custom_call" | custom-call | flops 3221225472 | bytes 11272212 | tf_op jit(solution)/shard_map/pallas_call | solution.py:31
  43.0 2.7 %collective-permute-start.3 = (f32[3072,128]{1,0:T(8,128)S(1)}, f32[3072,128]{1,0:T(8,128)S(1)}, u32[]{:S(2)}, u32[]{:S(2)}) collective-permute-start(f32[3072,128]{1,0:T(8,128)S(1)} %slice.4), channel_id=1, source_target_pairs={{0,32},{32,0},{1,33},{33,1},{2,34},{34,2},{3,35},{35,3},{4,36},{36... | collective-permute-start | bytes 4718600 | tf_op jit(solution)/shard_map/ppermute | solution.py:384
  45.7 2.2 %collective-permute-start.4 = (bf16[2,128,256]{2,1,0:T(8,128)(2,1)S(1)}, bf16[2,128,256]{2,1,0:T(8,128)(2,1)S(1)}, u32[]{:S(2)}, u32[]{:S(2)}) collective-permute-start(bf16[2,128,256]{2,1,0:T(8,128)(2,1)S(1)} %get-tuple-element.75), channel_id=1, source_target_pairs={{0,1},{1,2},{2,3},{3,4},{4,5},{5,6},{6,7},{8,9},{9,10},{10,11},{11... | collective-permute-start | bytes 393224 | tf_op jit(solution)/shard_map/ppermute | solution.py:390
  47.9 1.3 collective-permute-start.5
  49.2 0.7 shard_map.79
  49.9 0.7 collective-permute-done.4.refs_1_
  50.6 3.8 %collective-permute-done.5.refs_2_ = bf16[2,128,256]{2,1,0:T(8,128)(2,1)S(1)} collective-permute-done((bf16[2,128,256]{2,1,0:T(8,128)(2,1)S(1)}, bf16[2,128,256]{2,1,0:T(8,128)(2,1)S(1)}, u32[]{:S(2)}, u32[]{:S(2)}) %collective-permute-start.5) | collective-permute-done | bytes 131104 | tf_op jit(solution)/shard_map/ppermute | solution.py:390
  54.4 2.4 %collective-permute-start.6 = (bf16[768,128]{1,0:T(8,128)(2,1)S(1)}, bf16[768,128]{1,0:T(8,128)(2,1)S(1)}, u32[]{:S(2)}, u32[]{:S(2)}) collective-permute-start(bf16[768,128]{1,0:T(8,128)(2,1)S(1)} %get-tuple-element.78), channel_id=1, source_target_pairs={{0,8},{8,16},{16,24},{24,0},{1,9},{9,17},{17,25},{25,1},{2,10},{10... | collective-permute-start | bytes 589832 | tf_op jit(solution)/shard_map/ppermute | solution.py:396
  56.8 2.8 %collective-permute-start.7 = (bf16[768,128]{1,0:T(8,128)(2,1)S(1)}, bf16[768,128]{1,0:T(8,128)(2,1)S(1)}, u32[]{:S(2)}, u32[]{:S(2)}) collective-permute-start(bf16[768,128]{1,0:T(8,128)(2,1)S(1)} %get-tuple-element.79), channel_id=1, source_target_pairs={{0,16},{8,24},{16,0},{24,8},{1,17},{9,25},{17,1},{25,9},{2,18},{10... | collective-permute-start | bytes 589832 | tf_op jit(solution)/shard_map/ppermute | solution.py:396
  59.6 0.8 collective-permute-start.8
  60.4 5.2 %shard_map.80 = (f32[2,1024,256]{2,1,0:T(8,128)S(1)}, f32[1,8,128]{2,1,0:T(8,128)S(1)}) custom-call(bf16[2,1024,256]{2,1,0:T(8,128)(2,1)S(1)} %get-tuple-element.66.pg_ref.refs_0_, bf16[2,128,256]{2,1,0:T(8,128)(2,1)S(1)} %collective-permute-done.4.refs_1_, bf16[2,128,256]{2,1,0:T(8,128)(2,1)S(1)} %collective-permute-done.5.refs_2_, ...), custom_call_target="tpu_custom_call" | custom-call | flops 2415919104 | bytes 5672960 | tf_op jit(solution)/shard_map/pallas_call | solution.py:31
  65.6 1.3 copy-done.3
  67.5 0.7 shard_map.81
  68.2 4.9 %collective-permute-start.15 = (bf16[2,1024,256]{2,1,0:T(8,128)(2,1)S(1)}, bf16[2,1024,256]{2,1,0:T(8,128)(2,1)}, u32[]{:S(2)}, u32[]{:S(2)}) collective-permute-start(bf16[2,1024,256]{2,1,0:T(8,128)(2,1)S(1)} %get-tuple-element.107.hid_ref), channel_id=1, source_target_pairs={{0,8},{8,16},{16,24},{1,9},{9,17},{17,25},{2,10},{10,18},{18,26},{... | collective-permute-start | bytes 3145736 | tf_op jit(solution)/shard_map/ppermute | solution.py:390
  73.1 1.3 collective-permute-start.9
  74.4 2.6 %collective-permute-start.10 = (f32[192,128]{1,0:T(8,128)S(1)}, f32[192,128]{1,0:T(8,128)S(1)}, u32[]{:S(2)}, u32[]{:S(2)}) collective-permute-start(f32[192,128]{1,0:T(8,128)S(1)} %get-tuple-element.94), channel_id=1, source_target_pairs={{0,128},{64,192},{128,0},{192,64},{1,129},{65,193},{129,1},{193,65... | collective-permute-start | bytes 294920 | tf_op jit(solution)/shard_map/ppermute | solution.py:396
  77.0 1.1 collective-permute-start.11
  78.1 2.3 %collective-permute-done.10.b_ref = f32[192,128]{1,0:T(8,128)S(1)} collective-permute-done((f32[192,128]{1,0:T(8,128)S(1)}, f32[192,128]{1,0:T(8,128)S(1)}, u32[]{:S(2)}, u32[]{:S(2)}) %collective-permute-start.10) | collective-permute-done | bytes 98336 | tf_op jit(solution)/shard_map/ppermute | solution.py:396
  80.5 1.3 collective-permute-done.11.c_ref
  81.8 10.6 %all_to_all.15.u_ref = f32[8,32,128]{2,1,0:T(8,128)S(1)} all-to-all(f32[8,32,128]{2,1,0:T(8,128)S(1)} %shard_map.82), channel_id=1, replica_groups=mesh['y'=4,'core'=2,'tm'=4,'height'=8] {'height'}, dimensions={0} | all-to-all | bytes 262144 | tf_op jit(solution)/shard_map/all_to_all | solution.py:477
  92.4 0.6 copy-done.9
  93.0 4.0 %all-to-all-start.2 = ((bf16[8,24,128]{2,1,0:T(8,128)(2,1)}), bf16[8,24,128]{2,1,0:T(8,128)(2,1)}, u32[]{:S(2)}, u32[]{:S(2)}) async-start(bf16[8,24,128]{2,1,0:T(8,128)(2,1)} %copy-done.9), calls=%async_computation.2 | async-start | bytes 98304 | tf_op jit(solution)/shard_map/all_to_all | solution.py:479
  97.0 1.6 %copy-done.4 = f32[2,1024,256]{2,1,0:T(8,128)S(1)} copy-done((f32[2,1024,256]{2,1,0:T(8,128)S(1)}, f32[2,1024,256]{2,1,0:T(8,128)}, u32[]{:S(2)}) %copy-start.4) | copy-done | bytes 2097176
  98.6 0.8 copy-done.8
  99.3 1.9 %shard_map.84 = bf16[2,1024,256]{2,1,0:T(8,128)(2,1)} custom-call(bf16[2,1024,256]{2,1,0:T(8,128)(2,1)S(1)} %bitcast.15, bf16[2,1024,256]{2,1,0:T(8,128)(2,1)S(1)} %bitcast.20, f32[2,1024,256]{2,1,0:T(8,128)S(1)} %copy-done.4, f32[8,8,128]{2,1,0:T(8,128)S(1)} %copy-done.8, f32[1,8,128]{2,1,0:T(8,128)S(1)} %get-tuple-element.102.refs_4_), custom_call_target="tpu_custom_call" | custom-call | flops 2097152 | bytes 5279744 | tf_op jit(solution)/shard_map/pallas_call | solution.py:31
  101.3 2.8 %all-to-all-done.2 = bf16[8,24,128]{2,1,0:T(8,128)(2,1)} async-done(((bf16[8,24,128]{2,1,0:T(8,128)(2,1)}), bf16[8,24,128]{2,1,0:T(8,128)(2,1)}, u32[]{:S(2)}, u32[]{:S(2)}) %all-to-all-start.2) | async-done | bytes 49184 | tf_op jit(solution)/shard_map/all_to_all | solution.py:479
  104.0 2.3 %collective-permute-start.14 = (bf16[192,128]{1,0:T(8,128)(2,1)}, bf16[192,128]{1,0:T(8,128)(2,1)S(1)}, u32[]{:S(2)}, u32[]{:S(2)}) collective-permute-start(bf16[192,128]{1,0:T(8,128)(2,1)} %bitcast.8), channel_id=1, source_target_pairs={{0,192},{64,0},{128,64},{192,128},{1,193},{65,1},{129,65},{193,129... | collective-permute-start | bytes 147464 | tf_op jit(solution)/shard_map/ppermute | solution.py:396
  106.9 0.9 collective-permute-done.14
  107.8 3.3 %collective-permute-done.13 = bf16[192,128]{1,0:T(8,128)(2,1)S(1)} collective-permute-done((bf16[192,128]{1,0:T(8,128)(2,1)}, bf16[192,128]{1,0:T(8,128)(2,1)S(1)}, u32[]{:S(2)}, u32[]{:S(2)}) %collective-permute-start.13) | collective-permute-done | bytes 49184 | tf_op jit(solution)/shard_map/ppermute | solution.py:396
  111.2 0.8 pad_maximum_fusion.1
  112.1 1.0 collective-permute-start.17
  113.1 0.8 collective-permute-start.16
  113.9 4.4 %shard_map.85 = bf16[2,1024,256]{2,1,0:T(8,128)(2,1)} custom-call(bf16[2,1024,256]{2,1,0:T(8,128)(2,1)S(1)} %bitcast.16, bf16[2,1024,256]{2,1,0:T(8,128)(2,1)S(1)} %get-tuple-element.107.hid_ref, bf16[2,1024,256]{2,1,0:T(8,128)(2,1)} %collective-permute-done.15.prev_ref, bf16[3,256,256]{2,1,0:T(8,128)(2,1)S(1)} %copy-done.5), custom_call_target="tpu_custom_call" | custom-call | flops 805306368 | bytes 4587520 | tf_op jit(solution)/shard_map/pallas_call | solution.py:31
  118.3 2.0 %collective-permute-done.16 = bf16[768,128]{1,0:T(8,128)(2,1)S(1)} collective-permute-done((bf16[768,128]{1,0:T(8,128)(2,1)S(1)}, bf16[768,128]{1,0:T(8,128)(2,1)S(1)}, u32[]{:S(2)}, u32[]{:S(2)}) %collective-permute-start.16) | collective-permute-done | bytes 196640 | tf_op jit(solution)/shard_map/ppermute | solution.py:396
  120.4 7.1 %collective-permute-start.19 = (bf16[3072,128]{1,0:T(8,128)(2,1)S(1)}, bf16[3072,128]{1,0:T(8,128)(2,1)S(1)}, u32[]{:S(2)}, u32[]{:S(2)}) collective-permute-start(bf16[3072,128]{1,0:T(8,128)(2,1)S(1)} %pad_maximum_fusion.refs_1_), channel_id=1, source_target_pairs={{0,32},{32,0},{1,33},{33,1},{2,34},{34,2},{3,35},{35,3},{4,36},{36... | collective-permute-start | bytes 2359304 | tf_op jit(solution)/shard_map/ppermute | solution.py:384
  127.4 1.9 %collective-permute-done.19.refs_2_ = bf16[3072,128]{1,0:T(8,128)(2,1)S(1)} collective-permute-done((bf16[3072,128]{1,0:T(8,128)(2,1)S(1)}, bf16[3072,128]{1,0:T(8,128)(2,1)S(1)}, u32[]{:S(2)}, u32[]{:S(2)}) %collective-permute-start.19) | collective-permute-done | bytes 786464 | tf_op jit(solution)/shard_map/ppermute | solution.py:384
  129.4 4.3 %shard_map.86 = (f32[9,256,256]{2,1,0:T(8,128)}, f32[3,256,256]{2,1,0:T(8,128)}) custom-call(s32[5]{0:T(128)S(1)} %stack.23.refs_0_.info, bf16[3072,128]{1,0:T(8,128)(2,1)S(1)} %pad_maximum_fusion.refs_1_, bf16[3072,128]{1,0:T(8,128)(2,1)S(1)} %collective-permute-done.19.refs_2_), custom_call_target="tpu_custom_call" | custom-call | flops 2097152 | bytes 4718612 | tf_op jit(solution)/shard_map/pallas_call | solution.py:31
  (39 shorter events, 1.8 us)
Async XLA Ops:
  0.6 35.7 %collective-permute-start.2 = (bf16[2,1024,256]{2,1,0:T(8,128)(2,1)}, bf16[2,1024,256]{2,1,0:T(8,128)(2,1)S(1)}, u32[]{:S(2)}, u32[]{:S(2)}) collective-permute-start(bf16[2,1024,256]{2,1,0:T(8,128)(2,1)} %bitcast.17), channel_id=1, source_target_pairs={{8,0},{16,8},{24,16},{9,1},{17,9},{25,17},{10,2},{18,10},{26,18},{... | collective-permute-start | bytes 3145736 | tf_op jit(solution)/shard_map/ppermute | solution.py:390
  1.9 1.2 copy-start
  4.1 22.4 %collective-permute-start = (bf16[2,128,256]{2,1,0:T(8,128)(2,1)S(1)}, bf16[2,128,256]{2,1,0:T(8,128)(2,1)S(1)}, u32[]{:S(2)}, u32[]{:S(2)}) collective-permute-start(bf16[2,128,256]{2,1,0:T(8,128)(2,1)S(1)} %get-tuple-element.61), channel_id=1, source_target_pairs={{0,1},{1,2},{2,3},{3,4},{4,5},{5,6},{6,7},{8,9},{9,10},{10,11},{11... | collective-permute-start | bytes 393224 | tf_op jit(solution)/shard_map/ppermute | solution.py:390
  8.5 18.1 %collective-permute-start.1 = (bf16[2,128,256]{2,1,0:T(8,128)(2,1)S(1)}, bf16[2,128,256]{2,1,0:T(8,128)(2,1)S(1)}, u32[]{:S(2)}, u32[]{:S(2)}) collective-permute-start(bf16[2,128,256]{2,1,0:T(8,128)(2,1)S(1)} %get-tuple-element.62), channel_id=1, source_target_pairs={{1,0},{2,1},{3,2},{4,3},{5,4},{6,5},{7,6},{9,8},{10,9},{11,10},{12... | collective-permute-start | bytes 393224 | tf_op jit(solution)/shard_map/ppermute | solution.py:390
  9.8 16.8 %all-to-all-start = ((f32[8,8,128]{2,1,0:T(8,128)}), f32[8,8,128]{2,1,0:T(8,128)S(1)}, u32[]{:S(2)}, u32[]{:S(2)}) async-start(f32[8,8,128]{2,1,0:T(8,128)} %get-tuple-element.63), calls=%async_computation | async-start | bytes 65536 | tf_op jit(solution)/shard_map/all_to_all | solution.py:430
  26.6 0.6 copy-start.6
  26.6 0.7 copy-start.11
  27.2 0.7 copy-start.12
  27.9 8.5 %copy-start.2 = (bf16[1,2,8,128,256]{4,3,2,1,0:T(8,128)(2,1)S(1)}, bf16[1,2,8,128,256]{4,3,2,1,0:T(8,128)(2,1)}, u32[]{:S(2)}) copy-start(bf16[1,2,8,128,256]{4,3,2,1,0:T(8,128)(2,1)} %param.5) | copy-start | bytes 3145732
  27.9 8.5 %copy-start.5 = (bf16[3,256,256]{2,1,0:T(8,128)(2,1)S(1)}, bf16[3,256,256]{2,1,0:T(8,128)(2,1)}, u32[]{:S(2)}) copy-start(bf16[3,256,256]{2,1,0:T(8,128)(2,1)} %w_ref.3) | copy-start | bytes 1179652
  43.0 17.4 %copy-start.1 = (bf16[1,2,8,128,256]{4,3,2,1,0:T(8,128)(2,1)S(1)}, bf16[1,2,8,128,256]{4,3,2,1,0:T(8,128)(2,1)}, u32[]{:S(2)}) copy-start(bf16[1,2,8,128,256]{4,3,2,1,0:T(8,128)(2,1)} %param.4) | copy-start | bytes 3145732
  43.0 17.4 %copy-start.7 = (f32[8,8,128]{2,1,0:T(8,128)S(1)}, f32[8,8,128]{2,1,0:T(8,128)}, u32[]{:S(2)}) copy-start(f32[8,8,128]{2,1,0:T(8,128)} %copy-done.6) | copy-start | bytes 98308
  43.0 17.4 %copy-start.10 = (bf16[3,3,256,256]{3,2,1,0:T(8,128)(2,1)S(1)}, bf16[3,3,256,256]{3,2,1,0:T(8,128)(2,1)}, u32[]{:S(2)}) copy-start(bf16[3,3,256,256]{3,2,1,0:T(8,128)(2,1)} %refs_3_.1) | copy-start | bytes 3538948
  43.0 6.2 %collective-permute-start.3 = (f32[3072,128]{1,0:T(8,128)S(1)}, f32[3072,128]{1,0:T(8,128)S(1)}, u32[]{:S(2)}, u32[]{:S(2)}) collective-permute-start(f32[3072,128]{1,0:T(8,128)S(1)} %slice.4), channel_id=1, source_target_pairs={{0,32},{32,0},{1,33},{33,1},{2,34},{34,2},{3,35},{35,3},{4,36},{36... | collective-permute-start | bytes 4718600 | tf_op jit(solution)/shard_map/ppermute | solution.py:384
  45.7 4.9 %collective-permute-start.4 = (bf16[2,128,256]{2,1,0:T(8,128)(2,1)S(1)}, bf16[2,128,256]{2,1,0:T(8,128)(2,1)S(1)}, u32[]{:S(2)}, u32[]{:S(2)}) collective-permute-start(bf16[2,128,256]{2,1,0:T(8,128)(2,1)S(1)} %get-tuple-element.75), channel_id=1, source_target_pairs={{0,1},{1,2},{2,3},{3,4},{4,5},{5,6},{6,7},{8,9},{9,10},{10,11},{11... | collective-permute-start | bytes 393224 | tf_op jit(solution)/shard_map/ppermute | solution.py:390
  47.9 6.5 %collective-permute-start.5 = (bf16[2,128,256]{2,1,0:T(8,128)(2,1)S(1)}, bf16[2,128,256]{2,1,0:T(8,128)(2,1)S(1)}, u32[]{:S(2)}, u32[]{:S(2)}) collective-permute-start(bf16[2,128,256]{2,1,0:T(8,128)(2,1)S(1)} %get-tuple-element.76), channel_id=1, source_target_pairs={{1,0},{2,1},{3,2},{4,3},{5,4},{6,5},{7,6},{9,8},{10,9},{11,10},{12... | collective-permute-start | bytes 393224 | tf_op jit(solution)/shard_map/ppermute | solution.py:390
  54.4 12.5 %collective-permute-start.6 = (bf16[768,128]{1,0:T(8,128)(2,1)S(1)}, bf16[768,128]{1,0:T(8,128)(2,1)S(1)}, u32[]{:S(2)}, u32[]{:S(2)}) collective-permute-start(bf16[768,128]{1,0:T(8,128)(2,1)S(1)} %get-tuple-element.78), channel_id=1, source_target_pairs={{0,8},{8,16},{16,24},{24,0},{1,9},{9,17},{17,25},{25,1},{2,10},{10... | collective-permute-start | bytes 589832 | tf_op jit(solution)/shard_map/ppermute | solution.py:396
  56.8 10.7 %collective-permute-start.7 = (bf16[768,128]{1,0:T(8,128)(2,1)S(1)}, bf16[768,128]{1,0:T(8,128)(2,1)S(1)}, u32[]{:S(2)}, u32[]{:S(2)}) collective-permute-start(bf16[768,128]{1,0:T(8,128)(2,1)S(1)} %get-tuple-element.79), channel_id=1, source_target_pairs={{0,16},{8,24},{16,0},{24,8},{1,17},{9,25},{17,1},{25,9},{2,18},{10... | collective-permute-start | bytes 589832 | tf_op jit(solution)/shard_map/ppermute | solution.py:396
  59.6 7.9 %collective-permute-start.8 = (bf16[768,128]{1,0:T(8,128)(2,1)S(1)}, bf16[768,128]{1,0:T(8,128)(2,1)S(1)}, u32[]{:S(2)}, u32[]{:S(2)}) collective-permute-start(bf16[768,128]{1,0:T(8,128)(2,1)S(1)} %get-tuple-element.80), channel_id=1, source_target_pairs={{0,24},{8,0},{16,8},{24,16},{1,25},{9,1},{17,9},{25,17},{2,26},{10... | collective-permute-start | bytes 589832 | tf_op jit(solution)/shard_map/ppermute | solution.py:396
  65.6 1.3 copy-start.3
  68.2 43.8 %collective-permute-start.15 = (bf16[2,1024,256]{2,1,0:T(8,128)(2,1)S(1)}, bf16[2,1024,256]{2,1,0:T(8,128)(2,1)}, u32[]{:S(2)}, u32[]{:S(2)}) collective-permute-start(bf16[2,1024,256]{2,1,0:T(8,128)(2,1)S(1)} %get-tuple-element.107.hid_ref), channel_id=1, source_target_pairs={{0,8},{8,16},{16,24},{1,9},{9,17},{17,25},{2,10},{10,18},{18,26},{... | collective-permute-start | bytes 3145736 | tf_op jit(solution)/shard_map/ppermute | solution.py:390
  73.1 5.0 %collective-permute-start.9 = (f32[192,128]{1,0:T(8,128)S(1)}, f32[192,128]{1,0:T(8,128)S(1)}, u32[]{:S(2)}, u32[]{:S(2)}) collective-permute-start(f32[192,128]{1,0:T(8,128)S(1)} %get-tuple-element.93), channel_id=1, source_target_pairs={{0,64},{64,128},{128,192},{192,0},{1,65},{65,129},{129,193},{193,1... | collective-permute-start | bytes 294920 | tf_op jit(solution)/shard_map/ppermute | solution.py:396
  74.4 6.0 %collective-permute-start.10 = (f32[192,128]{1,0:T(8,128)S(1)}, f32[192,128]{1,0:T(8,128)S(1)}, u32[]{:S(2)}, u32[]{:S(2)}) collective-permute-start(f32[192,128]{1,0:T(8,128)S(1)} %get-tuple-element.94), channel_id=1, source_target_pairs={{0,128},{64,192},{128,0},{192,64},{1,129},{65,193},{129,1},{193,65... | collective-permute-start | bytes 294920 | tf_op jit(solution)/shard_map/ppermute | solution.py:396
  77.0 4.7 %collective-permute-start.11 = (f32[192,128]{1,0:T(8,128)S(1)}, f32[192,128]{1,0:T(8,128)S(1)}, u32[]{:S(2)}, u32[]{:S(2)}) collective-permute-start(f32[192,128]{1,0:T(8,128)S(1)} %get-tuple-element.95), channel_id=1, source_target_pairs={{0,192},{64,0},{128,64},{192,128},{1,193},{65,1},{129,65},{193,129... | collective-permute-start | bytes 294920 | tf_op jit(solution)/shard_map/ppermute | solution.py:396
  92.4 0.6 copy-start.9
  93.0 11.0 %all-to-all-start.2 = ((bf16[8,24,128]{2,1,0:T(8,128)(2,1)}), bf16[8,24,128]{2,1,0:T(8,128)(2,1)}, u32[]{:S(2)}, u32[]{:S(2)}) async-start(bf16[8,24,128]{2,1,0:T(8,128)(2,1)} %copy-done.9), calls=%async_computation.2 | async-start | bytes 98304 | tf_op jit(solution)/shard_map/all_to_all | solution.py:479
  97.0 1.6 %copy-start.4 = (f32[2,1024,256]{2,1,0:T(8,128)S(1)}, f32[2,1024,256]{2,1,0:T(8,128)}, u32[]{:S(2)}) copy-start(f32[2,1024,256]{2,1,0:T(8,128)} %copy-done.3) | copy-start | bytes 6291460
  98.6 0.8 copy-start.8
  104.0 3.8 %collective-permute-start.14 = (bf16[192,128]{1,0:T(8,128)(2,1)}, bf16[192,128]{1,0:T(8,128)(2,1)S(1)}, u32[]{:S(2)}, u32[]{:S(2)}) collective-permute-start(bf16[192,128]{1,0:T(8,128)(2,1)} %bitcast.8), channel_id=1, source_target_pairs={{0,192},{64,0},{128,64},{192,128},{1,193},{65,1},{129,65},{193,129... | collective-permute-start | bytes 147464 | tf_op jit(solution)/shard_map/ppermute | solution.py:396
  106.3 4.8 %collective-permute-start.13 = (bf16[192,128]{1,0:T(8,128)(2,1)}, bf16[192,128]{1,0:T(8,128)(2,1)S(1)}, u32[]{:S(2)}, u32[]{:S(2)}) collective-permute-start(bf16[192,128]{1,0:T(8,128)(2,1)} %bitcast.8), channel_id=1, source_target_pairs={{0,128},{64,192},{128,0},{192,64},{1,129},{65,193},{129,1},{193,65... | collective-permute-start | bytes 147464 | tf_op jit(solution)/shard_map/ppermute | solution.py:396
  106.3 4.9 %collective-permute-start.12 = (bf16[192,128]{1,0:T(8,128)(2,1)}, bf16[192,128]{1,0:T(8,128)(2,1)S(1)}, u32[]{:S(2)}, u32[]{:S(2)}) collective-permute-start(bf16[192,128]{1,0:T(8,128)(2,1)} %bitcast.8), channel_id=1, source_target_pairs={{0,64},{64,128},{128,192},{192,0},{1,65},{65,129},{129,193},{193,1... | collective-permute-start | bytes 147464 | tf_op jit(solution)/shard_map/ppermute | solution.py:396
  112.0 6.2 %collective-permute-start.18 = (bf16[768,128]{1,0:T(8,128)(2,1)S(1)}, bf16[768,128]{1,0:T(8,128)(2,1)S(1)}, u32[]{:S(2)}, u32[]{:S(2)}) collective-permute-start(bf16[768,128]{1,0:T(8,128)(2,1)S(1)} %pad_maximum_fusion.1), channel_id=1, source_target_pairs={{0,24},{8,0},{16,8},{24,16},{1,25},{9,1},{17,9},{25,17},{2,26},{10... | collective-permute-start | bytes 589832 | tf_op jit(solution)/shard_map/ppermute | solution.py:396
  112.1 6.2 %collective-permute-start.17 = (bf16[768,128]{1,0:T(8,128)(2,1)S(1)}, bf16[768,128]{1,0:T(8,128)(2,1)S(1)}, u32[]{:S(2)}, u32[]{:S(2)}) collective-permute-start(bf16[768,128]{1,0:T(8,128)(2,1)S(1)} %pad_maximum_fusion.1), channel_id=1, source_target_pairs={{0,16},{8,24},{16,0},{24,8},{1,17},{9,25},{17,1},{25,9},{2,18},{10... | collective-permute-start | bytes 589832 | tf_op jit(solution)/shard_map/ppermute | solution.py:396
  113.1 7.2 %collective-permute-start.16 = (bf16[768,128]{1,0:T(8,128)(2,1)S(1)}, bf16[768,128]{1,0:T(8,128)(2,1)S(1)}, u32[]{:S(2)}, u32[]{:S(2)}) collective-permute-start(bf16[768,128]{1,0:T(8,128)(2,1)S(1)} %pad_maximum_fusion.1), channel_id=1, source_target_pairs={{0,8},{8,16},{16,24},{24,0},{1,9},{9,17},{17,25},{25,1},{2,10},{10... | collective-permute-start | bytes 589832 | tf_op jit(solution)/shard_map/ppermute | solution.py:396
  120.4 9.0 %collective-permute-start.19 = (bf16[3072,128]{1,0:T(8,128)(2,1)S(1)}, bf16[3072,128]{1,0:T(8,128)(2,1)S(1)}, u32[]{:S(2)}, u32[]{:S(2)}) collective-permute-start(bf16[3072,128]{1,0:T(8,128)(2,1)S(1)} %pad_maximum_fusion.refs_1_), channel_id=1, source_target_pairs={{0,32},{32,0},{1,33},{33,1},{2,34},{34,2},{3,35},{35,3},{4,36},{36... | collective-permute-start | bytes 2359304 | tf_op jit(solution)/shard_map/ppermute | solution.py:384

commit v5 on v4

--- a/solution.py
+++ b/solution.py
@@ -25,14 +25,14 @@
 TN = (((0,), (0,)), ((), ()))
 
 
-def call(kernel, outs, args, flops, scratch=(), smem=0, limit=16, loose=()):
+def call(kernel, outs, args, flops, scratch=(), smem=0, limit=16, loose=(), outside=False):
     nbytes = sum(a.size * a.dtype.itemsize for a in (*args, *outs))
     specs = [SMEM] * smem + [ANY if i in loose else VMEM for i in range(smem, len(args))]
     return pl.pallas_call(
         kernel,
         out_shape=tuple(outs),
         in_specs=specs,
-        out_specs=tuple(VMEM for _ in outs),
+        out_specs=tuple(ANY if outside else VMEM for _ in outs),
         scratch_shapes=list(scratch),
         compiler_params=pltpu.CompilerParams(vmem_limit_bytes=limit << 20),
         cost_estimate=pl.CostEstimate(flops=flops, bytes_accessed=nbytes, transcendentals=0),
@@ -50,7 +50,7 @@
 
 
 def sigmoid(v):
-    return 1.0 / (1.0 + jnp.exp(-v))
+    return 0.5 + 0.5 * jnp.tanh(0.5 * v)
 
 
 def store_stats(o_ref, sums):
@@ -153,25 +153,25 @@
         lax.fori_loop(0, 8, line, 0)
 
         def conv(r, _):
-            at = pl.multiple_of(r * 256, 256)
+            at = pl.multiple_of(r * 512, 512)
             v = None
             for i in range(3):
-                lhs = act_ref[f, pl.ds(pl.multiple_of(at + i * 128, 128), 256), :]
+                lhs = act_ref[f, pl.ds(pl.multiple_of(at + i * 128, 128), 512), :]
                 part = dot(lhs, w_ref[i])
                 v = part if v is None else v + part
             s = sigmoid(v)
-            hid_ref[f, pl.ds(at, 256), :] = (v * s).astype(BF16)
-            slope_ref[f, pl.ds(at, 256), :] = s * (1.0 + v * (1.0 - s))
-            return 0
-
-        lax.fori_loop(0, 4, conv, 0)
+            hid_ref[f, pl.ds(at, 512), :] = (v * s).astype(BF16)
+            slope_ref[f, pl.ds(at, 512), :] = s * (1.0 + v * (1.0 - s))
+            return 0
+
+        lax.fori_loop(0, 2, conv, 0)
 
 
 def pregrad_kernel(cot_ref, later_ref, slope_ref, w_ref, pg_ref, top_ref, bot_ref):
     for f in range(2):
 
         def part(r, _):
-            at = pl.ds(pl.multiple_of(r * 256, 256), 256)
+            at = pl.ds(pl.multiple_of(r * 512, 512), 512)
             v = None
             for k in range(3):
                 g = f + 2 - k
@@ -181,7 +181,7 @@
             pg_ref[f, at, :] = (v * slope_ref[f, at, :]).astype(BF16)
             return 0
 
-        lax.fori_loop(0, 4, part, 0)
+        lax.fori_loop(0, 2, part, 0)
         top_ref[f] = pg_ref[f, 0:128, :]
         bot_ref[f] = pg_ref[f, 896:1024, :]
 
@@ -243,21 +243,21 @@
         lax.fori_loop(0, 8, line, 0)
 
         def conv(r, carry):
-            at = pl.multiple_of(r * 256, 256)
+            at = pl.multiple_of(r * 512, 512)
             v = None
             for i in range(3):
-                rows = pl.ds(pl.multiple_of(at + (2 - i) * 128, 128), 256)
+                rows = pl.ds(pl.multiple_of(at + (2 - i) * 128, 128), 512)
                 for j, ref in enumerate((a_ref, b_ref, c_ref)):
                     p = dot(ref[f, rows, :], w_ref[i, j], NT)
                     v = p if v is None else v + p
-            n = (x_ref[f, pl.ds(at, 256), :].astype(F32) - mean) * inv
+            n = (x_ref[f, pl.ds(at, 512), :].astype(F32) - mean) * inv
             s = sigmoid(n)
             ng = v * (s * (1.0 + n * (1.0 - s)))
-            ng_ref[f, pl.ds(at, 256), :] = ng
+            ng_ref[f, pl.ds(at, 512), :] = ng
             return carry[0] + fold(ng), carry[1] + fold(ng * n)
 
         zero = jnp.zeros((8, 256), F32)
-        sums.append(lax.fori_loop(0, 4, conv, (zero, zero)))
+        sums.append(lax.fori_loop(0, 2, conv, (zero, zero)))
     store_stats(o_ref, sums)
 
 
@@ -282,7 +282,7 @@
     for f in range(2):
 
         def part(r, _):
-            at = pl.ds(pl.multiple_of(r * 256, 256), 256)
+            at = pl.ds(pl.multiple_of(r * 512, 512), 512)
             v = None
             for k in range(3):
                 g = f - 2 + k
@@ -292,7 +292,7 @@
             o_ref[f, at, :] = (x_ref[f, at, :].astype(F32) + v).astype(BF16)
             return 0
 
-        lax.fori_loop(0, 4, part, 0)
+        lax.fori_loop(0, 2, part, 0)
 
 
 def coded(v):
@@ -336,44 +336,51 @@
         lax.fori_loop(0, 3, part, 0)
 
 
-def y_kernel(own_ref, a_ref, b_ref, c_ref, gst_ref, o_ref):
+def y_kernel(own_ref, a_ref, b_ref, c_ref, o_ref):
     for peer in range(8):
         rows = slice(peer * 24, peer * 24 + 24)
-        o_ref[peer, 0:24, :] = own_ref[rows, :] + a_ref[rows, :] + b_ref[rows, :] + c_ref[rows, :]
-        o_ref[peer, 24:32, :] = gst_ref[0]
-
-
-def z_kernel(u_ref, o_ref, gst_ref):
+        o_ref[peer] = own_ref[rows, :] + a_ref[rows, :] + b_ref[rows, :] + c_ref[rows, :]
+
+
+def z_kernel(u_ref, gst_ref, o_ref):
     total = u_ref[0]
     for peer in range(1, 8):
         total = total + u_ref[peer]
-    gst_ref[0] = total[24:32]
-    mine = coded(total[:24])
     for peer in range(8):
-        o_ref[peer] = mine
-
-
-def clip_kernel(clip_level, info, own_ref, other_ref, s_ref, t_ref):
+        o_ref[peer, 0:24, :] = total
+        o_ref[peer, 24:32, :] = gst_ref[0]
+
+
+def code_kernel(u_ref, o_ref, gst_ref):
+    for peer in range(0, 8, 2):
+        pair = jnp.concatenate([u_ref[peer, 0:24, :], u_ref[peer + 1, 0:24, :]], axis=0)
+        o_ref[peer * 24 : peer * 24 + 48, :] = coded(pair)
+    total = u_ref[0, 24:32, :]
+    for peer in range(1, 8):
+        total = total + u_ref[peer, 24:32, :]
+    gst_ref[0] = total
+
+
+def clip_kernel(clip_level, info, own_ref, other_ref, s_ref, t_ref, w_ref, sems):
     acc = jnp.zeros((8, 128), F32)
     for tap in range(12):
-        ref, k = (s_ref, tap) if tap < 9 else (t_ref, tap - 9)
         mine = info[0] == tap // 6
         for lh in range(2):
             for part in range(4):
                 at = pl.ds(slab_rows(info, (tap % 6) * 2 + lh, part), 64)
                 v = decoded(jnp.where(mine, own_ref[at, :], other_ref[at, :]))
-                ref[k, part * 64 : part * 64 + 64, lh * 128 : lh * 128 + 128] = v
+                w_ref[tap, part * 64 : part * 64 + 64, lh * 128 : lh * 128 + 128] = v
                 acc = acc + fold(v * v)
     total = jnp.sum(jnp.sum(acc, axis=0, keepdims=True), axis=1, keepdims=True)
     scale = clip_level / jnp.maximum(jnp.sqrt(total), clip_level)
-
-    def finish(k, _):
-        s_ref[k] = s_ref[k] * scale
-        return 0
-
-    lax.fori_loop(0, 9, finish, 0)
-    for k in range(3):
-        t_ref[k] = t_ref[k] * scale
+    copies = []
+    for tap in range(12):
+        w_ref[tap] = w_ref[tap] * scale
+        target = s_ref.at[tap] if tap < 9 else t_ref.at[tap - 9]
+        copies.append(pltpu.make_async_copy(w_ref.at[tap], target, sems.at[tap]))
+        copies[-1].start()
+    for c in copies:
+        c.wait()
 
 
 def in_hbm(x):
@@ -458,30 +465,31 @@
     own, *sent = call(
         pair_kernel, [out((768, 128), F32), quarter, quarter, quarter], [g, got], 1 << 21
     )
-    own, sent, gup, gdn = tied((own, sent, gup, gdn))
-    got = shifts(sent, TM)
+    got = tied(shifts(sent, TM))
+    part = out((192, 128), F32)
+    own, *sent = call(x_kernel, [part] * 4, [own, *got], 1 << 21)
+    got = tied(shifts(sent, "y"))
+    (pieces,) = call(y_kernel, [out((8, 24, 128), F32)], [own, *got], 1 << 20)
+    pieces, gup, gdn, hid_sent = tied((pieces, gup, gdn, hid))
+    pieces = lax.all_to_all(pieces, HEIGHT, 0, 0, tiled=True)
+    prev = moved(hid_sent, TM, 1)
     ng, gst = call(
         lambda *refs: backward_kernel(members, *refs),
         [out(flat, F32), out((1, 8, 128), F32)],
-        [pg, gup, gdn, w9, x, st],
+        [in_hbm(a) for a in (pg, gup, gdn, w9, x, st)],
         9 * gflop,
         scratch=[pltpu.VMEM((2, 1280, 256), BF16)] * 3,
     )
-    got, ng, gst = tied((got, ng, gst))
-    part = out((192, 128), F32)
-    own, *sent = call(x_kernel, [part] * 4, [own, *got], 1 << 21)
-    own, sent, hid_sent = tied((own, sent, hid))
-    got = tied(shifts(sent, "y"))
-    prev = moved(hid_sent, TM, 1)
-    (pieces,) = call(y_kernel, [out((8, 32, 128), F32)], [own, *got, gst], 1 << 20)
-    pieces = lax.all_to_all(pieces, HEIGHT, 0, 0, tiled=True)
-    copies, gst = call(z_kernel, [out((8, 24, 128), BF16), out((1, 8, 128), F32)], [pieces], 1 << 20)
-    mine = lax.all_to_all(copies, HEIGHT, 0, 0, tiled=True).reshape(192, 128)
+    pieces, ng, gst = tied((pieces, in_hbm(ng), gst))
+    (copies,) = call(z_kernel, [out((8, 32, 128), F32)], [pieces, gst], 1 << 20)
+    copies = lax.all_to_all(copies, HEIGHT, 0, 0, tiled=True)
+    mine, gst = call(code_kernel, [out((192, 128), BF16), out((1, 8, 128), F32)], [copies], 1 << 20)
+    mine, prev, gst = tied((mine, prev, gst))
     (input_grad,) = call(
-        lambda *refs: input_grad_kernel(members, *refs), [out(flat, BF16)], [x, cot, ng, st, gst], 1 << 21
-    )
+        lambda *refs: input_grad_kernel(members, *refs), [out(flat, BF16)], [x, cot, in_hbm(ng), in_hbm(st), gst], 1 << 21
+    )
+    mine = gathered(mine, "y")
     mine, input_grad = tied((mine, input_grad))
-    mine, prev = tied((gathered(mine, "y"), prev))
     (block_output,) = call(block_kernel, [out(flat, BF16)], [x, hid, prev, temporal_kernel], 3 * gflop)
     mine = gathered(mine, TM)
     mine, block_output = tied((mine, block_output))
@@ -491,6 +499,8 @@
         [info, mine, swapped(mine, "core")],
         1 << 21,
         smem=1,
+        outside=True,
+        scratch=[pltpu.VMEM((12, 256, 256), F32), pltpu.SemaphoreType.DMA((12,))],
     )
     return (
         block_output.reshape(video_latents.shape),

time: 134 us -> 133 us (level)
  waiting for transfers between devices: 26.6 us -> 22.7 us
  blocking collectives: 10.6 us -> 14.1 us
  Pallas kernels: 33.1 us -> 35 us
  local copies, waits for them, and re-layouts: 7.01 us -> 5.35 us
    ppermute x6, waiting for transfers between devices: 4.54 us -> 0.02 us  [moved(): return lax.ppermute(x, axes, route)]
    all_to_all x1, blocking collectives: 10.6 us -> 14.1 us  [body(): copies = lax.all_to_all(copies, HEIGHT, 0, 0, tiled=True)]
    ppermute x2, waiting for transfers between devices: 1.91 us -> 4.95 us  [swapped(): return lax.ppermute(x, axis, [(0, 1), (1, 0)])]
    all_to_all x1, waiting for transfers between devices: 2.76 us -> 0.01 us  [body(): pieces = lax.all_to_all(pieces, HEIGHT, 0, 0, tiled=True)]
    pallas_call x12 -> x13, Pallas kernels: 33.1 us -> 35 us  [call(): pl.pallas_call(kernel, out_shape=tuple(outs), in_specs=specs, out_specs=t...]
    unnamed x26 -> x22, local copies, waits for them, and re-layouts: 6.83 us -> 5.17 us
    ppermute x6, starting transfers between devices: 15.3 us -> 14 us  [moved(): return lax.ppermute(x, axes, route)]
  transfers between devices with their start and end apart: 22 -> 22, of which waited for: 13 -> 10; matrix products, arithmetic and copies ran while one was open for 1% -> 0% of each run, Pallas kernels for 16% -> 18%
where the time goes in v5:
time: 133 us; the launch traced here: 132 us
  starting transfers between devices  54.1 us (41%)
  Pallas kernels  35 us (26%)
  waiting for transfers between devices  22.7 us (17%)
  blocking collectives  14.1 us (11%)
  local copies, waits for them, and re-layouts  5.35 us (4%)
    pallas_call x13, Pallas kernels, call(): pl.pallas_call(kernel, out_shape=tuple(outs), in_specs=specs, out_specs=t...  35 us
    ppermute x12, starting transfers between devices, shifts(): lax.ppermute(m, axis, [(i, (i + d) % n) for i in range(n)])  16.6 us
    all_to_all x1, blocking collectives, body(): copies = lax.all_to_all(copies, HEIGHT, 0, 0, tiled=True)  14.1 us
    ppermute x6, starting transfers between devices, moved(): return lax.ppermute(x, axes, route)  14 us
    ppermute x12, waiting for transfers between devices, shifts(): lax.ppermute(m, axis, [(i, (i + d) % n) for i in range(n)])  10.9 us
    all_to_all x1, starting transfers between devices, body(): st = lax.all_to_all(st, HEIGHT, 0, 0, tiled=True)  9.85 us
    ppermute x2, starting transfers between devices, swapped(): return lax.ppermute(x, axis, [(0, 1), (1, 0)])  9.54 us
    all_to_all x1, waiting for transfers between devices, body(): st = lax.all_to_all(st, HEIGHT, 0, 0, tiled=True)  6.83 us
  transfers between devices with their start and end apart: 22, of which 10 were waited for; matrix products, arithmetic and copies ran while one was open for 0% of the time, Pallas kernels for 18%

profile of v5, /device:TPU:1, one launch (start us, length us, event | category | flops | bytes accessed | tf_op | source)
XLA Modules:
  0.0 132.3 jit_solution(18261242231320475801)
XLA Ops:
  0.6 1.3 collective-permute-start.2
  1.9 1.2 copy-done
  3.2 1.0 shard_map.75
  4.1 4.4 %collective-permute-start = (bf16[2,128,256]{2,1,0:T(8,128)(2,1)S(1)}, bf16[2,128,256]{2,1,0:T(8,128)(2,1)S(1)}, u32[]{:S(2)}, u32[]{:S(2)}) collective-permute-start(bf16[2,128,256]{2,1,0:T(8,128)(2,1)S(1)} %get-tuple-element.56), channel_id=1, source_target_pairs={{0,1},{1,2},{2,3},{3,4},{4,5},{5,6},{6,7},{8,9},{9,10},{10,11},{11... | collective-permute-start | bytes 393224 | tf_op jit(solution)/shard_map/ppermute | solution.py:397
  8.5 1.3 collective-permute-start.1
  9.8 9.8 %all-to-all-start = ((f32[8,8,128]{2,1,0:T(8,128)}), f32[8,8,128]{2,1,0:T(8,128)S(1)}, u32[]{:S(2)}, u32[]{:S(2)}) async-start(f32[8,8,128]{2,1,0:T(8,128)} %get-tuple-element.58), calls=%async_computation | async-start | bytes 65536 | tf_op jit(solution)/shard_map/all_to_all | solution.py:437
  19.7 6.8 %all-to-all-done.refs_4_.refs_5_.refs_3_ = f32[8,8,128]{2,1,0:T(8,128)S(1)} async-done(((f32[8,8,128]{2,1,0:T(8,128)}), f32[8,8,128]{2,1,0:T(8,128)S(1)}, u32[]{:S(2)}, u32[]{:S(2)}) %all-to-all-start) | async-done | bytes 32800 | tf_op jit(solution)/shard_map/all_to_all | solution.py:437
  26.6 0.6 copy-done.6
  27.2 0.7 copy-done.10
  27.9 7.5 %shard_map.76 = (bf16[2,1280,768]{2,1,0:T(8,128)(2,1)S(1)}, bf16[2,1024,256]{2,1,0:T(8,128)(2,1)S(1)}, f32[2,1024,256]{2,1,0:T(8,128)S(1)}) custom-call(s32[5]{0:T(128)S(1)} %stack.23.refs_0_.info, bf16[2,1024,256]{2,1,0:T(8,128)(2,1)} %bitcast.11, bf16[2,128,256]{2,1,0:T(8,128)(2,1)} %copy-done.9, bf16[2,128,256]{2,1,0:T(8,128)(2,1)} %copy-done.10, ...), custom_call_target="tpu_custom_call" | custom-call | flops 2415919104 | bytes 9601044 | tf_op jit(solution)/shard_map/pallas_call | solution.py:31
  35.5 1.6 %shard_map.77 = (bf16[2,1024,256]{2,1,0:T(8,128)(2,1)S(1)}, bf16[2,128,256]{2,1,0:T(8,128)(2,1)S(1)}, bf16[2,128,256]{2,1,0:T(8,128)(2,1)S(1)}) custom-call(bf16[2,1024,256]{2,1,0:T(8,128)(2,1)S(1)} %bitcast.17, bf16[2,1024,256]{2,1,0:T(8,128)(2,1)S(1)} %collective-permute-done.2.later_ref, f32[2,1024,256]{2,1,0:T(8,128)S(1)} %get-tuple-element.60.slope_ref, ...), custom_call_target="tpu_custom_call" | custom-call | flops 805306368 | bytes 5898240 | tf_op jit(solution)/shard_map/pallas_call | solution.py:31
  37.1 4.0 %shard_map.78.g_ref = f32[6144,128]{1,0:T(8,128)S(1)} custom-call(s32[5]{0:T(128)S(1)} %stack.23.refs_0_.info, bf16[2,1280,768]{2,1,0:T(8,128)(2,1)S(1)} %get-tuple-element.59.act_ref, bf16[2,1024,256]{2,1,0:T(8,128)(2,1)S(1)} %get-tuple-element.61.pg_ref.refs_0_, bf16[2,1024,256]{2,1,0:T(8,128)(2,1)S(1)} %get-tuple-element.90.hid_ref, ...), custom_call_target="tpu_custom_call" | custom-call | flops 3221225472 | bytes 11272212 | tf_op jit(solution)/shard_map/pallas_call | solution.py:31
  41.3 2.7 %collective-permute-start.3 = (f32[3072,128]{1,0:T(8,128)S(1)}, f32[3072,128]{1,0:T(8,128)S(1)}, u32[]{:S(2)}, u32[]{:S(2)}) collective-permute-start(f32[3072,128]{1,0:T(8,128)S(1)} %slice.4), channel_id=1, source_target_pairs={{0,32},{32,0},{1,33},{33,1},{2,34},{34,2},{3,35},{35,3},{4,36},{36... | collective-permute-start | bytes 4718600 | tf_op jit(solution)/shard_map/ppermute | solution.py:391
  44.0 3.0 %collective-permute-done.3.got_ref = f32[3072,128]{1,0:T(8,128)S(1)} collective-permute-done((f32[3072,128]{1,0:T(8,128)S(1)}, f32[3072,128]{1,0:T(8,128)S(1)}, u32[]{:S(2)}, u32[]{:S(2)}) %collective-permute-start.3) | collective-permute-done | bytes 1572896 | tf_op jit(solution)/shard_map/ppermute | solution.py:391
  47.0 0.7 shard_map.79
  47.7 2.4 %collective-permute-start.4 = (bf16[768,128]{1,0:T(8,128)(2,1)S(1)}, bf16[768,128]{1,0:T(8,128)(2,1)S(1)}, u32[]{:S(2)}, u32[]{:S(2)}) collective-permute-start(bf16[768,128]{1,0:T(8,128)(2,1)S(1)} %get-tuple-element.67), channel_id=1, source_target_pairs={{0,8},{8,16},{16,24},{24,0},{1,9},{9,17},{17,25},{25,1},{2,10},{10... | collective-permute-start | bytes 589832 | tf_op jit(solution)/shard_map/ppermute | solution.py:403
  50.2 2.8 %collective-permute-start.5 = (bf16[768,128]{1,0:T(8,128)(2,1)S(1)}, bf16[768,128]{1,0:T(8,128)(2,1)S(1)}, u32[]{:S(2)}, u32[]{:S(2)}) collective-permute-start(bf16[768,128]{1,0:T(8,128)(2,1)S(1)} %get-tuple-element.68), channel_id=1, source_target_pairs={{0,16},{8,24},{16,0},{24,8},{1,17},{9,25},{17,1},{25,9},{2,18},{10... | collective-permute-start | bytes 589832 | tf_op jit(solution)/shard_map/ppermute | solution.py:403
  53.0 0.8 collective-permute-start.6
  53.8 2.2 %collective-permute-start.10 = (bf16[2,128,256]{2,1,0:T(8,128)(2,1)S(1)}, bf16[2,128,256]{2,1,0:T(8,128)(2,1)S(1)}, u32[]{:S(2)}, u32[]{:S(2)}) collective-permute-start(bf16[2,128,256]{2,1,0:T(8,128)(2,1)S(1)} %get-tuple-element.80), channel_id=1, source_target_pairs={{0,1},{1,2},{2,3},{3,4},{4,5},{5,6},{6,7},{8,9},{9,10},{10,11},{11... | collective-permute-start | bytes 393224 | tf_op jit(solution)/shard_map/ppermute | solution.py:397
  55.9 1.3 collective-permute-start.11
  57.3 4.5 %collective-permute-done.5.b_ref = bf16[768,128]{1,0:T(8,128)(2,1)S(1)} collective-permute-done((bf16[768,128]{1,0:T(8,128)(2,1)S(1)}, bf16[768,128]{1,0:T(8,128)(2,1)S(1)}, u32[]{:S(2)}, u32[]{:S(2)}) %collective-permute-start.5) | collective-permute-done | bytes 196640 | tf_op jit(solution)/shard_map/ppermute | solution.py:403
  61.8 0.7 shard_map.80
  62.5 1.4 %collective-permute-start.7 = (f32[192,128]{1,0:T(8,128)S(1)}, f32[192,128]{1,0:T(8,128)S(1)}, u32[]{:S(2)}, u32[]{:S(2)}) collective-permute-start(f32[192,128]{1,0:T(8,128)S(1)} %get-tuple-element.74), channel_id=1, source_target_pairs={{0,64},{64,128},{128,192},{192,0},{1,65},{65,129},{129,193},{193,1... | collective-permute-start | bytes 294920 | tf_op jit(solution)/shard_map/ppermute | solution.py:403
  63.9 2.6 %collective-permute-start.8 = (f32[192,128]{1,0:T(8,128)S(1)}, f32[192,128]{1,0:T(8,128)S(1)}, u32[]{:S(2)}, u32[]{:S(2)}) collective-permute-start(f32[192,128]{1,0:T(8,128)S(1)} %get-tuple-element.75), channel_id=1, source_target_pairs={{0,128},{64,192},{128,0},{192,64},{1,129},{65,193},{129,1},{193,65... | collective-permute-start | bytes 294920 | tf_op jit(solution)/shard_map/ppermute | solution.py:403
  66.5 1.1 collective-permute-start.9
  67.6 2.4 %collective-permute-done.8.b_ref = f32[192,128]{1,0:T(8,128)S(1)} collective-permute-done((f32[192,128]{1,0:T(8,128)S(1)}, f32[192,128]{1,0:T(8,128)S(1)}, u32[]{:S(2)}, u32[]{:S(2)}) %collective-permute-start.8) | collective-permute-done | bytes 98336 | tf_op jit(solution)/shard_map/ppermute | solution.py:403
  70.0 1.2 collective-permute-done.9.c_ref
  71.2 0.7 shard_map.81
  71.8 0.6 copy-done.7
  72.5 0.7 copy-done.8
  73.1 3.6 %collective-permute-start.12 = (bf16[2,1024,256]{2,1,0:T(8,128)(2,1)S(1)}, bf16[2,1024,256]{2,1,0:T(8,128)(2,1)}, u32[]{:S(2)}, u32[]{:S(2)}) collective-permute-start(bf16[2,1024,256]{2,1,0:T(8,128)(2,1)S(1)} %get-tuple-element.90.hid_ref), channel_id=1, source_target_pairs={{0,8},{8,16},{16,24},{1,9},{9,17},{17,25},{2,10},{10,18},{18,26},{... | collective-permute-start | bytes 3145736 | tf_op jit(solution)/shard_map/ppermute | solution.py:397
  76.7 4.2 %all-to-all-start.1 = ((f32[8,24,128]{2,1,0:T(8,128)}), f32[8,24,128]{2,1,0:T(8,128)}, u32[]{:S(2)}, u32[]{:S(2)}) async-start(f32[8,24,128]{2,1,0:T(8,128)} %shard_map.81), calls=%async_computation.1 | async-start | bytes 196608 | tf_op jit(solution)/shard_map/all_to_all | solution.py:474
  80.9 6.4 %shard_map.82 = (f32[2,1024,256]{2,1,0:T(8,128)S(1)}, f32[1,8,128]{2,1,0:T(8,128)S(1)}) custom-call(bf16[2,1024,256]{2,1,0:T(8,128)(2,1)} %copy-done.5, bf16[2,128,256]{2,1,0:T(8,128)(2,1)} %copy-done.7, bf16[2,128,256]{2,1,0:T(8,128)(2,1)} %copy-done.8, bf16[3,3,256,256]{3,2,1,0:T(8,128)(2,1)} %refs_3_.1, bf16[2,1024,256]{2,1,0:T(8,128)(2,1)} %bitcast.12, ...), custom_call_target="tpu_custom_call" | custom-call | flops 2415919104 | bytes 5672960 | tf_op jit(solution)/shard_map/pallas_call | solution.py:31
  87.3 1.3 copy-done.3
  88.6 0.9 shard_map.83
  89.5 14.1 %all_to_all.15.u_ref = f32[8,32,128]{2,1,0:T(8,128)S(1)} all-to-all(f32[8,32,128]{2,1,0:T(8,128)S(1)} %shard_map.83), channel_id=1, replica_groups=mesh['y'=4,'core'=2,'tm'=4,'height'=8] {'height'}, dimensions={0} | all-to-all | bytes 262144 | tf_op jit(solution)/shard_map/all_to_all | solution.py:485
  103.6 2.5 %collective-permute-start.15 = (bf16[192,128]{1,0:T(8,128)(2,1)S(1)}, bf16[192,128]{1,0:T(8,128)(2,1)S(1)}, u32[]{:S(2)}, u32[]{:S(2)}) collective-permute-start(bf16[192,128]{1,0:T(8,128)(2,1)S(1)} %get-tuple-element.92), channel_id=1, source_target_pairs={{0,192},{64,0},{128,64},{192,128},{1,193},{65,1},{129,65},{193,129... | collective-permute-start | bytes 147464 | tf_op jit(solution)/shard_map/ppermute | solution.py:403
  106.1 0.6 collective-permute-start.13
  106.8 3.5 %shard_map.85 = bf16[2,1024,256]{2,1,0:T(8,128)(2,1)} custom-call(bf16[2,1024,256]{2,1,0:T(8,128)(2,1)S(1)} %bitcast.14, bf16[2,1024,256]{2,1,0:T(8,128)(2,1)S(1)} %bitcast.19, f32[2,1024,256]{2,1,0:T(8,128)} %copy-done.3, f32[8,8,128]{2,1,0:T(8,128)} %copy-done.6, f32[1,8,128]{2,1,0:T(8,128)S(1)} %get-tuple-element.97.refs_4_), custom_call_target="tpu_custom_call" | custom-call | flops 2097152 | bytes 5279744 | tf_op jit(solution)/shard_map/pallas_call | solution.py:31
  110.3 0.3 collective-permute-done.14
  110.9 1.5 %collective-permute-start.17 = (bf16[768,128]{1,0:T(8,128)(2,1)S(1)}, bf16[768,128]{1,0:T(8,128)(2,1)S(1)}, u32[]{:S(2)}, u32[]{:S(2)}) collective-permute-start(bf16[768,128]{1,0:T(8,128)(2,1)S(1)} %pad_maximum_fusion.1), channel_id=1, source_target_pairs={{0,16},{8,24},{16,0},{24,8},{1,17},{9,25},{17,1},{25,9},{2,18},{10... | collective-permute-start | bytes 589832 | tf_op jit(solution)/shard_map/ppermute | solution.py:403
  112.4 0.8 collective-permute-start.16
  113.2 3.7 %shard_map.86 = bf16[2,1024,256]{2,1,0:T(8,128)(2,1)} custom-call(bf16[2,1024,256]{2,1,0:T(8,128)(2,1)S(1)} %bitcast.15, bf16[2,1024,256]{2,1,0:T(8,128)(2,1)S(1)} %get-tuple-element.90.hid_ref, bf16[2,1024,256]{2,1,0:T(8,128)(2,1)} %collective-permute-done.12.prev_ref, bf16[3,256,256]{2,1,0:T(8,128)(2,1)S(1)} %copy-done.4), custom_call_target="tpu_custom_call" | custom-call | flops 805306368 | bytes 4587520 | tf_op jit(solution)/shard_map/pallas_call | solution.py:31
  116.9 0.3 collective-permute-done.17
  117.1 2.0 %collective-permute-done.16 = bf16[768,128]{1,0:T(8,128)(2,1)S(1)} collective-permute-done((bf16[768,128]{1,0:T(8,128)(2,1)S(1)}, bf16[768,128]{1,0:T(8,128)(2,1)S(1)}, u32[]{:S(2)}, u32[]{:S(2)}) %collective-permute-start.16) | collective-permute-done | bytes 196640 | tf_op jit(solution)/shard_map/ppermute | solution.py:403
  119.2 6.8 %collective-permute-start.19 = (bf16[3072,128]{1,0:T(8,128)(2,1)S(1)}, bf16[3072,128]{1,0:T(8,128)(2,1)S(1)}, u32[]{:S(2)}, u32[]{:S(2)}) collective-permute-start(bf16[3072,128]{1,0:T(8,128)(2,1)S(1)} %pad_maximum_fusion.refs_1_), channel_id=1, source_target_pairs={{0,32},{32,0},{1,33},{33,1},{2,34},{34,2},{3,35},{35,3},{4,36},{36... | collective-permute-start | bytes 2359304 | tf_op jit(solution)/shard_map/ppermute | solution.py:391
  126.0 1.9 %collective-permute-done.19.refs_2_ = bf16[3072,128]{1,0:T(8,128)(2,1)S(1)} collective-permute-done((bf16[3072,128]{1,0:T(8,128)(2,1)S(1)}, bf16[3072,128]{1,0:T(8,128)(2,1)S(1)}, u32[]{:S(2)}, u32[]{:S(2)}) %collective-permute-start.19) | collective-permute-done | bytes 786464 | tf_op jit(solution)/shard_map/ppermute | solution.py:391
  127.9 4.2 %shard_map.87 = (f32[9,256,256]{2,1,0:T(8,128)}, f32[3,256,256]{2,1,0:T(8,128)}) custom-call(s32[5]{0:T(128)S(1)} %stack.23.refs_0_.info, bf16[3072,128]{1,0:T(8,128)(2,1)S(1)} %pad_maximum_fusion.refs_1_, bf16[3072,128]{1,0:T(8,128)(2,1)S(1)} %collective-permute-done.19.refs_2_), custom_call_target="tpu_custom_call" | custom-call | flops 2097152 | bytes 4718612 | tf_op jit(solution)/shard_map/pallas_call | solution.py:31
  (36 shorter events, 0.7 us)
Async XLA Ops:
  0.6 34.8 %collective-permute-start.2 = (bf16[2,1024,256]{2,1,0:T(8,128)(2,1)}, bf16[2,1024,256]{2,1,0:T(8,128)(2,1)S(1)}, u32[]{:S(2)}, u32[]{:S(2)}) collective-permute-start(bf16[2,1024,256]{2,1,0:T(8,128)(2,1)} %bitcast.16), channel_id=1, source_target_pairs={{8,0},{16,8},{24,16},{9,1},{17,9},{25,17},{10,2},{18,10},{26,18},{... | collective-permute-start | bytes 3145736 | tf_op jit(solution)/shard_map/ppermute | solution.py:397
  1.9 1.2 copy-start
  4.1 22.4 %collective-permute-start = (bf16[2,128,256]{2,1,0:T(8,128)(2,1)S(1)}, bf16[2,128,256]{2,1,0:T(8,128)(2,1)S(1)}, u32[]{:S(2)}, u32[]{:S(2)}) collective-permute-start(bf16[2,128,256]{2,1,0:T(8,128)(2,1)S(1)} %get-tuple-element.56), channel_id=1, source_target_pairs={{0,1},{1,2},{2,3},{3,4},{4,5},{5,6},{6,7},{8,9},{9,10},{10,11},{11... | collective-permute-start | bytes 393224 | tf_op jit(solution)/shard_map/ppermute | solution.py:397
  8.5 18.1 %collective-permute-start.1 = (bf16[2,128,256]{2,1,0:T(8,128)(2,1)S(1)}, bf16[2,128,256]{2,1,0:T(8,128)(2,1)S(1)}, u32[]{:S(2)}, u32[]{:S(2)}) collective-permute-start(bf16[2,128,256]{2,1,0:T(8,128)(2,1)S(1)} %get-tuple-element.57), channel_id=1, source_target_pairs={{1,0},{2,1},{3,2},{4,3},{5,4},{6,5},{7,6},{9,8},{10,9},{11,10},{12... | collective-permute-start | bytes 393224 | tf_op jit(solution)/shard_map/ppermute | solution.py:397
  9.8 16.8 %all-to-all-start = ((f32[8,8,128]{2,1,0:T(8,128)}), f32[8,8,128]{2,1,0:T(8,128)S(1)}, u32[]{:S(2)}, u32[]{:S(2)}) async-start(f32[8,8,128]{2,1,0:T(8,128)} %get-tuple-element.58), calls=%async_computation | async-start | bytes 65536 | tf_op jit(solution)/shard_map/all_to_all | solution.py:437
  26.6 0.6 copy-start.6
  26.6 0.7 copy-start.9
  27.2 0.7 copy-start.10
  27.9 7.6 %copy-start.2 = (bf16[1,2,8,128,256]{4,3,2,1,0:T(8,128)(2,1)S(1)}, bf16[1,2,8,128,256]{4,3,2,1,0:T(8,128)(2,1)}, u32[]{:S(2)}) copy-start(bf16[1,2,8,128,256]{4,3,2,1,0:T(8,128)(2,1)} %param.5) | copy-start | bytes 3145732
  27.9 7.6 %copy-start.4 = (bf16[3,256,256]{2,1,0:T(8,128)(2,1)S(1)}, bf16[3,256,256]{2,1,0:T(8,128)(2,1)}, u32[]{:S(2)}) copy-start(bf16[3,256,256]{2,1,0:T(8,128)(2,1)} %w_ref.3) | copy-start | bytes 1179652
  37.1 4.1 %copy-start.5 = (bf16[2,1024,256]{2,1,0:T(8,128)(2,1)}, bf16[2,1024,256]{2,1,0:T(8,128)(2,1)S(1)}, u32[]{:S(2)}) copy-start(bf16[2,1024,256]{2,1,0:T(8,128)(2,1)S(1)} %get-tuple-element.61.pg_ref.refs_0_) | copy-start | bytes 3145732
  41.3 5.8 %collective-permute-start.3 = (f32[3072,128]{1,0:T(8,128)S(1)}, f32[3072,128]{1,0:T(8,128)S(1)}, u32[]{:S(2)}, u32[]{:S(2)}) collective-permute-start(f32[3072,128]{1,0:T(8,128)S(1)} %slice.4), channel_id=1, source_target_pairs={{0,32},{32,0},{1,33},{33,1},{2,34},{34,2},{3,35},{35,3},{4,36},{36... | collective-permute-start | bytes 4718600 | tf_op jit(solution)/shard_map/ppermute | solution.py:391
  47.7 9.5 %collective-permute-start.4 = (bf16[768,128]{1,0:T(8,128)(2,1)S(1)}, bf16[768,128]{1,0:T(8,128)(2,1)S(1)}, u32[]{:S(2)}, u32[]{:S(2)}) collective-permute-start(bf16[768,128]{1,0:T(8,128)(2,1)S(1)} %get-tuple-element.67), channel_id=1, source_target_pairs={{0,8},{8,16},{16,24},{24,0},{1,9},{9,17},{17,25},{25,1},{2,10},{10... | collective-permute-start | bytes 589832 | tf_op jit(solution)/shard_map/ppermute | solution.py:403
  50.2 11.6 %collective-permute-start.5 = (bf16[768,128]{1,0:T(8,128)(2,1)S(1)}, bf16[768,128]{1,0:T(8,128)(2,1)S(1)}, u32[]{:S(2)}, u32[]{:S(2)}) collective-permute-start(bf16[768,128]{1,0:T(8,128)(2,1)S(1)} %get-tuple-element.68), channel_id=1, source_target_pairs={{0,16},{8,24},{16,0},{24,8},{1,17},{9,25},{17,1},{25,9},{2,18},{10... | collective-permute-start | bytes 589832 | tf_op jit(solution)/shard_map/ppermute | solution.py:403
  53.0 8.8 %collective-permute-start.6 = (bf16[768,128]{1,0:T(8,128)(2,1)S(1)}, bf16[768,128]{1,0:T(8,128)(2,1)S(1)}, u32[]{:S(2)}, u32[]{:S(2)}) collective-permute-start(bf16[768,128]{1,0:T(8,128)(2,1)S(1)} %get-tuple-element.69), channel_id=1, source_target_pairs={{0,24},{8,0},{16,8},{24,16},{1,25},{9,1},{17,9},{25,17},{2,26},{10... | collective-permute-start | bytes 589832 | tf_op jit(solution)/shard_map/ppermute | solution.py:403
  53.8 18.1 %collective-permute-start.10 = (bf16[2,128,256]{2,1,0:T(8,128)(2,1)S(1)}, bf16[2,128,256]{2,1,0:T(8,128)(2,1)S(1)}, u32[]{:S(2)}, u32[]{:S(2)}) collective-permute-start(bf16[2,128,256]{2,1,0:T(8,128)(2,1)S(1)} %get-tuple-element.80), channel_id=1, source_target_pairs={{0,1},{1,2},{2,3},{3,4},{4,5},{5,6},{6,7},{8,9},{9,10},{10,11},{11... | collective-permute-start | bytes 393224 | tf_op jit(solution)/shard_map/ppermute | solution.py:397
  55.9 15.9 %collective-permute-start.11 = (bf16[2,128,256]{2,1,0:T(8,128)(2,1)S(1)}, bf16[2,128,256]{2,1,0:T(8,128)(2,1)S(1)}, u32[]{:S(2)}, u32[]{:S(2)}) collective-permute-start(bf16[2,128,256]{2,1,0:T(8,128)(2,1)S(1)} %get-tuple-element.81), channel_id=1, source_target_pairs={{1,0},{2,1},{3,2},{4,3},{5,4},{6,5},{7,6},{9,8},{10,9},{11,10},{12... | collective-permute-start | bytes 393224 | tf_op jit(solution)/shard_map/ppermute | solution.py:397
  62.5 5.1 %collective-permute-start.7 = (f32[192,128]{1,0:T(8,128)S(1)}, f32[192,128]{1,0:T(8,128)S(1)}, u32[]{:S(2)}, u32[]{:S(2)}) collective-permute-start(f32[192,128]{1,0:T(8,128)S(1)} %get-tuple-element.74), channel_id=1, source_target_pairs={{0,64},{64,128},{128,192},{192,0},{1,65},{65,129},{129,193},{193,1... | collective-permute-start | bytes 294920 | tf_op jit(solution)/shard_map/ppermute | solution.py:403
  63.9 6.1 %collective-permute-start.8 = (f32[192,128]{1,0:T(8,128)S(1)}, f32[192,128]{1,0:T(8,128)S(1)}, u32[]{:S(2)}, u32[]{:S(2)}) collective-permute-start(f32[192,128]{1,0:T(8,128)S(1)} %get-tuple-element.75), channel_id=1, source_target_pairs={{0,128},{64,192},{128,0},{192,64},{1,129},{65,193},{129,1},{193,65... | collective-permute-start | bytes 294920 | tf_op jit(solution)/shard_map/ppermute | solution.py:403
  66.5 4.7 %collective-permute-start.9 = (f32[192,128]{1,0:T(8,128)S(1)}, f32[192,128]{1,0:T(8,128)S(1)}, u32[]{:S(2)}, u32[]{:S(2)}) collective-permute-start(f32[192,128]{1,0:T(8,128)S(1)} %get-tuple-element.76), channel_id=1, source_target_pairs={{0,192},{64,0},{128,64},{192,128},{1,193},{65,1},{129,65},{193,129... | collective-permute-start | bytes 294920 | tf_op jit(solution)/shard_map/ppermute | solution.py:403
  71.8 0.7 copy-start.7
  72.5 0.7 copy-start.8
  73.1 30.5 %collective-permute-start.12 = (bf16[2,1024,256]{2,1,0:T(8,128)(2,1)S(1)}, bf16[2,1024,256]{2,1,0:T(8,128)(2,1)}, u32[]{:S(2)}, u32[]{:S(2)}) collective-permute-start(bf16[2,1024,256]{2,1,0:T(8,128)(2,1)S(1)} %get-tuple-element.90.hid_ref), channel_id=1, source_target_pairs={{0,8},{8,16},{16,24},{1,9},{9,17},{17,25},{2,10},{10,18},{18,26},{... | collective-permute-start | bytes 3145736 | tf_op jit(solution)/shard_map/ppermute | solution.py:397
  76.7 11.9 %all-to-all-start.1 = ((f32[8,24,128]{2,1,0:T(8,128)}), f32[8,24,128]{2,1,0:T(8,128)}, u32[]{:S(2)}, u32[]{:S(2)}) async-start(f32[8,24,128]{2,1,0:T(8,128)} %shard_map.81), calls=%async_computation.1 | async-start | bytes 196608 | tf_op jit(solution)/shard_map/all_to_all | solution.py:474
  80.9 25.9 %copy-start.1 = (bf16[1,2,8,128,256]{4,3,2,1,0:T(8,128)(2,1)S(1)}, bf16[1,2,8,128,256]{4,3,2,1,0:T(8,128)(2,1)}, u32[]{:S(2)}) copy-start(bf16[1,2,8,128,256]{4,3,2,1,0:T(8,128)(2,1)} %param.4) | copy-start | bytes 3145732
  87.2 1.3 copy-start.3
  103.6 6.7 %collective-permute-start.15 = (bf16[192,128]{1,0:T(8,128)(2,1)S(1)}, bf16[192,128]{1,0:T(8,128)(2,1)S(1)}, u32[]{:S(2)}, u32[]{:S(2)}) collective-permute-start(bf16[192,128]{1,0:T(8,128)(2,1)S(1)} %get-tuple-element.92), channel_id=1, source_target_pairs={{0,192},{64,0},{128,64},{192,128},{1,193},{65,1},{129,65},{193,129... | collective-permute-start | bytes 147464 | tf_op jit(solution)/shard_map/ppermute | solution.py:403
  106.1 4.5 %collective-permute-start.14 = (bf16[192,128]{1,0:T(8,128)(2,1)S(1)}, bf16[192,128]{1,0:T(8,128)(2,1)S(1)}, u32[]{:S(2)}, u32[]{:S(2)}) collective-permute-start(bf16[192,128]{1,0:T(8,128)(2,1)S(1)} %get-tuple-element.92), channel_id=1, source_target_pairs={{0,128},{64,192},{128,0},{192,64},{1,129},{65,193},{129,1},{193,65... | collective-permute-start | bytes 147464 | tf_op jit(solution)/shard_map/ppermute | solution.py:403
  106.1 4.7 %collective-permute-start.13 = (bf16[192,128]{1,0:T(8,128)(2,1)S(1)}, bf16[192,128]{1,0:T(8,128)(2,1)S(1)}, u32[]{:S(2)}, u32[]{:S(2)}) collective-permute-start(bf16[192,128]{1,0:T(8,128)(2,1)S(1)} %get-tuple-element.92), channel_id=1, source_target_pairs={{0,64},{64,128},{128,192},{192,0},{1,65},{65,129},{129,193},{193,1... | collective-permute-start | bytes 147464 | tf_op jit(solution)/shard_map/ppermute | solution.py:403
  110.8 6.0 %collective-permute-start.18 = (bf16[768,128]{1,0:T(8,128)(2,1)S(1)}, bf16[768,128]{1,0:T(8,128)(2,1)S(1)}, u32[]{:S(2)}, u32[]{:S(2)}) collective-permute-start(bf16[768,128]{1,0:T(8,128)(2,1)S(1)} %pad_maximum_fusion.1), channel_id=1, source_target_pairs={{0,24},{8,0},{16,8},{24,16},{1,25},{9,1},{17,9},{25,17},{2,26},{10... | collective-permute-start | bytes 589832 | tf_op jit(solution)/shard_map/ppermute | solution.py:403
  110.9 6.2 %collective-permute-start.17 = (bf16[768,128]{1,0:T(8,128)(2,1)S(1)}, bf16[768,128]{1,0:T(8,128)(2,1)S(1)}, u32[]{:S(2)}, u32[]{:S(2)}) collective-permute-start(bf16[768,128]{1,0:T(8,128)(2,1)S(1)} %pad_maximum_fusion.1), channel_id=1, source_target_pairs={{0,16},{8,24},{16,0},{24,8},{1,17},{9,25},{17,1},{25,9},{2,18},{10... | collective-permute-start | bytes 589832 | tf_op jit(solution)/shard_map/ppermute | solution.py:403
  112.4 6.7 %collective-permute-start.16 = (bf16[768,128]{1,0:T(8,128)(2,1)S(1)}, bf16[768,128]{1,0:T(8,128)(2,1)S(1)}, u32[]{:S(2)}, u32[]{:S(2)}) collective-permute-start(bf16[768,128]{1,0:T(8,128)(2,1)S(1)} %pad_maximum_fusion.1), channel_id=1, source_target_pairs={{0,8},{8,16},{16,24},{24,0},{1,9},{9,17},{17,25},{25,1},{2,10},{10... | collective-permute-start | bytes 589832 | tf_op jit(solution)/shard_map/ppermute | solution.py:403
  119.2 8.7 %collective-permute-start.19 = (bf16[3072,128]{1,0:T(8,128)(2,1)S(1)}, bf16[3072,128]{1,0:T(8,128)(2,1)S(1)}, u32[]{:S(2)}, u32[]{:S(2)}) collective-permute-start(bf16[3072,128]{1,0:T(8,128)(2,1)S(1)} %pad_maximum_fusion.refs_1_), channel_id=1, source_target_pairs={{0,32},{32,0},{1,33},{33,1},{2,34},{34,2},{3,35},{35,3},{4,36},{36... | collective-permute-start | bytes 2359304 | tf_op jit(solution)/shard_map/ppermute | solution.py:391

commit v6 on v5

--- a/solution.py
+++ b/solution.py
@@ -7,6 +7,7 @@
 from jax.experimental.pallas import tpu as pltpu
 from jax.sharding import Mesh
 from jax.sharding import PartitionSpec as P
+
 
 GROUPS = 32
 tied = lax.optimization_barrier
@@ -336,46 +337,58 @@
         lax.fori_loop(0, 3, part, 0)
 
 
-def y_kernel(own_ref, a_ref, b_ref, c_ref, o_ref):
+def y_kernel(own_ref, a_ref, b_ref, c_ref, gst_ref, o_ref):
+    code = coded(own_ref[...] + a_ref[...] + b_ref[...] + c_ref[...])
+    rest, pieces = gst_ref[0], []
+    for _ in range(3):
+        piece = rest.astype(BF16).astype(F32)
+        pieces.append(piece)
+        rest = rest - piece
+    sums = jnp.concatenate([*pieces, jnp.zeros_like(rest)], axis=0).astype(BF16)
     for peer in range(8):
-        rows = slice(peer * 24, peer * 24 + 24)
-        o_ref[peer] = own_ref[rows, :] + a_ref[rows, :] + b_ref[rows, :] + c_ref[rows, :]
-
-
-def z_kernel(u_ref, gst_ref, o_ref):
-    total = u_ref[0]
-    for peer in range(1, 8):
-        total = total + u_ref[peer]
+        o_ref[peer, 0:192, :] = code
+        o_ref[peer, 192:224, :] = sums
+
+
+def z_kernel(u_ref, o_ref, gst_ref):
+    def part(r, _):
+        rows = pl.ds(pl.multiple_of(r * 64, 64), 64)
+        total = decoded(u_ref[0, rows, :])
+        for peer in range(1, 8):
+            total = total + decoded(u_ref[peer, rows, :])
+        o_ref[rows, :] = coded(total)
+        return 0
+
+    lax.fori_loop(0, 3, part, 0)
+    sums = jnp.zeros((8, 128), F32)
     for peer in range(8):
-        o_ref[peer, 0:24, :] = total
-        o_ref[peer, 24:32, :] = gst_ref[0]
-
-
-def code_kernel(u_ref, o_ref, gst_ref):
-    for peer in range(0, 8, 2):
-        pair = jnp.concatenate([u_ref[peer, 0:24, :], u_ref[peer + 1, 0:24, :]], axis=0)
-        o_ref[peer * 24 : peer * 24 + 48, :] = coded(pair)
-    total = u_ref[0, 24:32, :]
-    for peer in range(1, 8):
-        total = total + u_ref[peer, 24:32, :]
-    gst_ref[0] = total
-
-
-def clip_kernel(clip_level, info, own_ref, other_ref, s_ref, t_ref, w_ref, sems):
+        v = u_ref[peer, 192:224, :].astype(F32)
+        sums = sums + ((v[0:8] + v[8:16]) + v[16:24])
+    gst_ref[0] = sums
+
+
+def half_kernel(info, u_ref, w_ref, acc_ref):
     acc = jnp.zeros((8, 128), F32)
-    for tap in range(12):
-        mine = info[0] == tap // 6
-        for lh in range(2):
-            for part in range(4):
-                at = pl.ds(slab_rows(info, (tap % 6) * 2 + lh, part), 64)
-                v = decoded(jnp.where(mine, own_ref[at, :], other_ref[at, :]))
-                w_ref[tap, part * 64 : part * 64 + 64, lh * 128 : lh * 128 + 128] = v
-                acc = acc + fold(v * v)
+    for unit in range(12):
+        for part in range(4):
+            v = decoded(u_ref[pl.ds(slab_rows(info, unit, part), 64), :])
+            w_ref[unit * 256 + part * 64 : unit * 256 + part * 64 + 64, :] = v
+            acc = acc + fold(v * v)
+    acc_ref[...] = acc
+
+
+def clip_kernel(clip_level, info, own_ref, acc_ref, other_ref, s_ref, t_ref, w_ref, b_ref, oacc_ref, sems):
+    half_kernel(info, other_ref, b_ref, oacc_ref)
+    acc = acc_ref[...] + oacc_ref[...]
     total = jnp.sum(jnp.sum(acc, axis=0, keepdims=True), axis=1, keepdims=True)
     scale = clip_level / jnp.maximum(jnp.sqrt(total), clip_level)
     copies = []
     for tap in range(12):
-        w_ref[tap] = w_ref[tap] * scale
+        mine = info[0] == tap // 6
+        for lh in range(2):
+            at = pl.ds(((tap % 6) * 2 + lh) * 256, 256)
+            v = jnp.where(mine, own_ref[at, :], b_ref[at, :])
+            w_ref[tap, :, lh * 128 : lh * 128 + 128] = v * scale
         target = s_ref.at[tap] if tap < 9 else t_ref.at[tap - 9]
         copies.append(pltpu.make_async_copy(w_ref.at[tap], target, sems.at[tap]))
         copies[-1].start()
@@ -430,17 +443,17 @@
     w3 = spatial_kernel.reshape(3, 768, 256)
     gflop = 2 * 2048 * 256 * 256
 
-    later = moved(cot, TM, -1)
     small = out((8, 8, 128), F32)
     edge = out((2, columns, 256), BF16)
-    st, x_top, x_bot = call(stats_kernel, [small, edge, edge], [x], 1 << 21)
-    st = lax.all_to_all(st, HEIGHT, 0, 0, tiled=True)
-    up = moved(x_bot, HEIGHT, 1)
-    dn = moved(x_top, HEIGHT, -1)
+    st, x_top, x_bot = call(stats_kernel, [small, edge, edge], [in_hbm(x)], 1 << 21)
+    st = in_hbm(lax.all_to_all(st, HEIGHT, 0, 0, tiled=True))
+    later = moved(cot, TM, -1)
+    up = in_hbm(moved(x_bot, HEIGHT, 1))
+    dn = in_hbm(moved(x_top, HEIGHT, -1))
     act, hid, slope = call(
         lambda *refs: forward_kernel(members, *refs),
         [out((2, 1280, 768), BF16), out(flat, BF16), out(flat, F32)],
-        [info, in_hbm(x), in_hbm(up), in_hbm(dn), in_hbm(st), in_hbm(w3)],
+        [info, in_hbm(x), up, dn, st, in_hbm(w3)],
         9 * gflop,
         smem=1,
         loose=(2, 3, 4),
@@ -465,42 +478,50 @@
     own, *sent = call(
         pair_kernel, [out((768, 128), F32), quarter, quarter, quarter], [g, got], 1 << 21
     )
-    got = tied(shifts(sent, TM))
+    got = shifts(sent, TM)
+    ng, gst = call(
+        lambda *refs: backward_kernel(members, *refs),
+        [out(flat, F32), out((1, 8, 128), F32)],
+        [pg, gup, gdn, in_hbm(w9), in_hbm(x), in_hbm(st)],
+        9 * gflop,
+        scratch=[pltpu.VMEM((2, 1280, 256), BF16)] * 3,
+    )
+    got, gst = tied((got, gst))
     part = out((192, 128), F32)
     own, *sent = call(x_kernel, [part] * 4, [own, *got], 1 << 21)
     got = tied(shifts(sent, "y"))
-    (pieces,) = call(y_kernel, [out((8, 24, 128), F32)], [own, *got], 1 << 20)
-    pieces, gup, gdn, hid_sent = tied((pieces, gup, gdn, hid))
+    (pieces,) = call(y_kernel, [out((8, 224, 128), BF16)], [own, *got, gst], 1 << 20)
+    pieces, hid_sent = tied((pieces, hid))
     pieces = lax.all_to_all(pieces, HEIGHT, 0, 0, tiled=True)
     prev = moved(hid_sent, TM, 1)
-    ng, gst = call(
-        lambda *refs: backward_kernel(members, *refs),
-        [out(flat, F32), out((1, 8, 128), F32)],
-        [in_hbm(a) for a in (pg, gup, gdn, w9, x, st)],
-        9 * gflop,
-        scratch=[pltpu.VMEM((2, 1280, 256), BF16)] * 3,
-    )
-    pieces, ng, gst = tied((pieces, in_hbm(ng), gst))
-    (copies,) = call(z_kernel, [out((8, 32, 128), F32)], [pieces, gst], 1 << 20)
-    copies = lax.all_to_all(copies, HEIGHT, 0, 0, tiled=True)
-    mine, gst = call(code_kernel, [out((192, 128), BF16), out((1, 8, 128), F32)], [copies], 1 << 20)
-    mine, prev, gst = tied((mine, prev, gst))
+    mine, gst = call(z_kernel, [out((192, 128), BF16), out((1, 8, 128), F32)], [pieces], 1 << 20)
     (input_grad,) = call(
-        lambda *refs: input_grad_kernel(members, *refs), [out(flat, BF16)], [x, cot, in_hbm(ng), in_hbm(st), gst], 1 << 21
+        lambda *refs: input_grad_kernel(members, *refs),
+        [out(flat, BF16)],
+        [x, cot, in_hbm(ng), in_hbm(st), gst],
+        1 << 21,
     )
     mine = gathered(mine, "y")
-    mine, input_grad = tied((mine, input_grad))
+    mine, prev, input_grad = tied((mine, prev, input_grad))
     (block_output,) = call(block_kernel, [out(flat, BF16)], [x, hid, prev, temporal_kernel], 3 * gflop)
     mine = gathered(mine, TM)
     mine, block_output = tied((mine, block_output))
+    slab = (3072, 128)
+    tile = out((8, 128), F32)
+    own, acc = call(half_kernel, [out(slab, F32), tile], [info, mine], 1 << 21, smem=1)
     clipped_spatial, clipped_temporal = call(
         lambda *refs: clip_kernel(clip_level, *refs),
         [out((9, 256, 256), F32), out((3, 256, 256), F32)],
-        [info, mine, swapped(mine, "core")],
+        [info, own, acc, swapped(mine, "core")],
         1 << 21,
         smem=1,
         outside=True,
-        scratch=[pltpu.VMEM((12, 256, 256), F32), pltpu.SemaphoreType.DMA((12,))],
+        scratch=[
+            pltpu.VMEM((12, 256, 256), F32),
+            pltpu.VMEM(slab, F32),
+            pltpu.VMEM(tile.shape, F32),
+            pltpu.SemaphoreType.DMA((12,)),
+        ],
     )
     return (
         block_output.reshape(video_latents.shape),

time: 133 us -> 121 us (0.910)
  waiting for transfers between devices: 22.7 us -> 15.5 us
  starting transfers between devices: 54.1 us -> 50.5 us
  blocking collectives: 14.1 us -> 17.6 us
  local copies, waits for them, and re-layouts: 5.35 us -> 2.2 us
    ppermute x2, waiting for transfers between devices: 4.95 us -> 0.54 us  [swapped(): return lax.ppermute(x, axis, [(0, 1), (1, 0)])]
    all_to_all x2 -> x1, starting transfers between devices: 14 us -> 9.85 us  [body(): st = in_hbm(lax.all_to_all(st, HEIGHT, 0, 0, tiled=True))]
    all_to_all x1, blocking collectives: 14.1 us -> 17.6 us  [body(): pieces = lax.all_to_all(pieces, HEIGHT, 0, 0, tiled=True)]
    unnamed x22 -> x14, local copies, waits for them, and re-layouts: 5.17 us -> 2.01 us
    ppermute x12, waiting for transfers between devices: 10.9 us -> 8.15 us  [shifts(): lax.ppermute(m, axis, [(i, (i + d) % n) for i in range(n)])]
    ppermute x12, starting transfers between devices: 16.6 us -> 18.7 us  [shifts(): lax.ppermute(m, axis, [(i, (i + d) % n) for i in range(n)])]
    all_to_all x2 -> x1, waiting for transfers between devices: 6.83 us -> 6.83 us  [body(): st = in_hbm(lax.all_to_all(st, HEIGHT, 0, 0, tiled=True))]
  transfers between devices with their start and end apart: 22 -> 21, of which waited for: 10 -> 9; matrix products, arithmetic and copies ran while one was open for 0% -> 0% of each run, Pallas kernels for 18% -> 20%
where the time goes in v6:
time: 121 us
  starting transfers between devices  50.5 us (42%)
  Pallas kernels  33.9 us (28%)
  blocking collectives  17.6 us (15%)
  waiting for transfers between devices  15.5 us (13%)
  local copies, waits for them, and re-layouts  2.2 us (2%)
    pallas_call x13, Pallas kernels, call(): pl.pallas_call(kernel, out_shape=tuple(outs), in_specs=specs, out_specs=t...  33.9 us
    ppermute x12, starting transfers between devices, shifts(): lax.ppermute(m, axis, [(i, (i + d) % n) for i in range(n)])  18.7 us
    all_to_all x1, blocking collectives, body(): pieces = lax.all_to_all(pieces, HEIGHT, 0, 0, tiled=True)  17.6 us
    ppermute x6, starting transfers between devices, moved(): return lax.ppermute(x, axes, route)  13 us
    all_to_all x1, starting transfers between devices, body(): st = in_hbm(lax.all_to_all(st, HEIGHT, 0, 0, tiled=True))  9.85 us
    ppermute x2, starting transfers between devices, swapped(): return lax.ppermute(x, axis, [(0, 1), (1, 0)])  8.88 us
    ppermute x12, waiting for transfers between devices, shifts(): lax.ppermute(m, axis, [(i, (i + d) % n) for i in range(n)])  8.15 us
    all_to_all x1, waiting for transfers between devices, body(): st = in_hbm(lax.all_to_all(st, HEIGHT, 0, 0, tiled=True))  6.83 us
  transfers between devices with their start and end apart: 21, of which 9 were waited for; matrix products, arithmetic and copies ran while one was open for 0% of the time, Pallas kernels for 20%

profile of v6, /device:TPU:1, one launch (start us, length us, event | category | flops | bytes accessed | tf_op | source)
XLA Modules:
  0.0 120.8 jit_solution(3259894199042644815)
XLA Ops:
  0.6 1.3 %collective-permute-start.2 = (bf16[2,1024,256]{2,1,0:T(8,128)(2,1)}, bf16[2,1024,256]{2,1,0:T(8,128)(2,1)S(1)}, u32[]{:S(2)}, u32[]{:S(2)}) collective-permute-start(bf16[2,1024,256]{2,1,0:T(8,128)(2,1)} %bitcast.16), channel_id=1, source_target_pairs={{8,0},{16,8},{24,16},{9,1},{17,9},{25,17},{10,2},{18,10},{26,18},{... | collective-permute-start | bytes 3145736 | tf_op jit(solution)/shard_map/ppermute | solution.py:410
  1.9 2.2 %shard_map.75 = (f32[8,8,128]{2,1,0:T(8,128)}, bf16[2,128,256]{2,1,0:T(8,128)(2,1)S(1)}, bf16[2,128,256]{2,1,0:T(8,128)(2,1)S(1)}) custom-call(bf16[2,1024,256]{2,1,0:T(8,128)(2,1)} %bitcast.11), custom_call_target="tpu_custom_call" | custom-call | flops 2097152 | bytes 1343488 | tf_op jit(solution)/shard_map/pallas_call | solution.py:32
  4.1 4.4 %collective-permute-start = (bf16[2,128,256]{2,1,0:T(8,128)(2,1)S(1)}, bf16[2,128,256]{2,1,0:T(8,128)(2,1)S(1)}, u32[]{:S(2)}, u32[]{:S(2)}) collective-permute-start(bf16[2,128,256]{2,1,0:T(8,128)(2,1)S(1)} %get-tuple-element.52), channel_id=1, source_target_pairs={{0,1},{1,2},{2,3},{3,4},{4,5},{5,6},{6,7},{8,9},{9,10},{10,11},{11... | collective-permute-start | bytes 393224 | tf_op jit(solution)/shard_map/ppermute | solution.py:410
  8.5 1.3 %collective-permute-start.1 = (bf16[2,128,256]{2,1,0:T(8,128)(2,1)S(1)}, bf16[2,128,256]{2,1,0:T(8,128)(2,1)S(1)}, u32[]{:S(2)}, u32[]{:S(2)}) collective-permute-start(bf16[2,128,256]{2,1,0:T(8,128)(2,1)S(1)} %get-tuple-element.53), channel_id=1, source_target_pairs={{1,0},{2,1},{3,2},{4,3},{5,4},{6,5},{7,6},{9,8},{10,9},{11,10},{12... | collective-permute-start | bytes 393224 | tf_op jit(solution)/shard_map/ppermute | solution.py:410
  9.8 9.8 %all-to-all-start = ((f32[8,8,128]{2,1,0:T(8,128)}), f32[8,8,128]{2,1,0:T(8,128)S(1)}, u32[]{:S(2)}, u32[]{:S(2)}) async-start(f32[8,8,128]{2,1,0:T(8,128)} %get-tuple-element.54), calls=%async_computation | async-start | bytes 65536 | tf_op jit(solution)/shard_map/all_to_all | solution.py:449
  19.6 0.1 stack.23.refs_0_.info
  19.7 6.8 %all-to-all-done.refs_4_.refs_5_.refs_3_ = f32[8,8,128]{2,1,0:T(8,128)S(1)} async-done(((f32[8,8,128]{2,1,0:T(8,128)}), f32[8,8,128]{2,1,0:T(8,128)S(1)}, u32[]{:S(2)}, u32[]{:S(2)}) %all-to-all-start) | async-done | bytes 32800 | tf_op jit(solution)/shard_map/all_to_all | solution.py:449
  26.6 0.6 copy-done.4
  27.3 7.5 %shard_map.76 = (bf16[2,1280,768]{2,1,0:T(8,128)(2,1)S(1)}, bf16[2,1024,256]{2,1,0:T(8,128)(2,1)S(1)}, f32[2,1024,256]{2,1,0:T(8,128)S(1)}) custom-call(s32[5]{0:T(128)S(1)} %stack.23.refs_0_.info, bf16[2,1024,256]{2,1,0:T(8,128)(2,1)} %bitcast.12, bf16[2,128,256]{2,1,0:T(8,128)(2,1)} %copy-done.5, bf16[2,128,256]{2,1,0:T(8,128)(2,1)} %copy-done.6, ...), custom_call_target="tpu_custom_call" | custom-call | flops 2415919104 | bytes 9601044 | tf_op jit(solution)/shard_map/pallas_call | solution.py:32
  34.8 1.6 %shard_map.77 = (bf16[2,1024,256]{2,1,0:T(8,128)(2,1)S(1)}, bf16[2,128,256]{2,1,0:T(8,128)(2,1)S(1)}, bf16[2,128,256]{2,1,0:T(8,128)(2,1)S(1)}) custom-call(bf16[2,1024,256]{2,1,0:T(8,128)(2,1)S(1)} %bitcast.17, bf16[2,1024,256]{2,1,0:T(8,128)(2,1)S(1)} %collective-permute-done.2.later_ref, f32[2,1024,256]{2,1,0:T(8,128)S(1)} %get-tuple-element.56.slope_ref, ...), custom_call_target="tpu_custom_call" | custom-call | flops 805306368 | bytes 5898240 | tf_op jit(solution)/shard_map/pallas_call | solution.py:32
  36.5 4.0 %shard_map.78.g_ref = f32[6144,128]{1,0:T(8,128)S(1)} custom-call(s32[5]{0:T(128)S(1)} %stack.23.refs_0_.info, bf16[2,1280,768]{2,1,0:T(8,128)(2,1)S(1)} %get-tuple-element.55.act_ref, bf16[2,1024,256]{2,1,0:T(8,128)(2,1)S(1)} %get-tuple-element.57.pg_ref.refs_0_, bf16[2,1024,256]{2,1,0:T(8,128)(2,1)S(1)} %get-tuple-element.85.hid_ref, ...), custom_call_target="tpu_custom_call" | custom-call | flops 3221225472 | bytes 11272212 | tf_op jit(solution)/shard_map/pallas_call | solution.py:32
  40.6 0.1 slice.4
  40.7 2.7 %collective-permute-start.3 = (f32[3072,128]{1,0:T(8,128)S(1)}, f32[3072,128]{1,0:T(8,128)S(1)}, u32[]{:S(2)}, u32[]{:S(2)}) collective-permute-start(f32[3072,128]{1,0:T(8,128)S(1)} %slice.4), channel_id=1, source_target_pairs={{0,32},{32,0},{1,33},{33,1},{2,34},{34,2},{3,35},{35,3},{4,36},{36... | collective-permute-start | bytes 4718600 | tf_op jit(solution)/shard_map/ppermute | solution.py:404
  43.4 2.2 %collective-permute-start.7 = (bf16[2,128,256]{2,1,0:T(8,128)(2,1)S(1)}, bf16[2,128,256]{2,1,0:T(8,128)(2,1)S(1)}, u32[]{:S(2)}, u32[]{:S(2)}) collective-permute-start(bf16[2,128,256]{2,1,0:T(8,128)(2,1)S(1)} %get-tuple-element.66), channel_id=1, source_target_pairs={{0,1},{1,2},{2,3},{3,4},{4,5},{5,6},{6,7},{8,9},{9,10},{10,11},{11... | collective-permute-start | bytes 393224 | tf_op jit(solution)/shard_map/ppermute | solution.py:410
  45.6 1.3 %collective-permute-start.8 = (bf16[2,128,256]{2,1,0:T(8,128)(2,1)S(1)}, bf16[2,128,256]{2,1,0:T(8,128)(2,1)S(1)}, u32[]{:S(2)}, u32[]{:S(2)}) collective-permute-start(bf16[2,128,256]{2,1,0:T(8,128)(2,1)S(1)} %get-tuple-element.67), channel_id=1, source_target_pairs={{1,0},{2,1},{3,2},{4,3},{5,4},{6,5},{7,6},{9,8},{10,9},{11,10},{12... | collective-permute-start | bytes 393224 | tf_op jit(solution)/shard_map/ppermute | solution.py:410
  46.9 0.7 shard_map.79
  47.6 2.4 %collective-permute-start.4 = (bf16[768,128]{1,0:T(8,128)(2,1)S(1)}, bf16[768,128]{1,0:T(8,128)(2,1)S(1)}, u32[]{:S(2)}, u32[]{:S(2)}) collective-permute-start(bf16[768,128]{1,0:T(8,128)(2,1)S(1)} %get-tuple-element.63), channel_id=1, source_target_pairs={{0,8},{8,16},{16,24},{24,0},{1,9},{9,17},{17,25},{25,1},{2,10},{10... | collective-permute-start | bytes 589832 | tf_op jit(solution)/shard_map/ppermute | solution.py:416
  50.0 2.8 %collective-permute-start.5 = (bf16[768,128]{1,0:T(8,128)(2,1)S(1)}, bf16[768,128]{1,0:T(8,128)(2,1)S(1)}, u32[]{:S(2)}, u32[]{:S(2)}) collective-permute-start(bf16[768,128]{1,0:T(8,128)(2,1)S(1)} %get-tuple-element.64), channel_id=1, source_target_pairs={{0,16},{8,24},{16,0},{24,8},{1,17},{9,25},{17,1},{25,9},{2,18},{10... | collective-permute-start | bytes 589832 | tf_op jit(solution)/shard_map/ppermute | solution.py:416
  52.8 0.8 collective-permute-start.6
  53.6 5.9 %shard_map.80 = (f32[2,1024,256]{2,1,0:T(8,128)S(1)}, f32[1,8,128]{2,1,0:T(8,128)S(1)}) custom-call(bf16[2,1024,256]{2,1,0:T(8,128)(2,1)S(1)} %get-tuple-element.57.pg_ref.refs_0_, bf16[2,128,256]{2,1,0:T(8,128)(2,1)S(1)} %collective-permute-done.7.refs_1_, bf16[2,128,256]{2,1,0:T(8,128)(2,1)S(1)} %collective-permute-done.8.refs_2_, ...), custom_call_target="tpu_custom_call" | custom-call | flops 2415919104 | bytes 5672960 | tf_op jit(solution)/shard_map/pallas_call | solution.py:32
  59.5 1.3 %copy-done.2 = f32[2,1024,256]{2,1,0:T(8,128)} copy-done((f32[2,1024,256]{2,1,0:T(8,128)}, f32[2,1024,256]{2,1,0:T(8,128)S(1)}, u32[]{:S(2)}) %copy-start.2) | copy-done | bytes 2097176
  60.8 0.9 collective-permute-done.5.b_ref
  61.7 0.7 shard_map.81
  62.4 1.4 %collective-permute-start.9 = (f32[192,128]{1,0:T(8,128)S(1)}, f32[192,128]{1,0:T(8,128)S(1)}, u32[]{:S(2)}, u32[]{:S(2)}) collective-permute-start(f32[192,128]{1,0:T(8,128)S(1)} %get-tuple-element.73), channel_id=1, source_target_pairs={{0,64},{64,128},{128,192},{192,0},{1,65},{65,129},{129,193},{193,1... | collective-permute-start | bytes 294920 | tf_op jit(solution)/shard_map/ppermute | solution.py:416
  63.8 2.6 %collective-permute-start.10 = (f32[192,128]{1,0:T(8,128)S(1)}, f32[192,128]{1,0:T(8,128)S(1)}, u32[]{:S(2)}, u32[]{:S(2)}) collective-permute-start(f32[192,128]{1,0:T(8,128)S(1)} %get-tuple-element.74), channel_id=1, source_target_pairs={{0,128},{64,192},{128,0},{192,64},{1,129},{65,193},{129,1},{193,65... | collective-permute-start | bytes 294920 | tf_op jit(solution)/shard_map/ppermute | solution.py:416
  66.4 1.1 collective-permute-start.11
  67.5 2.5 %collective-permute-done.10.b_ref = f32[192,128]{1,0:T(8,128)S(1)} collective-permute-done((f32[192,128]{1,0:T(8,128)S(1)}, f32[192,128]{1,0:T(8,128)S(1)}, u32[]{:S(2)}, u32[]{:S(2)}) %collective-permute-start.10) | collective-permute-done | bytes 98336 | tf_op jit(solution)/shard_map/ppermute | solution.py:416
  70.0 1.1 collective-permute-done.11.c_ref
  71.1 0.1 shard_map.82
  71.1 2.6 %collective-permute-start.15 = (bf16[2,1024,256]{2,1,0:T(8,128)(2,1)S(1)}, bf16[2,1024,256]{2,1,0:T(8,128)(2,1)S(1)}, u32[]{:S(2)}, u32[]{:S(2)}) collective-permute-start(bf16[2,1024,256]{2,1,0:T(8,128)(2,1)S(1)} %get-tuple-element.85.hid_ref), channel_id=1, source_target_pairs={{0,8},{8,16},{16,24},{1,9},{9,17},{17,25},{2,10},{10,18},{18,26},{... | collective-permute-start | bytes 3145736 | tf_op jit(solution)/shard_map/ppermute | solution.py:410
  73.8 17.6 %all_to_all.10.u_ref = bf16[8,224,128]{2,1,0:T(8,128)(2,1)S(1)} all-to-all(bf16[8,224,128]{2,1,0:T(8,128)(2,1)S(1)} %shard_map.82), channel_id=1, replica_groups=mesh['y'=4,'core'=2,'tm'=4,'height'=8] {'height'}, dimensions={0} | all-to-all | bytes 917504 | tf_op jit(solution)/shard_map/all_to_all | solution.py:495
  91.4 0.5 shard_map.83
  91.8 2.1 %collective-permute-start.14 = (bf16[192,128]{1,0:T(8,128)(2,1)S(1)}, bf16[192,128]{1,0:T(8,128)(2,1)S(1)}, u32[]{:S(2)}, u32[]{:S(2)}) collective-permute-start(bf16[192,128]{1,0:T(8,128)(2,1)S(1)} %get-tuple-element.81), channel_id=1, source_target_pairs={{0,192},{64,0},{128,64},{192,128},{1,193},{65,1},{129,65},{193,129... | collective-permute-start | bytes 147464 | tf_op jit(solution)/shard_map/ppermute | solution.py:416
  94.0 0.7 collective-permute-start.13
  94.7 3.6 %shard_map.84 = bf16[2,1024,256]{2,1,0:T(8,128)(2,1)} custom-call(bf16[2,1024,256]{2,1,0:T(8,128)(2,1)S(1)} %bitcast.14, bf16[2,1024,256]{2,1,0:T(8,128)(2,1)S(1)} %bitcast.19, f32[2,1024,256]{2,1,0:T(8,128)} %copy-done.2, f32[8,8,128]{2,1,0:T(8,128)} %copy-done.4, f32[1,8,128]{2,1,0:T(8,128)S(1)} %get-tuple-element.87.refs_4_), custom_call_target="tpu_custom_call" | custom-call | flops 2097152 | bytes 5279744 | tf_op jit(solution)/shard_map/pallas_call | solution.py:32
  98.2 0.2 collective-permute-done.13
  98.4 0.5 collective-permute-done.12
  99.0 2.1 %collective-permute-start.18 = (bf16[768,128]{1,0:T(8,128)(2,1)S(1)}, bf16[768,128]{1,0:T(8,128)(2,1)S(1)}, u32[]{:S(2)}, u32[]{:S(2)}) collective-permute-start(bf16[768,128]{1,0:T(8,128)(2,1)S(1)} %pad_maximum_fusion.1), channel_id=1, source_target_pairs={{0,24},{8,0},{16,8},{24,16},{1,25},{9,1},{17,9},{25,17},{2,26},{10... | collective-permute-start | bytes 589832 | tf_op jit(solution)/shard_map/ppermute | solution.py:416
  101.1 1.9 %collective-permute-start.17 = (bf16[768,128]{1,0:T(8,128)(2,1)S(1)}, bf16[768,128]{1,0:T(8,128)(2,1)S(1)}, u32[]{:S(2)}, u32[]{:S(2)}) collective-permute-start(bf16[768,128]{1,0:T(8,128)(2,1)S(1)} %pad_maximum_fusion.1), channel_id=1, source_target_pairs={{0,16},{8,24},{16,0},{24,8},{1,17},{9,25},{17,1},{25,9},{2,18},{10... | collective-permute-start | bytes 589832 | tf_op jit(solution)/shard_map/ppermute | solution.py:416
  103.0 0.8 collective-permute-start.16
  103.7 2.5 %shard_map.85 = bf16[2,1024,256]{2,1,0:T(8,128)(2,1)} custom-call(bf16[2,1024,256]{2,1,0:T(8,128)(2,1)S(1)} %bitcast.15, bf16[2,1024,256]{2,1,0:T(8,128)(2,1)S(1)} %get-tuple-element.85.hid_ref, bf16[2,1024,256]{2,1,0:T(8,128)(2,1)S(1)} %collective-permute-done.15.prev_ref, bf16[3,256,256]{2,1,0:T(8,128)(2,1)S(1)} %copy-done.3), custom_call_target="tpu_custom_call" | custom-call | flops 805306368 | bytes 4587520 | tf_op jit(solution)/shard_map/pallas_call | solution.py:32
  106.2 0.9 collective-permute-done.17
  107.2 2.1 %collective-permute-done.16 = bf16[768,128]{1,0:T(8,128)(2,1)S(1)} collective-permute-done((bf16[768,128]{1,0:T(8,128)(2,1)S(1)}, bf16[768,128]{1,0:T(8,128)(2,1)S(1)}, u32[]{:S(2)}, u32[]{:S(2)}) %collective-permute-start.16) | collective-permute-done | bytes 196640 | tf_op jit(solution)/shard_map/ppermute | solution.py:416
  109.2 0.1 pad_maximum_fusion.u_ref
  109.3 6.2 %collective-permute-start.19 = (bf16[3072,128]{1,0:T(8,128)(2,1)S(1)}, bf16[3072,128]{1,0:T(8,128)(2,1)S(1)}, u32[]{:S(2)}, u32[]{:S(2)}) collective-permute-start(bf16[3072,128]{1,0:T(8,128)(2,1)S(1)} %pad_maximum_fusion.u_ref), channel_id=1, source_target_pairs={{0,32},{32,0},{1,33},{33,1},{2,34},{34,2},{3,35},{35,3},{4,36},{36... | collective-permute-start | bytes 2359304 | tf_op jit(solution)/shard_map/ppermute | solution.py:404
  115.5 1.4 %shard_map.86 = (f32[3072,128]{1,0:T(8,128)S(1)}, f32[8,128]{1,0:T(8,128)S(1)}) custom-call(s32[5]{0:T(128)S(1)} %stack.23.refs_0_.info, bf16[3072,128]{1,0:T(8,128)(2,1)S(1)} %pad_maximum_fusion.u_ref), custom_call_target="tpu_custom_call" | custom-call | flops 2097152 | bytes 2363412 | tf_op jit(solution)/shard_map/pallas_call | solution.py:32
  116.8 0.5 collective-permute-done.19.refs_3_
  117.4 3.3 %shard_map.87 = (f32[9,256,256]{2,1,0:T(8,128)}, f32[3,256,256]{2,1,0:T(8,128)}) custom-call(s32[5]{0:T(128)S(1)} %stack.23.refs_0_.info, f32[3072,128]{1,0:T(8,128)S(1)} %get-tuple-element.96.refs_1_, f32[8,128]{1,0:T(8,128)S(1)} %get-tuple-element.97.refs_2_, bf16[3072,128]{1,0:T(8,128)(2,1)S(1)} %collective-permute-done.19.refs_3_), custom_call_target="tpu_custom_call" | custom-call | flops 2097152 | bytes 5509140 | tf_op jit(solution)/shard_map/pallas_call | solution.py:32
  (26 shorter events, 0.2 us)
Async XLA Ops:
  0.6 34.2 %collective-permute-start.2 = (bf16[2,1024,256]{2,1,0:T(8,128)(2,1)}, bf16[2,1024,256]{2,1,0:T(8,128)(2,1)S(1)}, u32[]{:S(2)}, u32[]{:S(2)}) collective-permute-start(bf16[2,1024,256]{2,1,0:T(8,128)(2,1)} %bitcast.16), channel_id=1, source_target_pairs={{8,0},{16,8},{24,16},{9,1},{17,9},{25,17},{10,2},{18,10},{26,18},{... | collective-permute-start | bytes 3145736 | tf_op jit(solution)/shard_map/ppermute | solution.py:410
  4.1 22.4 %collective-permute-start = (bf16[2,128,256]{2,1,0:T(8,128)(2,1)S(1)}, bf16[2,128,256]{2,1,0:T(8,128)(2,1)S(1)}, u32[]{:S(2)}, u32[]{:S(2)}) collective-permute-start(bf16[2,128,256]{2,1,0:T(8,128)(2,1)S(1)} %get-tuple-element.52), channel_id=1, source_target_pairs={{0,1},{1,2},{2,3},{3,4},{4,5},{5,6},{6,7},{8,9},{9,10},{10,11},{11... | collective-permute-start | bytes 393224 | tf_op jit(solution)/shard_map/ppermute | solution.py:410
  8.5 18.1 %collective-permute-start.1 = (bf16[2,128,256]{2,1,0:T(8,128)(2,1)S(1)}, bf16[2,128,256]{2,1,0:T(8,128)(2,1)S(1)}, u32[]{:S(2)}, u32[]{:S(2)}) collective-permute-start(bf16[2,128,256]{2,1,0:T(8,128)(2,1)S(1)} %get-tuple-element.53), channel_id=1, source_target_pairs={{1,0},{2,1},{3,2},{4,3},{5,4},{6,5},{7,6},{9,8},{10,9},{11,10},{12... | collective-permute-start | bytes 393224 | tf_op jit(solution)/shard_map/ppermute | solution.py:410
  9.8 16.8 %all-to-all-start = ((f32[8,8,128]{2,1,0:T(8,128)}), f32[8,8,128]{2,1,0:T(8,128)S(1)}, u32[]{:S(2)}, u32[]{:S(2)}) async-start(f32[8,8,128]{2,1,0:T(8,128)} %get-tuple-element.54), calls=%async_computation | async-start | bytes 65536 | tf_op jit(solution)/shard_map/all_to_all | solution.py:449
  26.6 0.6 copy-start.4
  26.6 0.7 copy-start.5
  26.6 0.7 copy-start.6
  27.3 7.6 %copy-start.1 = (bf16[1,2,8,128,256]{4,3,2,1,0:T(8,128)(2,1)S(1)}, bf16[1,2,8,128,256]{4,3,2,1,0:T(8,128)(2,1)}, u32[]{:S(2)}) copy-start(bf16[1,2,8,128,256]{4,3,2,1,0:T(8,128)(2,1)} %param.5) | copy-start | bytes 3145732
  27.3 7.6 %copy-start.3 = (bf16[3,256,256]{2,1,0:T(8,128)(2,1)S(1)}, bf16[3,256,256]{2,1,0:T(8,128)(2,1)}, u32[]{:S(2)}) copy-start(bf16[3,256,256]{2,1,0:T(8,128)(2,1)} %w_ref.3) | copy-start | bytes 1179652
  40.7 6.2 %collective-permute-start.3 = (f32[3072,128]{1,0:T(8,128)S(1)}, f32[3072,128]{1,0:T(8,128)S(1)}, u32[]{:S(2)}, u32[]{:S(2)}) collective-permute-start(f32[3072,128]{1,0:T(8,128)S(1)} %slice.4), channel_id=1, source_target_pairs={{0,32},{32,0},{1,33},{33,1},{2,34},{34,2},{3,35},{35,3},{4,36},{36... | collective-permute-start | bytes 4718600 | tf_op jit(solution)/shard_map/ppermute | solution.py:404
  43.4 10.2 %collective-permute-start.7 = (bf16[2,128,256]{2,1,0:T(8,128)(2,1)S(1)}, bf16[2,128,256]{2,1,0:T(8,128)(2,1)S(1)}, u32[]{:S(2)}, u32[]{:S(2)}) collective-permute-start(bf16[2,128,256]{2,1,0:T(8,128)(2,1)S(1)} %get-tuple-element.66), channel_id=1, source_target_pairs={{0,1},{1,2},{2,3},{3,4},{4,5},{5,6},{6,7},{8,9},{9,10},{10,11},{11... | collective-permute-start | bytes 393224 | tf_op jit(solution)/shard_map/ppermute | solution.py:410
  45.6 8.0 %collective-permute-start.8 = (bf16[2,128,256]{2,1,0:T(8,128)(2,1)S(1)}, bf16[2,128,256]{2,1,0:T(8,128)(2,1)S(1)}, u32[]{:S(2)}, u32[]{:S(2)}) collective-permute-start(bf16[2,128,256]{2,1,0:T(8,128)(2,1)S(1)} %get-tuple-element.67), channel_id=1, source_target_pairs={{1,0},{2,1},{3,2},{4,3},{5,4},{6,5},{7,6},{9,8},{10,9},{11,10},{12... | collective-permute-start | bytes 393224 | tf_op jit(solution)/shard_map/ppermute | solution.py:410
  47.6 13.3 %collective-permute-start.4 = (bf16[768,128]{1,0:T(8,128)(2,1)S(1)}, bf16[768,128]{1,0:T(8,128)(2,1)S(1)}, u32[]{:S(2)}, u32[]{:S(2)}) collective-permute-start(bf16[768,128]{1,0:T(8,128)(2,1)S(1)} %get-tuple-element.63), channel_id=1, source_target_pairs={{0,8},{8,16},{16,24},{24,0},{1,9},{9,17},{17,25},{25,1},{2,10},{10... | collective-permute-start | bytes 589832 | tf_op jit(solution)/shard_map/ppermute | solution.py:416
  50.0 11.7 %collective-permute-start.5 = (bf16[768,128]{1,0:T(8,128)(2,1)S(1)}, bf16[768,128]{1,0:T(8,128)(2,1)S(1)}, u32[]{:S(2)}, u32[]{:S(2)}) collective-permute-start(bf16[768,128]{1,0:T(8,128)(2,1)S(1)} %get-tuple-element.64), channel_id=1, source_target_pairs={{0,16},{8,24},{16,0},{24,8},{1,17},{9,25},{17,1},{25,9},{2,18},{10... | collective-permute-start | bytes 589832 | tf_op jit(solution)/shard_map/ppermute | solution.py:416
  52.8 8.9 %collective-permute-start.6 = (bf16[768,128]{1,0:T(8,128)(2,1)S(1)}, bf16[768,128]{1,0:T(8,128)(2,1)S(1)}, u32[]{:S(2)}, u32[]{:S(2)}) collective-permute-start(bf16[768,128]{1,0:T(8,128)(2,1)S(1)} %get-tuple-element.65), channel_id=1, source_target_pairs={{0,24},{8,0},{16,8},{24,16},{1,25},{9,1},{17,9},{25,17},{2,26},{10... | collective-permute-start | bytes 589832 | tf_op jit(solution)/shard_map/ppermute | solution.py:416
  59.5 1.3 %copy-start.2 = (f32[2,1024,256]{2,1,0:T(8,128)}, f32[2,1024,256]{2,1,0:T(8,128)S(1)}, u32[]{:S(2)}) copy-start(f32[2,1024,256]{2,1,0:T(8,128)S(1)} %get-tuple-element.86.refs_2_) | copy-start | bytes 6291460
  61.7 33.0 %copy-start = (bf16[1,2,8,128,256]{4,3,2,1,0:T(8,128)(2,1)S(1)}, bf16[1,2,8,128,256]{4,3,2,1,0:T(8,128)(2,1)}, u32[]{:S(2)}) copy-start(bf16[1,2,8,128,256]{4,3,2,1,0:T(8,128)(2,1)} %param.4) | copy-start | bytes 3145732
  62.4 5.1 %collective-permute-start.9 = (f32[192,128]{1,0:T(8,128)S(1)}, f32[192,128]{1,0:T(8,128)S(1)}, u32[]{:S(2)}, u32[]{:S(2)}) collective-permute-start(f32[192,128]{1,0:T(8,128)S(1)} %get-tuple-element.73), channel_id=1, source_target_pairs={{0,64},{64,128},{128,192},{192,0},{1,65},{65,129},{129,193},{193,1... | collective-permute-start | bytes 294920 | tf_op jit(solution)/shard_map/ppermute | solution.py:416
  63.8 6.2 %collective-permute-start.10 = (f32[192,128]{1,0:T(8,128)S(1)}, f32[192,128]{1,0:T(8,128)S(1)}, u32[]{:S(2)}, u32[]{:S(2)}) collective-permute-start(f32[192,128]{1,0:T(8,128)S(1)} %get-tuple-element.74), channel_id=1, source_target_pairs={{0,128},{64,192},{128,0},{192,64},{1,129},{65,193},{129,1},{193,65... | collective-permute-start | bytes 294920 | tf_op jit(solution)/shard_map/ppermute | solution.py:416
  66.4 4.6 %collective-permute-start.11 = (f32[192,128]{1,0:T(8,128)S(1)}, f32[192,128]{1,0:T(8,128)S(1)}, u32[]{:S(2)}, u32[]{:S(2)}) collective-permute-start(f32[192,128]{1,0:T(8,128)S(1)} %get-tuple-element.75), channel_id=1, source_target_pairs={{0,192},{64,0},{128,64},{192,128},{1,193},{65,1},{129,65},{193,129... | collective-permute-start | bytes 294920 | tf_op jit(solution)/shard_map/ppermute | solution.py:416
  71.1 27.8 %collective-permute-start.15 = (bf16[2,1024,256]{2,1,0:T(8,128)(2,1)S(1)}, bf16[2,1024,256]{2,1,0:T(8,128)(2,1)S(1)}, u32[]{:S(2)}, u32[]{:S(2)}) collective-permute-start(bf16[2,1024,256]{2,1,0:T(8,128)(2,1)S(1)} %get-tuple-element.85.hid_ref), channel_id=1, source_target_pairs={{0,8},{8,16},{16,24},{1,9},{9,17},{17,25},{2,10},{10,18},{18,26},{... | collective-permute-start | bytes 3145736 | tf_op jit(solution)/shard_map/ppermute | solution.py:410
  91.8 6.4 %collective-permute-start.14 = (bf16[192,128]{1,0:T(8,128)(2,1)S(1)}, bf16[192,128]{1,0:T(8,128)(2,1)S(1)}, u32[]{:S(2)}, u32[]{:S(2)}) collective-permute-start(bf16[192,128]{1,0:T(8,128)(2,1)S(1)} %get-tuple-element.81), channel_id=1, source_target_pairs={{0,192},{64,0},{128,64},{192,128},{1,193},{65,1},{129,65},{193,129... | collective-permute-start | bytes 147464 | tf_op jit(solution)/shard_map/ppermute | solution.py:416
  94.0 4.5 %collective-permute-start.13 = (bf16[192,128]{1,0:T(8,128)(2,1)S(1)}, bf16[192,128]{1,0:T(8,128)(2,1)S(1)}, u32[]{:S(2)}, u32[]{:S(2)}) collective-permute-start(bf16[192,128]{1,0:T(8,128)(2,1)S(1)} %get-tuple-element.81), channel_id=1, source_target_pairs={{0,128},{64,192},{128,0},{192,64},{1,129},{65,193},{129,1},{193,65... | collective-permute-start | bytes 147464 | tf_op jit(solution)/shard_map/ppermute | solution.py:416
  94.7 4.3 %collective-permute-start.12 = (bf16[192,128]{1,0:T(8,128)(2,1)S(1)}, bf16[192,128]{1,0:T(8,128)(2,1)S(1)}, u32[]{:S(2)}, u32[]{:S(2)}) collective-permute-start(bf16[192,128]{1,0:T(8,128)(2,1)S(1)} %get-tuple-element.81), channel_id=1, source_target_pairs={{0,64},{64,128},{128,192},{192,0},{1,65},{65,129},{129,193},{193,1... | collective-permute-start | bytes 147464 | tf_op jit(solution)/shard_map/ppermute | solution.py:416
  99.0 7.3 %collective-permute-start.18 = (bf16[768,128]{1,0:T(8,128)(2,1)S(1)}, bf16[768,128]{1,0:T(8,128)(2,1)S(1)}, u32[]{:S(2)}, u32[]{:S(2)}) collective-permute-start(bf16[768,128]{1,0:T(8,128)(2,1)S(1)} %pad_maximum_fusion.1), channel_id=1, source_target_pairs={{0,24},{8,0},{16,8},{24,16},{1,25},{9,1},{17,9},{25,17},{2,26},{10... | collective-permute-start | bytes 589832 | tf_op jit(solution)/shard_map/ppermute | solution.py:416
  101.1 6.1 %collective-permute-start.17 = (bf16[768,128]{1,0:T(8,128)(2,1)S(1)}, bf16[768,128]{1,0:T(8,128)(2,1)S(1)}, u32[]{:S(2)}, u32[]{:S(2)}) collective-permute-start(bf16[768,128]{1,0:T(8,128)(2,1)S(1)} %pad_maximum_fusion.1), channel_id=1, source_target_pairs={{0,16},{8,24},{16,0},{24,8},{1,17},{9,25},{17,1},{25,9},{2,18},{10... | collective-permute-start | bytes 589832 | tf_op jit(solution)/shard_map/ppermute | solution.py:416
  103.0 6.2 %collective-permute-start.16 = (bf16[768,128]{1,0:T(8,128)(2,1)S(1)}, bf16[768,128]{1,0:T(8,128)(2,1)S(1)}, u32[]{:S(2)}, u32[]{:S(2)}) collective-permute-start(bf16[768,128]{1,0:T(8,128)(2,1)S(1)} %pad_maximum_fusion.1), channel_id=1, source_target_pairs={{0,8},{8,16},{16,24},{24,0},{1,9},{9,17},{17,25},{25,1},{2,10},{10... | collective-permute-start | bytes 589832 | tf_op jit(solution)/shard_map/ppermute | solution.py:416
  109.3 8.1 %collective-permute-start.19 = (bf16[3072,128]{1,0:T(8,128)(2,1)S(1)}, bf16[3072,128]{1,0:T(8,128)(2,1)S(1)}, u32[]{:S(2)}, u32[]{:S(2)}) collective-permute-start(bf16[3072,128]{1,0:T(8,128)(2,1)S(1)} %pad_maximum_fusion.u_ref), channel_id=1, source_target_pairs={{0,32},{32,0},{1,33},{33,1},{2,34},{34,2},{3,35},{35,3},{4,36},{36... | collective-permute-start | bytes 2359304 | tf_op jit(solution)/shard_map/ppermute | solution.py:404

commit v7 on v6

--- a/solution.py
+++ b/solution.py
@@ -22,18 +22,19 @@
 VMEM = pl.BlockSpec(memory_space=pltpu.VMEM)
 SMEM = pl.BlockSpec(memory_space=pltpu.SMEM)
 ANY = pl.BlockSpec(memory_space=pl.ANY)
+HBM = pl.BlockSpec(memory_space=pltpu.HBM)
 NT = (((1,), (1,)), ((), ()))
 TN = (((0,), (0,)), ((), ()))
 
 
-def call(kernel, outs, args, flops, scratch=(), smem=0, limit=16, loose=(), outside=False):
+def call(kernel, outs, args, flops, scratch=(), smem=0, limit=16, loose=(), outside=()):
     nbytes = sum(a.size * a.dtype.itemsize for a in (*args, *outs))
     specs = [SMEM] * smem + [ANY if i in loose else VMEM for i in range(smem, len(args))]
     return pl.pallas_call(
         kernel,
-        out_shape=tuple(outs),
+        out_shape=tuple(pltpu.HBM(o.shape, o.dtype) if i in outside else o for i, o in enumerate(outs)),
         in_specs=specs,
-        out_specs=tuple(ANY if outside else VMEM for _ in outs),
+        out_specs=tuple(HBM if i in outside else VMEM for i in range(len(outs))),
         scratch_shapes=list(scratch),
         compiler_params=pltpu.CompilerParams(vmem_limit_bytes=limit << 20),
         cost_estimate=pl.CostEstimate(flops=flops, bytes_accessed=nbytes, transcendentals=0),
@@ -123,8 +124,11 @@
 
 
 def forward_kernel(
-    members, info, x_ref, up_hbm, dn_hbm, st_hbm, w_ref, act_ref, hid_ref, slope_ref, up_ref, dn_ref, st_ref, sems
+    members, info, x_ref, up_hbm, dn_hbm, st_hbm, w_hbm, act_ref, hid_ref, slope_ref,
+    up_ref, dn_ref, st_ref, w_ref, sems,
 ):
+    weights = pltpu.make_async_copy(w_hbm, w_ref, sems.at[3])
+    weights.start()
     fetched((st_hbm, st_ref), (up_hbm, up_ref), (dn_hbm, dn_ref), sems=sems)
     keep_up = (info[1] > 0).astype(F32)
     keep_dn = (info[2] > 0).astype(F32)
@@ -152,6 +156,8 @@
             return 0
 
         lax.fori_loop(0, 8, line, 0)
+        if f == 0:
+            weights.wait()
 
         def conv(r, _):
             at = pl.multiple_of(r * 512, 512)
@@ -219,11 +225,18 @@
         put(9 + k, v)
 
 
-def backward_kernel(members, pg_ref, up_ref, dn_ref, w_ref, x_ref, st_ref, ng_ref, o_ref, a_ref, b_ref, c_ref):
-    stats = moments(st_ref, members)
+def backward_kernel(
+    members, pg_ref, up_ref, dn_ref, w_hbm, x_hbm, st_hbm, ng_hbm, o_ref,
+    a_ref, b_ref, c_ref, w_ref, x_ref, st_ref, ng_ref, sems,
+):
+    loads = [(w_hbm, w_ref), (x_hbm, x_ref), (st_hbm, st_ref)]
+    loads = [pltpu.make_async_copy(a, b, sems.at[i]) for i, (a, b) in enumerate(loads)]
+    for c in loads:
+        c.start()
+    stats = None
+    stores = []
     sums = []
     for f in range(2):
-        mean, inv = stats[f]
 
         def put(v, row):
             v = v.astype(F32)
@@ -242,6 +255,11 @@
             return 0
 
         lax.fori_loop(0, 8, line, 0)
+        if f == 0:
+            for c in loads:
+                c.wait()
+            stats = moments(st_ref, members)
+        mean, inv = stats[f]
 
         def conv(r, carry):
             at = pl.multiple_of(r * 512, 512)
@@ -259,7 +277,11 @@
 
         zero = jnp.zeros((8, 256), F32)
         sums.append(lax.fori_loop(0, 2, conv, (zero, zero)))
+        stores.append(pltpu.make_async_copy(ng_ref.at[f], ng_hbm.at[f], sems.at[3 + f]))
+        stores[-1].start()
     store_stats(o_ref, sums)
+    for c in stores:
+        c.wait()
 
 
 def input_grad_kernel(members, x_ref, cot_ref, ng_ref, st_ref, gst_ref, o_ref):
@@ -456,12 +478,13 @@
         [info, in_hbm(x), up, dn, st, in_hbm(w3)],
         9 * gflop,
         smem=1,
-        loose=(2, 3, 4),
+        loose=(2, 3, 4, 5),
         scratch=[
             pltpu.VMEM(edge.shape, BF16),
             pltpu.VMEM(edge.shape, BF16),
             pltpu.VMEM(small.shape, F32),
-            pltpu.SemaphoreType.DMA((3,)),
+            pltpu.VMEM(w3.shape, BF16),
+            pltpu.SemaphoreType.DMA((4,)),
         ],
     )
     pg, top, bot = call(
@@ -482,18 +505,28 @@
     ng, gst = call(
         lambda *refs: backward_kernel(members, *refs),
         [out(flat, F32), out((1, 8, 128), F32)],
-        [pg, gup, gdn, in_hbm(w9), in_hbm(x), in_hbm(st)],
+        [pg, gup, gdn, in_hbm(w9), in_hbm(x), st],
         9 * gflop,
-        scratch=[pltpu.VMEM((2, 1280, 256), BF16)] * 3,
+        loose=(3, 4, 5),
+        outside=(0,),
+        scratch=[pltpu.VMEM((2, 1280, 256), BF16)] * 3
+        + [
+            pltpu.VMEM(w9.shape, BF16),
+            pltpu.VMEM(flat, BF16),
+            pltpu.VMEM(small.shape, F32),
+            pltpu.VMEM(flat, F32),
+            pltpu.SemaphoreType.DMA((5,)),
+        ],
     )
     got, gst = tied((got, gst))
     part = out((192, 128), F32)
     own, *sent = call(x_kernel, [part] * 4, [own, *got], 1 << 21)
-    got = tied(shifts(sent, "y"))
+    own, sent, hid_sent = tied((own, sent, hid))
+    prev = moved(hid_sent, TM, 1)
+    got = shifts(sent, "y")
+    got = tied(got)
     (pieces,) = call(y_kernel, [out((8, 224, 128), BF16)], [own, *got, gst], 1 << 20)
-    pieces, hid_sent = tied((pieces, hid))
     pieces = lax.all_to_all(pieces, HEIGHT, 0, 0, tiled=True)
-    prev = moved(hid_sent, TM, 1)
     mine, gst = call(z_kernel, [out((192, 128), BF16), out((1, 8, 128), F32)], [pieces], 1 << 20)
     (input_grad,) = call(
         lambda *refs: input_grad_kernel(members, *refs),
@@ -515,7 +548,7 @@
         [info, own, acc, swapped(mine, "core")],
         1 << 21,
         smem=1,
-        outside=True,
+        outside=(0, 1),
         scratch=[
             pltpu.VMEM((12, 256, 256), F32),
             pltpu.VMEM(slab, F32),

time: 121 us -> 120 us (level)
  local copies, waits for them, and re-layouts: 2.2 us -> 0.89 us
    unnamed x14 -> x12, local copies, waits for them, and re-layouts: 2.01 us -> 0.7 us
    ppermute x12, waiting for transfers between devices: 8.15 us -> 6.94 us  [shifts(): lax.ppermute(m, axis, [(i, (i + d) % n) for i in range(n)])]
  transfers between devices with their start and end apart: 21 -> 21, of which waited for: 9 -> 9; matrix products, arithmetic and copies ran while one was open for 0% -> 0% of each run, Pallas kernels for 20% -> 21%
where the time goes in v7:
time: 120 us
  starting transfers between devices  51.4 us (43%)
  Pallas kernels  34.6 us (29%)
  blocking collectives  17.2 us (14%)
  waiting for transfers between devices  14.3 us (12%)
    pallas_call x13, Pallas kernels, call(): pl.pallas_call(kernel, out_shape=tuple((pltpu.HBM(o.shape, o.dtype) if i...  34.6 us
    ppermute x12, starting transfers between devices, shifts(): lax.ppermute(m, axis, [(i, (i + d) % n) for i in range(n)])  18.8 us
    all_to_all x1, blocking collectives, body(): pieces = lax.all_to_all(pieces, HEIGHT, 0, 0, tiled=True)  17.2 us
    ppermute x6, starting transfers between devices, moved(): return lax.ppermute(x, axes, route)  13.6 us
    all_to_all x1, starting transfers between devices, body(): st = in_hbm(lax.all_to_all(st, HEIGHT, 0, 0, tiled=True))  9.85 us
    ppermute x2, starting transfers between devices, swapped(): return lax.ppermute(x, axis, [(0, 1), (1, 0)])  9.18 us
    ppermute x12, waiting for transfers between devices, shifts(): lax.ppermute(m, axis, [(i, (i + d) % n) for i in range(n)])  6.94 us
    all_to_all x1, waiting for transfers between devices, body(): st = in_hbm(lax.all_to_all(st, HEIGHT, 0, 0, tiled=True))  6.83 us
  transfers between devices with their start and end apart: 21, of which 9 were waited for; matrix products, arithmetic and copies ran while one was open for 0% of the time, Pallas kernels for 21%

profile of v7, /device:TPU:1, one launch (start us, length us, event | category | flops | bytes accessed | tf_op | source)
XLA Modules:
  0.0 119.5 jit_solution(15627949717380194830)
XLA Ops:
  0.6 1.3 %collective-permute-start.2 = (bf16[2,1024,256]{2,1,0:T(8,128)(2,1)}, bf16[2,1024,256]{2,1,0:T(8,128)(2,1)S(1)}, u32[]{:S(2)}, u32[]{:S(2)}) collective-permute-start(bf16[2,1024,256]{2,1,0:T(8,128)(2,1)} %bitcast.16), channel_id=1, source_target_pairs={{8,0},{16,8},{24,16},{9,1},{17,9},{25,17},{10,2},{18,10},{26,18},{... | collective-permute-start | bytes 3145736 | tf_op jit(solution)/shard_map/ppermute | solution.py:432
  1.9 2.2 %shard_map.75 = (f32[8,8,128]{2,1,0:T(8,128)}, bf16[2,128,256]{2,1,0:T(8,128)(2,1)S(1)}, bf16[2,128,256]{2,1,0:T(8,128)(2,1)S(1)}) custom-call(bf16[2,1024,256]{2,1,0:T(8,128)(2,1)} %bitcast.11), custom_call_target="tpu_custom_call" | custom-call | flops 2097152 | bytes 1343488 | tf_op jit(solution)/shard_map/pallas_call | solution.py:33
  4.1 4.4 %collective-permute-start = (bf16[2,128,256]{2,1,0:T(8,128)(2,1)S(1)}, bf16[2,128,256]{2,1,0:T(8,128)(2,1)S(1)}, u32[]{:S(2)}, u32[]{:S(2)}) collective-permute-start(bf16[2,128,256]{2,1,0:T(8,128)(2,1)S(1)} %get-tuple-element.55), channel_id=1, source_target_pairs={{0,1},{1,2},{2,3},{3,4},{4,5},{5,6},{6,7},{8,9},{9,10},{10,11},{11... | collective-permute-start | bytes 393224 | tf_op jit(solution)/shard_map/ppermute | solution.py:432
  8.5 1.3 %collective-permute-start.1 = (bf16[2,128,256]{2,1,0:T(8,128)(2,1)S(1)}, bf16[2,128,256]{2,1,0:T(8,128)(2,1)S(1)}, u32[]{:S(2)}, u32[]{:S(2)}) collective-permute-start(bf16[2,128,256]{2,1,0:T(8,128)(2,1)S(1)} %get-tuple-element.56), channel_id=1, source_target_pairs={{1,0},{2,1},{3,2},{4,3},{5,4},{6,5},{7,6},{9,8},{10,9},{11,10},{12... | collective-permute-start | bytes 393224 | tf_op jit(solution)/shard_map/ppermute | solution.py:432
  9.8 9.8 %all-to-all-start = ((f32[8,8,128]{2,1,0:T(8,128)}), f32[8,8,128]{2,1,0:T(8,128)S(1)}, u32[]{:S(2)}, u32[]{:S(2)}) async-start(f32[8,8,128]{2,1,0:T(8,128)} %get-tuple-element.57), calls=%async_computation | async-start | bytes 65536 | tf_op jit(solution)/shard_map/all_to_all | solution.py:471
  19.6 0.1 stack.23.refs_0_.info
  19.7 6.8 %all-to-all-done.refs_4_.refs_5_.refs_3_ = f32[8,8,128]{2,1,0:T(8,128)S(1)} async-done(((f32[8,8,128]{2,1,0:T(8,128)}), f32[8,8,128]{2,1,0:T(8,128)S(1)}, u32[]{:S(2)}, u32[]{:S(2)}) %all-to-all-start) | async-done | bytes 32800 | tf_op jit(solution)/shard_map/all_to_all | solution.py:471
  26.6 0.6 copy-done.3
  27.2 0.1 copy-done.4
  27.2 0.0 copy-done.5
  27.3 7.5 %shard_map.76 = (bf16[2,1280,768]{2,1,0:T(8,128)(2,1)S(1)}, bf16[2,1024,256]{2,1,0:T(8,128)(2,1)S(1)}, f32[2,1024,256]{2,1,0:T(8,128)S(1)}) custom-call(s32[5]{0:T(128)S(1)} %stack.23.refs_0_.info, bf16[2,1024,256]{2,1,0:T(8,128)(2,1)} %bitcast.12, bf16[2,128,256]{2,1,0:T(8,128)(2,1)} %copy-done.4, bf16[2,128,256]{2,1,0:T(8,128)(2,1)} %copy-done.5, ...), custom_call_target="tpu_custom_call" | custom-call | flops 2415919104 | bytes 9601044 | tf_op jit(solution)/shard_map/pallas_call | solution.py:33
  34.8 1.6 %shard_map.77 = (bf16[2,1024,256]{2,1,0:T(8,128)(2,1)S(1)}, bf16[2,128,256]{2,1,0:T(8,128)(2,1)S(1)}, bf16[2,128,256]{2,1,0:T(8,128)(2,1)S(1)}) custom-call(bf16[2,1024,256]{2,1,0:T(8,128)(2,1)S(1)} %bitcast.17, bf16[2,1024,256]{2,1,0:T(8,128)(2,1)S(1)} %collective-permute-done.2.later_ref, f32[2,1024,256]{2,1,0:T(8,128)S(1)} %get-tuple-element.59.slope_ref, ...), custom_call_target="tpu_custom_call" | custom-call | flops 805306368 | bytes 5898240 | tf_op jit(solution)/shard_map/pallas_call | solution.py:33
  36.5 4.0 %shard_map.78.g_ref = f32[6144,128]{1,0:T(8,128)S(1)} custom-call(s32[5]{0:T(128)S(1)} %stack.23.refs_0_.info, bf16[2,1280,768]{2,1,0:T(8,128)(2,1)S(1)} %get-tuple-element.58.act_ref, bf16[2,1024,256]{2,1,0:T(8,128)(2,1)S(1)} %get-tuple-element.60.pg_ref.refs_0_, bf16[2,1024,256]{2,1,0:T(8,128)(2,1)S(1)} %get-tuple-element.91.hid_ref, ...), custom_call_target="tpu_custom_call" | custom-call | flops 3221225472 | bytes 11272212 | tf_op jit(solution)/shard_map/pallas_call | solution.py:33
  40.5 0.1 slice.4
  40.6 2.7 %collective-permute-start.3 = (f32[3072,128]{1,0:T(8,128)S(1)}, f32[3072,128]{1,0:T(8,128)S(1)}, u32[]{:S(2)}, u32[]{:S(2)}) collective-permute-start(f32[3072,128]{1,0:T(8,128)S(1)} %slice.4), channel_id=1, source_target_pairs={{0,32},{32,0},{1,33},{33,1},{2,34},{34,2},{3,35},{35,3},{4,36},{36... | collective-permute-start | bytes 4718600 | tf_op jit(solution)/shard_map/ppermute | solution.py:426
  43.4 2.2 %collective-permute-start.7 = (bf16[2,128,256]{2,1,0:T(8,128)(2,1)S(1)}, bf16[2,128,256]{2,1,0:T(8,128)(2,1)S(1)}, u32[]{:S(2)}, u32[]{:S(2)}) collective-permute-start(bf16[2,128,256]{2,1,0:T(8,128)(2,1)S(1)} %get-tuple-element.69), channel_id=1, source_target_pairs={{0,1},{1,2},{2,3},{3,4},{4,5},{5,6},{6,7},{8,9},{9,10},{10,11},{11... | collective-permute-start | bytes 393224 | tf_op jit(solution)/shard_map/ppermute | solution.py:432
  45.6 1.3 %collective-permute-start.8 = (bf16[2,128,256]{2,1,0:T(8,128)(2,1)S(1)}, bf16[2,128,256]{2,1,0:T(8,128)(2,1)S(1)}, u32[]{:S(2)}, u32[]{:S(2)}) collective-permute-start(bf16[2,128,256]{2,1,0:T(8,128)(2,1)S(1)} %get-tuple-element.70), channel_id=1, source_target_pairs={{1,0},{2,1},{3,2},{4,3},{5,4},{6,5},{7,6},{9,8},{10,9},{11,10},{12... | collective-permute-start | bytes 393224 | tf_op jit(solution)/shard_map/ppermute | solution.py:432
  46.9 0.7 shard_map.79
  47.5 2.4 %collective-permute-start.4 = (bf16[768,128]{1,0:T(8,128)(2,1)S(1)}, bf16[768,128]{1,0:T(8,128)(2,1)S(1)}, u32[]{:S(2)}, u32[]{:S(2)}) collective-permute-start(bf16[768,128]{1,0:T(8,128)(2,1)S(1)} %get-tuple-element.66), channel_id=1, source_target_pairs={{0,8},{8,16},{16,24},{24,0},{1,9},{9,17},{17,25},{25,1},{2,10},{10... | collective-permute-start | bytes 589832 | tf_op jit(solution)/shard_map/ppermute | solution.py:438
  50.0 2.8 %collective-permute-start.5 = (bf16[768,128]{1,0:T(8,128)(2,1)S(1)}, bf16[768,128]{1,0:T(8,128)(2,1)S(1)}, u32[]{:S(2)}, u32[]{:S(2)}) collective-permute-start(bf16[768,128]{1,0:T(8,128)(2,1)S(1)} %get-tuple-element.67), channel_id=1, source_target_pairs={{0,16},{8,24},{16,0},{24,8},{1,17},{9,25},{17,1},{25,9},{2,18},{10... | collective-permute-start | bytes 589832 | tf_op jit(solution)/shard_map/ppermute | solution.py:438
  52.8 0.8 collective-permute-start.6
  53.6 6.6 %shard_map.80 = (f32[2,1024,256]{2,1,0:T(8,128)}, f32[1,8,128]{2,1,0:T(8,128)S(1)}) custom-call(bf16[2,1024,256]{2,1,0:T(8,128)(2,1)S(1)} %get-tuple-element.60.pg_ref.refs_0_, bf16[2,128,256]{2,1,0:T(8,128)(2,1)S(1)} %collective-permute-done.7.refs_1_, bf16[2,128,256]{2,1,0:T(8,128)(2,1)S(1)} %collective-permute-done.8.refs_2_, ...), custom_call_target="tpu_custom_call" | custom-call | flops 2415919104 | bytes 5672960 | tf_op jit(solution)/shard_map/pallas_call | solution.py:33
  60.2 1.5 %collective-permute-done.5.b_ref = bf16[768,128]{1,0:T(8,128)(2,1)S(1)} collective-permute-done((bf16[768,128]{1,0:T(8,128)(2,1)S(1)}, bf16[768,128]{1,0:T(8,128)(2,1)S(1)}, u32[]{:S(2)}, u32[]{:S(2)}) %collective-permute-start.5) | collective-permute-done | bytes 196640 | tf_op jit(solution)/shard_map/ppermute | solution.py:438
  61.7 0.7 shard_map.81
  62.4 1.4 %collective-permute-start.9 = (f32[192,128]{1,0:T(8,128)S(1)}, f32[192,128]{1,0:T(8,128)S(1)}, u32[]{:S(2)}, u32[]{:S(2)}) collective-permute-start(f32[192,128]{1,0:T(8,128)S(1)} %get-tuple-element.80), channel_id=1, source_target_pairs={{0,64},{64,128},{128,192},{192,0},{1,65},{65,129},{129,193},{193,1... | collective-permute-start | bytes 294920 | tf_op jit(solution)/shard_map/ppermute | solution.py:438
  63.8 2.6 %collective-permute-start.10 = (f32[192,128]{1,0:T(8,128)S(1)}, f32[192,128]{1,0:T(8,128)S(1)}, u32[]{:S(2)}, u32[]{:S(2)}) collective-permute-start(f32[192,128]{1,0:T(8,128)S(1)} %get-tuple-element.81), channel_id=1, source_target_pairs={{0,128},{64,192},{128,0},{192,64},{1,129},{65,193},{129,1},{193,65... | collective-permute-start | bytes 294920 | tf_op jit(solution)/shard_map/ppermute | solution.py:438
  66.4 1.1 collective-permute-start.11
  67.5 3.2 %collective-permute-start.15 = (bf16[2,1024,256]{2,1,0:T(8,128)(2,1)S(1)}, bf16[2,1024,256]{2,1,0:T(8,128)(2,1)S(1)}, u32[]{:S(2)}, u32[]{:S(2)}) collective-permute-start(bf16[2,1024,256]{2,1,0:T(8,128)(2,1)S(1)} %get-tuple-element.91.hid_ref), channel_id=1, source_target_pairs={{0,8},{8,16},{16,24},{1,9},{9,17},{17,25},{2,10},{10,18},{18,26},{... | collective-permute-start | bytes 3145736 | tf_op jit(solution)/shard_map/ppermute | solution.py:432
  70.7 0.4 collective-permute-done.11.c_ref
  71.0 0.1 shard_map.82
  71.1 17.2 %all_to_all.10.u_ref = bf16[8,224,128]{2,1,0:T(8,128)(2,1)S(1)} all-to-all(bf16[8,224,128]{2,1,0:T(8,128)(2,1)S(1)} %shard_map.82), channel_id=1, replica_groups=mesh['y'=4,'core'=2,'tm'=4,'height'=8] {'height'}, dimensions={0} | all-to-all | bytes 917504 | tf_op jit(solution)/shard_map/all_to_all | solution.py:529
  88.3 0.5 shard_map.83
  88.7 2.1 %collective-permute-start.14 = (bf16[192,128]{1,0:T(8,128)(2,1)S(1)}, bf16[192,128]{1,0:T(8,128)(2,1)S(1)}, u32[]{:S(2)}, u32[]{:S(2)}) collective-permute-start(bf16[192,128]{1,0:T(8,128)(2,1)S(1)} %get-tuple-element.87), channel_id=1, source_target_pairs={{0,192},{64,0},{128,64},{192,128},{1,193},{65,1},{129,65},{193,129... | collective-permute-start | bytes 147464 | tf_op jit(solution)/shard_map/ppermute | solution.py:438
  90.9 0.7 collective-permute-start.12
  91.5 3.6 %shard_map.84 = bf16[2,1024,256]{2,1,0:T(8,128)(2,1)} custom-call(bf16[2,1024,256]{2,1,0:T(8,128)(2,1)S(1)} %bitcast.14, bf16[2,1024,256]{2,1,0:T(8,128)(2,1)S(1)} %bitcast.19, f32[2,1024,256]{2,1,0:T(8,128)} %get-tuple-element.92.refs_2_, f32[8,8,128]{2,1,0:T(8,128)} %copy-done.3, f32[1,8,128]{2,1,0:T(8,128)S(1)} %get-tuple-element.93.refs_4_), custom_call_target="tpu_custom_call" | custom-call | flops 2097152 | bytes 5279744 | tf_op jit(solution)/shard_map/pallas_call | solution.py:33
  95.1 0.3 collective-permute-done.13
  95.4 0.1 collective-permute-done.12
  95.6 4.2 %collective-permute-start.18 = (bf16[768,128]{1,0:T(8,128)(2,1)S(1)}, bf16[768,128]{1,0:T(8,128)(2,1)S(1)}, u32[]{:S(2)}, u32[]{:S(2)}) collective-permute-start(bf16[768,128]{1,0:T(8,128)(2,1)S(1)} %pad_maximum_fusion.1), channel_id=1, source_target_pairs={{0,24},{8,0},{16,8},{24,16},{1,25},{9,1},{17,9},{25,17},{2,26},{10... | collective-permute-start | bytes 589832 | tf_op jit(solution)/shard_map/ppermute | solution.py:438
  99.8 0.7 collective-permute-start.16
  100.5 2.5 %shard_map.85 = bf16[2,1024,256]{2,1,0:T(8,128)(2,1)} custom-call(bf16[2,1024,256]{2,1,0:T(8,128)(2,1)S(1)} %bitcast.15, bf16[2,1024,256]{2,1,0:T(8,128)(2,1)S(1)} %get-tuple-element.91.hid_ref, bf16[2,1024,256]{2,1,0:T(8,128)(2,1)S(1)} %collective-permute-done.15.prev_ref, bf16[3,256,256]{2,1,0:T(8,128)(2,1)S(1)} %copy-done.2), custom_call_target="tpu_custom_call" | custom-call | flops 805306368 | bytes 4587520 | tf_op jit(solution)/shard_map/pallas_call | solution.py:33
  103.0 1.5 %collective-permute-done.18 = bf16[768,128]{1,0:T(8,128)(2,1)S(1)} collective-permute-done((bf16[768,128]{1,0:T(8,128)(2,1)S(1)}, bf16[768,128]{1,0:T(8,128)(2,1)S(1)}, u32[]{:S(2)}, u32[]{:S(2)}) %collective-permute-start.18) | collective-permute-done | bytes 196640 | tf_op jit(solution)/shard_map/ppermute | solution.py:438
  104.5 1.4 %collective-permute-done.17 = bf16[768,128]{1,0:T(8,128)(2,1)S(1)} collective-permute-done((bf16[768,128]{1,0:T(8,128)(2,1)S(1)}, bf16[768,128]{1,0:T(8,128)(2,1)S(1)}, u32[]{:S(2)}, u32[]{:S(2)}) %collective-permute-start.17) | collective-permute-done | bytes 196640 | tf_op jit(solution)/shard_map/ppermute | solution.py:438
  105.9 1.7 %collective-permute-done.16 = bf16[768,128]{1,0:T(8,128)(2,1)S(1)} collective-permute-done((bf16[768,128]{1,0:T(8,128)(2,1)S(1)}, bf16[768,128]{1,0:T(8,128)(2,1)S(1)}, u32[]{:S(2)}, u32[]{:S(2)}) %collective-permute-start.16) | collective-permute-done | bytes 196640 | tf_op jit(solution)/shard_map/ppermute | solution.py:438
  107.6 0.1 pad_maximum_fusion.u_ref
  107.7 6.5 %collective-permute-start.19 = (bf16[3072,128]{1,0:T(8,128)(2,1)S(1)}, bf16[3072,128]{1,0:T(8,128)(2,1)S(1)}, u32[]{:S(2)}, u32[]{:S(2)}) collective-permute-start(bf16[3072,128]{1,0:T(8,128)(2,1)S(1)} %pad_maximum_fusion.u_ref), channel_id=1, source_target_pairs={{0,32},{32,0},{1,33},{33,1},{2,34},{34,2},{3,35},{35,3},{4,36},{36... | collective-permute-start | bytes 2359304 | tf_op jit(solution)/shard_map/ppermute | solution.py:426
  114.1 1.4 %shard_map.86 = (f32[3072,128]{1,0:T(8,128)S(1)}, f32[8,128]{1,0:T(8,128)S(1)}) custom-call(s32[5]{0:T(128)S(1)} %stack.23.refs_0_.info, bf16[3072,128]{1,0:T(8,128)(2,1)S(1)} %pad_maximum_fusion.u_ref), custom_call_target="tpu_custom_call" | custom-call | flops 2097152 | bytes 2363412 | tf_op jit(solution)/shard_map/pallas_call | solution.py:33
  115.5 0.5 collective-permute-done.19.refs_3_
  116.1 3.3 %shard_map.87 = (f32[9,256,256]{2,1,0:T(8,128)}, f32[3,256,256]{2,1,0:T(8,128)}) custom-call(s32[5]{0:T(128)S(1)} %stack.23.refs_0_.info, f32[3072,128]{1,0:T(8,128)S(1)} %get-tuple-element.102.refs_1_, f32[8,128]{1,0:T(8,128)S(1)} %get-tuple-element.103.refs_2_, bf16[3072,128]{1,0:T(8,128)(2,1)S(1)} %collective-permute-done.19.refs_3_), custom_call_target="tpu_custom_call" | custom-call | flops 2097152 | bytes 5509140 | tf_op jit(solution)/shard_map/pallas_call | solution.py:33
  (24 shorter events, 0.1 us)
Async XLA Ops:
  0.6 34.2 %collective-permute-start.2 = (bf16[2,1024,256]{2,1,0:T(8,128)(2,1)}, bf16[2,1024,256]{2,1,0:T(8,128)(2,1)S(1)}, u32[]{:S(2)}, u32[]{:S(2)}) collective-permute-start(bf16[2,1024,256]{2,1,0:T(8,128)(2,1)} %bitcast.16), channel_id=1, source_target_pairs={{8,0},{16,8},{24,16},{9,1},{17,9},{25,17},{10,2},{18,10},{26,18},{... | collective-permute-start | bytes 3145736 | tf_op jit(solution)/shard_map/ppermute | solution.py:432
  4.1 22.4 %collective-permute-start = (bf16[2,128,256]{2,1,0:T(8,128)(2,1)S(1)}, bf16[2,128,256]{2,1,0:T(8,128)(2,1)S(1)}, u32[]{:S(2)}, u32[]{:S(2)}) collective-permute-start(bf16[2,128,256]{2,1,0:T(8,128)(2,1)S(1)} %get-tuple-element.55), channel_id=1, source_target_pairs={{0,1},{1,2},{2,3},{3,4},{4,5},{5,6},{6,7},{8,9},{9,10},{10,11},{11... | collective-permute-start | bytes 393224 | tf_op jit(solution)/shard_map/ppermute | solution.py:432
  8.5 18.1 %collective-permute-start.1 = (bf16[2,128,256]{2,1,0:T(8,128)(2,1)S(1)}, bf16[2,128,256]{2,1,0:T(8,128)(2,1)S(1)}, u32[]{:S(2)}, u32[]{:S(2)}) collective-permute-start(bf16[2,128,256]{2,1,0:T(8,128)(2,1)S(1)} %get-tuple-element.56), channel_id=1, source_target_pairs={{1,0},{2,1},{3,2},{4,3},{5,4},{6,5},{7,6},{9,8},{10,9},{11,10},{12... | collective-permute-start | bytes 393224 | tf_op jit(solution)/shard_map/ppermute | solution.py:432
  9.8 16.8 %all-to-all-start = ((f32[8,8,128]{2,1,0:T(8,128)}), f32[8,8,128]{2,1,0:T(8,128)S(1)}, u32[]{:S(2)}, u32[]{:S(2)}) async-start(f32[8,8,128]{2,1,0:T(8,128)} %get-tuple-element.57), calls=%async_computation | async-start | bytes 65536 | tf_op jit(solution)/shard_map/all_to_all | solution.py:471
  26.6 0.6 copy-start.3
  26.6 0.7 copy-start.4
  26.6 0.7 copy-start.5
  27.3 7.5 %copy-start.1 = (bf16[1,2,8,128,256]{4,3,2,1,0:T(8,128)(2,1)S(1)}, bf16[1,2,8,128,256]{4,3,2,1,0:T(8,128)(2,1)}, u32[]{:S(2)}) copy-start(bf16[1,2,8,128,256]{4,3,2,1,0:T(8,128)(2,1)} %param.5) | copy-start | bytes 3145732
  27.3 7.6 %copy-start.2 = (bf16[3,256,256]{2,1,0:T(8,128)(2,1)S(1)}, bf16[3,256,256]{2,1,0:T(8,128)(2,1)}, u32[]{:S(2)}) copy-start(bf16[3,256,256]{2,1,0:T(8,128)(2,1)} %w_ref.3) | copy-start | bytes 1179652
  40.6 6.2 %collective-permute-start.3 = (f32[3072,128]{1,0:T(8,128)S(1)}, f32[3072,128]{1,0:T(8,128)S(1)}, u32[]{:S(2)}, u32[]{:S(2)}) collective-permute-start(f32[3072,128]{1,0:T(8,128)S(1)} %slice.4), channel_id=1, source_target_pairs={{0,32},{32,0},{1,33},{33,1},{2,34},{34,2},{3,35},{35,3},{4,36},{36... | collective-permute-start | bytes 4718600 | tf_op jit(solution)/shard_map/ppermute | solution.py:426
  43.4 10.2 %collective-permute-start.7 = (bf16[2,128,256]{2,1,0:T(8,128)(2,1)S(1)}, bf16[2,128,256]{2,1,0:T(8,128)(2,1)S(1)}, u32[]{:S(2)}, u32[]{:S(2)}) collective-permute-start(bf16[2,128,256]{2,1,0:T(8,128)(2,1)S(1)} %get-tuple-element.69), channel_id=1, source_target_pairs={{0,1},{1,2},{2,3},{3,4},{4,5},{5,6},{6,7},{8,9},{9,10},{10,11},{11... | collective-permute-start | bytes 393224 | tf_op jit(solution)/shard_map/ppermute | solution.py:432
  45.6 8.0 %collective-permute-start.8 = (bf16[2,128,256]{2,1,0:T(8,128)(2,1)S(1)}, bf16[2,128,256]{2,1,0:T(8,128)(2,1)S(1)}, u32[]{:S(2)}, u32[]{:S(2)}) collective-permute-start(bf16[2,128,256]{2,1,0:T(8,128)(2,1)S(1)} %get-tuple-element.70), channel_id=1, source_target_pairs={{1,0},{2,1},{3,2},{4,3},{5,4},{6,5},{7,6},{9,8},{10,9},{11,10},{12... | collective-permute-start | bytes 393224 | tf_op jit(solution)/shard_map/ppermute | solution.py:432
  47.5 12.7 %collective-permute-start.4 = (bf16[768,128]{1,0:T(8,128)(2,1)S(1)}, bf16[768,128]{1,0:T(8,128)(2,1)S(1)}, u32[]{:S(2)}, u32[]{:S(2)}) collective-permute-start(bf16[768,128]{1,0:T(8,128)(2,1)S(1)} %get-tuple-element.66), channel_id=1, source_target_pairs={{0,8},{8,16},{16,24},{24,0},{1,9},{9,17},{17,25},{25,1},{2,10},{10... | collective-permute-start | bytes 589832 | tf_op jit(solution)/shard_map/ppermute | solution.py:438
  50.0 11.7 %collective-permute-start.5 = (bf16[768,128]{1,0:T(8,128)(2,1)S(1)}, bf16[768,128]{1,0:T(8,128)(2,1)S(1)}, u32[]{:S(2)}, u32[]{:S(2)}) collective-permute-start(bf16[768,128]{1,0:T(8,128)(2,1)S(1)} %get-tuple-element.67), channel_id=1, source_target_pairs={{0,16},{8,24},{16,0},{24,8},{1,17},{9,25},{17,1},{25,9},{2,18},{10... | collective-permute-start | bytes 589832 | tf_op jit(solution)/shard_map/ppermute | solution.py:438
  52.8 8.9 %collective-permute-start.6 = (bf16[768,128]{1,0:T(8,128)(2,1)S(1)}, bf16[768,128]{1,0:T(8,128)(2,1)S(1)}, u32[]{:S(2)}, u32[]{:S(2)}) collective-permute-start(bf16[768,128]{1,0:T(8,128)(2,1)S(1)} %get-tuple-element.68), channel_id=1, source_target_pairs={{0,24},{8,0},{16,8},{24,16},{1,25},{9,1},{17,9},{25,17},{2,26},{10... | collective-permute-start | bytes 589832 | tf_op jit(solution)/shard_map/ppermute | solution.py:438
  61.7 29.9 %copy-start = (bf16[1,2,8,128,256]{4,3,2,1,0:T(8,128)(2,1)S(1)}, bf16[1,2,8,128,256]{4,3,2,1,0:T(8,128)(2,1)}, u32[]{:S(2)}) copy-start(bf16[1,2,8,128,256]{4,3,2,1,0:T(8,128)(2,1)} %param.4) | copy-start | bytes 3145732
  62.4 8.2 %collective-permute-start.9 = (f32[192,128]{1,0:T(8,128)S(1)}, f32[192,128]{1,0:T(8,128)S(1)}, u32[]{:S(2)}, u32[]{:S(2)}) collective-permute-start(f32[192,128]{1,0:T(8,128)S(1)} %get-tuple-element.80), channel_id=1, source_target_pairs={{0,64},{64,128},{128,192},{192,0},{1,65},{65,129},{129,193},{193,1... | collective-permute-start | bytes 294920 | tf_op jit(solution)/shard_map/ppermute | solution.py:438
  63.8 6.9 %collective-permute-start.10 = (f32[192,128]{1,0:T(8,128)S(1)}, f32[192,128]{1,0:T(8,128)S(1)}, u32[]{:S(2)}, u32[]{:S(2)}) collective-permute-start(f32[192,128]{1,0:T(8,128)S(1)} %get-tuple-element.81), channel_id=1, source_target_pairs={{0,128},{64,192},{128,0},{192,64},{1,129},{65,193},{129,1},{193,65... | collective-permute-start | bytes 294920 | tf_op jit(solution)/shard_map/ppermute | solution.py:438
  66.4 4.6 %collective-permute-start.11 = (f32[192,128]{1,0:T(8,128)S(1)}, f32[192,128]{1,0:T(8,128)S(1)}, u32[]{:S(2)}, u32[]{:S(2)}) collective-permute-start(f32[192,128]{1,0:T(8,128)S(1)} %get-tuple-element.82), channel_id=1, source_target_pairs={{0,192},{64,0},{128,64},{192,128},{1,193},{65,1},{129,65},{193,129... | collective-permute-start | bytes 294920 | tf_op jit(solution)/shard_map/ppermute | solution.py:438
  67.5 28.1 %collective-permute-start.15 = (bf16[2,1024,256]{2,1,0:T(8,128)(2,1)S(1)}, bf16[2,1024,256]{2,1,0:T(8,128)(2,1)S(1)}, u32[]{:S(2)}, u32[]{:S(2)}) collective-permute-start(bf16[2,1024,256]{2,1,0:T(8,128)(2,1)S(1)} %get-tuple-element.91.hid_ref), channel_id=1, source_target_pairs={{0,8},{8,16},{16,24},{1,9},{9,17},{17,25},{2,10},{10,18},{18,26},{... | collective-permute-start | bytes 3145736 | tf_op jit(solution)/shard_map/ppermute | solution.py:432
  88.7 6.4 %collective-permute-start.14 = (bf16[192,128]{1,0:T(8,128)(2,1)S(1)}, bf16[192,128]{1,0:T(8,128)(2,1)S(1)}, u32[]{:S(2)}, u32[]{:S(2)}) collective-permute-start(bf16[192,128]{1,0:T(8,128)(2,1)S(1)} %get-tuple-element.87), channel_id=1, source_target_pairs={{0,192},{64,0},{128,64},{192,128},{1,193},{65,1},{129,65},{193,129... | collective-permute-start | bytes 147464 | tf_op jit(solution)/shard_map/ppermute | solution.py:438
  90.9 4.5 %collective-permute-start.13 = (bf16[192,128]{1,0:T(8,128)(2,1)S(1)}, bf16[192,128]{1,0:T(8,128)(2,1)S(1)}, u32[]{:S(2)}, u32[]{:S(2)}) collective-permute-start(bf16[192,128]{1,0:T(8,128)(2,1)S(1)} %get-tuple-element.87), channel_id=1, source_target_pairs={{0,128},{64,192},{128,0},{192,64},{1,129},{65,193},{129,1},{193,65... | collective-permute-start | bytes 147464 | tf_op jit(solution)/shard_map/ppermute | solution.py:438
  90.9 4.7 %collective-permute-start.12 = (bf16[192,128]{1,0:T(8,128)(2,1)S(1)}, bf16[192,128]{1,0:T(8,128)(2,1)S(1)}, u32[]{:S(2)}, u32[]{:S(2)}) collective-permute-start(bf16[192,128]{1,0:T(8,128)(2,1)S(1)} %get-tuple-element.87), channel_id=1, source_target_pairs={{0,64},{64,128},{128,192},{192,0},{1,65},{65,129},{129,193},{193,1... | collective-permute-start | bytes 147464 | tf_op jit(solution)/shard_map/ppermute | solution.py:438
  95.6 8.9 %collective-permute-start.18 = (bf16[768,128]{1,0:T(8,128)(2,1)S(1)}, bf16[768,128]{1,0:T(8,128)(2,1)S(1)}, u32[]{:S(2)}, u32[]{:S(2)}) collective-permute-start(bf16[768,128]{1,0:T(8,128)(2,1)S(1)} %pad_maximum_fusion.1), channel_id=1, source_target_pairs={{0,24},{8,0},{16,8},{24,16},{1,25},{9,1},{17,9},{25,17},{2,26},{10... | collective-permute-start | bytes 589832 | tf_op jit(solution)/shard_map/ppermute | solution.py:438
  99.8 6.1 %collective-permute-start.17 = (bf16[768,128]{1,0:T(8,128)(2,1)S(1)}, bf16[768,128]{1,0:T(8,128)(2,1)S(1)}, u32[]{:S(2)}, u32[]{:S(2)}) collective-permute-start(bf16[768,128]{1,0:T(8,128)(2,1)S(1)} %pad_maximum_fusion.1), channel_id=1, source_target_pairs={{0,16},{8,24},{16,0},{24,8},{1,17},{9,25},{17,1},{25,9},{2,18},{10... | collective-permute-start | bytes 589832 | tf_op jit(solution)/shard_map/ppermute | solution.py:438
  99.8 7.8 %collective-permute-start.16 = (bf16[768,128]{1,0:T(8,128)(2,1)S(1)}, bf16[768,128]{1,0:T(8,128)(2,1)S(1)}, u32[]{:S(2)}, u32[]{:S(2)}) collective-permute-start(bf16[768,128]{1,0:T(8,128)(2,1)S(1)} %pad_maximum_fusion.1), channel_id=1, source_target_pairs={{0,8},{8,16},{16,24},{24,0},{1,9},{9,17},{17,25},{25,1},{2,10},{10... | collective-permute-start | bytes 589832 | tf_op jit(solution)/shard_map/ppermute | solution.py:438
  107.7 8.4 %collective-permute-start.19 = (bf16[3072,128]{1,0:T(8,128)(2,1)S(1)}, bf16[3072,128]{1,0:T(8,128)(2,1)S(1)}, u32[]{:S(2)}, u32[]{:S(2)}) collective-permute-start(bf16[3072,128]{1,0:T(8,128)(2,1)S(1)} %pad_maximum_fusion.u_ref), channel_id=1, source_target_pairs={{0,32},{32,0},{1,33},{33,1},{2,34},{34,2},{3,35},{35,3},{4,36},{36... | collective-permute-start | bytes 2359304 | tf_op jit(solution)/shard_map/ppermute | solution.py:426

commit v8 on v7

--- a/solution.py
+++ b/solution.py
@@ -89,6 +89,25 @@
     return res
 
 
+CHUNK = 256
+
+
+def woven(put, conv, ready):
+    chunks = 1024 // CHUNK
+    for line in range(10):
+        put(0, line)
+    ready()
+    done = 0
+    for c in range(chunks):
+        conv(0, c * CHUNK)
+        upto = 10 * (c + 1) // chunks
+        for line in range(done, upto):
+            put(1, line)
+        done = upto
+    for c in range(chunks):
+        conv(1, c * CHUNK)
+
+
 def fetched(*pairs, sems):
     copies = [pltpu.make_async_copy(a, b, sems.at[i]) for i, (a, b) in enumerate(pairs)]
     for c in copies:
@@ -133,45 +152,32 @@
     keep_up = (info[1] > 0).astype(F32)
     keep_dn = (info[2] > 0).astype(F32)
     stats = moments(st_ref, members)
-    for f in range(2):
+
+    def put(f, line):
         mean, inv = stats[f]
-
-        def put(v, row, keep=None):
-            n = (v.astype(F32) - mean) * inv
-            a = n * sigmoid(n)
-            if keep is not None:
-                a = a * keep
-            before, after = shifted(a)
-            at = pl.ds(row, 128)
-            act_ref[f, at, 0:256] = before.astype(BF16)
-            act_ref[f, at, 256:512] = a.astype(BF16)
-            act_ref[f, at, 512:768] = after.astype(BF16)
-
-        put(up_ref[f], 0, keep_up)
-        put(dn_ref[f], 9 * 128, keep_dn)
-
-        def line(r, _):
-            at = pl.multiple_of(r * 128, 128)
-            put(x_ref[f, pl.ds(at, 128), :], pl.multiple_of(at + 128, 128))
-            return 0
-
-        lax.fori_loop(0, 8, line, 0)
-        if f == 0:
-            weights.wait()
-
-        def conv(r, _):
-            at = pl.multiple_of(r * 512, 512)
-            v = None
-            for i in range(3):
-                lhs = act_ref[f, pl.ds(pl.multiple_of(at + i * 128, 128), 512), :]
-                part = dot(lhs, w_ref[i])
-                v = part if v is None else v + part
-            s = sigmoid(v)
-            hid_ref[f, pl.ds(at, 512), :] = (v * s).astype(BF16)
-            slope_ref[f, pl.ds(at, 512), :] = s * (1.0 + v * (1.0 - s))
-            return 0
-
-        lax.fori_loop(0, 2, conv, 0)
+        v = up_ref[f] if line == 0 else dn_ref[f] if line == 9 else x_ref[f, line * 128 - 128 : line * 128, :]
+        n = (v.astype(F32) - mean) * inv
+        a = n * sigmoid(n)
+        if line == 0:
+            a = a * keep_up
+        if line == 9:
+            a = a * keep_dn
+        before, after = shifted(a)
+        rows = slice(line * 128, line * 128 + 128)
+        act_ref[f, rows, 0:256] = before.astype(BF16)
+        act_ref[f, rows, 256:512] = a.astype(BF16)
+        act_ref[f, rows, 512:768] = after.astype(BF16)
+
+    def conv(f, at):
+        v = None
+        for i in range(3):
+            part = dot(act_ref[f, at + i * 128 : at + i * 128 + CHUNK, :], w_ref[i])
+            v = part if v is None else v + part
+        s = sigmoid(v)
+        hid_ref[f, at : at + CHUNK, :] = (v * s).astype(BF16)
+        slope_ref[f, at : at + CHUNK, :] = s * (1.0 + v * (1.0 - s))
+
+    woven(put, conv, weights.wait)
 
 
 def pregrad_kernel(cot_ref, later_ref, slope_ref, w_ref, pg_ref, top_ref, bot_ref):
@@ -227,61 +233,49 @@
 
 def backward_kernel(
     members, pg_ref, up_ref, dn_ref, w_hbm, x_hbm, st_hbm, ng_hbm, o_ref,
-    a_ref, b_ref, c_ref, w_ref, x_ref, st_ref, ng_ref, sems,
+    g_ref, w_ref, x_ref, st_ref, ng_ref, sems,
 ):
-    loads = [(w_hbm, w_ref), (x_hbm, x_ref), (st_hbm, st_ref)]
+    loads = [(x_hbm, x_ref), (st_hbm, st_ref)]
+    for i in range(3):
+        for j in range(3):
+            loads.append((w_hbm.at[i, j], w_ref.at[i, :, j * 256 : j * 256 + 256]))
     loads = [pltpu.make_async_copy(a, b, sems.at[i]) for i, (a, b) in enumerate(loads)]
     for c in loads:
         c.start()
-    stats = None
-    stores = []
-    sums = []
-    for f in range(2):
-
-        def put(v, row):
-            v = v.astype(F32)
-            before, after = shifted(v)
-            at = pl.ds(row, 128)
-            a_ref[f, at, :] = after.astype(BF16)
-            b_ref[f, at, :] = v.astype(BF16)
-            c_ref[f, at, :] = before.astype(BF16)
-
-        put(up_ref[f], 0)
-        put(dn_ref[f], 9 * 128)
-
-        def line(r, _):
-            at = pl.multiple_of(r * 128, 128)
-            put(pg_ref[f, pl.ds(at, 128), :], pl.multiple_of(at + 128, 128))
-            return 0
-
-        lax.fori_loop(0, 8, line, 0)
-        if f == 0:
-            for c in loads:
-                c.wait()
-            stats = moments(st_ref, members)
-        mean, inv = stats[f]
-
-        def conv(r, carry):
-            at = pl.multiple_of(r * 512, 512)
-            v = None
-            for i in range(3):
-                rows = pl.ds(pl.multiple_of(at + (2 - i) * 128, 128), 512)
-                for j, ref in enumerate((a_ref, b_ref, c_ref)):
-                    p = dot(ref[f, rows, :], w_ref[i, j], NT)
-                    v = p if v is None else v + p
-            n = (x_ref[f, pl.ds(at, 512), :].astype(F32) - mean) * inv
-            s = sigmoid(n)
-            ng = v * (s * (1.0 + n * (1.0 - s)))
-            ng_ref[f, pl.ds(at, 512), :] = ng
-            return carry[0] + fold(ng), carry[1] + fold(ng * n)
-
-        zero = jnp.zeros((8, 256), F32)
-        sums.append(lax.fori_loop(0, 2, conv, (zero, zero)))
-        stores.append(pltpu.make_async_copy(ng_ref.at[f], ng_hbm.at[f], sems.at[3 + f]))
-        stores[-1].start()
+    state = []
+    sums = [[jnp.zeros((8, 256), F32)] * 2 for _ in range(2)]
+
+    def ready():
+        for c in loads:
+            c.wait()
+        state.extend(moments(st_ref, members))
+
+    def put(f, line):
+        v = up_ref[f] if line == 0 else dn_ref[f] if line == 9 else pg_ref[f, line * 128 - 128 : line * 128, :]
+        before, after = shifted(v.astype(F32))
+        rows = slice(line * 128, line * 128 + 128)
+        g_ref[f, rows, 0:256] = after.astype(BF16)
+        g_ref[f, rows, 256:512] = v
+        g_ref[f, rows, 512:768] = before.astype(BF16)
+
+    def conv(f, at):
+        mean, inv = state[f]
+        v = None
+        for i in range(3):
+            start = at + (2 - i) * 128
+            p = dot(g_ref[f, start : start + CHUNK, :], w_ref[i], NT)
+            v = p if v is None else v + p
+        n = (x_ref[f, at : at + CHUNK, :].astype(F32) - mean) * inv
+        s = sigmoid(n)
+        ng = v * (s * (1.0 + n * (1.0 - s)))
+        ng_ref[f, at : at + CHUNK, :] = ng
+        sums[f] = [sums[f][0] + fold(ng), sums[f][1] + fold(ng * n)]
+
+    woven(put, conv, ready)
     store_stats(o_ref, sums)
-    for c in stores:
-        c.wait()
+    store = pltpu.make_async_copy(ng_ref, ng_hbm, sems.at[11])
+    store.start()
+    store.wait()
 
 
 def input_grad_kernel(members, x_ref, cot_ref, ng_ref, st_ref, gst_ref, o_ref):
@@ -509,13 +503,13 @@
         9 * gflop,
         loose=(3, 4, 5),
         outside=(0,),
-        scratch=[pltpu.VMEM((2, 1280, 256), BF16)] * 3
-        + [
-            pltpu.VMEM(w9.shape, BF16),
+        scratch=[
+            pltpu.VMEM((2, 1280, 768), BF16),
+            pltpu.VMEM((3, 256, 768), BF16),
             pltpu.VMEM(flat, BF16),
             pltpu.VMEM(small.shape, F32),
             pltpu.VMEM(flat, F32),
-            pltpu.SemaphoreType.DMA((5,)),
+            pltpu.SemaphoreType.DMA((12,)),
         ],
     )
     got, gst = tied((got, gst))

time: 120 us -> 119 us (level)
  Pallas kernels: 34.6 us -> 33.3 us
    pallas_call x13, Pallas kernels: 34.6 us -> 33.3 us  [call(): pl.pallas_call(kernel, out_shape=tuple((pltpu.HBM(o.shape, o.dtype) if i...]
    ppermute x12, starting transfers between devices: 18.8 us -> 17.6 us  [shifts(): lax.ppermute(m, axis, [(i, (i + d) % n) for i in range(n)])]
  transfers between devices with their start and end apart: 21 -> 21, of which waited for: 9 -> 9; matrix products, arithmetic and copies ran while one was open for 0% -> 0% of each run, Pallas kernels for 21% -> 20%
where the time goes in v8:
time: 119 us; the launch traced here: 118 us
  starting transfers between devices  50.6 us (43%)
  Pallas kernels  33.3 us (28%)
  blocking collectives  17.3 us (15%)
  waiting for transfers between devices  14.8 us (12%)
    pallas_call x13, Pallas kernels, call(): pl.pallas_call(kernel, out_shape=tuple((pltpu.HBM(o.shape, o.dtype) if i...  33.3 us
    ppermute x12, starting transfers between devices, shifts(): lax.ppermute(m, axis, [(i, (i + d) % n) for i in range(n)])  17.6 us
    all_to_all x1, blocking collectives, body(): pieces = lax.all_to_all(pieces, HEIGHT, 0, 0, tiled=True)  17.3 us
    ppermute x6, starting transfers between devices, moved(): return lax.ppermute(x, axes, route)  13.6 us
    all_to_all x1, starting transfers between devices, body(): st = in_hbm(lax.all_to_all(st, HEIGHT, 0, 0, tiled=True))  9.85 us
    ppermute x2, starting transfers between devices, swapped(): return lax.ppermute(x, axis, [(0, 1), (1, 0)])  9.58 us
    ppermute x12, waiting for transfers between devices, shifts(): lax.ppermute(m, axis, [(i, (i + d) % n) for i in range(n)])  7.4 us
    all_to_all x1, waiting for transfers between devices, body(): st = in_hbm(lax.all_to_all(st, HEIGHT, 0, 0, tiled=True))  6.83 us
  transfers between devices with their start and end apart: 21, of which 9 were waited for; matrix products, arithmetic and copies ran while one was open for 0% of the time, Pallas kernels for 20%

profile of v8, /device:TPU:1, one launch (start us, length us, event | category | flops | bytes accessed | tf_op | source)
XLA Modules:
  0.0 118.0 jit_solution(14967067730400276759)
XLA Ops:
  0.6 1.3 %collective-permute-start.2 = (bf16[2,1024,256]{2,1,0:T(8,128)(2,1)}, bf16[2,1024,256]{2,1,0:T(8,128)(2,1)S(1)}, u32[]{:S(2)}, u32[]{:S(2)}) collective-permute-start(bf16[2,1024,256]{2,1,0:T(8,128)(2,1)} %bitcast.16), channel_id=1, source_target_pairs={{8,0},{16,8},{24,16},{9,1},{17,9},{25,17},{10,2},{18,10},{26,18},{... | collective-permute-start | bytes 3145736 | tf_op jit(solution)/shard_map/ppermute | solution.py:426
  1.9 2.2 %shard_map.75 = (f32[8,8,128]{2,1,0:T(8,128)}, bf16[2,128,256]{2,1,0:T(8,128)(2,1)S(1)}, bf16[2,128,256]{2,1,0:T(8,128)(2,1)S(1)}) custom-call(bf16[2,1024,256]{2,1,0:T(8,128)(2,1)} %bitcast.11), custom_call_target="tpu_custom_call" | custom-call | flops 2097152 | bytes 1343488 | tf_op jit(solution)/shard_map/pallas_call | solution.py:33
  4.1 4.4 %collective-permute-start = (bf16[2,128,256]{2,1,0:T(8,128)(2,1)S(1)}, bf16[2,128,256]{2,1,0:T(8,128)(2,1)S(1)}, u32[]{:S(2)}, u32[]{:S(2)}) collective-permute-start(bf16[2,128,256]{2,1,0:T(8,128)(2,1)S(1)} %get-tuple-element.55), channel_id=1, source_target_pairs={{0,1},{1,2},{2,3},{3,4},{4,5},{5,6},{6,7},{8,9},{9,10},{10,11},{11... | collective-permute-start | bytes 393224 | tf_op jit(solution)/shard_map/ppermute | solution.py:426
  8.5 1.3 %collective-permute-start.1 = (bf16[2,128,256]{2,1,0:T(8,128)(2,1)S(1)}, bf16[2,128,256]{2,1,0:T(8,128)(2,1)S(1)}, u32[]{:S(2)}, u32[]{:S(2)}) collective-permute-start(bf16[2,128,256]{2,1,0:T(8,128)(2,1)S(1)} %get-tuple-element.56), channel_id=1, source_target_pairs={{1,0},{2,1},{3,2},{4,3},{5,4},{6,5},{7,6},{9,8},{10,9},{11,10},{12... | collective-permute-start | bytes 393224 | tf_op jit(solution)/shard_map/ppermute | solution.py:426
  9.8 9.8 %all-to-all-start = ((f32[8,8,128]{2,1,0:T(8,128)}), f32[8,8,128]{2,1,0:T(8,128)S(1)}, u32[]{:S(2)}, u32[]{:S(2)}) async-start(f32[8,8,128]{2,1,0:T(8,128)} %get-tuple-element.57), calls=%async_computation | async-start | bytes 65536 | tf_op jit(solution)/shard_map/all_to_all | solution.py:465
  19.6 0.1 stack.23.refs_0_.info
  19.7 6.8 %all-to-all-done.refs_4_.refs_5_.refs_3_ = f32[8,8,128]{2,1,0:T(8,128)S(1)} async-done(((f32[8,8,128]{2,1,0:T(8,128)}), f32[8,8,128]{2,1,0:T(8,128)S(1)}, u32[]{:S(2)}, u32[]{:S(2)}) %all-to-all-start) | async-done | bytes 32800 | tf_op jit(solution)/shard_map/all_to_all | solution.py:465
  26.6 0.6 copy-done.3
  27.2 0.1 copy-done.4
  27.2 0.0 copy-done.5
  27.3 6.8 %shard_map.76 = (bf16[2,1280,768]{2,1,0:T(8,128)(2,1)S(1)}, bf16[2,1024,256]{2,1,0:T(8,128)(2,1)S(1)}, f32[2,1024,256]{2,1,0:T(8,128)S(1)}) custom-call(s32[5]{0:T(128)S(1)} %stack.23.refs_0_.info, bf16[2,1024,256]{2,1,0:T(8,128)(2,1)} %bitcast.12, bf16[2,128,256]{2,1,0:T(8,128)(2,1)} %copy-done.4, bf16[2,128,256]{2,1,0:T(8,128)(2,1)} %copy-done.5, ...), custom_call_target="tpu_custom_call" | custom-call | flops 2415919104 | bytes 9601044 | tf_op jit(solution)/shard_map/pallas_call | solution.py:33
  34.1 1.6 %shard_map.77 = (bf16[2,1024,256]{2,1,0:T(8,128)(2,1)S(1)}, bf16[2,128,256]{2,1,0:T(8,128)(2,1)S(1)}, bf16[2,128,256]{2,1,0:T(8,128)(2,1)S(1)}) custom-call(bf16[2,1024,256]{2,1,0:T(8,128)(2,1)S(1)} %bitcast.17, bf16[2,1024,256]{2,1,0:T(8,128)(2,1)S(1)} %collective-permute-done.2.later_ref, f32[2,1024,256]{2,1,0:T(8,128)S(1)} %get-tuple-element.59.slope_ref, ...), custom_call_target="tpu_custom_call" | custom-call | flops 805306368 | bytes 5898240 | tf_op jit(solution)/shard_map/pallas_call | solution.py:33
  35.7 4.0 %shard_map.78.g_ref = f32[6144,128]{1,0:T(8,128)S(1)} custom-call(s32[5]{0:T(128)S(1)} %stack.23.refs_0_.info, bf16[2,1280,768]{2,1,0:T(8,128)(2,1)S(1)} %get-tuple-element.58.act_ref, bf16[2,1024,256]{2,1,0:T(8,128)(2,1)S(1)} %get-tuple-element.60.pg_ref.refs_0_, bf16[2,1024,256]{2,1,0:T(8,128)(2,1)S(1)} %get-tuple-element.91.hid_ref, ...), custom_call_target="tpu_custom_call" | custom-call | flops 3221225472 | bytes 11272212 | tf_op jit(solution)/shard_map/pallas_call | solution.py:33
  39.8 0.1 slice.4
  39.9 2.7 %collective-permute-start.3 = (f32[3072,128]{1,0:T(8,128)S(1)}, f32[3072,128]{1,0:T(8,128)S(1)}, u32[]{:S(2)}, u32[]{:S(2)}) collective-permute-start(f32[3072,128]{1,0:T(8,128)S(1)} %slice.4), channel_id=1, source_target_pairs={{0,32},{32,0},{1,33},{33,1},{2,34},{34,2},{3,35},{35,3},{4,36},{36... | collective-permute-start | bytes 4718600 | tf_op jit(solution)/shard_map/ppermute | solution.py:420
  42.6 2.2 %collective-permute-start.7 = (bf16[2,128,256]{2,1,0:T(8,128)(2,1)S(1)}, bf16[2,128,256]{2,1,0:T(8,128)(2,1)S(1)}, u32[]{:S(2)}, u32[]{:S(2)}) collective-permute-start(bf16[2,128,256]{2,1,0:T(8,128)(2,1)S(1)} %get-tuple-element.69), channel_id=1, source_target_pairs={{0,1},{1,2},{2,3},{3,4},{4,5},{5,6},{6,7},{8,9},{9,10},{10,11},{11... | collective-permute-start | bytes 393224 | tf_op jit(solution)/shard_map/ppermute | solution.py:426
  44.8 1.3 %collective-permute-start.8 = (bf16[2,128,256]{2,1,0:T(8,128)(2,1)S(1)}, bf16[2,128,256]{2,1,0:T(8,128)(2,1)S(1)}, u32[]{:S(2)}, u32[]{:S(2)}) collective-permute-start(bf16[2,128,256]{2,1,0:T(8,128)(2,1)S(1)} %get-tuple-element.70), channel_id=1, source_target_pairs={{1,0},{2,1},{3,2},{4,3},{5,4},{6,5},{7,6},{9,8},{10,9},{11,10},{12... | collective-permute-start | bytes 393224 | tf_op jit(solution)/shard_map/ppermute | solution.py:426
  46.1 0.7 shard_map.79
  46.8 2.4 %collective-permute-start.4 = (bf16[768,128]{1,0:T(8,128)(2,1)S(1)}, bf16[768,128]{1,0:T(8,128)(2,1)S(1)}, u32[]{:S(2)}, u32[]{:S(2)}) collective-permute-start(bf16[768,128]{1,0:T(8,128)(2,1)S(1)} %get-tuple-element.66), channel_id=1, source_target_pairs={{0,8},{8,16},{16,24},{24,0},{1,9},{9,17},{17,25},{25,1},{2,10},{10... | collective-permute-start | bytes 589832 | tf_op jit(solution)/shard_map/ppermute | solution.py:432
  49.2 2.8 %collective-permute-start.5 = (bf16[768,128]{1,0:T(8,128)(2,1)S(1)}, bf16[768,128]{1,0:T(8,128)(2,1)S(1)}, u32[]{:S(2)}, u32[]{:S(2)}) collective-permute-start(bf16[768,128]{1,0:T(8,128)(2,1)S(1)} %get-tuple-element.67), channel_id=1, source_target_pairs={{0,16},{8,24},{16,0},{24,8},{1,17},{9,25},{17,1},{25,9},{2,18},{10... | collective-permute-start | bytes 589832 | tf_op jit(solution)/shard_map/ppermute | solution.py:432
  52.0 0.8 collective-permute-start.6
  52.8 6.1 %shard_map.80 = (f32[2,1024,256]{2,1,0:T(8,128)}, f32[1,8,128]{2,1,0:T(8,128)S(1)}) custom-call(bf16[2,1024,256]{2,1,0:T(8,128)(2,1)S(1)} %get-tuple-element.60.pg_ref.refs_0_, bf16[2,128,256]{2,1,0:T(8,128)(2,1)S(1)} %collective-permute-done.7.refs_1_, bf16[2,128,256]{2,1,0:T(8,128)(2,1)S(1)} %collective-permute-done.8.refs_2_, ...), custom_call_target="tpu_custom_call" | custom-call | flops 2415919104 | bytes 5672960 | tf_op jit(solution)/shard_map/pallas_call | solution.py:33
  58.9 2.0 %collective-permute-done.5.b_ref = bf16[768,128]{1,0:T(8,128)(2,1)S(1)} collective-permute-done((bf16[768,128]{1,0:T(8,128)(2,1)S(1)}, bf16[768,128]{1,0:T(8,128)(2,1)S(1)}, u32[]{:S(2)}, u32[]{:S(2)}) %collective-permute-start.5) | collective-permute-done | bytes 196640 | tf_op jit(solution)/shard_map/ppermute | solution.py:432
  60.9 0.7 shard_map.81
  61.6 1.4 %collective-permute-start.9 = (f32[192,128]{1,0:T(8,128)S(1)}, f32[192,128]{1,0:T(8,128)S(1)}, u32[]{:S(2)}, u32[]{:S(2)}) collective-permute-start(f32[192,128]{1,0:T(8,128)S(1)} %get-tuple-element.80), channel_id=1, source_target_pairs={{0,64},{64,128},{128,192},{192,0},{1,65},{65,129},{129,193},{193,1... | collective-permute-start | bytes 294920 | tf_op jit(solution)/shard_map/ppermute | solution.py:432
  63.0 2.6 %collective-permute-start.10 = (f32[192,128]{1,0:T(8,128)S(1)}, f32[192,128]{1,0:T(8,128)S(1)}, u32[]{:S(2)}, u32[]{:S(2)}) collective-permute-start(f32[192,128]{1,0:T(8,128)S(1)} %get-tuple-element.81), channel_id=1, source_target_pairs={{0,128},{64,192},{128,0},{192,64},{1,129},{65,193},{129,1},{193,65... | collective-permute-start | bytes 294920 | tf_op jit(solution)/shard_map/ppermute | solution.py:432
  65.6 1.1 collective-permute-start.11
  66.7 3.2 %collective-permute-start.15 = (bf16[2,1024,256]{2,1,0:T(8,128)(2,1)S(1)}, bf16[2,1024,256]{2,1,0:T(8,128)(2,1)S(1)}, u32[]{:S(2)}, u32[]{:S(2)}) collective-permute-start(bf16[2,1024,256]{2,1,0:T(8,128)(2,1)S(1)} %get-tuple-element.91.hid_ref), channel_id=1, source_target_pairs={{0,8},{8,16},{16,24},{1,9},{9,17},{17,25},{2,10},{10,18},{18,26},{... | collective-permute-start | bytes 3145736 | tf_op jit(solution)/shard_map/ppermute | solution.py:426
  69.9 0.3 collective-permute-done.11.c_ref
  70.2 0.1 shard_map.82
  70.3 17.3 %all_to_all.10.u_ref = bf16[8,224,128]{2,1,0:T(8,128)(2,1)S(1)} all-to-all(bf16[8,224,128]{2,1,0:T(8,128)(2,1)S(1)} %shard_map.82), channel_id=1, replica_groups=mesh['y'=4,'core'=2,'tm'=4,'height'=8] {'height'}, dimensions={0} | all-to-all | bytes 917504 | tf_op jit(solution)/shard_map/all_to_all | solution.py:523
  87.6 0.5 shard_map.83
  88.1 2.1 %collective-permute-start.14 = (bf16[192,128]{1,0:T(8,128)(2,1)S(1)}, bf16[192,128]{1,0:T(8,128)(2,1)S(1)}, u32[]{:S(2)}, u32[]{:S(2)}) collective-permute-start(bf16[192,128]{1,0:T(8,128)(2,1)S(1)} %get-tuple-element.87), channel_id=1, source_target_pairs={{0,192},{64,0},{128,64},{192,128},{1,193},{65,1},{129,65},{193,129... | collective-permute-start | bytes 147464 | tf_op jit(solution)/shard_map/ppermute | solution.py:432
  90.2 0.7 collective-permute-start.12
  90.8 3.6 %shard_map.84 = bf16[2,1024,256]{2,1,0:T(8,128)(2,1)} custom-call(bf16[2,1024,256]{2,1,0:T(8,128)(2,1)S(1)} %bitcast.14, bf16[2,1024,256]{2,1,0:T(8,128)(2,1)S(1)} %bitcast.19, f32[2,1024,256]{2,1,0:T(8,128)} %get-tuple-element.92.refs_2_, f32[8,8,128]{2,1,0:T(8,128)} %copy-done.3, f32[1,8,128]{2,1,0:T(8,128)S(1)} %get-tuple-element.93.refs_4_), custom_call_target="tpu_custom_call" | custom-call | flops 2097152 | bytes 5279744 | tf_op jit(solution)/shard_map/pallas_call | solution.py:33
  94.4 0.3 collective-permute-done.13
  94.7 0.1 collective-permute-done.12
  94.9 3.0 %collective-permute-start.18 = (bf16[768,128]{1,0:T(8,128)(2,1)S(1)}, bf16[768,128]{1,0:T(8,128)(2,1)S(1)}, u32[]{:S(2)}, u32[]{:S(2)}) collective-permute-start(bf16[768,128]{1,0:T(8,128)(2,1)S(1)} %pad_maximum_fusion.1), channel_id=1, source_target_pairs={{0,24},{8,0},{16,8},{24,16},{1,25},{9,1},{17,9},{25,17},{2,26},{10... | collective-permute-start | bytes 589832 | tf_op jit(solution)/shard_map/ppermute | solution.py:432
  97.9 0.7 collective-permute-start.16
  98.6 2.5 %shard_map.85 = bf16[2,1024,256]{2,1,0:T(8,128)(2,1)} custom-call(bf16[2,1024,256]{2,1,0:T(8,128)(2,1)S(1)} %bitcast.15, bf16[2,1024,256]{2,1,0:T(8,128)(2,1)S(1)} %get-tuple-element.91.hid_ref, bf16[2,1024,256]{2,1,0:T(8,128)(2,1)S(1)} %collective-permute-done.15.prev_ref, bf16[3,256,256]{2,1,0:T(8,128)(2,1)S(1)} %copy-done.2), custom_call_target="tpu_custom_call" | custom-call | flops 805306368 | bytes 4587520 | tf_op jit(solution)/shard_map/pallas_call | solution.py:33
  101.1 1.5 %collective-permute-done.18 = bf16[768,128]{1,0:T(8,128)(2,1)S(1)} collective-permute-done((bf16[768,128]{1,0:T(8,128)(2,1)S(1)}, bf16[768,128]{1,0:T(8,128)(2,1)S(1)}, u32[]{:S(2)}, u32[]{:S(2)}) %collective-permute-start.18) | collective-permute-done | bytes 196640 | tf_op jit(solution)/shard_map/ppermute | solution.py:432
  102.6 1.4 %collective-permute-done.17 = bf16[768,128]{1,0:T(8,128)(2,1)S(1)} collective-permute-done((bf16[768,128]{1,0:T(8,128)(2,1)S(1)}, bf16[768,128]{1,0:T(8,128)(2,1)S(1)}, u32[]{:S(2)}, u32[]{:S(2)}) %collective-permute-start.17) | collective-permute-done | bytes 196640 | tf_op jit(solution)/shard_map/ppermute | solution.py:432
  104.0 1.7 %collective-permute-done.16 = bf16[768,128]{1,0:T(8,128)(2,1)S(1)} collective-permute-done((bf16[768,128]{1,0:T(8,128)(2,1)S(1)}, bf16[768,128]{1,0:T(8,128)(2,1)S(1)}, u32[]{:S(2)}, u32[]{:S(2)}) %collective-permute-start.16) | collective-permute-done | bytes 196640 | tf_op jit(solution)/shard_map/ppermute | solution.py:432
  105.7 0.1 pad_maximum_fusion.u_ref
  105.8 6.9 %collective-permute-start.19 = (bf16[3072,128]{1,0:T(8,128)(2,1)S(1)}, bf16[3072,128]{1,0:T(8,128)(2,1)S(1)}, u32[]{:S(2)}, u32[]{:S(2)}) collective-permute-start(bf16[3072,128]{1,0:T(8,128)(2,1)S(1)} %pad_maximum_fusion.u_ref), channel_id=1, source_target_pairs={{0,32},{32,0},{1,33},{33,1},{2,34},{34,2},{3,35},{35,3},{4,36},{36... | collective-permute-start | bytes 2359304 | tf_op jit(solution)/shard_map/ppermute | solution.py:420
  112.6 1.4 %shard_map.86 = (f32[3072,128]{1,0:T(8,128)S(1)}, f32[8,128]{1,0:T(8,128)S(1)}) custom-call(s32[5]{0:T(128)S(1)} %stack.23.refs_0_.info, bf16[3072,128]{1,0:T(8,128)(2,1)S(1)} %pad_maximum_fusion.u_ref), custom_call_target="tpu_custom_call" | custom-call | flops 2097152 | bytes 2363412 | tf_op jit(solution)/shard_map/pallas_call | solution.py:33
  114.0 0.5 collective-permute-done.19.refs_3_
  114.6 3.3 %shard_map.87 = (f32[9,256,256]{2,1,0:T(8,128)}, f32[3,256,256]{2,1,0:T(8,128)}) custom-call(s32[5]{0:T(128)S(1)} %stack.23.refs_0_.info, f32[3072,128]{1,0:T(8,128)S(1)} %get-tuple-element.102.refs_1_, f32[8,128]{1,0:T(8,128)S(1)} %get-tuple-element.103.refs_2_, bf16[3072,128]{1,0:T(8,128)(2,1)S(1)} %collective-permute-done.19.refs_3_), custom_call_target="tpu_custom_call" | custom-call | flops 2097152 | bytes 5509140 | tf_op jit(solution)/shard_map/pallas_call | solution.py:33
  (24 shorter events, 0.1 us)
Async XLA Ops:
  0.6 33.4 %collective-permute-start.2 = (bf16[2,1024,256]{2,1,0:T(8,128)(2,1)}, bf16[2,1024,256]{2,1,0:T(8,128)(2,1)S(1)}, u32[]{:S(2)}, u32[]{:S(2)}) collective-permute-start(bf16[2,1024,256]{2,1,0:T(8,128)(2,1)} %bitcast.16), channel_id=1, source_target_pairs={{8,0},{16,8},{24,16},{9,1},{17,9},{25,17},{10,2},{18,10},{26,18},{... | collective-permute-start | bytes 3145736 | tf_op jit(solution)/shard_map/ppermute | solution.py:426
  4.1 22.4 %collective-permute-start = (bf16[2,128,256]{2,1,0:T(8,128)(2,1)S(1)}, bf16[2,128,256]{2,1,0:T(8,128)(2,1)S(1)}, u32[]{:S(2)}, u32[]{:S(2)}) collective-permute-start(bf16[2,128,256]{2,1,0:T(8,128)(2,1)S(1)} %get-tuple-element.55), channel_id=1, source_target_pairs={{0,1},{1,2},{2,3},{3,4},{4,5},{5,6},{6,7},{8,9},{9,10},{10,11},{11... | collective-permute-start | bytes 393224 | tf_op jit(solution)/shard_map/ppermute | solution.py:426
  8.5 18.1 %collective-permute-start.1 = (bf16[2,128,256]{2,1,0:T(8,128)(2,1)S(1)}, bf16[2,128,256]{2,1,0:T(8,128)(2,1)S(1)}, u32[]{:S(2)}, u32[]{:S(2)}) collective-permute-start(bf16[2,128,256]{2,1,0:T(8,128)(2,1)S(1)} %get-tuple-element.56), channel_id=1, source_target_pairs={{1,0},{2,1},{3,2},{4,3},{5,4},{6,5},{7,6},{9,8},{10,9},{11,10},{12... | collective-permute-start | bytes 393224 | tf_op jit(solution)/shard_map/ppermute | solution.py:426
  9.8 16.8 %all-to-all-start = ((f32[8,8,128]{2,1,0:T(8,128)}), f32[8,8,128]{2,1,0:T(8,128)S(1)}, u32[]{:S(2)}, u32[]{:S(2)}) async-start(f32[8,8,128]{2,1,0:T(8,128)} %get-tuple-element.57), calls=%async_computation | async-start | bytes 65536 | tf_op jit(solution)/shard_map/all_to_all | solution.py:465
  26.6 0.6 copy-start.3
  26.6 0.7 copy-start.4
  26.6 0.7 copy-start.5
  27.3 6.8 %copy-start.1 = (bf16[1,2,8,128,256]{4,3,2,1,0:T(8,128)(2,1)S(1)}, bf16[1,2,8,128,256]{4,3,2,1,0:T(8,128)(2,1)}, u32[]{:S(2)}) copy-start(bf16[1,2,8,128,256]{4,3,2,1,0:T(8,128)(2,1)} %param.5) | copy-start | bytes 3145732
  27.3 6.8 %copy-start.2 = (bf16[3,256,256]{2,1,0:T(8,128)(2,1)S(1)}, bf16[3,256,256]{2,1,0:T(8,128)(2,1)}, u32[]{:S(2)}) copy-start(bf16[3,256,256]{2,1,0:T(8,128)(2,1)} %w_ref.3) | copy-start | bytes 1179652
  39.9 6.2 %collective-permute-start.3 = (f32[3072,128]{1,0:T(8,128)S(1)}, f32[3072,128]{1,0:T(8,128)S(1)}, u32[]{:S(2)}, u32[]{:S(2)}) collective-permute-start(f32[3072,128]{1,0:T(8,128)S(1)} %slice.4), channel_id=1, source_target_pairs={{0,32},{32,0},{1,33},{33,1},{2,34},{34,2},{3,35},{35,3},{4,36},{36... | collective-permute-start | bytes 4718600 | tf_op jit(solution)/shard_map/ppermute | solution.py:420
  42.6 10.2 %collective-permute-start.7 = (bf16[2,128,256]{2,1,0:T(8,128)(2,1)S(1)}, bf16[2,128,256]{2,1,0:T(8,128)(2,1)S(1)}, u32[]{:S(2)}, u32[]{:S(2)}) collective-permute-start(bf16[2,128,256]{2,1,0:T(8,128)(2,1)S(1)} %get-tuple-element.69), channel_id=1, source_target_pairs={{0,1},{1,2},{2,3},{3,4},{4,5},{5,6},{6,7},{8,9},{9,10},{10,11},{11... | collective-permute-start | bytes 393224 | tf_op jit(solution)/shard_map/ppermute | solution.py:426
  44.8 8.0 %collective-permute-start.8 = (bf16[2,128,256]{2,1,0:T(8,128)(2,1)S(1)}, bf16[2,128,256]{2,1,0:T(8,128)(2,1)S(1)}, u32[]{:S(2)}, u32[]{:S(2)}) collective-permute-start(bf16[2,128,256]{2,1,0:T(8,128)(2,1)S(1)} %get-tuple-element.70), channel_id=1, source_target_pairs={{1,0},{2,1},{3,2},{4,3},{5,4},{6,5},{7,6},{9,8},{10,9},{11,10},{12... | collective-permute-start | bytes 393224 | tf_op jit(solution)/shard_map/ppermute | solution.py:426
  46.8 12.2 %collective-permute-start.4 = (bf16[768,128]{1,0:T(8,128)(2,1)S(1)}, bf16[768,128]{1,0:T(8,128)(2,1)S(1)}, u32[]{:S(2)}, u32[]{:S(2)}) collective-permute-start(bf16[768,128]{1,0:T(8,128)(2,1)S(1)} %get-tuple-element.66), channel_id=1, source_target_pairs={{0,8},{8,16},{16,24},{24,0},{1,9},{9,17},{17,25},{25,1},{2,10},{10... | collective-permute-start | bytes 589832 | tf_op jit(solution)/shard_map/ppermute | solution.py:432
  49.2 11.7 %collective-permute-start.5 = (bf16[768,128]{1,0:T(8,128)(2,1)S(1)}, bf16[768,128]{1,0:T(8,128)(2,1)S(1)}, u32[]{:S(2)}, u32[]{:S(2)}) collective-permute-start(bf16[768,128]{1,0:T(8,128)(2,1)S(1)} %get-tuple-element.67), channel_id=1, source_target_pairs={{0,16},{8,24},{16,0},{24,8},{1,17},{9,25},{17,1},{25,9},{2,18},{10... | collective-permute-start | bytes 589832 | tf_op jit(solution)/shard_map/ppermute | solution.py:432
  52.0 8.9 %collective-permute-start.6 = (bf16[768,128]{1,0:T(8,128)(2,1)S(1)}, bf16[768,128]{1,0:T(8,128)(2,1)S(1)}, u32[]{:S(2)}, u32[]{:S(2)}) collective-permute-start(bf16[768,128]{1,0:T(8,128)(2,1)S(1)} %get-tuple-element.68), channel_id=1, source_target_pairs={{0,24},{8,0},{16,8},{24,16},{1,25},{9,1},{17,9},{25,17},{2,26},{10... | collective-permute-start | bytes 589832 | tf_op jit(solution)/shard_map/ppermute | solution.py:432
  60.9 29.9 %copy-start = (bf16[1,2,8,128,256]{4,3,2,1,0:T(8,128)(2,1)S(1)}, bf16[1,2,8,128,256]{4,3,2,1,0:T(8,128)(2,1)}, u32[]{:S(2)}) copy-start(bf16[1,2,8,128,256]{4,3,2,1,0:T(8,128)(2,1)} %param.4) | copy-start | bytes 3145732
  61.6 8.3 %collective-permute-start.9 = (f32[192,128]{1,0:T(8,128)S(1)}, f32[192,128]{1,0:T(8,128)S(1)}, u32[]{:S(2)}, u32[]{:S(2)}) collective-permute-start(f32[192,128]{1,0:T(8,128)S(1)} %get-tuple-element.80), channel_id=1, source_target_pairs={{0,64},{64,128},{128,192},{192,0},{1,65},{65,129},{129,193},{193,1... | collective-permute-start | bytes 294920 | tf_op jit(solution)/shard_map/ppermute | solution.py:432
  63.0 6.9 %collective-permute-start.10 = (f32[192,128]{1,0:T(8,128)S(1)}, f32[192,128]{1,0:T(8,128)S(1)}, u32[]{:S(2)}, u32[]{:S(2)}) collective-permute-start(f32[192,128]{1,0:T(8,128)S(1)} %get-tuple-element.81), channel_id=1, source_target_pairs={{0,128},{64,192},{128,0},{192,64},{1,129},{65,193},{129,1},{193,65... | collective-permute-start | bytes 294920 | tf_op jit(solution)/shard_map/ppermute | solution.py:432
  65.6 4.6 %collective-permute-start.11 = (f32[192,128]{1,0:T(8,128)S(1)}, f32[192,128]{1,0:T(8,128)S(1)}, u32[]{:S(2)}, u32[]{:S(2)}) collective-permute-start(f32[192,128]{1,0:T(8,128)S(1)} %get-tuple-element.82), channel_id=1, source_target_pairs={{0,192},{64,0},{128,64},{192,128},{1,193},{65,1},{129,65},{193,129... | collective-permute-start | bytes 294920 | tf_op jit(solution)/shard_map/ppermute | solution.py:432
  66.7 28.2 %collective-permute-start.15 = (bf16[2,1024,256]{2,1,0:T(8,128)(2,1)S(1)}, bf16[2,1024,256]{2,1,0:T(8,128)(2,1)S(1)}, u32[]{:S(2)}, u32[]{:S(2)}) collective-permute-start(bf16[2,1024,256]{2,1,0:T(8,128)(2,1)S(1)} %get-tuple-element.91.hid_ref), channel_id=1, source_target_pairs={{0,8},{8,16},{16,24},{1,9},{9,17},{17,25},{2,10},{10,18},{18,26},{... | collective-permute-start | bytes 3145736 | tf_op jit(solution)/shard_map/ppermute | solution.py:426
  88.1 6.3 %collective-permute-start.14 = (bf16[192,128]{1,0:T(8,128)(2,1)S(1)}, bf16[192,128]{1,0:T(8,128)(2,1)S(1)}, u32[]{:S(2)}, u32[]{:S(2)}) collective-permute-start(bf16[192,128]{1,0:T(8,128)(2,1)S(1)} %get-tuple-element.87), channel_id=1, source_target_pairs={{0,192},{64,0},{128,64},{192,128},{1,193},{65,1},{129,65},{193,129... | collective-permute-start | bytes 147464 | tf_op jit(solution)/shard_map/ppermute | solution.py:432
  90.2 4.5 %collective-permute-start.13 = (bf16[192,128]{1,0:T(8,128)(2,1)S(1)}, bf16[192,128]{1,0:T(8,128)(2,1)S(1)}, u32[]{:S(2)}, u32[]{:S(2)}) collective-permute-start(bf16[192,128]{1,0:T(8,128)(2,1)S(1)} %get-tuple-element.87), channel_id=1, source_target_pairs={{0,128},{64,192},{128,0},{192,64},{1,129},{65,193},{129,1},{193,65... | collective-permute-start | bytes 147464 | tf_op jit(solution)/shard_map/ppermute | solution.py:432
  90.2 4.7 %collective-permute-start.12 = (bf16[192,128]{1,0:T(8,128)(2,1)S(1)}, bf16[192,128]{1,0:T(8,128)(2,1)S(1)}, u32[]{:S(2)}, u32[]{:S(2)}) collective-permute-start(bf16[192,128]{1,0:T(8,128)(2,1)S(1)} %get-tuple-element.87), channel_id=1, source_target_pairs={{0,64},{64,128},{128,192},{192,0},{1,65},{65,129},{129,193},{193,1... | collective-permute-start | bytes 147464 | tf_op jit(solution)/shard_map/ppermute | solution.py:432
  94.9 7.7 %collective-permute-start.18 = (bf16[768,128]{1,0:T(8,128)(2,1)S(1)}, bf16[768,128]{1,0:T(8,128)(2,1)S(1)}, u32[]{:S(2)}, u32[]{:S(2)}) collective-permute-start(bf16[768,128]{1,0:T(8,128)(2,1)S(1)} %pad_maximum_fusion.1), channel_id=1, source_target_pairs={{0,24},{8,0},{16,8},{24,16},{1,25},{9,1},{17,9},{25,17},{2,26},{10... | collective-permute-start | bytes 589832 | tf_op jit(solution)/shard_map/ppermute | solution.py:432
  97.9 6.1 %collective-permute-start.17 = (bf16[768,128]{1,0:T(8,128)(2,1)S(1)}, bf16[768,128]{1,0:T(8,128)(2,1)S(1)}, u32[]{:S(2)}, u32[]{:S(2)}) collective-permute-start(bf16[768,128]{1,0:T(8,128)(2,1)S(1)} %pad_maximum_fusion.1), channel_id=1, source_target_pairs={{0,16},{8,24},{16,0},{24,8},{1,17},{9,25},{17,1},{25,9},{2,18},{10... | collective-permute-start | bytes 589832 | tf_op jit(solution)/shard_map/ppermute | solution.py:432
  97.9 7.8 %collective-permute-start.16 = (bf16[768,128]{1,0:T(8,128)(2,1)S(1)}, bf16[768,128]{1,0:T(8,128)(2,1)S(1)}, u32[]{:S(2)}, u32[]{:S(2)}) collective-permute-start(bf16[768,128]{1,0:T(8,128)(2,1)S(1)} %pad_maximum_fusion.1), channel_id=1, source_target_pairs={{0,8},{8,16},{16,24},{24,0},{1,9},{9,17},{17,25},{25,1},{2,10},{10... | collective-permute-start | bytes 589832 | tf_op jit(solution)/shard_map/ppermute | solution.py:432
  105.8 8.8 %collective-permute-start.19 = (bf16[3072,128]{1,0:T(8,128)(2,1)S(1)}, bf16[3072,128]{1,0:T(8,128)(2,1)S(1)}, u32[]{:S(2)}, u32[]{:S(2)}) collective-permute-start(bf16[3072,128]{1,0:T(8,128)(2,1)S(1)} %pad_maximum_fusion.u_ref), channel_id=1, source_target_pairs={{0,32},{32,0},{1,33},{33,1},{2,34},{34,2},{3,35},{35,3},{4,36},{36... | collective-permute-start | bytes 2359304 | tf_op jit(solution)/shard_map/ppermute | solution.py:420

commit v9 on v8

--- a/solution.py
+++ b/solution.py
@@ -199,10 +199,15 @@
         bot_ref[f] = pg_ref[f, 896:1024, :]
 
 
-def slab_rows(info, unit, part):
+def slab_rows(x, y, unit, part):
     piece = (unit % 3) * 4 + part
-    x, y = (unit // 3 - info[3]) & 3, (piece // 3 - info[4]) & 3
+    x, y = (unit // 3 - x) & 3, (piece // 3 - y) & 3
     return pl.multiple_of(x * 768 + y * 192 + (piece % 3) * 64, 64)
+
+
+def row_of(unit, part):
+    piece = (unit % 3) * 4 + part
+    return unit // 3 * 768 + piece // 3 * 192 + piece % 3 * 64
 
 
 def grads_kernel(info, act_ref, pg_ref, hid_ref, cot_ref, later_ref, g_ref):
@@ -210,7 +215,7 @@
         base = ((tap // 6) ^ info[0]) * 3072
         for lh in range(2):
             for part in range(4):
-                at = pl.multiple_of(base + slab_rows(info, (tap % 6) * 2 + lh, part), 64)
+                at = pl.multiple_of(base + row_of((tap % 6) * 2 + lh, part), 64)
                 g_ref[pl.ds(at, 64), :] = v[part * 64 : part * 64 + 64, lh * 128 : lh * 128 + 128]
 
     for i in range(3):
@@ -324,37 +329,35 @@
     return jnp.where(size < 1e-37, 0.0, jnp.where(u < 0, -root, root))
 
 
-def pair_kernel(g_ref, got_ref, own_ref, *sent):
+def pair_kernel(g_ref, got_ref, o_hbm, o_ref, sems):
+    copies = []
     for k in range(4):
 
         def part(r, _):
-            at = pl.multiple_of(r * 128, 128)
-            rows = pl.ds(pl.multiple_of(at + k * 768, 128), 128)
-            v = g_ref[rows, :] + got_ref[rows, :]
-            if k == 0:
-                own_ref[pl.ds(at, 128), :] = v
-            else:
-                sent[k - 1][pl.ds(at, 128), :] = coded(v)
+            rows = pl.ds(pl.multiple_of(r * 128 + k * 768, 128), 128)
+            o_ref[rows, :] = coded(g_ref[rows, :] + got_ref[rows, :])
             return 0
 
         lax.fori_loop(0, 6, part, 0)
-
-
-def x_kernel(own_ref, a_ref, b_ref, c_ref, mine_ref, *sent):
-    for k in range(4):
-
-        def part(r, _):
-            at = pl.multiple_of(r * 64, 64)
-            rows = pl.ds(pl.multiple_of(at + k * 192, 64), 64)
-            v = own_ref[rows, :] + decoded(a_ref[rows, :]) + decoded(b_ref[rows, :]) + decoded(c_ref[rows, :])
-            (mine_ref, *sent)[k][pl.ds(at, 64), :] = v
-            return 0
-
-        lax.fori_loop(0, 3, part, 0)
-
-
-def y_kernel(own_ref, a_ref, b_ref, c_ref, gst_ref, o_ref):
-    code = coded(own_ref[...] + a_ref[...] + b_ref[...] + c_ref[...])
+        rows = pl.ds(k * 768, 768)
+        copies.append(pltpu.make_async_copy(o_ref.at[rows, :], o_hbm.at[rows, :], sems.at[k]))
+        copies[-1].start()
+    for c in copies:
+        c.wait()
+
+
+def xy_kernel(u_ref, gst_ref, o_ref):
+    def part(r, _):
+        rows = pl.ds(pl.multiple_of(r * 64, 64), 64)
+        total = decoded(u_ref[0, rows, :])
+        for peer in range(1, 16):
+            total = total + decoded(u_ref[peer, rows, :])
+        code = coded(total)
+        for peer in range(8):
+            o_ref[peer, rows, :] = code
+        return 0
+
+    lax.fori_loop(0, 3, part, 0)
     rest, pieces = gst_ref[0], []
     for _ in range(3):
         piece = rest.astype(BF16).astype(F32)
@@ -362,7 +365,6 @@
         rest = rest - piece
     sums = jnp.concatenate([*pieces, jnp.zeros_like(rest)], axis=0).astype(BF16)
     for peer in range(8):
-        o_ref[peer, 0:192, :] = code
         o_ref[peer, 192:224, :] = sums
 
 
@@ -387,7 +389,7 @@
     acc = jnp.zeros((8, 128), F32)
     for unit in range(12):
         for part in range(4):
-            v = decoded(u_ref[pl.ds(slab_rows(info, unit, part), 64), :])
+            v = decoded(u_ref[pl.ds(slab_rows(info[3], info[4], unit, part), 64), :])
             w_ref[unit * 256 + part * 64 : unit * 256 + part * 64 + 64, :] = v
             acc = acc + fold(v * v)
     acc_ref[...] = acc
@@ -491,15 +493,21 @@
     got = swapped(send, "core")
     gup = moved(bot, HEIGHT, 1)
     gdn = moved(top, HEIGHT, -1)
-    quarter = out((768, 128), BF16)
-    own, *sent = call(
-        pair_kernel, [out((768, 128), F32), quarter, quarter, quarter], [g, got], 1 << 21
-    )
-    got = shifts(sent, TM)
+    slab = (3072, 128)
+    (code,) = call(
+        pair_kernel,
+        [out(slab, BF16)],
+        [g, got],
+        1 << 21,
+        outside=(0,),
+        scratch=[pltpu.VMEM(slab, BF16), pltpu.SemaphoreType.DMA((4,))],
+    )
+    code, pg_late = tied((code, pg))
+    code = lax.all_to_all(code.reshape(16, 192, 128), (TM, "y"), 0, 0, tiled=True)
     ng, gst = call(
         lambda *refs: backward_kernel(members, *refs),
         [out(flat, F32), out((1, 8, 128), F32)],
-        [pg, gup, gdn, in_hbm(w9), in_hbm(x), st],
+        [pg_late, gup, gdn, in_hbm(w9), in_hbm(x), st],
         9 * gflop,
         loose=(3, 4, 5),
         outside=(0,),
@@ -512,14 +520,10 @@
             pltpu.SemaphoreType.DMA((12,)),
         ],
     )
-    got, gst = tied((got, gst))
-    part = out((192, 128), F32)
-    own, *sent = call(x_kernel, [part] * 4, [own, *got], 1 << 21)
-    own, sent, hid_sent = tied((own, sent, hid))
+    gst, hid_sent = tied((gst, hid))
     prev = moved(hid_sent, TM, 1)
-    got = shifts(sent, "y")
-    got = tied(got)
-    (pieces,) = call(y_kernel, [out((8, 224, 128), BF16)], [own, *got, gst], 1 << 20)
+    code, gst = tied((code, gst))
+    (pieces,) = call(xy_kernel, [out((8, 224, 128), BF16)], [code, gst], 1 << 20)
     pieces = lax.all_to_all(pieces, HEIGHT, 0, 0, tiled=True)
     mine, gst = call(z_kernel, [out((192, 128), BF16), out((1, 8, 128), F32)], [pieces], 1 << 20)
     (input_grad,) = call(
@@ -533,7 +537,6 @@
     (block_output,) = call(block_kernel, [out(flat, BF16)], [x, hid, prev, temporal_kernel], 3 * gflop)
     mine = gathered(mine, TM)
     mine, block_output = tied((mine, block_output))
-    slab = (3072, 128)
     tile = out((8, 128), F32)
     own, acc = call(half_kernel, [out(slab, F32), tile], [info, mine], 1 << 21, smem=1)
     clipped_spatial, clipped_temporal = call(

time: 119 us -> 122 us (1.025)
  Pallas kernels: 33.3 us -> 37.8 us
  waiting for transfers between devices: 14.8 us -> 17.3 us
  starting transfers between devices: 50.6 us -> 48.5 us
  blocking collectives: 17.3 us -> 15.3 us
    ppermute x12 -> x6, starting transfers between devices: 17.6 us -> 5.83 us  [shifts(): lax.ppermute(m, axis, [(i, (i + d) % n) for i in range(n)])]
    all_to_all x0 -> x1, starting transfers between devices: none -> 8.14 us  [body(): lax.all_to_all(code.reshape(16, 192, 128), (TM, 'y'), 0, 0, tiled=True)]
    ppermute x12 -> x6, waiting for transfers between devices: 7.4 us -> 2.35 us  [shifts(): lax.ppermute(m, axis, [(i, (i + d) % n) for i in range(n)])]
    ppermute x6, waiting for transfers between devices: 0.02 us -> 4.54 us  [moved(): return lax.ppermute(x, axes, route)]
    pallas_call x13 -> x12, Pallas kernels: 33.3 us -> 37.8 us  [call(): pl.pallas_call(kernel, out_shape=tuple((pltpu.HBM(o.shape, o.dtype) if i...]
    ppermute x2, waiting for transfers between devices: 0.54 us -> 3.57 us  [swapped(): return lax.ppermute(x, axis, [(0, 1), (1, 0)])]
    all_to_all x1, blocking collectives: 17.3 us -> 15.3 us  [body(): pieces = lax.all_to_all(pieces, HEIGHT, 0, 0, tiled=True)]
    ppermute x6, starting transfers between devices: 13.6 us -> 15 us  [moved(): return lax.ppermute(x, axes, route)]
  transfers between devices with their start and end apart: 21 -> 16, of which waited for: 9 -> 7; matrix products, arithmetic and copies ran while one was open for 0% -> 0% of each run, Pallas kernels for 20% -> 22%
where the time goes in v9:
time: 122 us; the launch traced here: 121 us
  starting transfers between devices  48.5 us (40%)
  Pallas kernels  37.8 us (31%)
  waiting for transfers between devices  17.3 us (14%)
  blocking collectives  15.3 us (13%)
    pallas_call x12, Pallas kernels, call(): pl.pallas_call(kernel, out_shape=tuple((pltpu.HBM(o.shape, o.dtype) if i...  37.8 us
    all_to_all x1, blocking collectives, body(): pieces = lax.all_to_all(pieces, HEIGHT, 0, 0, tiled=True)  15.3 us
    ppermute x6, starting transfers between devices, moved(): return lax.ppermute(x, axes, route)  15 us
    all_to_all x1, starting transfers between devices, body(): st = in_hbm(lax.all_to_all(st, HEIGHT, 0, 0, tiled=True))  9.85 us
    ppermute x2, starting transfers between devices, swapped(): return lax.ppermute(x, axis, [(0, 1), (1, 0)])  9.74 us
    all_to_all x1, starting transfers between devices, body(): lax.all_to_all(code.reshape(16, 192, 128), (TM, 'y'), 0, 0, tiled=True)  8.14 us
    all_to_all x1, waiting for transfers between devices, body(): st = in_hbm(lax.all_to_all(st, HEIGHT, 0, 0, tiled=True))  6.83 us
    ppermute x6, starting transfers between devices, shifts(): lax.ppermute(m, axis, [(i, (i + d) % n) for i in range(n)])  5.83 us
  transfers between devices with their start and end apart: 16, of which 7 were waited for; matrix products, arithmetic and copies ran while one was open for 0% of the time, Pallas kernels for 22%

profile of v9, /device:TPU:1, one launch (start us, length us, event | category | flops | bytes accessed | tf_op | source)
XLA Modules:
  0.0 121.0 jit_solution(4685412112372010625)
XLA Ops:
  0.6 1.3 %collective-permute-start.2 = (bf16[2,1024,256]{2,1,0:T(8,128)(2,1)}, bf16[2,1024,256]{2,1,0:T(8,128)(2,1)S(1)}, u32[]{:S(2)}, u32[]{:S(2)}) collective-permute-start(bf16[2,1024,256]{2,1,0:T(8,128)(2,1)} %bitcast.17), channel_id=1, source_target_pairs={{8,0},{16,8},{24,16},{9,1},{17,9},{25,17},{10,2},{18,10},{26,18},{... | collective-permute-start | bytes 3145736 | tf_op jit(solution)/shard_map/ppermute | solution.py:428
  1.9 2.2 %shard_map.75 = (f32[8,8,128]{2,1,0:T(8,128)}, bf16[2,128,256]{2,1,0:T(8,128)(2,1)S(1)}, bf16[2,128,256]{2,1,0:T(8,128)(2,1)S(1)}) custom-call(bf16[2,1024,256]{2,1,0:T(8,128)(2,1)} %bitcast.12), custom_call_target="tpu_custom_call" | custom-call | flops 2097152 | bytes 1343488 | tf_op jit(solution)/shard_map/pallas_call | solution.py:33
  4.1 4.4 %collective-permute-start = (bf16[2,128,256]{2,1,0:T(8,128)(2,1)S(1)}, bf16[2,128,256]{2,1,0:T(8,128)(2,1)S(1)}, u32[]{:S(2)}, u32[]{:S(2)}) collective-permute-start(bf16[2,128,256]{2,1,0:T(8,128)(2,1)S(1)} %get-tuple-element.41), channel_id=1, source_target_pairs={{0,1},{1,2},{2,3},{3,4},{4,5},{5,6},{6,7},{8,9},{9,10},{10,11},{11... | collective-permute-start | bytes 393224 | tf_op jit(solution)/shard_map/ppermute | solution.py:428
  8.5 1.3 %collective-permute-start.1 = (bf16[2,128,256]{2,1,0:T(8,128)(2,1)S(1)}, bf16[2,128,256]{2,1,0:T(8,128)(2,1)S(1)}, u32[]{:S(2)}, u32[]{:S(2)}) collective-permute-start(bf16[2,128,256]{2,1,0:T(8,128)(2,1)S(1)} %get-tuple-element.42), channel_id=1, source_target_pairs={{1,0},{2,1},{3,2},{4,3},{5,4},{6,5},{7,6},{9,8},{10,9},{11,10},{12... | collective-permute-start | bytes 393224 | tf_op jit(solution)/shard_map/ppermute | solution.py:428
  9.8 9.8 %all-to-all-start = ((f32[8,8,128]{2,1,0:T(8,128)}), f32[8,8,128]{2,1,0:T(8,128)S(1)}, u32[]{:S(2)}, u32[]{:S(2)}) async-start(f32[8,8,128]{2,1,0:T(8,128)} %get-tuple-element.43), calls=%async_computation | async-start | bytes 65536 | tf_op jit(solution)/shard_map/all_to_all | solution.py:467
  19.6 0.1 stack.23.refs_0_.info
  19.7 6.8 %all-to-all-done.refs_4_.refs_5_.refs_3_ = f32[8,8,128]{2,1,0:T(8,128)S(1)} async-done(((f32[8,8,128]{2,1,0:T(8,128)}), f32[8,8,128]{2,1,0:T(8,128)S(1)}, u32[]{:S(2)}, u32[]{:S(2)}) %all-to-all-start) | async-done | bytes 32800 | tf_op jit(solution)/shard_map/all_to_all | solution.py:467
  26.6 0.0 copy-start.7
  26.6 0.6 copy-done.5
  27.2 0.1 copy-done.6
  27.2 0.0 copy-done.7
  27.3 7.8 %shard_map.76 = (bf16[2,1280,768]{2,1,0:T(8,128)(2,1)S(1)}, bf16[2,1024,256]{2,1,0:T(8,128)(2,1)}, f32[2,1024,256]{2,1,0:T(8,128)S(1)}) custom-call(s32[5]{0:T(128)S(1)} %stack.23.refs_0_.info, bf16[2,1024,256]{2,1,0:T(8,128)(2,1)} %bitcast.13, bf16[2,128,256]{2,1,0:T(8,128)(2,1)} %copy-done.6, bf16[2,128,256]{2,1,0:T(8,128)(2,1)} %copy-done.7, ...), custom_call_target="tpu_custom_call" | custom-call | flops 2415919104 | bytes 9601044 | tf_op jit(solution)/shard_map/pallas_call | solution.py:33
  35.0 0.0 collective-permute-done.2.later_ref
  35.1 1.6 %shard_map.77 = (bf16[2,1024,256]{2,1,0:T(8,128)(2,1)S(1)}, bf16[2,128,256]{2,1,0:T(8,128)(2,1)S(1)}, bf16[2,128,256]{2,1,0:T(8,128)(2,1)S(1)}) custom-call(bf16[2,1024,256]{2,1,0:T(8,128)(2,1)S(1)} %bitcast.18, bf16[2,1024,256]{2,1,0:T(8,128)(2,1)S(1)} %collective-permute-done.2.later_ref, f32[2,1024,256]{2,1,0:T(8,128)S(1)} %get-tuple-element.45.slope_ref, ...), custom_call_target="tpu_custom_call" | custom-call | flops 805306368 | bytes 5898240 | tf_op jit(solution)/shard_map/pallas_call | solution.py:33
  36.7 0.0 copy-start.3
  36.7 5.1 %shard_map.78.g_ref = f32[6144,128]{1,0:T(8,128)S(1)} custom-call(s32[5]{0:T(128)S(1)} %stack.23.refs_0_.info, bf16[2,1280,768]{2,1,0:T(8,128)(2,1)S(1)} %get-tuple-element.44.act_ref, bf16[2,1024,256]{2,1,0:T(8,128)(2,1)S(1)} %get-tuple-element.52.pg_ref.refs_0_, bf16[2,1024,256]{2,1,0:T(8,128)(2,1)} %get-tuple-element.63.hid_ref, ...), custom_call_target="tpu_custom_call" | custom-call | flops 3221225472 | bytes 11272212 | tf_op jit(solution)/shard_map/pallas_call | solution.py:33
  41.8 0.1 slice.4
  41.9 2.7 %collective-permute-start.3 = (f32[3072,128]{1,0:T(8,128)S(1)}, f32[3072,128]{1,0:T(8,128)S(1)}, u32[]{:S(2)}, u32[]{:S(2)}) collective-permute-start(f32[3072,128]{1,0:T(8,128)S(1)} %slice.4), channel_id=1, source_target_pairs={{0,32},{32,0},{1,33},{33,1},{2,34},{34,2},{3,35},{35,3},{4,36},{36... | collective-permute-start | bytes 4718600 | tf_op jit(solution)/shard_map/ppermute | solution.py:422
  44.7 3.0 %collective-permute-done.3.got_ref = f32[3072,128]{1,0:T(8,128)S(1)} collective-permute-done((f32[3072,128]{1,0:T(8,128)S(1)}, f32[3072,128]{1,0:T(8,128)S(1)}, u32[]{:S(2)}, u32[]{:S(2)}) %collective-permute-start.3) | collective-permute-done | bytes 1572896 | tf_op jit(solution)/shard_map/ppermute | solution.py:422
  47.7 1.5 %shard_map.79 = bf16[3072,128]{1,0:T(8,128)(2,1)} custom-call(f32[6144,128]{1,0:T(8,128)S(1)} %shard_map.78.g_ref, f32[3072,128]{1,0:T(8,128)S(1)} %collective-permute-done.3.got_ref), custom_call_target="tpu_custom_call" | custom-call | flops 2097152 | bytes 5505024 | tf_op jit(solution)/shard_map/pallas_call | solution.py:33
  49.2 0.0 copy-start.4
  49.2 8.1 %all-to-all-start.1 = ((bf16[16,192,128]{2,1,0:T(8,128)(2,1)}), bf16[16,192,128]{2,1,0:T(8,128)(2,1)S(1)}, u32[]{:S(2)}, u32[]{:S(2)}) async-start(bf16[16,192,128]{2,1,0:T(8,128)(2,1)} %bitcast.21), calls=%async_computation.1 | async-start | bytes 1572864 | tf_op jit(solution)/shard_map/all_to_all | solution.py:506
  57.4 2.2 %collective-permute-start.4 = (bf16[2,128,256]{2,1,0:T(8,128)(2,1)S(1)}, bf16[2,128,256]{2,1,0:T(8,128)(2,1)S(1)}, u32[]{:S(2)}, u32[]{:S(2)}) collective-permute-start(bf16[2,128,256]{2,1,0:T(8,128)(2,1)S(1)} %get-tuple-element.53), channel_id=1, source_target_pairs={{0,1},{1,2},{2,3},{3,4},{4,5},{5,6},{6,7},{8,9},{9,10},{10,11},{11... | collective-permute-start | bytes 393224 | tf_op jit(solution)/shard_map/ppermute | solution.py:428
  59.6 1.5 %collective-permute-start.5 = (bf16[2,128,256]{2,1,0:T(8,128)(2,1)S(1)}, bf16[2,128,256]{2,1,0:T(8,128)(2,1)S(1)}, u32[]{:S(2)}, u32[]{:S(2)}) collective-permute-start(bf16[2,128,256]{2,1,0:T(8,128)(2,1)S(1)} %get-tuple-element.54), channel_id=1, source_target_pairs={{1,0},{2,1},{3,2},{4,3},{5,4},{6,5},{7,6},{9,8},{10,9},{11,10},{12... | collective-permute-start | bytes 393224 | tf_op jit(solution)/shard_map/ppermute | solution.py:428
  61.1 0.7 collective-permute-done.4.refs_1_
  61.8 3.8 %collective-permute-done.5.refs_2_ = bf16[2,128,256]{2,1,0:T(8,128)(2,1)S(1)} collective-permute-done((bf16[2,128,256]{2,1,0:T(8,128)(2,1)S(1)}, bf16[2,128,256]{2,1,0:T(8,128)(2,1)S(1)}, u32[]{:S(2)}, u32[]{:S(2)}) %collective-permute-start.5) | collective-permute-done | bytes 131104 | tf_op jit(solution)/shard_map/ppermute | solution.py:428
  65.6 6.1 %shard_map.80 = (f32[2,1024,256]{2,1,0:T(8,128)}, f32[1,8,128]{2,1,0:T(8,128)S(1)}) custom-call(bf16[2,1024,256]{2,1,0:T(8,128)(2,1)S(1)} %copy-done.4, bf16[2,128,256]{2,1,0:T(8,128)(2,1)S(1)} %collective-permute-done.4.refs_1_, bf16[2,128,256]{2,1,0:T(8,128)(2,1)S(1)} %collective-permute-done.5.refs_2_, bf16[3,3,256,256]{3,2,1,0:T(8,128)(2,1)} %refs_3_.1, ...), custom_call_target="tpu_custom_call" | custom-call | flops 2415919104 | bytes 5672960 | tf_op jit(solution)/shard_map/pallas_call | solution.py:33
  71.7 0.0 copy-start
  71.7 4.4 %collective-permute-start.9 = (bf16[2,1024,256]{2,1,0:T(8,128)(2,1)}, bf16[2,1024,256]{2,1,0:T(8,128)(2,1)}, u32[]{:S(2)}, u32[]{:S(2)}) collective-permute-start(bf16[2,1024,256]{2,1,0:T(8,128)(2,1)} %get-tuple-element.63.hid_ref), channel_id=1, source_target_pairs={{0,8},{8,16},{16,24},{1,9},{9,17},{17,25},{2,10},{10,18},{18,26},{... | collective-permute-start | bytes 3145736 | tf_op jit(solution)/shard_map/ppermute | solution.py:428
  76.1 0.0 all-to-all-done.1.u_ref
  76.1 0.9 shard_map.81
  76.9 15.3 %all_to_all.15.u_ref = bf16[8,224,128]{2,1,0:T(8,128)(2,1)S(1)} all-to-all(bf16[8,224,128]{2,1,0:T(8,128)(2,1)S(1)} %shard_map.81), channel_id=1, replica_groups=mesh['y'=4,'core'=2,'tm'=4,'height'=8] {'height'}, dimensions={0} | all-to-all | bytes 917504 | tf_op jit(solution)/shard_map/all_to_all | solution.py:527
  92.3 0.5 shard_map.82
  92.7 2.5 %collective-permute-start.8 = (bf16[192,128]{1,0:T(8,128)(2,1)S(1)}, bf16[192,128]{1,0:T(8,128)(2,1)S(1)}, u32[]{:S(2)}, u32[]{:S(2)}) collective-permute-start(bf16[192,128]{1,0:T(8,128)(2,1)S(1)} %get-tuple-element.59), channel_id=1, source_target_pairs={{0,192},{64,0},{128,64},{192,128},{1,193},{65,1},{129,65},{193,129... | collective-permute-start | bytes 147464 | tf_op jit(solution)/shard_map/ppermute | solution.py:434
  95.2 0.6 collective-permute-start.7
  95.8 0.4 collective-permute-start.6
  96.2 3.5 %shard_map.83 = bf16[2,1024,256]{2,1,0:T(8,128)(2,1)} custom-call(bf16[2,1024,256]{2,1,0:T(8,128)(2,1)S(1)} %bitcast.15, bf16[2,1024,256]{2,1,0:T(8,128)(2,1)S(1)} %bitcast.20, f32[2,1024,256]{2,1,0:T(8,128)} %get-tuple-element.64.refs_2_, f32[8,8,128]{2,1,0:T(8,128)} %copy-done.5, f32[1,8,128]{2,1,0:T(8,128)S(1)} %get-tuple-element.65.refs_4_), custom_call_target="tpu_custom_call" | custom-call | flops 2097152 | bytes 5279744 | tf_op jit(solution)/shard_map/pallas_call | solution.py:33
  99.7 0.4 collective-permute-done.6
  100.2 0.1 collective-permute-start.12
  100.3 2.0 %collective-permute-start.11 = (bf16[768,128]{1,0:T(8,128)(2,1)S(1)}, bf16[768,128]{1,0:T(8,128)(2,1)S(1)}, u32[]{:S(2)}, u32[]{:S(2)}) collective-permute-start(bf16[768,128]{1,0:T(8,128)(2,1)S(1)} %pad_maximum_fusion.1), channel_id=1, source_target_pairs={{0,16},{8,24},{16,0},{24,8},{1,17},{9,25},{17,1},{25,9},{2,18},{10... | collective-permute-start | bytes 589832 | tf_op jit(solution)/shard_map/ppermute | solution.py:434
  102.3 0.3 collective-permute-start.10
  102.6 4.0 %shard_map.84 = bf16[2,1024,256]{2,1,0:T(8,128)(2,1)} custom-call(bf16[2,1024,256]{2,1,0:T(8,128)(2,1)S(1)} %bitcast.16, bf16[2,1024,256]{2,1,0:T(8,128)(2,1)} %get-tuple-element.63.hid_ref, bf16[2,1024,256]{2,1,0:T(8,128)(2,1)} %collective-permute-done.9.prev_ref, bf16[3,256,256]{2,1,0:T(8,128)(2,1)S(1)} %copy-done.2), custom_call_target="tpu_custom_call" | custom-call | flops 805306368 | bytes 4587520 | tf_op jit(solution)/shard_map/pallas_call | solution.py:33
  106.6 1.9 %collective-permute-done.10 = bf16[768,128]{1,0:T(8,128)(2,1)S(1)} collective-permute-done((bf16[768,128]{1,0:T(8,128)(2,1)S(1)}, bf16[768,128]{1,0:T(8,128)(2,1)S(1)}, u32[]{:S(2)}, u32[]{:S(2)}) %collective-permute-start.10) | collective-permute-done | bytes 196640 | tf_op jit(solution)/shard_map/ppermute | solution.py:434
  108.5 0.1 pad_maximum_fusion.u_ref
  108.6 7.0 %collective-permute-start.13 = (bf16[3072,128]{1,0:T(8,128)(2,1)S(1)}, bf16[3072,128]{1,0:T(8,128)(2,1)S(1)}, u32[]{:S(2)}, u32[]{:S(2)}) collective-permute-start(bf16[3072,128]{1,0:T(8,128)(2,1)S(1)} %pad_maximum_fusion.u_ref), channel_id=1, source_target_pairs={{0,32},{32,0},{1,33},{33,1},{2,34},{34,2},{3,35},{35,3},{4,36},{36... | collective-permute-start | bytes 2359304 | tf_op jit(solution)/shard_map/ppermute | solution.py:422
  115.6 1.4 %shard_map.85 = (f32[3072,128]{1,0:T(8,128)S(1)}, f32[8,128]{1,0:T(8,128)S(1)}) custom-call(s32[5]{0:T(128)S(1)} %stack.23.refs_0_.info, bf16[3072,128]{1,0:T(8,128)(2,1)S(1)} %pad_maximum_fusion.u_ref), custom_call_target="tpu_custom_call" | custom-call | flops 2097152 | bytes 2363412 | tf_op jit(solution)/shard_map/pallas_call | solution.py:33
  117.0 0.5 collective-permute-done.13.refs_3_
  117.5 3.3 %shard_map.86 = (f32[9,256,256]{2,1,0:T(8,128)}, f32[3,256,256]{2,1,0:T(8,128)}) custom-call(s32[5]{0:T(128)S(1)} %stack.23.refs_0_.info, f32[3072,128]{1,0:T(8,128)S(1)} %get-tuple-element.74.refs_1_, f32[8,128]{1,0:T(8,128)S(1)} %get-tuple-element.75.refs_2_, bf16[3072,128]{1,0:T(8,128)(2,1)S(1)} %collective-permute-done.13.refs_3_), custom_call_target="tpu_custom_call" | custom-call | flops 2097152 | bytes 5509140 | tf_op jit(solution)/shard_map/pallas_call | solution.py:33
  (17 shorter events, 0.0 us)
Async XLA Ops:
  0.6 34.4 %collective-permute-start.2 = (bf16[2,1024,256]{2,1,0:T(8,128)(2,1)}, bf16[2,1024,256]{2,1,0:T(8,128)(2,1)S(1)}, u32[]{:S(2)}, u32[]{:S(2)}) collective-permute-start(bf16[2,1024,256]{2,1,0:T(8,128)(2,1)} %bitcast.17), channel_id=1, source_target_pairs={{8,0},{16,8},{24,16},{9,1},{17,9},{25,17},{10,2},{18,10},{26,18},{... | collective-permute-start | bytes 3145736 | tf_op jit(solution)/shard_map/ppermute | solution.py:428
  4.1 22.4 %collective-permute-start = (bf16[2,128,256]{2,1,0:T(8,128)(2,1)S(1)}, bf16[2,128,256]{2,1,0:T(8,128)(2,1)S(1)}, u32[]{:S(2)}, u32[]{:S(2)}) collective-permute-start(bf16[2,128,256]{2,1,0:T(8,128)(2,1)S(1)} %get-tuple-element.41), channel_id=1, source_target_pairs={{0,1},{1,2},{2,3},{3,4},{4,5},{5,6},{6,7},{8,9},{9,10},{10,11},{11... | collective-permute-start | bytes 393224 | tf_op jit(solution)/shard_map/ppermute | solution.py:428
  8.5 18.1 %collective-permute-start.1 = (bf16[2,128,256]{2,1,0:T(8,128)(2,1)S(1)}, bf16[2,128,256]{2,1,0:T(8,128)(2,1)S(1)}, u32[]{:S(2)}, u32[]{:S(2)}) collective-permute-start(bf16[2,128,256]{2,1,0:T(8,128)(2,1)S(1)} %get-tuple-element.42), channel_id=1, source_target_pairs={{1,0},{2,1},{3,2},{4,3},{5,4},{6,5},{7,6},{9,8},{10,9},{11,10},{12... | collective-permute-start | bytes 393224 | tf_op jit(solution)/shard_map/ppermute | solution.py:428
  9.8 16.8 %all-to-all-start = ((f32[8,8,128]{2,1,0:T(8,128)}), f32[8,8,128]{2,1,0:T(8,128)S(1)}, u32[]{:S(2)}, u32[]{:S(2)}) async-start(f32[8,8,128]{2,1,0:T(8,128)} %get-tuple-element.43), calls=%async_computation | async-start | bytes 65536 | tf_op jit(solution)/shard_map/all_to_all | solution.py:467
  26.6 0.6 copy-start.5
  26.6 0.7 copy-start.6
  26.6 0.7 copy-start.7
  27.3 7.8 %copy-start.1 = (bf16[1,2,8,128,256]{4,3,2,1,0:T(8,128)(2,1)S(1)}, bf16[1,2,8,128,256]{4,3,2,1,0:T(8,128)(2,1)}, u32[]{:S(2)}) copy-start(bf16[1,2,8,128,256]{4,3,2,1,0:T(8,128)(2,1)} %param.5) | copy-start | bytes 3145732
  27.3 7.8 %copy-start.2 = (bf16[3,256,256]{2,1,0:T(8,128)(2,1)S(1)}, bf16[3,256,256]{2,1,0:T(8,128)(2,1)}, u32[]{:S(2)}) copy-start(bf16[3,256,256]{2,1,0:T(8,128)(2,1)} %w_ref.3) | copy-start | bytes 1179652
  36.7 5.1 %copy-start.3 = (bf16[2,1024,256]{2,1,0:T(8,128)(2,1)}, bf16[2,1024,256]{2,1,0:T(8,128)(2,1)S(1)}, u32[]{:S(2)}) copy-start(bf16[2,1024,256]{2,1,0:T(8,128)(2,1)S(1)} %get-tuple-element.52.pg_ref.refs_0_) | copy-start | bytes 3145732
  41.9 5.8 %collective-permute-start.3 = (f32[3072,128]{1,0:T(8,128)S(1)}, f32[3072,128]{1,0:T(8,128)S(1)}, u32[]{:S(2)}, u32[]{:S(2)}) collective-permute-start(f32[3072,128]{1,0:T(8,128)S(1)} %slice.4), channel_id=1, source_target_pairs={{0,32},{32,0},{1,33},{33,1},{2,34},{34,2},{3,35},{35,3},{4,36},{36... | collective-permute-start | bytes 4718600 | tf_op jit(solution)/shard_map/ppermute | solution.py:422
  49.2 16.4 %copy-start.4 = (bf16[2,1024,256]{2,1,0:T(8,128)(2,1)S(1)}, bf16[2,1024,256]{2,1,0:T(8,128)(2,1)}, u32[]{:S(2)}) copy-start(bf16[2,1024,256]{2,1,0:T(8,128)(2,1)} %copy-done.3) | copy-start | bytes 3145732
  49.2 26.8 %all-to-all-start.1 = ((bf16[16,192,128]{2,1,0:T(8,128)(2,1)}), bf16[16,192,128]{2,1,0:T(8,128)(2,1)S(1)}, u32[]{:S(2)}, u32[]{:S(2)}) async-start(bf16[16,192,128]{2,1,0:T(8,128)(2,1)} %bitcast.21), calls=%async_computation.1 | async-start | bytes 1572864 | tf_op jit(solution)/shard_map/all_to_all | solution.py:506
  57.4 4.4 %collective-permute-start.4 = (bf16[2,128,256]{2,1,0:T(8,128)(2,1)S(1)}, bf16[2,128,256]{2,1,0:T(8,128)(2,1)S(1)}, u32[]{:S(2)}, u32[]{:S(2)}) collective-permute-start(bf16[2,128,256]{2,1,0:T(8,128)(2,1)S(1)} %get-tuple-element.53), channel_id=1, source_target_pairs={{0,1},{1,2},{2,3},{3,4},{4,5},{5,6},{6,7},{8,9},{9,10},{10,11},{11... | collective-permute-start | bytes 393224 | tf_op jit(solution)/shard_map/ppermute | solution.py:428
  59.6 6.0 %collective-permute-start.5 = (bf16[2,128,256]{2,1,0:T(8,128)(2,1)S(1)}, bf16[2,128,256]{2,1,0:T(8,128)(2,1)S(1)}, u32[]{:S(2)}, u32[]{:S(2)}) collective-permute-start(bf16[2,128,256]{2,1,0:T(8,128)(2,1)S(1)} %get-tuple-element.54), channel_id=1, source_target_pairs={{1,0},{2,1},{3,2},{4,3},{5,4},{6,5},{7,6},{9,8},{10,9},{11,10},{12... | collective-permute-start | bytes 393224 | tf_op jit(solution)/shard_map/ppermute | solution.py:428
  71.7 24.5 %copy-start = (bf16[1,2,8,128,256]{4,3,2,1,0:T(8,128)(2,1)S(1)}, bf16[1,2,8,128,256]{4,3,2,1,0:T(8,128)(2,1)}, u32[]{:S(2)}) copy-start(bf16[1,2,8,128,256]{4,3,2,1,0:T(8,128)(2,1)} %param.4) | copy-start | bytes 3145732
  71.7 28.5 %collective-permute-start.9 = (bf16[2,1024,256]{2,1,0:T(8,128)(2,1)}, bf16[2,1024,256]{2,1,0:T(8,128)(2,1)}, u32[]{:S(2)}, u32[]{:S(2)}) collective-permute-start(bf16[2,1024,256]{2,1,0:T(8,128)(2,1)} %get-tuple-element.63.hid_ref), channel_id=1, source_target_pairs={{0,8},{8,16},{16,24},{1,9},{9,17},{17,25},{2,10},{10,18},{18,26},{... | collective-permute-start | bytes 3145736 | tf_op jit(solution)/shard_map/ppermute | solution.py:428
  92.7 7.0 %collective-permute-start.8 = (bf16[192,128]{1,0:T(8,128)(2,1)S(1)}, bf16[192,128]{1,0:T(8,128)(2,1)S(1)}, u32[]{:S(2)}, u32[]{:S(2)}) collective-permute-start(bf16[192,128]{1,0:T(8,128)(2,1)S(1)} %get-tuple-element.59), channel_id=1, source_target_pairs={{0,192},{64,0},{128,64},{192,128},{1,193},{65,1},{129,65},{193,129... | collective-permute-start | bytes 147464 | tf_op jit(solution)/shard_map/ppermute | solution.py:434
  95.2 4.5 %collective-permute-start.7 = (bf16[192,128]{1,0:T(8,128)(2,1)S(1)}, bf16[192,128]{1,0:T(8,128)(2,1)S(1)}, u32[]{:S(2)}, u32[]{:S(2)}) collective-permute-start(bf16[192,128]{1,0:T(8,128)(2,1)S(1)} %get-tuple-element.59), channel_id=1, source_target_pairs={{0,128},{64,192},{128,0},{192,64},{1,129},{65,193},{129,1},{193,65... | collective-permute-start | bytes 147464 | tf_op jit(solution)/shard_map/ppermute | solution.py:434
  95.8 4.4 %collective-permute-start.6 = (bf16[192,128]{1,0:T(8,128)(2,1)S(1)}, bf16[192,128]{1,0:T(8,128)(2,1)S(1)}, u32[]{:S(2)}, u32[]{:S(2)}) collective-permute-start(bf16[192,128]{1,0:T(8,128)(2,1)S(1)} %get-tuple-element.59), channel_id=1, source_target_pairs={{0,64},{64,128},{128,192},{192,0},{1,65},{65,129},{129,193},{193,1... | collective-permute-start | bytes 147464 | tf_op jit(solution)/shard_map/ppermute | solution.py:434
  100.2 6.4 %collective-permute-start.12 = (bf16[768,128]{1,0:T(8,128)(2,1)S(1)}, bf16[768,128]{1,0:T(8,128)(2,1)S(1)}, u32[]{:S(2)}, u32[]{:S(2)}) collective-permute-start(bf16[768,128]{1,0:T(8,128)(2,1)S(1)} %pad_maximum_fusion.1), channel_id=1, source_target_pairs={{0,24},{8,0},{16,8},{24,16},{1,25},{9,1},{17,9},{25,17},{2,26},{10... | collective-permute-start | bytes 589832 | tf_op jit(solution)/shard_map/ppermute | solution.py:434
  100.3 6.3 %collective-permute-start.11 = (bf16[768,128]{1,0:T(8,128)(2,1)S(1)}, bf16[768,128]{1,0:T(8,128)(2,1)S(1)}, u32[]{:S(2)}, u32[]{:S(2)}) collective-permute-start(bf16[768,128]{1,0:T(8,128)(2,1)S(1)} %pad_maximum_fusion.1), channel_id=1, source_target_pairs={{0,16},{8,24},{16,0},{24,8},{1,17},{9,25},{17,1},{25,9},{2,18},{10... | collective-permute-start | bytes 589832 | tf_op jit(solution)/shard_map/ppermute | solution.py:434
  102.3 6.2 %collective-permute-start.10 = (bf16[768,128]{1,0:T(8,128)(2,1)S(1)}, bf16[768,128]{1,0:T(8,128)(2,1)S(1)}, u32[]{:S(2)}, u32[]{:S(2)}) collective-permute-start(bf16[768,128]{1,0:T(8,128)(2,1)S(1)} %pad_maximum_fusion.1), channel_id=1, source_target_pairs={{0,8},{8,16},{16,24},{24,0},{1,9},{9,17},{17,25},{25,1},{2,10},{10... | collective-permute-start | bytes 589832 | tf_op jit(solution)/shard_map/ppermute | solution.py:434
  108.6 8.9 %collective-permute-start.13 = (bf16[3072,128]{1,0:T(8,128)(2,1)S(1)}, bf16[3072,128]{1,0:T(8,128)(2,1)S(1)}, u32[]{:S(2)}, u32[]{:S(2)}) collective-permute-start(bf16[3072,128]{1,0:T(8,128)(2,1)S(1)} %pad_maximum_fusion.u_ref), channel_id=1, source_target_pairs={{0,32},{32,0},{1,33},{33,1},{2,34},{34,2},{3,35},{35,3},{4,36},{36... | collective-permute-start | bytes 2359304 | tf_op jit(solution)/shard_map/ppermute | solution.py:422

commit v10 on v9

--- a/solution.py
+++ b/solution.py
@@ -143,17 +143,22 @@
 
 
 def forward_kernel(
-    members, info, x_ref, up_hbm, dn_hbm, st_hbm, w_hbm, act_ref, hid_ref, slope_ref,
-    up_ref, dn_ref, st_ref, w_ref, sems,
+    members, info, x_hbm, up_hbm, dn_hbm, st_hbm, w_hbm, act_ref, hid_ref, slope_ref, far_hbm,
+    up_ref, dn_ref, st_ref, w_ref, x_ref, sems,
 ):
+    fields = [pltpu.make_async_copy(x_hbm.at[f], x_ref.at[f], sems.at[6 + f]) for f in range(2)]
+    fields[0].start()
     weights = pltpu.make_async_copy(w_hbm, w_ref, sems.at[3])
     weights.start()
+    fields[1].start()
     fetched((st_hbm, st_ref), (up_hbm, up_ref), (dn_hbm, dn_ref), sems=sems)
     keep_up = (info[1] > 0).astype(F32)
     keep_dn = (info[2] > 0).astype(F32)
     stats = moments(st_ref, members)
 
     def put(f, line):
+        if line == 0:
+            fields[f].wait()
         mean, inv = stats[f]
         v = up_ref[f] if line == 0 else dn_ref[f] if line == 9 else x_ref[f, line * 128 - 128 : line * 128, :]
         n = (v.astype(F32) - mean) * inv
@@ -177,7 +182,13 @@
         hid_ref[f, at : at + CHUNK, :] = (v * s).astype(BF16)
         slope_ref[f, at : at + CHUNK, :] = s * (1.0 + v * (1.0 - s))
 
+        if at + CHUNK == 1024:
+            far[f].start()
+
+    far = [pltpu.make_async_copy(hid_ref.at[f], far_hbm.at[f], sems.at[4 + f]) for f in range(2)]
     woven(put, conv, weights.wait)
+    for c in far:
+        c.wait()
 
 
 def pregrad_kernel(cot_ref, later_ref, slope_ref, w_ref, pg_ref, top_ref, bot_ref):
@@ -468,19 +479,21 @@
     later = moved(cot, TM, -1)
     up = in_hbm(moved(x_bot, HEIGHT, 1))
     dn = in_hbm(moved(x_top, HEIGHT, -1))
-    act, hid, slope = call(
+    act, hid, slope, hid_far = call(
         lambda *refs: forward_kernel(members, *refs),
-        [out((2, 1280, 768), BF16), out(flat, BF16), out(flat, F32)],
+        [out((2, 1280, 768), BF16), out(flat, BF16), out(flat, F32), out(flat, BF16)],
         [info, in_hbm(x), up, dn, st, in_hbm(w3)],
         9 * gflop,
         smem=1,
-        loose=(2, 3, 4, 5),
+        loose=(1, 2, 3, 4, 5),
+        outside=(3,),
         scratch=[
             pltpu.VMEM(edge.shape, BF16),
             pltpu.VMEM(edge.shape, BF16),
             pltpu.VMEM(small.shape, F32),
             pltpu.VMEM(w3.shape, BF16),
-            pltpu.SemaphoreType.DMA((4,)),
+            pltpu.VMEM(flat, BF16),
+            pltpu.SemaphoreType.DMA((8,)),
         ],
     )
     pg, top, bot = call(
@@ -520,7 +533,7 @@
             pltpu.SemaphoreType.DMA((12,)),
         ],
     )
-    gst, hid_sent = tied((gst, hid))
+    gst, hid_sent = tied((gst, hid_far))
     prev = moved(hid_sent, TM, 1)
     code, gst = tied((code, gst))
     (pieces,) = call(xy_kernel, [out((8, 224, 128), BF16)], [code, gst], 1 << 20)
@@ -534,7 +547,7 @@
     )
     mine = gathered(mine, "y")
     mine, prev, input_grad = tied((mine, prev, input_grad))
-    (block_output,) = call(block_kernel, [out(flat, BF16)], [x, hid, prev, temporal_kernel], 3 * gflop)
+    (block_output,) = call(block_kernel, [out(flat, BF16)], [x, hid_far, prev, temporal_kernel], 3 * gflop)
     mine = gathered(mine, TM)
     mine, block_output = tied((mine, block_output))
     tile = out((8, 128), F32)

time: 122 us -> 120 us (0.984)
  no operation moved by 1% of the time
where the time goes in v10:
time: 120 us
  starting transfers between devices  48.5 us (40%)
  Pallas kernels  36.6 us (30%)
  waiting for transfers between devices  17.3 us (14%)
  blocking collectives  15.3 us (13%)
    pallas_call x12, Pallas kernels, call(): pl.pallas_call(kernel, out_shape=tuple((pltpu.HBM(o.shape, o.dtype) if i...  36.6 us
    all_to_all x1, blocking collectives, body(): pieces = lax.all_to_all(pieces, HEIGHT, 0, 0, tiled=True)  15.3 us
    ppermute x6, starting transfers between devices, moved(): return lax.ppermute(x, axes, route)  15 us
    all_to_all x1, starting transfers between devices, body(): st = in_hbm(lax.all_to_all(st, HEIGHT, 0, 0, tiled=True))  9.85 us
    ppermute x2, starting transfers between devices, swapped(): return lax.ppermute(x, axis, [(0, 1), (1, 0)])  9.73 us
    all_to_all x1, starting transfers between devices, body(): lax.all_to_all(code.reshape(16, 192, 128), (TM, 'y'), 0, 0, tiled=True)  8.14 us
    all_to_all x1, waiting for transfers between devices, body(): st = in_hbm(lax.all_to_all(st, HEIGHT, 0, 0, tiled=True))  6.83 us
    ppermute x6, starting transfers between devices, shifts(): lax.ppermute(m, axis, [(i, (i + d) % n) for i in range(n)])  5.81 us
  transfers between devices with their start and end apart: 16, of which 7 were waited for; matrix products, arithmetic and copies ran while one was open for 0% of the time, Pallas kernels for 22%

profile of v10, /device:TPU:1, one launch (start us, length us, event | category | flops | bytes accessed | tf_op | source)
XLA Modules:
  0.0 119.7 jit_solution(8859633408561669307)
XLA Ops:
  0.6 1.3 %collective-permute-start.2 = (bf16[2,1024,256]{2,1,0:T(8,128)(2,1)}, bf16[2,1024,256]{2,1,0:T(8,128)(2,1)S(1)}, u32[]{:S(2)}, u32[]{:S(2)}) collective-permute-start(bf16[2,1024,256]{2,1,0:T(8,128)(2,1)} %bitcast.17), channel_id=1, source_target_pairs={{8,0},{16,8},{24,16},{9,1},{17,9},{25,17},{10,2},{18,10},{26,18},{... | collective-permute-start | bytes 3145736 | tf_op jit(solution)/shard_map/ppermute | solution.py:439
  1.9 2.2 %shard_map.75 = (f32[8,8,128]{2,1,0:T(8,128)}, bf16[2,128,256]{2,1,0:T(8,128)(2,1)S(1)}, bf16[2,128,256]{2,1,0:T(8,128)(2,1)S(1)}) custom-call(bf16[2,1024,256]{2,1,0:T(8,128)(2,1)} %bitcast.12), custom_call_target="tpu_custom_call" | custom-call | flops 2097152 | bytes 1343488 | tf_op jit(solution)/shard_map/pallas_call | solution.py:33
  4.1 4.4 %collective-permute-start = (bf16[2,128,256]{2,1,0:T(8,128)(2,1)S(1)}, bf16[2,128,256]{2,1,0:T(8,128)(2,1)S(1)}, u32[]{:S(2)}, u32[]{:S(2)}) collective-permute-start(bf16[2,128,256]{2,1,0:T(8,128)(2,1)S(1)} %get-tuple-element.42), channel_id=1, source_target_pairs={{0,1},{1,2},{2,3},{3,4},{4,5},{5,6},{6,7},{8,9},{9,10},{10,11},{11... | collective-permute-start | bytes 393224 | tf_op jit(solution)/shard_map/ppermute | solution.py:439
  8.5 1.3 %collective-permute-start.1 = (bf16[2,128,256]{2,1,0:T(8,128)(2,1)S(1)}, bf16[2,128,256]{2,1,0:T(8,128)(2,1)S(1)}, u32[]{:S(2)}, u32[]{:S(2)}) collective-permute-start(bf16[2,128,256]{2,1,0:T(8,128)(2,1)S(1)} %get-tuple-element.43), channel_id=1, source_target_pairs={{1,0},{2,1},{3,2},{4,3},{5,4},{6,5},{7,6},{9,8},{10,9},{11,10},{12... | collective-permute-start | bytes 393224 | tf_op jit(solution)/shard_map/ppermute | solution.py:439
  9.8 9.8 %all-to-all-start = ((f32[8,8,128]{2,1,0:T(8,128)}), f32[8,8,128]{2,1,0:T(8,128)S(1)}, u32[]{:S(2)}, u32[]{:S(2)}) async-start(f32[8,8,128]{2,1,0:T(8,128)} %get-tuple-element.44), calls=%async_computation | async-start | bytes 65536 | tf_op jit(solution)/shard_map/all_to_all | solution.py:478
  19.6 0.1 stack.23.refs_0_.info
  19.7 6.8 %all-to-all-done.refs_4_.refs_5_.refs_3_ = f32[8,8,128]{2,1,0:T(8,128)S(1)} async-done(((f32[8,8,128]{2,1,0:T(8,128)}), f32[8,8,128]{2,1,0:T(8,128)S(1)}, u32[]{:S(2)}, u32[]{:S(2)}) %all-to-all-start) | async-done | bytes 32800 | tf_op jit(solution)/shard_map/all_to_all | solution.py:478
  26.6 0.0 copy-start.7
  26.6 0.6 copy-done.5
  27.2 0.1 copy-done.6
  27.2 0.0 copy-done.7
  27.3 7.6 %shard_map.76 = (bf16[2,1280,768]{2,1,0:T(8,128)(2,1)S(1)}, bf16[2,1024,256]{2,1,0:T(8,128)(2,1)S(1)}, f32[2,1024,256]{2,1,0:T(8,128)S(1)}, bf16[2,1024,256]{2,1,0:T(8,128)(2,1)}) custom-call(s32[5]{0:T(128)S(1)} %stack.23.refs_0_.info, bf16[2,1024,256]{2,1,0:T(8,128)(2,1)} %bitcast.13, bf16[2,128,256]{2,1,0:T(8,128)(2,1)} %copy-done.6, ...), custom_call_target="tpu_custom_call" | custom-call | flops 2415919104 | bytes 10649620 | tf_op jit(solution)/shard_map/pallas_call | solution.py:33
  34.9 0.0 collective-permute-done.2.later_ref
  34.9 1.6 %shard_map.77 = (bf16[2,1024,256]{2,1,0:T(8,128)(2,1)S(1)}, bf16[2,128,256]{2,1,0:T(8,128)(2,1)S(1)}, bf16[2,128,256]{2,1,0:T(8,128)(2,1)S(1)}) custom-call(bf16[2,1024,256]{2,1,0:T(8,128)(2,1)S(1)} %bitcast.18, bf16[2,1024,256]{2,1,0:T(8,128)(2,1)S(1)} %collective-permute-done.2.later_ref, f32[2,1024,256]{2,1,0:T(8,128)S(1)} %get-tuple-element.46.slope_ref, ...), custom_call_target="tpu_custom_call" | custom-call | flops 805306368 | bytes 5898240 | tf_op jit(solution)/shard_map/pallas_call | solution.py:33
  36.6 0.0 copy-start.3
  36.6 4.0 %shard_map.78.g_ref = f32[6144,128]{1,0:T(8,128)S(1)} custom-call(s32[5]{0:T(128)S(1)} %stack.23.refs_0_.info, bf16[2,1280,768]{2,1,0:T(8,128)(2,1)S(1)} %get-tuple-element.45.act_ref, bf16[2,1024,256]{2,1,0:T(8,128)(2,1)S(1)} %get-tuple-element.53.pg_ref.refs_0_, bf16[2,1024,256]{2,1,0:T(8,128)(2,1)S(1)} %get-tuple-element.48.hid_ref, ...), custom_call_target="tpu_custom_call" | custom-call | flops 3221225472 | bytes 11272212 | tf_op jit(solution)/shard_map/pallas_call | solution.py:33
  40.6 0.1 slice.4
  40.7 2.7 %collective-permute-start.3 = (f32[3072,128]{1,0:T(8,128)S(1)}, f32[3072,128]{1,0:T(8,128)S(1)}, u32[]{:S(2)}, u32[]{:S(2)}) collective-permute-start(f32[3072,128]{1,0:T(8,128)S(1)} %slice.4), channel_id=1, source_target_pairs={{0,32},{32,0},{1,33},{33,1},{2,34},{34,2},{3,35},{35,3},{4,36},{36... | collective-permute-start | bytes 4718600 | tf_op jit(solution)/shard_map/ppermute | solution.py:433
  43.4 3.0 %collective-permute-done.3.got_ref = f32[3072,128]{1,0:T(8,128)S(1)} collective-permute-done((f32[3072,128]{1,0:T(8,128)S(1)}, f32[3072,128]{1,0:T(8,128)S(1)}, u32[]{:S(2)}, u32[]{:S(2)}) %collective-permute-start.3) | collective-permute-done | bytes 1572896 | tf_op jit(solution)/shard_map/ppermute | solution.py:433
  46.5 1.5 %shard_map.79 = bf16[3072,128]{1,0:T(8,128)(2,1)} custom-call(f32[6144,128]{1,0:T(8,128)S(1)} %shard_map.78.g_ref, f32[3072,128]{1,0:T(8,128)S(1)} %collective-permute-done.3.got_ref), custom_call_target="tpu_custom_call" | custom-call | flops 2097152 | bytes 5505024 | tf_op jit(solution)/shard_map/pallas_call | solution.py:33
  48.0 0.0 copy-start.4
  48.0 8.1 %all-to-all-start.1 = ((bf16[16,192,128]{2,1,0:T(8,128)(2,1)}), bf16[16,192,128]{2,1,0:T(8,128)(2,1)S(1)}, u32[]{:S(2)}, u32[]{:S(2)}) async-start(bf16[16,192,128]{2,1,0:T(8,128)(2,1)} %bitcast.21), calls=%async_computation.1 | async-start | bytes 1572864 | tf_op jit(solution)/shard_map/all_to_all | solution.py:519
  56.2 2.2 %collective-permute-start.4 = (bf16[2,128,256]{2,1,0:T(8,128)(2,1)S(1)}, bf16[2,128,256]{2,1,0:T(8,128)(2,1)S(1)}, u32[]{:S(2)}, u32[]{:S(2)}) collective-permute-start(bf16[2,128,256]{2,1,0:T(8,128)(2,1)S(1)} %get-tuple-element.54), channel_id=1, source_target_pairs={{0,1},{1,2},{2,3},{3,4},{4,5},{5,6},{6,7},{8,9},{9,10},{10,11},{11... | collective-permute-start | bytes 393224 | tf_op jit(solution)/shard_map/ppermute | solution.py:439
  58.4 1.5 %collective-permute-start.5 = (bf16[2,128,256]{2,1,0:T(8,128)(2,1)S(1)}, bf16[2,128,256]{2,1,0:T(8,128)(2,1)S(1)}, u32[]{:S(2)}, u32[]{:S(2)}) collective-permute-start(bf16[2,128,256]{2,1,0:T(8,128)(2,1)S(1)} %get-tuple-element.55), channel_id=1, source_target_pairs={{1,0},{2,1},{3,2},{4,3},{5,4},{6,5},{7,6},{9,8},{10,9},{11,10},{12... | collective-permute-start | bytes 393224 | tf_op jit(solution)/shard_map/ppermute | solution.py:439
  59.8 0.7 collective-permute-done.4.refs_1_
  60.5 3.8 %collective-permute-done.5.refs_2_ = bf16[2,128,256]{2,1,0:T(8,128)(2,1)S(1)} collective-permute-done((bf16[2,128,256]{2,1,0:T(8,128)(2,1)S(1)}, bf16[2,128,256]{2,1,0:T(8,128)(2,1)S(1)}, u32[]{:S(2)}, u32[]{:S(2)}) %collective-permute-start.5) | collective-permute-done | bytes 131104 | tf_op jit(solution)/shard_map/ppermute | solution.py:439
  64.4 6.1 %shard_map.80 = (f32[2,1024,256]{2,1,0:T(8,128)}, f32[1,8,128]{2,1,0:T(8,128)S(1)}) custom-call(bf16[2,1024,256]{2,1,0:T(8,128)(2,1)S(1)} %copy-done.4, bf16[2,128,256]{2,1,0:T(8,128)(2,1)S(1)} %collective-permute-done.4.refs_1_, bf16[2,128,256]{2,1,0:T(8,128)(2,1)S(1)} %collective-permute-done.5.refs_2_, bf16[3,3,256,256]{3,2,1,0:T(8,128)(2,1)} %refs_3_.1, ...), custom_call_target="tpu_custom_call" | custom-call | flops 2415919104 | bytes 5672960 | tf_op jit(solution)/shard_map/pallas_call | solution.py:33
  70.5 0.0 copy-start
  70.5 4.4 %collective-permute-start.9 = (bf16[2,1024,256]{2,1,0:T(8,128)(2,1)}, bf16[2,1024,256]{2,1,0:T(8,128)(2,1)}, u32[]{:S(2)}, u32[]{:S(2)}) collective-permute-start(bf16[2,1024,256]{2,1,0:T(8,128)(2,1)} %get-tuple-element.65.hid_ref), channel_id=1, source_target_pairs={{0,8},{8,16},{16,24},{1,9},{9,17},{17,25},{2,10},{10,18},{18,26},{... | collective-permute-start | bytes 3145736 | tf_op jit(solution)/shard_map/ppermute | solution.py:439
  74.9 0.0 all-to-all-done.1.u_ref
  74.9 0.9 shard_map.81
  75.7 15.3 %all_to_all.15.u_ref = bf16[8,224,128]{2,1,0:T(8,128)(2,1)S(1)} all-to-all(bf16[8,224,128]{2,1,0:T(8,128)(2,1)S(1)} %shard_map.81), channel_id=1, replica_groups=mesh['y'=4,'core'=2,'tm'=4,'height'=8] {'height'}, dimensions={0} | all-to-all | bytes 917504 | tf_op jit(solution)/shard_map/all_to_all | solution.py:540
  91.1 0.5 shard_map.82
  91.5 2.5 %collective-permute-start.8 = (bf16[192,128]{1,0:T(8,128)(2,1)S(1)}, bf16[192,128]{1,0:T(8,128)(2,1)S(1)}, u32[]{:S(2)}, u32[]{:S(2)}) collective-permute-start(bf16[192,128]{1,0:T(8,128)(2,1)S(1)} %get-tuple-element.61), channel_id=1, source_target_pairs={{0,192},{64,0},{128,64},{192,128},{1,193},{65,1},{129,65},{193,129... | collective-permute-start | bytes 147464 | tf_op jit(solution)/shard_map/ppermute | solution.py:445
  94.0 0.6 collective-permute-start.7
  94.6 0.4 collective-permute-start.6
  95.0 3.5 %shard_map.83 = bf16[2,1024,256]{2,1,0:T(8,128)(2,1)} custom-call(bf16[2,1024,256]{2,1,0:T(8,128)(2,1)S(1)} %bitcast.15, bf16[2,1024,256]{2,1,0:T(8,128)(2,1)S(1)} %bitcast.20, f32[2,1024,256]{2,1,0:T(8,128)} %get-tuple-element.66.refs_2_, f32[8,8,128]{2,1,0:T(8,128)} %copy-done.5, f32[1,8,128]{2,1,0:T(8,128)S(1)} %get-tuple-element.67.refs_4_), custom_call_target="tpu_custom_call" | custom-call | flops 2097152 | bytes 5279744 | tf_op jit(solution)/shard_map/pallas_call | solution.py:33
  98.5 0.5 collective-permute-done.6
  99.0 0.1 collective-permute-start.12
  99.1 2.0 %collective-permute-start.11 = (bf16[768,128]{1,0:T(8,128)(2,1)S(1)}, bf16[768,128]{1,0:T(8,128)(2,1)S(1)}, u32[]{:S(2)}, u32[]{:S(2)}) collective-permute-start(bf16[768,128]{1,0:T(8,128)(2,1)S(1)} %pad_maximum_fusion.1), channel_id=1, source_target_pairs={{0,16},{8,24},{16,0},{24,8},{1,17},{9,25},{17,1},{25,9},{2,18},{10... | collective-permute-start | bytes 589832 | tf_op jit(solution)/shard_map/ppermute | solution.py:445
  101.1 0.3 collective-permute-start.10
  101.4 4.0 %shard_map.84 = bf16[2,1024,256]{2,1,0:T(8,128)(2,1)} custom-call(bf16[2,1024,256]{2,1,0:T(8,128)(2,1)S(1)} %bitcast.16, bf16[2,1024,256]{2,1,0:T(8,128)(2,1)} %get-tuple-element.65.hid_ref, bf16[2,1024,256]{2,1,0:T(8,128)(2,1)} %collective-permute-done.9.prev_ref, bf16[3,256,256]{2,1,0:T(8,128)(2,1)S(1)} %copy-done.2), custom_call_target="tpu_custom_call" | custom-call | flops 805306368 | bytes 4587520 | tf_op jit(solution)/shard_map/pallas_call | solution.py:33
  105.4 1.9 %collective-permute-done.10 = bf16[768,128]{1,0:T(8,128)(2,1)S(1)} collective-permute-done((bf16[768,128]{1,0:T(8,128)(2,1)S(1)}, bf16[768,128]{1,0:T(8,128)(2,1)S(1)}, u32[]{:S(2)}, u32[]{:S(2)}) %collective-permute-start.10) | collective-permute-done | bytes 196640 | tf_op jit(solution)/shard_map/ppermute | solution.py:445
  107.3 0.1 pad_maximum_fusion.u_ref
  107.4 7.0 %collective-permute-start.13 = (bf16[3072,128]{1,0:T(8,128)(2,1)S(1)}, bf16[3072,128]{1,0:T(8,128)(2,1)S(1)}, u32[]{:S(2)}, u32[]{:S(2)}) collective-permute-start(bf16[3072,128]{1,0:T(8,128)(2,1)S(1)} %pad_maximum_fusion.u_ref), channel_id=1, source_target_pairs={{0,32},{32,0},{1,33},{33,1},{2,34},{34,2},{3,35},{35,3},{4,36},{36... | collective-permute-start | bytes 2359304 | tf_op jit(solution)/shard_map/ppermute | solution.py:433
  114.4 1.4 %shard_map.85 = (f32[3072,128]{1,0:T(8,128)S(1)}, f32[8,128]{1,0:T(8,128)S(1)}) custom-call(s32[5]{0:T(128)S(1)} %stack.23.refs_0_.info, bf16[3072,128]{1,0:T(8,128)(2,1)S(1)} %pad_maximum_fusion.u_ref), custom_call_target="tpu_custom_call" | custom-call | flops 2097152 | bytes 2363412 | tf_op jit(solution)/shard_map/pallas_call | solution.py:33
  115.7 0.5 collective-permute-done.13.refs_3_
  116.3 3.3 %shard_map.86 = (f32[9,256,256]{2,1,0:T(8,128)}, f32[3,256,256]{2,1,0:T(8,128)}) custom-call(s32[5]{0:T(128)S(1)} %stack.23.refs_0_.info, f32[3072,128]{1,0:T(8,128)S(1)} %get-tuple-element.76.refs_1_, f32[8,128]{1,0:T(8,128)S(1)} %get-tuple-element.77.refs_2_, bf16[3072,128]{1,0:T(8,128)(2,1)S(1)} %collective-permute-done.13.refs_3_), custom_call_target="tpu_custom_call" | custom-call | flops 2097152 | bytes 5509140 | tf_op jit(solution)/shard_map/pallas_call | solution.py:33
  (17 shorter events, 0.0 us)
Async XLA Ops:
  0.6 34.3 %collective-permute-start.2 = (bf16[2,1024,256]{2,1,0:T(8,128)(2,1)}, bf16[2,1024,256]{2,1,0:T(8,128)(2,1)S(1)}, u32[]{:S(2)}, u32[]{:S(2)}) collective-permute-start(bf16[2,1024,256]{2,1,0:T(8,128)(2,1)} %bitcast.17), channel_id=1, source_target_pairs={{8,0},{16,8},{24,16},{9,1},{17,9},{25,17},{10,2},{18,10},{26,18},{... | collective-permute-start | bytes 3145736 | tf_op jit(solution)/shard_map/ppermute | solution.py:439
  4.1 22.4 %collective-permute-start = (bf16[2,128,256]{2,1,0:T(8,128)(2,1)S(1)}, bf16[2,128,256]{2,1,0:T(8,128)(2,1)S(1)}, u32[]{:S(2)}, u32[]{:S(2)}) collective-permute-start(bf16[2,128,256]{2,1,0:T(8,128)(2,1)S(1)} %get-tuple-element.42), channel_id=1, source_target_pairs={{0,1},{1,2},{2,3},{3,4},{4,5},{5,6},{6,7},{8,9},{9,10},{10,11},{11... | collective-permute-start | bytes 393224 | tf_op jit(solution)/shard_map/ppermute | solution.py:439
  8.5 18.1 %collective-permute-start.1 = (bf16[2,128,256]{2,1,0:T(8,128)(2,1)S(1)}, bf16[2,128,256]{2,1,0:T(8,128)(2,1)S(1)}, u32[]{:S(2)}, u32[]{:S(2)}) collective-permute-start(bf16[2,128,256]{2,1,0:T(8,128)(2,1)S(1)} %get-tuple-element.43), channel_id=1, source_target_pairs={{1,0},{2,1},{3,2},{4,3},{5,4},{6,5},{7,6},{9,8},{10,9},{11,10},{12... | collective-permute-start | bytes 393224 | tf_op jit(solution)/shard_map/ppermute | solution.py:439
  9.8 16.8 %all-to-all-start = ((f32[8,8,128]{2,1,0:T(8,128)}), f32[8,8,128]{2,1,0:T(8,128)S(1)}, u32[]{:S(2)}, u32[]{:S(2)}) async-start(f32[8,8,128]{2,1,0:T(8,128)} %get-tuple-element.44), calls=%async_computation | async-start | bytes 65536 | tf_op jit(solution)/shard_map/all_to_all | solution.py:478
  26.6 0.6 copy-start.5
  26.6 0.7 copy-start.6
  26.6 0.7 copy-start.7
  27.3 7.6 %copy-start.1 = (bf16[1,2,8,128,256]{4,3,2,1,0:T(8,128)(2,1)S(1)}, bf16[1,2,8,128,256]{4,3,2,1,0:T(8,128)(2,1)}, u32[]{:S(2)}) copy-start(bf16[1,2,8,128,256]{4,3,2,1,0:T(8,128)(2,1)} %param.5) | copy-start | bytes 3145732
  27.3 7.7 %copy-start.2 = (bf16[3,256,256]{2,1,0:T(8,128)(2,1)S(1)}, bf16[3,256,256]{2,1,0:T(8,128)(2,1)}, u32[]{:S(2)}) copy-start(bf16[3,256,256]{2,1,0:T(8,128)(2,1)} %w_ref.3) | copy-start | bytes 1179652
  36.6 4.0 %copy-start.3 = (bf16[2,1024,256]{2,1,0:T(8,128)(2,1)}, bf16[2,1024,256]{2,1,0:T(8,128)(2,1)S(1)}, u32[]{:S(2)}) copy-start(bf16[2,1024,256]{2,1,0:T(8,128)(2,1)S(1)} %get-tuple-element.53.pg_ref.refs_0_) | copy-start | bytes 3145732
  40.7 5.8 %collective-permute-start.3 = (f32[3072,128]{1,0:T(8,128)S(1)}, f32[3072,128]{1,0:T(8,128)S(1)}, u32[]{:S(2)}, u32[]{:S(2)}) collective-permute-start(f32[3072,128]{1,0:T(8,128)S(1)} %slice.4), channel_id=1, source_target_pairs={{0,32},{32,0},{1,33},{33,1},{2,34},{34,2},{3,35},{35,3},{4,36},{36... | collective-permute-start | bytes 4718600 | tf_op jit(solution)/shard_map/ppermute | solution.py:433
  48.0 16.4 %copy-start.4 = (bf16[2,1024,256]{2,1,0:T(8,128)(2,1)S(1)}, bf16[2,1024,256]{2,1,0:T(8,128)(2,1)}, u32[]{:S(2)}) copy-start(bf16[2,1024,256]{2,1,0:T(8,128)(2,1)} %copy-done.3) | copy-start | bytes 3145732
  48.0 26.8 %all-to-all-start.1 = ((bf16[16,192,128]{2,1,0:T(8,128)(2,1)}), bf16[16,192,128]{2,1,0:T(8,128)(2,1)S(1)}, u32[]{:S(2)}, u32[]{:S(2)}) async-start(bf16[16,192,128]{2,1,0:T(8,128)(2,1)} %bitcast.21), calls=%async_computation.1 | async-start | bytes 1572864 | tf_op jit(solution)/shard_map/all_to_all | solution.py:519
  56.2 4.4 %collective-permute-start.4 = (bf16[2,128,256]{2,1,0:T(8,128)(2,1)S(1)}, bf16[2,128,256]{2,1,0:T(8,128)(2,1)S(1)}, u32[]{:S(2)}, u32[]{:S(2)}) collective-permute-start(bf16[2,128,256]{2,1,0:T(8,128)(2,1)S(1)} %get-tuple-element.54), channel_id=1, source_target_pairs={{0,1},{1,2},{2,3},{3,4},{4,5},{5,6},{6,7},{8,9},{9,10},{10,11},{11... | collective-permute-start | bytes 393224 | tf_op jit(solution)/shard_map/ppermute | solution.py:439
  58.4 6.0 %collective-permute-start.5 = (bf16[2,128,256]{2,1,0:T(8,128)(2,1)S(1)}, bf16[2,128,256]{2,1,0:T(8,128)(2,1)S(1)}, u32[]{:S(2)}, u32[]{:S(2)}) collective-permute-start(bf16[2,128,256]{2,1,0:T(8,128)(2,1)S(1)} %get-tuple-element.55), channel_id=1, source_target_pairs={{1,0},{2,1},{3,2},{4,3},{5,4},{6,5},{7,6},{9,8},{10,9},{11,10},{12... | collective-permute-start | bytes 393224 | tf_op jit(solution)/shard_map/ppermute | solution.py:439
  70.5 24.5 %copy-start = (bf16[1,2,8,128,256]{4,3,2,1,0:T(8,128)(2,1)S(1)}, bf16[1,2,8,128,256]{4,3,2,1,0:T(8,128)(2,1)}, u32[]{:S(2)}) copy-start(bf16[1,2,8,128,256]{4,3,2,1,0:T(8,128)(2,1)} %param.4) | copy-start | bytes 3145732
  70.5 28.5 %collective-permute-start.9 = (bf16[2,1024,256]{2,1,0:T(8,128)(2,1)}, bf16[2,1024,256]{2,1,0:T(8,128)(2,1)}, u32[]{:S(2)}, u32[]{:S(2)}) collective-permute-start(bf16[2,1024,256]{2,1,0:T(8,128)(2,1)} %get-tuple-element.65.hid_ref), channel_id=1, source_target_pairs={{0,8},{8,16},{16,24},{1,9},{9,17},{17,25},{2,10},{10,18},{18,26},{... | collective-permute-start | bytes 3145736 | tf_op jit(solution)/shard_map/ppermute | solution.py:439
  91.5 7.0 %collective-permute-start.8 = (bf16[192,128]{1,0:T(8,128)(2,1)S(1)}, bf16[192,128]{1,0:T(8,128)(2,1)S(1)}, u32[]{:S(2)}, u32[]{:S(2)}) collective-permute-start(bf16[192,128]{1,0:T(8,128)(2,1)S(1)} %get-tuple-element.61), channel_id=1, source_target_pairs={{0,192},{64,0},{128,64},{192,128},{1,193},{65,1},{129,65},{193,129... | collective-permute-start | bytes 147464 | tf_op jit(solution)/shard_map/ppermute | solution.py:445
  94.0 4.5 %collective-permute-start.7 = (bf16[192,128]{1,0:T(8,128)(2,1)S(1)}, bf16[192,128]{1,0:T(8,128)(2,1)S(1)}, u32[]{:S(2)}, u32[]{:S(2)}) collective-permute-start(bf16[192,128]{1,0:T(8,128)(2,1)S(1)} %get-tuple-element.61), channel_id=1, source_target_pairs={{0,128},{64,192},{128,0},{192,64},{1,129},{65,193},{129,1},{193,65... | collective-permute-start | bytes 147464 | tf_op jit(solution)/shard_map/ppermute | solution.py:445
  94.6 4.4 %collective-permute-start.6 = (bf16[192,128]{1,0:T(8,128)(2,1)S(1)}, bf16[192,128]{1,0:T(8,128)(2,1)S(1)}, u32[]{:S(2)}, u32[]{:S(2)}) collective-permute-start(bf16[192,128]{1,0:T(8,128)(2,1)S(1)} %get-tuple-element.61), channel_id=1, source_target_pairs={{0,64},{64,128},{128,192},{192,0},{1,65},{65,129},{129,193},{193,1... | collective-permute-start | bytes 147464 | tf_op jit(solution)/shard_map/ppermute | solution.py:445
  99.0 6.4 %collective-permute-start.12 = (bf16[768,128]{1,0:T(8,128)(2,1)S(1)}, bf16[768,128]{1,0:T(8,128)(2,1)S(1)}, u32[]{:S(2)}, u32[]{:S(2)}) collective-permute-start(bf16[768,128]{1,0:T(8,128)(2,1)S(1)} %pad_maximum_fusion.1), channel_id=1, source_target_pairs={{0,24},{8,0},{16,8},{24,16},{1,25},{9,1},{17,9},{25,17},{2,26},{10... | collective-permute-start | bytes 589832 | tf_op jit(solution)/shard_map/ppermute | solution.py:445
  99.1 6.3 %collective-permute-start.11 = (bf16[768,128]{1,0:T(8,128)(2,1)S(1)}, bf16[768,128]{1,0:T(8,128)(2,1)S(1)}, u32[]{:S(2)}, u32[]{:S(2)}) collective-permute-start(bf16[768,128]{1,0:T(8,128)(2,1)S(1)} %pad_maximum_fusion.1), channel_id=1, source_target_pairs={{0,16},{8,24},{16,0},{24,8},{1,17},{9,25},{17,1},{25,9},{2,18},{10... | collective-permute-start | bytes 589832 | tf_op jit(solution)/shard_map/ppermute | solution.py:445
  101.1 6.2 %collective-permute-start.10 = (bf16[768,128]{1,0:T(8,128)(2,1)S(1)}, bf16[768,128]{1,0:T(8,128)(2,1)S(1)}, u32[]{:S(2)}, u32[]{:S(2)}) collective-permute-start(bf16[768,128]{1,0:T(8,128)(2,1)S(1)} %pad_maximum_fusion.1), channel_id=1, source_target_pairs={{0,8},{8,16},{16,24},{24,0},{1,9},{9,17},{17,25},{25,1},{2,10},{10... | collective-permute-start | bytes 589832 | tf_op jit(solution)/shard_map/ppermute | solution.py:445
  107.4 8.9 %collective-permute-start.13 = (bf16[3072,128]{1,0:T(8,128)(2,1)S(1)}, bf16[3072,128]{1,0:T(8,128)(2,1)S(1)}, u32[]{:S(2)}, u32[]{:S(2)}) collective-permute-start(bf16[3072,128]{1,0:T(8,128)(2,1)S(1)} %pad_maximum_fusion.u_ref), channel_id=1, source_target_pairs={{0,32},{32,0},{1,33},{33,1},{2,34},{34,2},{3,35},{35,3},{4,36},{36... | collective-permute-start | bytes 2359304 | tf_op jit(solution)/shard_map/ppermute | solution.py:433

commit v11 on v10

--- a/solution.py
+++ b/solution.py
@@ -89,7 +89,7 @@
     return res
 
 
-CHUNK = 256
+CHUNK = 512
 
 
 def woven(put, conv, ready):
@@ -143,22 +143,17 @@
 
 
 def forward_kernel(
-    members, info, x_hbm, up_hbm, dn_hbm, st_hbm, w_hbm, act_ref, hid_ref, slope_ref, far_hbm,
-    up_ref, dn_ref, st_ref, w_ref, x_ref, sems,
+    members, info, x_ref, up_hbm, dn_hbm, st_hbm, w_hbm, act_ref, hid_ref, slope_ref, far_hbm,
+    up_ref, dn_ref, st_ref, w_ref, sems,
 ):
-    fields = [pltpu.make_async_copy(x_hbm.at[f], x_ref.at[f], sems.at[6 + f]) for f in range(2)]
-    fields[0].start()
     weights = pltpu.make_async_copy(w_hbm, w_ref, sems.at[3])
     weights.start()
-    fields[1].start()
     fetched((st_hbm, st_ref), (up_hbm, up_ref), (dn_hbm, dn_ref), sems=sems)
     keep_up = (info[1] > 0).astype(F32)
     keep_dn = (info[2] > 0).astype(F32)
     stats = moments(st_ref, members)
 
     def put(f, line):
-        if line == 0:
-            fields[f].wait()
         mean, inv = stats[f]
         v = up_ref[f] if line == 0 else dn_ref[f] if line == 9 else x_ref[f, line * 128 - 128 : line * 128, :]
         n = (v.astype(F32) - mean) * inv
@@ -485,15 +480,14 @@
         [info, in_hbm(x), up, dn, st, in_hbm(w3)],
         9 * gflop,
         smem=1,
-        loose=(1, 2, 3, 4, 5),
+        loose=(2, 3, 4, 5),
         outside=(3,),
         scratch=[
             pltpu.VMEM(edge.shape, BF16),
             pltpu.VMEM(edge.shape, BF16),
             pltpu.VMEM(small.shape, F32),
             pltpu.VMEM(w3.shape, BF16),
-            pltpu.VMEM(flat, BF16),
-            pltpu.SemaphoreType.DMA((8,)),
+            pltpu.SemaphoreType.DMA((6,)),
         ],
     )
     pg, top, bot = call(

time: 120 us -> 121 us (level)
  no operation moved by 1% of the time
where the time goes in v11:
time: 121 us; the launch traced here: 120 us
  starting transfers between devices  48.5 us (40%)
  Pallas kernels  37 us (31%)
  waiting for transfers between devices  17.3 us (14%)
  blocking collectives  15.3 us (13%)
    pallas_call x12, Pallas kernels, call(): pl.pallas_call(kernel, out_shape=tuple((pltpu.HBM(o.shape, o.dtype) if i...  37 us
    all_to_all x1, blocking collectives, body(): pieces = lax.all_to_all(pieces, HEIGHT, 0, 0, tiled=True)  15.3 us
    ppermute x6, starting transfers between devices, moved(): return lax.ppermute(x, axes, route)  15 us
    all_to_all x1, starting transfers between devices, body(): st = in_hbm(lax.all_to_all(st, HEIGHT, 0, 0, tiled=True))  9.85 us
    ppermute x2, starting transfers between devices, swapped(): return lax.ppermute(x, axis, [(0, 1), (1, 0)])  9.73 us
    all_to_all x1, starting transfers between devices, body(): lax.all_to_all(code.reshape(16, 192, 128), (TM, 'y'), 0, 0, tiled=True)  8.14 us
    all_to_all x1, waiting for transfers between devices, body(): st = in_hbm(lax.all_to_all(st, HEIGHT, 0, 0, tiled=True))  6.83 us
    ppermute x6, starting transfers between devices, shifts(): lax.ppermute(m, axis, [(i, (i + d) % n) for i in range(n)])  5.84 us
  transfers between devices with their start and end apart: 16, of which 7 were waited for; matrix products, arithmetic and copies ran while one was open for 0% of the time, Pallas kernels for 22%

profile of v11, /device:TPU:1, one launch (start us, length us, event | category | flops | bytes accessed | tf_op | source)
XLA Modules:
  0.0 120.1 jit_solution(6372621164860143930)
XLA Ops:
  0.6 1.3 %collective-permute-start.2 = (bf16[2,1024,256]{2,1,0:T(8,128)(2,1)}, bf16[2,1024,256]{2,1,0:T(8,128)(2,1)S(1)}, u32[]{:S(2)}, u32[]{:S(2)}) collective-permute-start(bf16[2,1024,256]{2,1,0:T(8,128)(2,1)} %bitcast.17), channel_id=1, source_target_pairs={{8,0},{16,8},{24,16},{9,1},{17,9},{25,17},{10,2},{18,10},{26,18},{... | collective-permute-start | bytes 3145736 | tf_op jit(solution)/shard_map/ppermute | solution.py:434
  1.9 2.2 %shard_map.75 = (f32[8,8,128]{2,1,0:T(8,128)}, bf16[2,128,256]{2,1,0:T(8,128)(2,1)S(1)}, bf16[2,128,256]{2,1,0:T(8,128)(2,1)S(1)}) custom-call(bf16[2,1024,256]{2,1,0:T(8,128)(2,1)} %bitcast.12), custom_call_target="tpu_custom_call" | custom-call | flops 2097152 | bytes 1343488 | tf_op jit(solution)/shard_map/pallas_call | solution.py:33
  4.1 4.4 %collective-permute-start = (bf16[2,128,256]{2,1,0:T(8,128)(2,1)S(1)}, bf16[2,128,256]{2,1,0:T(8,128)(2,1)S(1)}, u32[]{:S(2)}, u32[]{:S(2)}) collective-permute-start(bf16[2,128,256]{2,1,0:T(8,128)(2,1)S(1)} %get-tuple-element.42), channel_id=1, source_target_pairs={{0,1},{1,2},{2,3},{3,4},{4,5},{5,6},{6,7},{8,9},{9,10},{10,11},{11... | collective-permute-start | bytes 393224 | tf_op jit(solution)/shard_map/ppermute | solution.py:434
  8.5 1.3 %collective-permute-start.1 = (bf16[2,128,256]{2,1,0:T(8,128)(2,1)S(1)}, bf16[2,128,256]{2,1,0:T(8,128)(2,1)S(1)}, u32[]{:S(2)}, u32[]{:S(2)}) collective-permute-start(bf16[2,128,256]{2,1,0:T(8,128)(2,1)S(1)} %get-tuple-element.43), channel_id=1, source_target_pairs={{1,0},{2,1},{3,2},{4,3},{5,4},{6,5},{7,6},{9,8},{10,9},{11,10},{12... | collective-permute-start | bytes 393224 | tf_op jit(solution)/shard_map/ppermute | solution.py:434
  9.8 9.8 %all-to-all-start = ((f32[8,8,128]{2,1,0:T(8,128)}), f32[8,8,128]{2,1,0:T(8,128)S(1)}, u32[]{:S(2)}, u32[]{:S(2)}) async-start(f32[8,8,128]{2,1,0:T(8,128)} %get-tuple-element.44), calls=%async_computation | async-start | bytes 65536 | tf_op jit(solution)/shard_map/all_to_all | solution.py:473
  19.6 0.1 stack.23.refs_0_.info
  19.7 6.8 %all-to-all-done.refs_4_.refs_5_.refs_3_ = f32[8,8,128]{2,1,0:T(8,128)S(1)} async-done(((f32[8,8,128]{2,1,0:T(8,128)}), f32[8,8,128]{2,1,0:T(8,128)S(1)}, u32[]{:S(2)}, u32[]{:S(2)}) %all-to-all-start) | async-done | bytes 32800 | tf_op jit(solution)/shard_map/all_to_all | solution.py:473
  26.6 0.0 copy-start.7
  26.6 0.6 copy-done.5
  27.2 0.1 copy-done.6
  27.2 0.0 copy-done.7
  27.3 7.8 %shard_map.76 = (bf16[2,1280,768]{2,1,0:T(8,128)(2,1)S(1)}, bf16[2,1024,256]{2,1,0:T(8,128)(2,1)S(1)}, f32[2,1024,256]{2,1,0:T(8,128)S(1)}, bf16[2,1024,256]{2,1,0:T(8,128)(2,1)}) custom-call(s32[5]{0:T(128)S(1)} %stack.23.refs_0_.info, bf16[2,1024,256]{2,1,0:T(8,128)(2,1)} %bitcast.13, bf16[2,128,256]{2,1,0:T(8,128)(2,1)} %copy-done.6, ...), custom_call_target="tpu_custom_call" | custom-call | flops 2415919104 | bytes 10649620 | tf_op jit(solution)/shard_map/pallas_call | solution.py:33
  35.1 1.6 %shard_map.77 = (bf16[2,1024,256]{2,1,0:T(8,128)(2,1)S(1)}, bf16[2,128,256]{2,1,0:T(8,128)(2,1)S(1)}, bf16[2,128,256]{2,1,0:T(8,128)(2,1)S(1)}) custom-call(bf16[2,1024,256]{2,1,0:T(8,128)(2,1)S(1)} %bitcast.18, bf16[2,1024,256]{2,1,0:T(8,128)(2,1)S(1)} %collective-permute-done.2.later_ref, f32[2,1024,256]{2,1,0:T(8,128)S(1)} %get-tuple-element.46.slope_ref, ...), custom_call_target="tpu_custom_call" | custom-call | flops 805306368 | bytes 5898240 | tf_op jit(solution)/shard_map/pallas_call | solution.py:33
  36.8 0.0 copy-start.3
  36.8 4.0 %shard_map.78.g_ref = f32[6144,128]{1,0:T(8,128)S(1)} custom-call(s32[5]{0:T(128)S(1)} %stack.23.refs_0_.info, bf16[2,1280,768]{2,1,0:T(8,128)(2,1)S(1)} %get-tuple-element.45.act_ref, bf16[2,1024,256]{2,1,0:T(8,128)(2,1)S(1)} %get-tuple-element.53.pg_ref.refs_0_, bf16[2,1024,256]{2,1,0:T(8,128)(2,1)S(1)} %get-tuple-element.48.hid_ref, ...), custom_call_target="tpu_custom_call" | custom-call | flops 3221225472 | bytes 11272212 | tf_op jit(solution)/shard_map/pallas_call | solution.py:33
  40.8 0.1 slice.4
  40.9 2.7 %collective-permute-start.3 = (f32[3072,128]{1,0:T(8,128)S(1)}, f32[3072,128]{1,0:T(8,128)S(1)}, u32[]{:S(2)}, u32[]{:S(2)}) collective-permute-start(f32[3072,128]{1,0:T(8,128)S(1)} %slice.4), channel_id=1, source_target_pairs={{0,32},{32,0},{1,33},{33,1},{2,34},{34,2},{3,35},{35,3},{4,36},{36... | collective-permute-start | bytes 4718600 | tf_op jit(solution)/shard_map/ppermute | solution.py:428
  43.7 3.0 %collective-permute-done.3.got_ref = f32[3072,128]{1,0:T(8,128)S(1)} collective-permute-done((f32[3072,128]{1,0:T(8,128)S(1)}, f32[3072,128]{1,0:T(8,128)S(1)}, u32[]{:S(2)}, u32[]{:S(2)}) %collective-permute-start.3) | collective-permute-done | bytes 1572896 | tf_op jit(solution)/shard_map/ppermute | solution.py:428
  46.7 1.5 %shard_map.79 = bf16[3072,128]{1,0:T(8,128)(2,1)} custom-call(f32[6144,128]{1,0:T(8,128)S(1)} %shard_map.78.g_ref, f32[3072,128]{1,0:T(8,128)S(1)} %collective-permute-done.3.got_ref), custom_call_target="tpu_custom_call" | custom-call | flops 2097152 | bytes 5505024 | tf_op jit(solution)/shard_map/pallas_call | solution.py:33
  48.2 0.0 copy-start.4
  48.2 8.1 %all-to-all-start.1 = ((bf16[16,192,128]{2,1,0:T(8,128)(2,1)}), bf16[16,192,128]{2,1,0:T(8,128)(2,1)S(1)}, u32[]{:S(2)}, u32[]{:S(2)}) async-start(bf16[16,192,128]{2,1,0:T(8,128)(2,1)} %bitcast.21), calls=%async_computation.1 | async-start | bytes 1572864 | tf_op jit(solution)/shard_map/all_to_all | solution.py:513
  56.4 2.2 %collective-permute-start.4 = (bf16[2,128,256]{2,1,0:T(8,128)(2,1)S(1)}, bf16[2,128,256]{2,1,0:T(8,128)(2,1)S(1)}, u32[]{:S(2)}, u32[]{:S(2)}) collective-permute-start(bf16[2,128,256]{2,1,0:T(8,128)(2,1)S(1)} %get-tuple-element.54), channel_id=1, source_target_pairs={{0,1},{1,2},{2,3},{3,4},{4,5},{5,6},{6,7},{8,9},{9,10},{10,11},{11... | collective-permute-start | bytes 393224 | tf_op jit(solution)/shard_map/ppermute | solution.py:434
  58.6 1.5 %collective-permute-start.5 = (bf16[2,128,256]{2,1,0:T(8,128)(2,1)S(1)}, bf16[2,128,256]{2,1,0:T(8,128)(2,1)S(1)}, u32[]{:S(2)}, u32[]{:S(2)}) collective-permute-start(bf16[2,128,256]{2,1,0:T(8,128)(2,1)S(1)} %get-tuple-element.55), channel_id=1, source_target_pairs={{1,0},{2,1},{3,2},{4,3},{5,4},{6,5},{7,6},{9,8},{10,9},{11,10},{12... | collective-permute-start | bytes 393224 | tf_op jit(solution)/shard_map/ppermute | solution.py:434
  60.1 0.7 collective-permute-done.4.refs_1_
  60.8 3.8 %collective-permute-done.5.refs_2_ = bf16[2,128,256]{2,1,0:T(8,128)(2,1)S(1)} collective-permute-done((bf16[2,128,256]{2,1,0:T(8,128)(2,1)S(1)}, bf16[2,128,256]{2,1,0:T(8,128)(2,1)S(1)}, u32[]{:S(2)}, u32[]{:S(2)}) %collective-permute-start.5) | collective-permute-done | bytes 131104 | tf_op jit(solution)/shard_map/ppermute | solution.py:434
  64.6 6.2 %shard_map.80 = (f32[2,1024,256]{2,1,0:T(8,128)}, f32[1,8,128]{2,1,0:T(8,128)S(1)}) custom-call(bf16[2,1024,256]{2,1,0:T(8,128)(2,1)S(1)} %copy-done.4, bf16[2,128,256]{2,1,0:T(8,128)(2,1)S(1)} %collective-permute-done.4.refs_1_, bf16[2,128,256]{2,1,0:T(8,128)(2,1)S(1)} %collective-permute-done.5.refs_2_, bf16[3,3,256,256]{3,2,1,0:T(8,128)(2,1)} %refs_3_.1, ...), custom_call_target="tpu_custom_call" | custom-call | flops 2415919104 | bytes 5672960 | tf_op jit(solution)/shard_map/pallas_call | solution.py:33
  70.9 0.0 copy-start
  70.9 4.4 %collective-permute-start.9 = (bf16[2,1024,256]{2,1,0:T(8,128)(2,1)}, bf16[2,1024,256]{2,1,0:T(8,128)(2,1)}, u32[]{:S(2)}, u32[]{:S(2)}) collective-permute-start(bf16[2,1024,256]{2,1,0:T(8,128)(2,1)} %get-tuple-element.65.hid_ref), channel_id=1, source_target_pairs={{0,8},{8,16},{16,24},{1,9},{9,17},{17,25},{2,10},{10,18},{18,26},{... | collective-permute-start | bytes 3145736 | tf_op jit(solution)/shard_map/ppermute | solution.py:434
  75.3 0.9 shard_map.81
  76.1 15.3 %all_to_all.15.u_ref = bf16[8,224,128]{2,1,0:T(8,128)(2,1)S(1)} all-to-all(bf16[8,224,128]{2,1,0:T(8,128)(2,1)S(1)} %shard_map.81), channel_id=1, replica_groups=mesh['y'=4,'core'=2,'tm'=4,'height'=8] {'height'}, dimensions={0} | all-to-all | bytes 917504 | tf_op jit(solution)/shard_map/all_to_all | solution.py:534
  91.4 0.5 shard_map.82
  91.9 2.5 %collective-permute-start.8 = (bf16[192,128]{1,0:T(8,128)(2,1)S(1)}, bf16[192,128]{1,0:T(8,128)(2,1)S(1)}, u32[]{:S(2)}, u32[]{:S(2)}) collective-permute-start(bf16[192,128]{1,0:T(8,128)(2,1)S(1)} %get-tuple-element.61), channel_id=1, source_target_pairs={{0,192},{64,0},{128,64},{192,128},{1,193},{65,1},{129,65},{193,129... | collective-permute-start | bytes 147464 | tf_op jit(solution)/shard_map/ppermute | solution.py:440
  94.4 0.6 collective-permute-start.7
  94.9 0.4 collective-permute-start.6
  95.4 3.5 %shard_map.83 = bf16[2,1024,256]{2,1,0:T(8,128)(2,1)} custom-call(bf16[2,1024,256]{2,1,0:T(8,128)(2,1)S(1)} %bitcast.15, bf16[2,1024,256]{2,1,0:T(8,128)(2,1)S(1)} %bitcast.20, f32[2,1024,256]{2,1,0:T(8,128)} %get-tuple-element.66.refs_2_, f32[8,8,128]{2,1,0:T(8,128)} %copy-done.5, f32[1,8,128]{2,1,0:T(8,128)S(1)} %get-tuple-element.67.refs_4_), custom_call_target="tpu_custom_call" | custom-call | flops 2097152 | bytes 5279744 | tf_op jit(solution)/shard_map/pallas_call | solution.py:33
  98.9 0.4 collective-permute-done.6
  99.4 0.1 collective-permute-start.12
  99.5 2.0 %collective-permute-start.11 = (bf16[768,128]{1,0:T(8,128)(2,1)S(1)}, bf16[768,128]{1,0:T(8,128)(2,1)S(1)}, u32[]{:S(2)}, u32[]{:S(2)}) collective-permute-start(bf16[768,128]{1,0:T(8,128)(2,1)S(1)} %pad_maximum_fusion.1), channel_id=1, source_target_pairs={{0,16},{8,24},{16,0},{24,8},{1,17},{9,25},{17,1},{25,9},{2,18},{10... | collective-permute-start | bytes 589832 | tf_op jit(solution)/shard_map/ppermute | solution.py:440
  101.5 0.3 collective-permute-start.10
  101.7 4.0 %shard_map.84 = bf16[2,1024,256]{2,1,0:T(8,128)(2,1)} custom-call(bf16[2,1024,256]{2,1,0:T(8,128)(2,1)S(1)} %bitcast.16, bf16[2,1024,256]{2,1,0:T(8,128)(2,1)} %get-tuple-element.65.hid_ref, bf16[2,1024,256]{2,1,0:T(8,128)(2,1)} %collective-permute-done.9.prev_ref, bf16[3,256,256]{2,1,0:T(8,128)(2,1)S(1)} %copy-done.2), custom_call_target="tpu_custom_call" | custom-call | flops 805306368 | bytes 4587520 | tf_op jit(solution)/shard_map/pallas_call | solution.py:33
  105.8 0.0 collective-permute-done.12
  105.8 0.0 collective-permute-done.11
  105.8 1.9 %collective-permute-done.10 = bf16[768,128]{1,0:T(8,128)(2,1)S(1)} collective-permute-done((bf16[768,128]{1,0:T(8,128)(2,1)S(1)}, bf16[768,128]{1,0:T(8,128)(2,1)S(1)}, u32[]{:S(2)}, u32[]{:S(2)}) %collective-permute-start.10) | collective-permute-done | bytes 196640 | tf_op jit(solution)/shard_map/ppermute | solution.py:440
  107.7 0.1 pad_maximum_fusion.u_ref
  107.7 7.0 %collective-permute-start.13 = (bf16[3072,128]{1,0:T(8,128)(2,1)S(1)}, bf16[3072,128]{1,0:T(8,128)(2,1)S(1)}, u32[]{:S(2)}, u32[]{:S(2)}) collective-permute-start(bf16[3072,128]{1,0:T(8,128)(2,1)S(1)} %pad_maximum_fusion.u_ref), channel_id=1, source_target_pairs={{0,32},{32,0},{1,33},{33,1},{2,34},{34,2},{3,35},{35,3},{4,36},{36... | collective-permute-start | bytes 2359304 | tf_op jit(solution)/shard_map/ppermute | solution.py:428
  114.7 1.4 %shard_map.85 = (f32[3072,128]{1,0:T(8,128)S(1)}, f32[8,128]{1,0:T(8,128)S(1)}) custom-call(s32[5]{0:T(128)S(1)} %stack.23.refs_0_.info, bf16[3072,128]{1,0:T(8,128)(2,1)S(1)} %pad_maximum_fusion.u_ref), custom_call_target="tpu_custom_call" | custom-call | flops 2097152 | bytes 2363412 | tf_op jit(solution)/shard_map/pallas_call | solution.py:33
  116.1 0.5 collective-permute-done.13.refs_3_
  116.7 3.3 %shard_map.86 = (f32[9,256,256]{2,1,0:T(8,128)}, f32[3,256,256]{2,1,0:T(8,128)}) custom-call(s32[5]{0:T(128)S(1)} %stack.23.refs_0_.info, f32[3072,128]{1,0:T(8,128)S(1)} %get-tuple-element.76.refs_1_, f32[8,128]{1,0:T(8,128)S(1)} %get-tuple-element.77.refs_2_, bf16[3072,128]{1,0:T(8,128)(2,1)S(1)} %collective-permute-done.13.refs_3_), custom_call_target="tpu_custom_call" | custom-call | flops 2097152 | bytes 5509140 | tf_op jit(solution)/shard_map/pallas_call | solution.py:33
  (17 shorter events, 0.0 us)
Async XLA Ops:
  0.6 34.5 %collective-permute-start.2 = (bf16[2,1024,256]{2,1,0:T(8,128)(2,1)}, bf16[2,1024,256]{2,1,0:T(8,128)(2,1)S(1)}, u32[]{:S(2)}, u32[]{:S(2)}) collective-permute-start(bf16[2,1024,256]{2,1,0:T(8,128)(2,1)} %bitcast.17), channel_id=1, source_target_pairs={{8,0},{16,8},{24,16},{9,1},{17,9},{25,17},{10,2},{18,10},{26,18},{... | collective-permute-start | bytes 3145736 | tf_op jit(solution)/shard_map/ppermute | solution.py:434
  4.1 22.4 %collective-permute-start = (bf16[2,128,256]{2,1,0:T(8,128)(2,1)S(1)}, bf16[2,128,256]{2,1,0:T(8,128)(2,1)S(1)}, u32[]{:S(2)}, u32[]{:S(2)}) collective-permute-start(bf16[2,128,256]{2,1,0:T(8,128)(2,1)S(1)} %get-tuple-element.42), channel_id=1, source_target_pairs={{0,1},{1,2},{2,3},{3,4},{4,5},{5,6},{6,7},{8,9},{9,10},{10,11},{11... | collective-permute-start | bytes 393224 | tf_op jit(solution)/shard_map/ppermute | solution.py:434
  8.5 18.1 %collective-permute-start.1 = (bf16[2,128,256]{2,1,0:T(8,128)(2,1)S(1)}, bf16[2,128,256]{2,1,0:T(8,128)(2,1)S(1)}, u32[]{:S(2)}, u32[]{:S(2)}) collective-permute-start(bf16[2,128,256]{2,1,0:T(8,128)(2,1)S(1)} %get-tuple-element.43), channel_id=1, source_target_pairs={{1,0},{2,1},{3,2},{4,3},{5,4},{6,5},{7,6},{9,8},{10,9},{11,10},{12... | collective-permute-start | bytes 393224 | tf_op jit(solution)/shard_map/ppermute | solution.py:434
  9.8 16.8 %all-to-all-start = ((f32[8,8,128]{2,1,0:T(8,128)}), f32[8,8,128]{2,1,0:T(8,128)S(1)}, u32[]{:S(2)}, u32[]{:S(2)}) async-start(f32[8,8,128]{2,1,0:T(8,128)} %get-tuple-element.44), calls=%async_computation | async-start | bytes 65536 | tf_op jit(solution)/shard_map/all_to_all | solution.py:473
  26.6 0.6 copy-start.5
  26.6 0.7 copy-start.6
  26.6 0.7 copy-start.7
  27.3 7.9 %copy-start.1 = (bf16[1,2,8,128,256]{4,3,2,1,0:T(8,128)(2,1)S(1)}, bf16[1,2,8,128,256]{4,3,2,1,0:T(8,128)(2,1)}, u32[]{:S(2)}) copy-start(bf16[1,2,8,128,256]{4,3,2,1,0:T(8,128)(2,1)} %param.5) | copy-start | bytes 3145732
  27.3 7.9 %copy-start.2 = (bf16[3,256,256]{2,1,0:T(8,128)(2,1)S(1)}, bf16[3,256,256]{2,1,0:T(8,128)(2,1)}, u32[]{:S(2)}) copy-start(bf16[3,256,256]{2,1,0:T(8,128)(2,1)} %w_ref.3) | copy-start | bytes 1179652
  36.8 4.0 %copy-start.3 = (bf16[2,1024,256]{2,1,0:T(8,128)(2,1)}, bf16[2,1024,256]{2,1,0:T(8,128)(2,1)S(1)}, u32[]{:S(2)}) copy-start(bf16[2,1024,256]{2,1,0:T(8,128)(2,1)S(1)} %get-tuple-element.53.pg_ref.refs_0_) | copy-start | bytes 3145732
  40.9 5.8 %collective-permute-start.3 = (f32[3072,128]{1,0:T(8,128)S(1)}, f32[3072,128]{1,0:T(8,128)S(1)}, u32[]{:S(2)}, u32[]{:S(2)}) collective-permute-start(f32[3072,128]{1,0:T(8,128)S(1)} %slice.4), channel_id=1, source_target_pairs={{0,32},{32,0},{1,33},{33,1},{2,34},{34,2},{3,35},{35,3},{4,36},{36... | collective-permute-start | bytes 4718600 | tf_op jit(solution)/shard_map/ppermute | solution.py:428
  48.2 16.4 %copy-start.4 = (bf16[2,1024,256]{2,1,0:T(8,128)(2,1)S(1)}, bf16[2,1024,256]{2,1,0:T(8,128)(2,1)}, u32[]{:S(2)}) copy-start(bf16[2,1024,256]{2,1,0:T(8,128)(2,1)} %copy-done.3) | copy-start | bytes 3145732
  48.2 27.0 %all-to-all-start.1 = ((bf16[16,192,128]{2,1,0:T(8,128)(2,1)}), bf16[16,192,128]{2,1,0:T(8,128)(2,1)S(1)}, u32[]{:S(2)}, u32[]{:S(2)}) async-start(bf16[16,192,128]{2,1,0:T(8,128)(2,1)} %bitcast.21), calls=%async_computation.1 | async-start | bytes 1572864 | tf_op jit(solution)/shard_map/all_to_all | solution.py:513
  56.4 4.4 %collective-permute-start.4 = (bf16[2,128,256]{2,1,0:T(8,128)(2,1)S(1)}, bf16[2,128,256]{2,1,0:T(8,128)(2,1)S(1)}, u32[]{:S(2)}, u32[]{:S(2)}) collective-permute-start(bf16[2,128,256]{2,1,0:T(8,128)(2,1)S(1)} %get-tuple-element.54), channel_id=1, source_target_pairs={{0,1},{1,2},{2,3},{3,4},{4,5},{5,6},{6,7},{8,9},{9,10},{10,11},{11... | collective-permute-start | bytes 393224 | tf_op jit(solution)/shard_map/ppermute | solution.py:434
  58.6 6.0 %collective-permute-start.5 = (bf16[2,128,256]{2,1,0:T(8,128)(2,1)S(1)}, bf16[2,128,256]{2,1,0:T(8,128)(2,1)S(1)}, u32[]{:S(2)}, u32[]{:S(2)}) collective-permute-start(bf16[2,128,256]{2,1,0:T(8,128)(2,1)S(1)} %get-tuple-element.55), channel_id=1, source_target_pairs={{1,0},{2,1},{3,2},{4,3},{5,4},{6,5},{7,6},{9,8},{10,9},{11,10},{12... | collective-permute-start | bytes 393224 | tf_op jit(solution)/shard_map/ppermute | solution.py:434
  70.9 24.5 %copy-start = (bf16[1,2,8,128,256]{4,3,2,1,0:T(8,128)(2,1)S(1)}, bf16[1,2,8,128,256]{4,3,2,1,0:T(8,128)(2,1)}, u32[]{:S(2)}) copy-start(bf16[1,2,8,128,256]{4,3,2,1,0:T(8,128)(2,1)} %param.4) | copy-start | bytes 3145732
  70.9 28.5 %collective-permute-start.9 = (bf16[2,1024,256]{2,1,0:T(8,128)(2,1)}, bf16[2,1024,256]{2,1,0:T(8,128)(2,1)}, u32[]{:S(2)}, u32[]{:S(2)}) collective-permute-start(bf16[2,1024,256]{2,1,0:T(8,128)(2,1)} %get-tuple-element.65.hid_ref), channel_id=1, source_target_pairs={{0,8},{8,16},{16,24},{1,9},{9,17},{17,25},{2,10},{10,18},{18,26},{... | collective-permute-start | bytes 3145736 | tf_op jit(solution)/shard_map/ppermute | solution.py:434
  91.9 7.0 %collective-permute-start.8 = (bf16[192,128]{1,0:T(8,128)(2,1)S(1)}, bf16[192,128]{1,0:T(8,128)(2,1)S(1)}, u32[]{:S(2)}, u32[]{:S(2)}) collective-permute-start(bf16[192,128]{1,0:T(8,128)(2,1)S(1)} %get-tuple-element.61), channel_id=1, source_target_pairs={{0,192},{64,0},{128,64},{192,128},{1,193},{65,1},{129,65},{193,129... | collective-permute-start | bytes 147464 | tf_op jit(solution)/shard_map/ppermute | solution.py:440
  94.4 4.5 %collective-permute-start.7 = (bf16[192,128]{1,0:T(8,128)(2,1)S(1)}, bf16[192,128]{1,0:T(8,128)(2,1)S(1)}, u32[]{:S(2)}, u32[]{:S(2)}) collective-permute-start(bf16[192,128]{1,0:T(8,128)(2,1)S(1)} %get-tuple-element.61), channel_id=1, source_target_pairs={{0,128},{64,192},{128,0},{192,64},{1,129},{65,193},{129,1},{193,65... | collective-permute-start | bytes 147464 | tf_op jit(solution)/shard_map/ppermute | solution.py:440
  94.9 4.4 %collective-permute-start.6 = (bf16[192,128]{1,0:T(8,128)(2,1)S(1)}, bf16[192,128]{1,0:T(8,128)(2,1)S(1)}, u32[]{:S(2)}, u32[]{:S(2)}) collective-permute-start(bf16[192,128]{1,0:T(8,128)(2,1)S(1)} %get-tuple-element.61), channel_id=1, source_target_pairs={{0,64},{64,128},{128,192},{192,0},{1,65},{65,129},{129,193},{193,1... | collective-permute-start | bytes 147464 | tf_op jit(solution)/shard_map/ppermute | solution.py:440
  99.4 6.4 %collective-permute-start.12 = (bf16[768,128]{1,0:T(8,128)(2,1)S(1)}, bf16[768,128]{1,0:T(8,128)(2,1)S(1)}, u32[]{:S(2)}, u32[]{:S(2)}) collective-permute-start(bf16[768,128]{1,0:T(8,128)(2,1)S(1)} %pad_maximum_fusion.1), channel_id=1, source_target_pairs={{0,24},{8,0},{16,8},{24,16},{1,25},{9,1},{17,9},{25,17},{2,26},{10... | collective-permute-start | bytes 589832 | tf_op jit(solution)/shard_map/ppermute | solution.py:440
  99.5 6.3 %collective-permute-start.11 = (bf16[768,128]{1,0:T(8,128)(2,1)S(1)}, bf16[768,128]{1,0:T(8,128)(2,1)S(1)}, u32[]{:S(2)}, u32[]{:S(2)}) collective-permute-start(bf16[768,128]{1,0:T(8,128)(2,1)S(1)} %pad_maximum_fusion.1), channel_id=1, source_target_pairs={{0,16},{8,24},{16,0},{24,8},{1,17},{9,25},{17,1},{25,9},{2,18},{10... | collective-permute-start | bytes 589832 | tf_op jit(solution)/shard_map/ppermute | solution.py:440
  101.5 6.2 %collective-permute-start.10 = (bf16[768,128]{1,0:T(8,128)(2,1)S(1)}, bf16[768,128]{1,0:T(8,128)(2,1)S(1)}, u32[]{:S(2)}, u32[]{:S(2)}) collective-permute-start(bf16[768,128]{1,0:T(8,128)(2,1)S(1)} %pad_maximum_fusion.1), channel_id=1, source_target_pairs={{0,8},{8,16},{16,24},{24,0},{1,9},{9,17},{17,25},{25,1},{2,10},{10... | collective-permute-start | bytes 589832 | tf_op jit(solution)/shard_map/ppermute | solution.py:440
  107.7 8.9 %collective-permute-start.13 = (bf16[3072,128]{1,0:T(8,128)(2,1)S(1)}, bf16[3072,128]{1,0:T(8,128)(2,1)S(1)}, u32[]{:S(2)}, u32[]{:S(2)}) collective-permute-start(bf16[3072,128]{1,0:T(8,128)(2,1)S(1)} %pad_maximum_fusion.u_ref), channel_id=1, source_target_pairs={{0,32},{32,0},{1,33},{33,1},{2,34},{34,2},{3,35},{35,3},{4,36},{36... | collective-permute-start | bytes 2359304 | tf_op jit(solution)/shard_map/ppermute | solution.py:428
